TPU v7x, 32 devices: a whole 2x2x4 slice. The times are simulated.
32 devices in a mesh: pipe: 2 (over x), dir: 2 (over core), dp: 8 (over z, y).
Axes of the slice: x: 2, y: 2, z: 4, core: 2. Of those that a mesh axis runs over, the one named last changes fastest.
Arguments:
- chars: int32 [128, 16, 50], P('dp'), may hold values from 0 to 261
- lengths: int32 [128], P('dp'), may hold values from 1 to 16, as said below
- char_emb: float32 [262, 16], replicated, may hold values from -6 to 6
- conv_weight: float32 [112, 2048], P(None, ('dir', 'dp')), may hold values from -0.5 to 0.5
- conv_bias: float32 [2048], replicated, may hold values from -6 to 6
- highway_weight: float32 [2, 2048, 4096], P(None, None, ('dir', 'dp')), may hold values from -0.125 to 0.125
- highway_bias: float32 [2, 4096], replicated, may hold values from -6 to 6
- proj_weight: float32 [2048, 512], P(('dir', 'dp')), may hold values from -0.0625 to 0.0625
- proj_bias: float32 [512], replicated, may hold values from -6 to 6
- gate_weight: float32 [2, 2, 1024, 16384], P('pipe', 'dir', 'dp'), may hold values from -0.1875 to 0.1875
- gate_bias: float32 [2, 2, 16384], P('pipe', 'dir'), may hold values from -6 to 6
- cell_proj: float32 [2, 2, 4096, 512], P('pipe', 'dir', 'dp'), may hold values from -0.1875 to 0.1875
- cotangent: bfloat16 [2, 2, 128, 16, 512], P('pipe', 'dir', 'dp'), may hold values from -6 to 6
Outputs:
- activations: bfloat16 [2, 2, 128, 16, 512], P('pipe', 'dir', 'dp')
- char_emb_grad: float32 [262, 16], replicated
- conv_weight_grad: float32 [112, 2048], P(None, ('pipe', 'dir', 'dp'))
- conv_bias_grad: float32 [2048], replicated
- highway_weight_grad: float32 [2, 2048, 4096], P(None, None, ('pipe', 'dir', 'dp'))
- highway_bias_grad: float32 [2, 4096], replicated
- proj_weight_grad: float32 [2048, 512], P(('pipe', 'dir', 'dp'))
- proj_bias_grad: float32 [512], replicated
- gate_weight_grad: float32 [2, 2, 1024, 16384], P('pipe', 'dir', 'dp')
- gate_bias_grad: float32 [2, 2, 16384], P('pipe', 'dir', 'dp')
- cell_proj_grad: float32 [2, 2, 4096, 512], P('pipe', 'dir', 'dp')
Inputs may be any that keep to these rules, and one draw needn't show every extreme that they name: `lengths`: in each aligned block of 8 sequences (one micro-batch of one index of dp), one sequence has 16 tokens.
All inputs are finite; a program needn't handle non-finite values.
Results may differ from a plain program's by a relative error of at most 0.023.
The roundings to bfloat16 on the way count: a program that leaves them out, or rounds other values in their place, can miss the bound.
Values may be sent and summed in bfloat16 or wider, within the bound.
A program may use at most 1.3125 GiB of HBM per device.

v0:
```python
import math

import jax
import jax.numpy as jnp
from jax import lax
from jax.sharding import PartitionSpec as P

FILTERS = 2048
CDIM = 16
CVOCAB = 262
CHARS = 50
KMAX = 7
MICRO = 2


CLIP_LIMIT = 3.0
MASKED_FILL = -1000000000.0


def shifted(value, axis, steps):
    count = lax.axis_size(axis)
    initial, last = (max(0, -steps), min(count, count - steps))
    return lax.ppermute(value, axis, [(source, source + steps) for source in range(initial, last)])


def soft_clip(value):
    return CLIP_LIMIT * jnp.tanh(value / CLIP_LIMIT)


def silu_slope(value):
    sig = jax.nn.sigmoid(value)
    return sig * (1.0 + value * (1.0 - sig))


def filter_widths(filter_count):
    filter_index = jnp.arange(filter_count, dtype=jnp.int32)
    filter_width = jnp.ones((filter_count,), jnp.int32)
    for doubling in range(6):
        filter_width = filter_width + (filter_index >= filter_count // 64 * (1 << doubling)).astype(
            jnp.int32
        )
    return filter_width


def conv_masks(filter_count):
    filter_width = filter_widths(filter_count)
    offset_rows = jnp.arange(KMAX * CDIM, dtype=jnp.int32) // CDIM
    weight_mask = (offset_rows[:, None] < filter_width[None, :]).astype(jnp.float32)
    valid_place = jnp.arange(CHARS, dtype=jnp.int32)[:, None] <= CHARS - filter_width[None, :]
    return (weight_mask, valid_place)


def make_windows(embedded):
    padded = jnp.pad(embedded, ((0, 0), (0, KMAX - 1), (0, 0)))
    return jnp.concatenate(
        [padded[:, offset : offset + CHARS, :] for offset in range(KMAX)], axis=2
    )


def conv_response(ids_block, table_low, conv_low, valid_place):
    embedded = jnp.take(table_low, ids_block, axis=0)
    windows = make_windows(embedded)
    response = jnp.einsum("bpk,kf->bpf", windows, conv_low, preferred_element_type=jnp.float32)
    return (windows, jnp.where(valid_place[None], response, MASKED_FILL))


def encoder_saved_blank(token_count):
    return (
        jnp.zeros((token_count, FILTERS), jnp.float32),
        jnp.zeros((2, token_count, FILTERS), jnp.float32),
        jnp.zeros((2, token_count, 2 * FILTERS), jnp.float32),
        jnp.zeros((token_count, FILTERS), jnp.float32),
    )


def encoder_grad_blank(model_width):
    return (
        jnp.zeros((CVOCAB, CDIM), jnp.float32),
        jnp.zeros((KMAX * CDIM, FILTERS), jnp.float32),
        jnp.zeros((FILTERS,), jnp.float32),
        jnp.zeros((2, FILTERS, 2 * FILTERS), jnp.float32),
        jnp.zeros((2, 2 * FILTERS), jnp.float32),
        jnp.zeros((FILTERS, model_width), jnp.float32),
        jnp.zeros((model_width,), jnp.float32),
    )


def encode_forward(ids, weights):
    table_low, conv_low, conv_bias, highway_low, highway_bias, proj_low, proj_bias = weights
    token_count = ids.shape[0]
    block_size = math.gcd(token_count, 64)
    valid_place = conv_masks(FILTERS)[1]

    def pool_block(ids_block):
        return jax.nn.logsumexp(
            conv_response(ids_block, table_low, conv_low, valid_place)[1], axis=1
        )

    pooled = lax.map(pool_block, ids.reshape(token_count // block_size, block_size, CHARS)).reshape(
        token_count, FILTERS
    )
    features = jax.nn.silu(pooled + conv_bias)
    layer_inputs = []
    layer_mixed = []
    for layer_index in range(2):
        mixed_pre = (
            jnp.dot(
                features.astype(jnp.bfloat16),
                highway_low[layer_index],
                preferred_element_type=jnp.float32,
            )
            + highway_bias[layer_index]
        )
        layer_inputs.append(features)
        layer_mixed.append(mixed_pre)
        carry_gate = jax.nn.sigmoid(mixed_pre[:, FILTERS:])
        features = carry_gate * features + (1.0 - carry_gate) * jax.nn.silu(mixed_pre[:, :FILTERS])
    encoded = (
        jnp.dot(features.astype(jnp.bfloat16), proj_low, preferred_element_type=jnp.float32)
        + proj_bias
    )
    return (encoded, (pooled, jnp.stack(layer_inputs), jnp.stack(layer_mixed), features))


def encode_backward(ids, weights, saved, grad_encoded):
    table_low, conv_low, conv_bias, highway_low, highway_bias, proj_low, proj_bias = weights
    pooled, layer_inputs, layer_mixed, features = saved
    token_count = ids.shape[0]
    block_size = math.gcd(token_count, 64)
    block_count = token_count // block_size
    weight_mask, valid_place = conv_masks(FILTERS)
    grad_proj = jnp.einsum(
        "tf,td->fd", features.astype(jnp.bfloat16), grad_encoded, preferred_element_type=jnp.float32
    )
    grad_proj_bias = jnp.sum(grad_encoded.astype(jnp.float32), axis=0)
    grad_features = jnp.einsum(
        "td,fd->tf", grad_encoded, proj_low, preferred_element_type=jnp.float32
    )
    grad_highway = [None, None]
    grad_highway_bias = [None, None]
    for layer_index in (1, 0):
        layer_input = layer_inputs[layer_index]
        mixed_pre = layer_mixed[layer_index]
        nonlinear = mixed_pre[:, :FILTERS]
        carry_gate = jax.nn.sigmoid(mixed_pre[:, FILTERS:])
        grad_nonlinear = grad_features * (1.0 - carry_gate) * silu_slope(nonlinear)
        grad_gate = (
            grad_features * (layer_input - jax.nn.silu(nonlinear)) * carry_gate * (1.0 - carry_gate)
        )
        grad_mixed = jnp.concatenate([grad_nonlinear, grad_gate], axis=1).astype(jnp.bfloat16)
        grad_highway[layer_index] = jnp.einsum(
            "tf,tg->fg",
            layer_input.astype(jnp.bfloat16),
            grad_mixed,
            preferred_element_type=jnp.float32,
        )
        grad_highway_bias[layer_index] = jnp.sum(grad_mixed.astype(jnp.float32), axis=0)
        grad_features = grad_features * carry_gate + jnp.einsum(
            "tg,fg->tf", grad_mixed, highway_low[layer_index], preferred_element_type=jnp.float32
        )
    grad_before = grad_features * silu_slope(pooled + conv_bias)
    grad_conv_bias = jnp.sum(grad_before, axis=0)
    vocab_ids = jnp.arange(CVOCAB, dtype=jnp.int32)

    def conv_step(running, packed):
        ids_block, grad_block = packed
        windows, response = conv_response(ids_block, table_low, conv_low, valid_place)
        pool_share = jax.nn.softmax(response, axis=1)
        grad_response = (grad_block[:, None, :] * pool_share).astype(jnp.bfloat16)
        grad_conv = running[0] + jnp.einsum(
            "bpk,bpf->kf", windows, grad_response, preferred_element_type=jnp.float32
        )
        grad_windows = jnp.einsum(
            "bpf,kf->bpk", grad_response, conv_low, preferred_element_type=jnp.float32
        )
        grad_embedded = jnp.zeros((ids_block.shape[0], CHARS + KMAX - 1, CDIM), jnp.float32)
        for offset in range(KMAX):
            grad_embedded = grad_embedded + jnp.pad(
                grad_windows[:, :, offset * CDIM : (offset + 1) * CDIM],
                ((0, 0), (offset, KMAX - 1 - offset), (0, 0)),
            )
        grad_embedded = grad_embedded[:, :CHARS].astype(jnp.bfloat16)
        one_hot = (ids_block[:, :, None] == vocab_ids).astype(jnp.bfloat16)
        grad_table = running[1] + jnp.einsum(
            "bpv,bpc->vc", one_hot, grad_embedded, preferred_element_type=jnp.float32
        )
        return ((grad_conv, grad_table), None)

    start_value = (
        jnp.zeros((KMAX * CDIM, FILTERS), jnp.float32),
        jnp.zeros((CVOCAB, CDIM), jnp.float32),
    )
    (grad_conv, grad_table), _ = lax.scan(
        conv_step,
        start_value,
        (
            ids.reshape(block_count, block_size, CHARS),
            grad_before.reshape(block_count, block_size, FILTERS),
        ),
    )
    return (
        grad_table,
        grad_conv * weight_mask,
        grad_conv_bias,
        jnp.stack(grad_highway),
        jnp.stack(grad_highway_bias),
        grad_proj,
        grad_proj_bias,
    )


def lstm_forward(inputs, gate_low, gate_bias, cell_low):
    row_count, time_steps, model_width = inputs.shape
    cell_count = cell_low.shape[0]
    inputs_low = jnp.transpose(inputs, (1, 0, 2)).astype(jnp.bfloat16)
    input_part = jnp.einsum(
        "trd,dg->trg", inputs_low, gate_low[:model_width], preferred_element_type=jnp.float32
    )
    state_weight = gate_low[model_width:]

    def advance(running, step_input):
        cell_state, hidden_low = running
        gate_values = (
            step_input
            + jnp.dot(hidden_low, state_weight, preferred_element_type=jnp.float32)
            + gate_bias
        )
        in_gate = jax.nn.sigmoid(gate_values[:, :cell_count])
        forget = jax.nn.sigmoid(gate_values[:, cell_count : 2 * cell_count])
        memory = jnp.tanh(gate_values[:, 2 * cell_count : 3 * cell_count])
        out_gate = jax.nn.sigmoid(gate_values[:, 3 * cell_count :])
        raw_cell = in_gate * memory + forget * cell_state
        new_cell = soft_clip(raw_cell)
        emitted = (out_gate * jnp.tanh(new_cell)).astype(jnp.bfloat16)
        projected = jnp.dot(emitted, cell_low, preferred_element_type=jnp.float32)
        hidden = soft_clip(projected)
        activated = jnp.concatenate([in_gate, forget, memory, out_gate], axis=1)
        return (
            (new_cell, hidden.astype(jnp.bfloat16)),
            (hidden, activated, raw_cell, cell_state, emitted, projected, hidden_low),
        )

    start_value = (
        jnp.zeros((row_count, cell_count), jnp.float32),
        jnp.zeros((row_count, model_width), jnp.bfloat16),
    )
    _, traced = lax.scan(advance, start_value, input_part)
    return (jnp.transpose(traced[0], (1, 0, 2)), traced[1:])


def lstm_blank(row_count, time_steps, model_width, cell_count, gate_count):
    return (
        jnp.zeros((row_count, time_steps, model_width), jnp.float32),
        (
            jnp.zeros((time_steps, row_count, gate_count), jnp.float32),
            jnp.zeros((time_steps, row_count, cell_count), jnp.float32),
            jnp.zeros((time_steps, row_count, cell_count), jnp.float32),
            jnp.zeros((time_steps, row_count, cell_count), jnp.bfloat16),
            jnp.zeros((time_steps, row_count, model_width), jnp.float32),
            jnp.zeros((time_steps, row_count, model_width), jnp.bfloat16),
        ),
    )


def lstm_backward(upstream, inputs, saved, gate_low, cell_low):
    activated, raw_cells, prev_cells, emitted, projected, prev_hidden = saved
    row_count, time_steps, model_width = inputs.shape
    cell_count = cell_low.shape[0]
    inputs_low = jnp.transpose(inputs, (1, 0, 2)).astype(jnp.bfloat16)
    grad_output = jnp.transpose(upstream, (1, 0, 2))
    state_weight = gate_low[model_width:]

    def retreat(running, packed):
        grad_cell, grad_recur = running
        grad_out, act_now, raw_cell, prev_cell, proj_now = packed
        total_grad = grad_out + grad_recur
        hidden_ratio = jnp.tanh(proj_now / CLIP_LIMIT)
        grad_proj = (total_grad * (1.0 - hidden_ratio * hidden_ratio)).astype(jnp.bfloat16)
        grad_emit = jnp.einsum("rd,cd->rc", grad_proj, cell_low, preferred_element_type=jnp.float32)
        in_gate = act_now[:, :cell_count]
        forget = act_now[:, cell_count : 2 * cell_count]
        memory = act_now[:, 2 * cell_count : 3 * cell_count]
        out_gate = act_now[:, 3 * cell_count :]
        cell_ratio = jnp.tanh(raw_cell / CLIP_LIMIT)
        squashed = jnp.tanh(CLIP_LIMIT * cell_ratio)
        grad_now = grad_emit * out_gate * (1.0 - squashed * squashed) + grad_cell
        grad_raw = grad_now * (1.0 - cell_ratio * cell_ratio)
        grad_gates = jnp.concatenate(
            [
                grad_raw * memory * in_gate * (1.0 - in_gate),
                grad_raw * prev_cell * forget * (1.0 - forget),
                grad_raw * in_gate * (1.0 - memory * memory),
                grad_emit * squashed * out_gate * (1.0 - out_gate),
            ],
            axis=1,
        ).astype(jnp.bfloat16)
        grad_recur_next = jnp.einsum(
            "rg,dg->rd", grad_gates, state_weight, preferred_element_type=jnp.float32
        )
        return ((grad_raw * forget, grad_recur_next), (grad_gates, grad_proj))

    start_value = (
        jnp.zeros((row_count, cell_count), jnp.float32),
        jnp.zeros((row_count, model_width), jnp.float32),
    )
    _, (grad_gates, grad_proj) = lax.scan(
        retreat,
        start_value,
        (grad_output, activated, raw_cells, prev_cells, projected),
        reverse=True,
    )
    token_count = time_steps * row_count
    stacked = jnp.concatenate([inputs_low, prev_hidden], axis=2).reshape(
        token_count, 2 * model_width
    )
    flat_gates = grad_gates.reshape(token_count, -1)
    grad_gate_weight = jnp.einsum(
        "tk,tg->kg", stacked, flat_gates, preferred_element_type=jnp.float32
    )
    grad_gate_bias = jnp.sum(flat_gates.astype(jnp.float32), axis=0)
    grad_cell_weight = jnp.einsum(
        "tc,td->cd",
        emitted.reshape(token_count, cell_count),
        grad_proj.reshape(token_count, model_width),
        preferred_element_type=jnp.float32,
    )
    grad_inputs = jnp.einsum(
        "trg,dg->rtd", grad_gates, gate_low[:model_width], preferred_element_type=jnp.float32
    )
    return (grad_inputs, (grad_gate_weight, grad_gate_bias, grad_cell_weight))


def local(
    chars,
    lengths,
    char_emb,
    conv_weight,
    conv_bias,
    highway_weight,
    highway_bias,
    proj_weight,
    proj_bias,
    gate_weight,
    gate_bias,
    cell_proj,
    cotangent,
):
    section_index = lax.axis_index("pipe")
    direction = lax.axis_index("dir")
    depth = 1 - section_index
    first_section = section_index == 1
    later_section = (section_index == 0).astype(jnp.float32)
    conv_full, highway_full, proj_full = (
        lax.all_gather(conv_weight.astype(jnp.bfloat16), ("dir", "dp"), axis=1, tiled=True),
        lax.all_gather(highway_weight.astype(jnp.bfloat16), ("dir", "dp"), axis=2, tiled=True),
        lax.all_gather(proj_weight.astype(jnp.bfloat16), ("dir", "dp"), axis=0, tiled=True),
    )
    weight_mask = conv_masks(FILTERS)[0]
    enc_weights = (
        char_emb.astype(jnp.bfloat16),
        conv_full * weight_mask.astype(jnp.bfloat16),
        conv_bias,
        highway_full,
        highway_bias,
        proj_full,
        proj_bias,
    )
    gate_full, cell_full = (
        lax.all_gather(gate_weight[0, 0].astype(jnp.bfloat16), "dp", axis=0, tiled=True),
        lax.all_gather(cell_proj[0, 0].astype(jnp.bfloat16), "dp", axis=0, tiled=True),
    )
    layer_bias = gate_bias[0, 0]
    seq_count, time_steps, char_count = chars.shape
    micro_rows = seq_count // MICRO
    half_rows = micro_rows // 2
    model_width = cell_full.shape[1]
    cell_count = cell_full.shape[0]
    gate_count = gate_full.shape[1]
    half_tokens = half_rows * time_steps
    position = jnp.arange(time_steps, dtype=jnp.int32)[None, :]
    live = position < lengths[:, None]
    live_mask = live.astype(jnp.float32)
    reversed_place = jnp.where(live, lengths[:, None] - 1 - position, position)
    position_order = jnp.where(
        direction == 1, reversed_place, jnp.broadcast_to(position, reversed_place.shape)
    )
    cot_ordered = jnp.take_along_axis(cotangent[0, 0], position_order[:, :, None], axis=1)
    received = jnp.zeros((micro_rows, time_steps, model_width), jnp.bfloat16)
    outputs = jnp.zeros((seq_count, time_steps, model_width), jnp.bfloat16)
    kept_ticks = []
    for tick_index in range(MICRO + 1):
        micro_index = tick_index - depth
        valid_now = (micro_index >= 0) & (micro_index < MICRO)
        micro_slot = jnp.clip(micro_index, 0, MICRO - 1)
        half_start = micro_slot * micro_rows + direction * half_rows
        ids_now = lax.dynamic_slice_in_dim(chars, half_start, half_rows, 0).reshape(
            half_tokens, char_count
        )
        mask_now = lax.dynamic_slice_in_dim(live_mask, micro_slot * micro_rows, micro_rows, 0)
        order_now = lax.dynamic_slice_in_dim(position_order, micro_slot * micro_rows, micro_rows, 0)

        def run_encoder():
            encoded, saved_now = encode_forward(ids_now, enc_weights)
            return (
                encoded.reshape(half_rows, time_steps, model_width).astype(jnp.bfloat16),
                saved_now,
            )

        def skip_encoder():
            return (
                jnp.zeros((half_rows, time_steps, model_width), jnp.bfloat16),
                encoder_saved_blank(half_tokens),
            )

        encoded_half, enc_saved = lax.cond(first_section & valid_now, run_encoder, skip_encoder)
        encoded_all = lax.all_gather(encoded_half, "dir", axis=0, tiled=True)
        encoded_own = jnp.take_along_axis(encoded_all, order_now[:, :, None], axis=1)
        layer_in = jnp.where(
            first_section, encoded_own.astype(jnp.float32), received.astype(jnp.float32)
        )

        def run_layer():
            return lstm_forward(layer_in, gate_full, layer_bias, cell_full)

        def skip_layer():
            return lstm_blank(micro_rows, time_steps, model_width, cell_count, gate_count)

        hidden_seq, lstm_saved = lax.cond(valid_now, run_layer, skip_layer)
        out_low = (mask_now[:, :, None] * (hidden_seq + later_section * layer_in)).astype(
            jnp.bfloat16
        )
        outputs = jnp.where(
            valid_now,
            lax.dynamic_update_slice_in_dim(outputs, out_low, micro_slot * micro_rows, 0),
            outputs,
        )
        received = shifted(out_low, "pipe", -1)
        kept_ticks.append((layer_in, enc_saved, lstm_saved, valid_now, micro_slot))
    dp_size = lax.axis_size("dp")
    enc_grads = encoder_grad_blank(model_width)
    layer_total = (
        jnp.zeros((2 * model_width, gate_count), jnp.float32),
        jnp.zeros((cell_count, model_width), jnp.float32),
        jnp.zeros((gate_count,), jnp.float32),
    )
    layer_shards = (
        jnp.zeros((2 * model_width // dp_size, gate_count), jnp.float32),
        jnp.zeros((cell_count // dp_size, model_width), jnp.float32),
        jnp.zeros((gate_count // dp_size,), jnp.float32),
    )
    grad_received = jnp.zeros((micro_rows, time_steps, model_width), jnp.bfloat16)
    for turn_index in range(MICRO + 1):
        layer_in, enc_saved, lstm_saved, valid_now, micro_slot = kept_ticks[MICRO - turn_index]
        half_start = micro_slot * micro_rows + direction * half_rows
        ids_now = lax.dynamic_slice_in_dim(chars, half_start, half_rows, 0).reshape(
            half_tokens, char_count
        )
        mask_now = lax.dynamic_slice_in_dim(live_mask, micro_slot * micro_rows, micro_rows, 0)
        order_now = lax.dynamic_slice_in_dim(position_order, micro_slot * micro_rows, micro_rows, 0)
        cot_now = lax.dynamic_slice_in_dim(
            cot_ordered, micro_slot * micro_rows, micro_rows, 0
        ).astype(jnp.float32)
        upstream = (cot_now + grad_received.astype(jnp.float32)) * mask_now[:, :, None]

        def run_layer_back():
            return lstm_backward(upstream, layer_in, lstm_saved, gate_full, cell_full)

        def skip_layer_back():
            return (
                jnp.zeros((micro_rows, time_steps, model_width), jnp.float32),
                (
                    jnp.zeros((2 * model_width, gate_count), jnp.float32),
                    jnp.zeros((gate_count,), jnp.float32),
                    jnp.zeros((cell_count, model_width), jnp.float32),
                ),
            )

        grad_lstm_in, step_grads = lax.cond(valid_now, run_layer_back, skip_layer_back)
        grad_full = upstream * later_section + grad_lstm_in
        grad_stored = jnp.take_along_axis(grad_full, order_now[:, :, None], axis=1)
        grad_half = lax.psum_scatter(
            grad_stored.astype(jnp.bfloat16), "dir", scatter_dimension=0, tiled=True
        )

        def run_encoder_back():
            return encode_backward(
                ids_now, enc_weights, enc_saved, grad_half.reshape(half_tokens, model_width)
            )

        def skip_encoder_back():
            return encoder_grad_blank(model_width)

        enc_step = lax.cond(first_section & valid_now, run_encoder_back, skip_encoder_back)
        enc_grads = jax.tree.map(jnp.add, enc_grads, enc_step)
        layer_total = (
            layer_total[0] + step_grads[0],
            layer_total[1] + step_grads[2],
            layer_total[2] + step_grads[1],
        )
        grad_received = shifted(grad_full.astype(jnp.bfloat16), "pipe", 1)
    layer_shards = (
        lax.psum_scatter(
            layer_total[0].astype(jnp.bfloat16), "dp", scatter_dimension=0, tiled=True
        ).astype(jnp.float32),
        lax.psum_scatter(
            layer_total[1].astype(jnp.bfloat16), "dp", scatter_dimension=0, tiled=True
        ).astype(jnp.float32),
        lax.psum_scatter(
            layer_total[2].astype(jnp.bfloat16), "dp", scatter_dimension=0, tiled=True
        ).astype(jnp.float32),
    )
    section_sums = lax.psum((enc_grads[0], enc_grads[2], enc_grads[4], enc_grads[6]), ("dir", "dp"))
    small_sums = (
        lax.psum(section_sums[0].astype(jnp.bfloat16), "pipe").astype(jnp.float32),
        lax.psum(section_sums[1].astype(jnp.bfloat16), "pipe").astype(jnp.float32),
        lax.psum(section_sums[2].astype(jnp.bfloat16), "pipe").astype(jnp.float32),
        lax.psum(section_sums[3].astype(jnp.bfloat16), "pipe").astype(jnp.float32),
    )
    large_shards = (
        lax.psum_scatter(enc_grads[1], ("pipe", "dir", "dp"), scatter_dimension=1, tiled=True),
        lax.psum_scatter(enc_grads[3], ("pipe", "dir", "dp"), scatter_dimension=2, tiled=True),
        lax.psum_scatter(enc_grads[5], ("pipe", "dir", "dp"), scatter_dimension=0, tiled=True),
    )
    activations = jnp.take_along_axis(outputs, position_order[:, :, None], axis=1)[None, None]
    return (
        activations,
        small_sums[0],
        large_shards[0],
        small_sums[1],
        large_shards[1],
        small_sums[2],
        large_shards[2],
        small_sums[3],
        layer_shards[0][None, None],
        layer_shards[2][None, None],
        layer_shards[1][None, None],
    )


def solution(mesh):
    return jax.shard_map(
        local,
        mesh=mesh,
        in_specs=(
            P("dp", None, None),
            P("dp"),
            P(),
            P(None, ("dir", "dp")),
            P(),
            P(None, None, ("dir", "dp")),
            P(),
            P(("dir", "dp"), None),
            P(),
            P("pipe", "dir", "dp", None),
            P("pipe", "dir", None),
            P("pipe", "dir", "dp", None),
            P("pipe", "dir", "dp", None, None),
        ),
        out_specs=(
            P("pipe", "dir", "dp", None, None),
            P(),
            P(None, ("pipe", "dir", "dp")),
            P(),
            P(None, None, ("pipe", "dir", "dp")),
            P(),
            P(("pipe", "dir", "dp"), None),
            P(),
            P("pipe", "dir", "dp", None),
            P("pipe", "dir", "dp"),
            P("pipe", "dir", "dp", None),
        ),
        check_vma=False,
    )
```

profile of v0, /device:TPU:3, one launch (start us, length us, event | category | flops | bytes accessed | tf_op | source)
XLA Modules:
  0.0 5121.5 jit_solution(8843437250346545370)
XLA Ops:
  63.7 170.2 %all-gather.7.cloned.1.call-done = bf16[2,2048,4096]{2,1,0:T(8,128)(2,1)} async-done(((bf16[2,2048,256]{2,1,0:T(8,128)(2,1)}), bf16[2,2048,4096]{2,1,0:T(8,128)(2,1)}) %all-gather.7.cloned.1.call-update) | async-done | bytes 33554448 | tf_op jit(solution)/shard_map/all_gather | solution.py:355
  233.9 67.5 %conditional.12 = (bf16[4,16,512]{2,1,0:T(8,128)(2,1)S(1)}, f32[64,2048]{1,0:T(8,128)}, f32[2,64,2048]{2,1,0:T(8,128)}, f32[2,64,4096]{2,1,0:T(8,128)}, f32[64,2048]{1,0:T(8,128)}) conditional(s32[]{:T(128)} %convert_element_type.871, () %tuple.193, (s32[4,16,50]{2,1,0:T(8,128)}, bf16[262,16]{1,0:T(8,128)(2,1)S(1)}, bf16[112,2048]{1,0:T(8,128)(2,1)S(1)}, ...), branch_computations={%region_0.1_spmd, %region_1.5_spmd} | conditional | flops 3790368768 | bytes 121374792 | solution.py:415
  306.7 639.2 %all-gather.11.cloned.1.call-done = bf16[1,1,1024,16384]{3,2,1,0:T(8,128)(2,1)} async-done(((bf16[1,1,128,16384]{3,2,1,0:T(8,128)(2,1)}), bf16[1,1,1024,16384]{3,2,1,0:T(8,128)(2,1)}) %all-gather.11.cloned.1.call-update) | async-done | bytes 33554448 | tf_op jit(solution)/shard_map/all_gather | solution.py:369
  945.9 229.3 %conditional.13 = (f32[16,8,16384]{2,1,0:T(8,128)}, f32[16,8,4096]{2,1,0:T(8,128)}, f32[16,8,4096]{2,1,0:T(8,128)}, bf16[16,8,4096]{2,1,0:T(8,128)(2,1)}, f32[16...) conditional(s32[]{:T(128)} %convert_element_type.870, () %tuple.192, ...), branch_computations={%region_4.7_spmd, %region_5.10_spmd} | conditional | flops 2316824576 | bytes 102334872 | solution.py:428
  971.7 202.4 %while.160 = (s32[]{:T(128)}, f32[8,4096]{1,0:T(8,128)S(1)}, bf16[8,512]{1,0:T(8,128)(2,1)S(1)}, f32[16,8,512]{2,1,0:T(8,128)}, f32[16,8,16384]{2,1,0:T(8,128)},...) while((s32[]{:T(128)}, f32[8,4096]{1,0:T(8,128)S(1)}, ...), condition=%wide.region_7.9_spmd.clone, body=%wide.region_6.8_spmd.clone.sunk | while | flops 169340928 | bytes 42959064 | solution.py:247
  1181.5 71.7 %conditional.14 = (bf16[4,16,512]{2,1,0:T(8,128)(2,1)S(1)}, f32[64,2048]{1,0:T(8,128)}, f32[2,64,2048]{2,1,0:T(8,128)}, f32[2,64,4096]{2,1,0:T(8,128)}, f32[64,2048]{1,0:T(8,128)}) conditional(s32[]{:T(128)} %convert_element_type.892, () %tuple.197, (s32[4,16,50]{2,1,0:T(8,128)S(1)}, bf16[262,16]{1,0:T(8,128)(2,1)S(1)}, ...), branch_computations={%region_8.11_spmd, %region_9.14_spmd} | conditional | flops 3790368768 | bytes 113408608 | solution.py:415
  1258.8 229.0 %conditional.15 = (f32[16,8,16384]{2,1,0:T(8,128)}, f32[16,8,4096]{2,1,0:T(8,128)}, f32[16,8,4096]{2,1,0:T(8,128)}, bf16[16,8,4096]{2,1,0:T(8,128)(2,1)}, f32[16...) conditional(s32[]{:T(128)} %convert_element_type.891, () %tuple.196, ...), branch_computations={%region_12.15_spmd, %region_13.18_spmd} | conditional | flops 2316824576 | bytes 102465944 | solution.py:428
  1284.2 202.4 %while.161 = (s32[]{:T(128)}, f32[8,4096]{1,0:T(8,128)S(1)}, bf16[8,512]{1,0:T(8,128)(2,1)S(1)}, f32[16,8,512]{2,1,0:T(8,128)}, f32[16,8,16384]{2,1,0:T(8,128)},...) while((s32[]{:T(128)}, f32[8,4096]{1,0:T(8,128)S(1)}, ...), condition=%wide.region_15.17_spmd.clone, body=%wide.region_14.16_spmd.clone.sunk | while | flops 169340928 | bytes 42959064 | solution.py:247
  1549.9 527.1 %collective-permute-done.2 = bf16[8,16,512]{2,1,0:T(8,128)(2,1)S(1)} collective-permute-done((bf16[8,16,512]{2,1,0:T(8,128)(2,1)S(1)}, bf16[8,16,512]{2,1,0:T(8,128)(2,1)S(1)}, u32[]{:S(2)}, u32[]{:S(2)}) %collective-permute-start.2) | collective-permute-done | bytes 131104 | tf_op jit(solution)/shard_map/ppermute | solution.py:23
  2077.1 346.6 %conditional.20 = (f32[1024,16384]{1,0:T(8,128)}, f32[16384]{0:T(1024)S(1)}, f32[8,16,512]{2,1,0:T(8,128)S(1)}, f32[4096,512]{1,0:T(8,128)}) conditional(s32[]{:T(128)} %convert_element_type.891, () %tuple.209, (f32[8,16,512]{2,1,0:T(8,128)S(1)}, bf16[1024,16384]{1,0:T(8,128)(2,1)}, f32[16,8,512]{2,1,0:T(8,128)}, bf16[4096,512]{1,0:T(8,128)(2,1)}, ...), branch_computations={%region_38.43_spmd, %region_39.47_spmd} | conditional | flops 7155032064 | bytes 204513664 | solution.py:478
  2094.5 273.9 %while.169 = (s32[]{:T(128)}, f32[8,4096]{1,0:T(8,128)S(1)}, f32[8,512]{1,0:T(8,128)S(1)}, bf16[16,8,16384]{2,1,0:T(8,128)(2,1)}, bf16[16,8,512]{2,1,0:T(8,128)(...) while((s32[]{:T(128)}, f32[8,4096]{1,0:T(8,128)S(1)}, ...), condition=%wide.region_41.45_spmd.clone, body=%wide.region_40.44_spmd.clone.sunk | while | flops 170942464 | bytes 24731840 | solution.py:306
  2431.0 346.4 %conditional.22 = (f32[1024,16384]{1,0:T(8,128)}, f32[16384]{0:T(1024)S(1)}, f32[8,16,512]{2,1,0:T(8,128)S(1)}, f32[4096,512]{1,0:T(8,128)}) conditional(s32[]{:T(128)} %convert_element_type.870, () %tuple.213, (f32[8,16,512]{2,1,0:T(8,128)S(1)}, bf16[1024,16384]{1,0:T(8,128)(2,1)}, f32[16,8,512]{2,1,0:T(8,128)}, bf16[4096,512]{1,0:T(8,128)(2,1)}, ...), branch_computations={%region_52.57_spmd, %region_53.61_spmd} | conditional | flops 7154966528 | bytes 204120448 | solution.py:478
  2448.3 273.8 %while.170 = (s32[]{:T(128)}, f32[8,4096]{1,0:T(8,128)S(1)}, f32[8,512]{1,0:T(8,128)S(1)}, bf16[16,8,16384]{2,1,0:T(8,128)(2,1)}, bf16[16,8,512]{2,1,0:T(8,128)(...) while((s32[]{:T(128)}, f32[8,4096]{1,0:T(8,128)S(1)}, ...), condition=%wide.region_55.59_spmd.clone, body=%wide.region_54.58_spmd.clone.sunk | while | flops 170942464 | bytes 24731840 | solution.py:306
  2791.2 73.5 %add_convert_fusion = bf16[1024,16384]{1,0:T(8,128)(2,1)} fusion(f32[1024,16384]{1,0:T(8,128)} %get-tuple-element.1523, f32[1024,16384]{1,0:T(8,128)} %get-tuple-element.1521, f32[1024,16384]{1,0:T(8,128)} %get-tuple-element.1522), kind=kLoop, calls=%fused_computation.722 | loop fusion | flops 50331648 | bytes 234881024 | tf_op jit(solution)/shard_map/convert_element_type | solution.py:503
  2901.5 261.3 %conditional.21 = (f32[262,16]{0,1:T(8,128)S(1)}, f32[112,2048]{1,0:T(8,128)}, f32[2048]{0:T(1024)S(1)}, f32[2,4096]{1,0:T(2,128)S(1)}, f32[2048,512]{1,0:T(8,12...) conditional(s32[]{:T(128)} %convert_element_type.892, () %tuple.208, (s32[4,16,50]{2,1,0:T(8,128)S(1)}, ...), branch_computations={%region_44.49_spmd, %region_45.56_spmd} | conditional | flops 9093095424 | bytes 695362752 | solution.py:493
  3053.4 45.6 pad_maximum_fusion.14
  3099.0 63.6 %copy.296 = f32[2,2048,4096]{2,1,0:T(8,128)} copy(f32[2,2048,4096]{1,2,0:T(8,128)} %pad_maximum_fusion.14) | data formatting | bytes 134217728 | tf_op jit(solution)/shard_map/cond | solution.py:493
  3163.4 253.0 %conditional.23 = (f32[262,16]{0,1:T(8,128)S(1)}, f32[112,2048]{1,0:T(8,128)}, f32[2048]{0:T(1024)S(1)}, f32[2,4096]{1,0:T(2,128)S(1)}, f32[2048,512]{1,0:T(8,12...) conditional(s32[]{:T(128)} %convert_element_type.871, () %tuple.212, (s32[4,16,50]{2,1,0:T(8,128)}, ...), branch_computations={%region_58.63_spmd, %region_59.70_spmd} | conditional | flops 9093095424 | bytes 697166656 | solution.py:493
  3307.9 45.9 pad_maximum_fusion.22
  3353.8 62.3 %copy.302 = f32[2,2048,4096]{2,1,0:T(8,128)} copy(f32[2,2048,4096]{1,2,0:T(8,128)} %pad_maximum_fusion.22) | data formatting | bytes 134217728 | tf_op jit(solution)/shard_map/cond | solution.py:493
  3428.1 85.0 %add_add_fusion = f32[2,2048,4096]{2,1,0:T(8,128)} fusion(f32[2,2048,4096]{2,1,0:T(8,128)} %get-tuple-element.2025, f32[2,2048,4096]{2,1,0:T(8,128)} %get-tuple-element.2019, f32[2,2048,4096]{2,1,0:T(8,128)} %get-tuple-element.2022), kind=kLoop, calls=%fused_computation.723 | loop fusion | flops 33554432 | bytes 268435456 | tf_op jit(solution)/shard_map/add | solution.py:494
  3545.7 69.4 %all-reduce.28 = (bf16[262,16]{0,1:T(8,128)(2,1)S(1)}, bf16[2048]{0:T(1024)(128)(2,1)S(1)}, bf16[2,4096]{1,0:T(2,128)(2,1)S(1)}, bf16[512]{0:T(512)(128)(2,1)S(1)}) all-reduce(f32[262,16]{0,1:T(8,128)S(1)} %add_add_fusion.4, f32[2048]{0:T(1024)S(1)} %add_add_fusion.5, ...), channel_id=1, replica_groups=mesh['pipe'=2,'dir'=2,'dp'=8] {'dir','dp'}, use_global_device_ids=true, to_apply=%region_66.71 | all-reduce | flops 14944 | bytes 89664 | tf_op jit(solution)/shard_map/psum | solution.py:512
  3631.9 71.7 %reduce-scatter.19.cloned.1.call-done = f32[64,512]{1,0:T(8,128)} async-done(((f32[2048,512]{1,0:T(8,128)}), f32[64,512]{1,0:T(8,128)}) %reduce-scatter.19.cloned.1.call-update) | async-done | bytes 131088 | tf_op jit(solution)/shard_map/reduce_scatter | solution.py:522
  3703.6 1410.6 %reduce-scatter.17.cloned.1.call-done = f32[2,2048,128]{2,1,0:T(8,128)} async-done(((f32[2,2048,4096]{2,1,0:T(8,128)}), f32[2,2048,128]{2,1,0:T(8,128)}) %reduce-scatter.17.cloned.1.call-update) | async-done | bytes 2097168 | tf_op jit(solution)/shard_map/reduce_scatter | solution.py:521
  (1097 shorter events, 1901.9 us)
Async XLA Ops:
  7.2 56.5 %all-gather.9.cloned.1.call-start = ((), (), s32[]{:S(2)}) async-start(), calls=%async_computation.9 | async-start | bytes 2228224 | tf_op jit(solution)/shard_map/all_gather | solution.py:356
  9.0 224.9 %all-gather.7.cloned.1.call-start = ((), (), s32[]{:S(2)}) async-start(), calls=%async_computation.8 | async-start | bytes 35651584 | tf_op jit(solution)/shard_map/all_gather | solution.py:355
  12.8 293.9 %all-gather.13.cloned.1.call-start = ((), (), s32[]{:S(2)}) async-start(), calls=%async_computation.18 | async-start | bytes 4718592 | tf_op jit(solution)/shard_map/all_gather | solution.py:370
  13.8 932.1 %all-gather.11.cloned.1.call-start = ((), (), s32[]{:S(2)}) async-start(), calls=%async_computation.17 | async-start | bytes 37748736 | tf_op jit(solution)/shard_map/all_gather | solution.py:369
  19.8 2845.1 %reduce-scatter.11.cloned.1.call-start = ((), (), s32[]{:S(2)}) async-start(), calls=%async_computation.10 | async-start | bytes 196608 | tf_op jit(solution)/shard_map/reduce_scatter | solution.py:481
  21.0 1471.3 %copy-start.2 = (bf16[262,16]{1,0:T(8,128)(2,1)}, bf16[262,16]{1,0:T(8,128)(2,1)S(1)}, u32[]{:S(2)}) copy-start(bf16[262,16]{1,0:T(8,128)(2,1)S(1)} %copy.251) | copy-start | bytes 25156
  25.1 1150.9 %copy-start.101 = (f32[8,16]{1,0:T(8,128)}, f32[8,16]{1,0:T(8,128)S(1)}, u32[]{:S(2)}) copy-start(f32[8,16]{1,0:T(8,128)S(1)} %get-tuple-element.2370) | copy-start | bytes 1540
  25.7 1155.8 %copy-start.44 = (s32[4,16,50]{2,1,0:T(8,128)}, s32[4,16,50]{2,1,0:T(8,128)S(1)}, u32[]{:S(2)}) copy-start(s32[4,16,50]{2,1,0:T(8,128)S(1)} %get-tuple-element.2367) | copy-start | bytes 38404
  63.4 1116.2 %copy-start.115 = (pred[16,16]{1,0:T(8,128)(4,1)}, pred[16,16]{1,0:T(8,128)(4,1)S(1)}, u32[]{:S(2)}) copy-start(pred[16,16]{1,0:T(8,128)(4,1)S(1)} %fusion.397) | copy-start | bytes 772
  63.7 1428.6 %copy-start.28 = (bf16[112,2048]{1,0:T(8,128)(2,1)}, bf16[112,2048]{1,0:T(8,128)(2,1)S(1)}, u32[]{:S(2)}) copy-start(bf16[112,2048]{1,0:T(8,128)(2,1)S(1)} %fusion.390) | copy-start | bytes 1376260
  233.9 712.0 %copy-start.33 = (f32[1,1,16384]{2,1,0:T(1,128)S(1)}, f32[1,1,16384]{2,1,0:T(1,128)}, u32[]{:S(2)}) copy-start(f32[1,1,16384]{2,1,0:T(1,128)} %param.67) | copy-start | bytes 196612
  304.7 641.2 %copy-start.42 = (bf16[8,16,512]{2,1,0:T(8,128)(2,1)}, bf16[8,16,512]{2,1,0:T(8,128)(2,1)S(1)}, u32[]{:S(2)}) copy-start(bf16[8,16,512]{2,1,0:T(8,128)(2,1)S(1)} %convert_select_fusion.2) | copy-start | bytes 393220
  1177.7 80.0 %collective-permute-start = (bf16[8,16,512]{2,1,0:T(8,128)(2,1)}, bf16[8,16,512]{2,1,0:T(8,128)(2,1)}, u32[]{:S(2)}, u32[]{:S(2)}) collective-permute-start(bf16[8,16,512]{2,1,0:T(8,128)(2,1)} %get-tuple-element.2217), channel_id=1, source_target_pairs={{16,0},{17,1},{18,2},{19,3},{20,4},{21,5},{22,6},{23,7},{24,8},{25... | collective-permute-start | bytes 393224 | tf_op jit(solution)/shard_map/ppermute | solution.py:23
  1488.6 12.5 collective-permute-start.1
  1547.7 529.2 %collective-permute-start.2 = (bf16[8,16,512]{2,1,0:T(8,128)(2,1)S(1)}, bf16[8,16,512]{2,1,0:T(8,128)(2,1)S(1)}, u32[]{:S(2)}, u32[]{:S(2)}) collective-permute-start(bf16[8,16,512]{2,1,0:T(8,128)(2,1)S(1)} %get-tuple-element.2377), channel_id=1, source_target_pairs={{0,16},{1,17},{2,18},{3,19},{4,20},{5,21},{6,22},{7,23},{8,24},{9,... | collective-permute-start | bytes 393224 | tf_op jit(solution)/shard_map/ppermute | solution.py:23
  1549.8 1351.1 %reduce-scatter.13.cloned.1.call-start = ((), (), s32[]{:S(2)}) async-start(), calls=%async_computation.11 | async-start | bytes 196608 | tf_op jit(solution)/shard_map/reduce_scatter | solution.py:481
  2425.1 5.7 collective-permute-start.3
  2427.2 735.7 %reduce-scatter.15.cloned.1.call-start = ((), (), s32[]{:S(2)}) async-start(), calls=%async_computation.12 | async-start | bytes 196608 | tf_op jit(solution)/shard_map/reduce_scatter | solution.py:481
  2779.5 843.8 %reduce-scatter.23.cloned.1.call-start = ((), (), s32[]{:S(2)}) async-start(), calls=%async_computation.16 | async-start | bytes 4718592 | tf_op jit(solution)/shard_map/reduce_scatter | solution.py:505
  2791.2 834.3 %reduce-scatter.21.cloned.1.call-start = ((), (), s32[]{:S(2)}) async-start(), calls=%async_computation.15 | async-start | bytes 37748736 | tf_op jit(solution)/shard_map/reduce_scatter | solution.py:502
  2864.8 767.1 %reduce-scatter.25.cloned.1.call-start = ((), (), s32[]{:S(2)}) async-start(), calls=%async_computation.19 | async-start | bytes 1081344
  3419.7 284.0 %reduce-scatter.19.cloned.1.call-start = ((), (), s32[]{:S(2)}) async-start(), calls=%async_computation.14 | async-start | bytes 4325376 | tf_op jit(solution)/shard_map/reduce_scatter | solution.py:522
  3428.1 1686.1 %reduce-scatter.17.cloned.1.call-start = ((), (), s32[]{:S(2)}) async-start(), calls=%async_computation.13 | async-start | bytes 69206016 | tf_op jit(solution)/shard_map/reduce_scatter | solution.py:521
  3623.3 1490.9 %copy-start.1 = (bf16[1,1,16,16,512]{4,3,2,1,0:T(8,128)(2,1)S(1)}, bf16[1,1,16,16,512]{4,3,2,1,0:T(8,128)(2,1)}, u32[]{:S(2)}) copy-start(bf16[1,1,16,16,512]{4,3,2,1,0:T(8,128)(2,1)} %param.69) | copy-start | bytes 786436
  (145 other events, 9247.6 us)
Sparse Core Ops, SparseCore 0:
  10.8 44.1 all-gather.8
  57.1 176.7 all-gather.6
  236.0 70.6 all-gather.12
  308.6 637.2 all-gather.10
  1549.9 532.1 reduce-scatter.10
  2427.3 10.2 reduce-scatter.12
  2779.6 10.1 reduce-scatter.14
  2793.5 88.3 reduce-scatter.22
  2886.2 544.5 reduce-scatter.20
  3433.6 125.3 reduce-scatter.24
  3561.9 141.7 reduce-scatter.18
  3706.4 1407.7 reduce-scatter.16
where the time goes:
time: 5140 us; the launch traced here: 5120 us
  waiting for transfers between devices  2820 us (55%)
  matrix products  1060 us (21%)
  other arithmetic  602 us (12%)
  local copies, waits for them, and re-layouts  443 us (9%)
  blocking collectives  146 us (3%)
    reduce_scatter x1, waiting for transfers between devices, local(): lax.psum_scatter(enc_grads[3], ('pipe', 'dir', 'dp'), scatter_dimension=2...  1410 us
    all_gather x1, waiting for transfers between devices, local(): lax.all_gather(gate_weight[0, 0].astype(jnp.bfloat16), 'dp', axis=0, tile...  639 us
    ppermute x4, waiting for transfers between devices, shifted(): lax.ppermute(value, axis, [(source, source + steps) for source in range(i...  531 us
    dot_general x32, matrix products, retreat(): jnp.einsum('rg,dg->rd', grad_gates, state_weight, preferred_element_type=...  326 us
    dot_general x32, matrix products, advance(): jnp.dot(hidden_low, state_weight, preferred_element_type=jnp.float32)  264 us
    all_gather x1, waiting for transfers between devices, local(): lax.all_gather(highway_weight.astype(jnp.bfloat16), ('dir', 'dp'), axis=2...  170 us
    dynamic_update_slice x192, other arithmetic, lstm_forward(): _, traced = lax.scan(advance, start_value, input_part)  138 us
    cond x2, local copies, waits for them, and re-layouts, local(): lax.cond(first_section & valid_now, run_encoder_back, skip_encoder_back)  126 us
  transfers between devices with their start and end apart: 16, of which 7 were waited for; matrix products, arithmetic and copies ran while one was open for 31% of the time, Pallas kernels for 0%

commit v1 on v0

v1 whole, which is shorter than its diff:
```python
import functools
import math

import jax
import jax.numpy as jnp
from jax import lax
from jax.experimental import pallas as pl
from jax.experimental.pallas import tpu as pltpu
from jax.sharding import PartitionSpec as P

FILTERS = 2048
CDIM = 16
CVOCAB = 262
CHARS = 50
KMAX = 7
CLIP_LIMIT = 3.0
MASKED_FILL = -1000000000.0
MESH = pl.DeviceIdType.MESH
BF = jnp.bfloat16
F32 = jnp.float32
ALL = ("pipe", "dir", "dp")


def silu_slope(value):
    sig = jax.nn.sigmoid(value)
    return sig * (1.0 + value * (1.0 - sig))


def filter_widths(filter_count):
    filter_index = jnp.arange(filter_count, dtype=jnp.int32)
    filter_width = jnp.ones((filter_count,), jnp.int32)
    for doubling in range(6):
        filter_width = filter_width + (filter_index >= filter_count // 64 * (1 << doubling)).astype(
            jnp.int32
        )
    return filter_width


def conv_masks(filter_count):
    filter_width = filter_widths(filter_count)
    offset_rows = jnp.arange(KMAX * CDIM, dtype=jnp.int32) // CDIM
    weight_mask = (offset_rows[:, None] < filter_width[None, :]).astype(jnp.float32)
    valid_place = jnp.arange(CHARS, dtype=jnp.int32)[:, None] <= CHARS - filter_width[None, :]
    return (weight_mask, valid_place)


def make_windows(embedded):
    padded = jnp.pad(embedded, ((0, 0), (0, KMAX - 1), (0, 0)))
    return jnp.concatenate(
        [padded[:, offset : offset + CHARS, :] for offset in range(KMAX)], axis=2
    )


def conv_response(ids_block, table_low, conv_low, valid_place):
    embedded = jnp.take(table_low, ids_block, axis=0)
    windows = make_windows(embedded)
    response = jnp.einsum("bpk,kf->bpf", windows, conv_low, preferred_element_type=jnp.float32)
    return (windows, jnp.where(valid_place[None], response, MASKED_FILL))


def over(count, step):
    if count <= 9:
        for off in range(1, count):
            step(off)
    else:
        lax.fori_loop(1, count, lambda off, _: (step(off), 0)[1], 0)


def lstm_kernel(
    n, chunk,
    x_hbm, wx, wh, bias, p, wxt, wht, pt, cot,
    out_ref, dx_ref, x_all, h_all, da_all, e_all, dq_all,
    xbuf, hbuf, dqbuf, gates, cells, ebuf, hown, gscr, escr, dabuf, ucell,
    stage, inbox, stage2, inbox2, relay, gbuf, rown,
    load_sem, ag_send, ag_recv, dq_send, dq_recv, rs_send, rs_recv, dx_send, dx_recv,
    x_send, x_recv, g_send, g_recv, da_sem, st_sem,
):
    steps, _, rows, width = xbuf.shape
    total = n * rows
    cell = cells.shape[2]
    pipe = lax.axis_index("pipe")
    direction = lax.axis_index("dir")
    me = lax.axis_index("dp")
    first = pipe == 1
    second = pipe == 0
    partner = (1 - pipe, direction, me)

    def peer(off):
        return lax.rem(me + off, n)

    barrier = pltpu.get_barrier_semaphore()
    over(n, lambda off: pl.semaphore_signal(
        barrier, inc=1, device_id=(pipe, direction, peer(off)), device_id_type=MESH))
    pl.semaphore_signal(barrier, inc=1, device_id=partner, device_id_type=MESH)

    @pl.when(first)
    def _():
        load = pltpu.make_async_copy(x_hbm, xbuf, load_sem)
        load.start()
        load.wait()

    hbuf[0] = jnp.zeros((n, rows, width), BF)
    cells[0] = jnp.zeros((total, cell), F32)
    pl.semaphore_wait(barrier, n)

    def ag_copy(buf, slot, off):
        out, into = (ag_send, ag_recv) if buf is hbuf else (dq_send, dq_recv)
        return pltpu.make_async_remote_copy(
            src_ref=buf.at[slot, me], dst_ref=buf.at[slot, me],
            send_sem=out.at[off], recv_sem=into.at[off],
            device_id=(pipe, direction, peer(off)), device_id_type=MESH)

    def rs_copy(off):
        return pltpu.make_async_remote_copy(
            src_ref=stage.at[peer(off)], dst_ref=inbox.at[me],
            send_sem=rs_send.at[off], recv_sem=rs_recv.at[off],
            device_id=(pipe, direction, peer(off)), device_id_type=MESH)

    def dx_copy(slot, off):
        return pltpu.make_async_remote_copy(
            src_ref=stage2.at[slot, peer(off)], dst_ref=inbox2.at[slot, me],
            send_sem=dx_send.at[slot, off], recv_sem=dx_recv.at[slot, off],
            device_id=(pipe, direction, peer(off)), device_id_type=MESH)

    def x_copy(t):
        return pltpu.make_async_remote_copy(
            src_ref=hbuf.at[t + 1], dst_ref=xbuf.at[t],
            send_sem=x_send.at[t], recv_sem=x_recv.at[t],
            device_id=partner, device_id_type=MESH)

    def g_copy(t):
        return pltpu.make_async_remote_copy(
            src_ref=relay.at[t], dst_ref=gbuf.at[t],
            send_sem=g_send.at[t], recv_sem=g_recv.at[t],
            device_id=partner, device_id_type=MESH)

    def ag_wait(buf, slot):
        def both(off):
            ag_copy(buf, slot, off).wait_send()
            ag_copy(buf, slot, off).wait_recv()
        over(n, both)

    def rs_wait():
        def both(off):
            rs_copy(off).wait_send()
            rs_copy(off).wait_recv()
        over(n, both)

    def forward(t, _):
        @pl.when(second)
        def _():
            x_copy(t).wait_recv()

        gscr[...] = jnp.dot(
            xbuf[t].reshape(total, width), wx[...], preferred_element_type=F32) + bias[...]

        @pl.when(t > 0)
        def _():
            ag_wait(hbuf, t)

            @pl.when(first)
            def _():
                x_copy(t - 1).start()

        gscr[...] += jnp.dot(
            hbuf[t].reshape(total, width), wh[...], preferred_element_type=F32)

        def rows_step(k, _):
            at = pl.ds(pl.multiple_of(k * chunk, chunk), chunk)
            g = gscr[at, :]
            i = jax.nn.sigmoid(g[:, :cell])
            f = jax.nn.sigmoid(g[:, cell:2 * cell])
            m = jnp.tanh(g[:, 2 * cell:3 * cell])
            o = jax.nn.sigmoid(g[:, 3 * cell:])
            c = 3.0 * jnp.tanh((i * m + f * cells[t, at, :]) * (1.0 / 3.0))
            cells[t + 1, at, :] = c
            ebuf[t, at, :] = (o * jnp.tanh(c)).astype(BF)
            kind = gates.dtype
            gates[t, at, :cell] = i.astype(kind)
            gates[t, at, cell:2 * cell] = f.astype(kind)
            gates[t, at, 2 * cell:3 * cell] = m.astype(kind)
            gates[t, at, 3 * cell:] = o.astype(kind)
            return 0

        lax.fori_loop(0, total // chunk, rows_step, 0)
        q = jnp.dot(ebuf[t], p[...], preferred_element_type=F32)
        stage[...] = q.astype(BF).reshape(n, rows, width)
        over(n, lambda off: rs_copy(off).start())
        inbox[me] = stage[me]
        rs_wait()
        h = 3.0 * jnp.tanh(jnp.sum(inbox[...].astype(F32), axis=0) * (1.0 / 3.0))
        hown[t] = h
        hbuf[t + 1, me] = h.astype(BF)
        over(n, lambda off: ag_copy(hbuf, t + 1, off).start())
        add = jnp.where(second, 1.0, 0.0)
        out_ref[t] = (h + add * xbuf[t, me].astype(F32)).astype(BF)
        return 0

    lax.fori_loop(0, steps, forward, 0)
    ag_wait(hbuf, steps)

    @pl.when(first)
    def _():
        x_copy(steps - 1).start()
        lax.fori_loop(0, steps, lambda t, _: (x_copy(t).wait_send(), 0)[1], 0)

    rown[...] = jnp.zeros((rows, width), F32)
    ucell[...] = jnp.zeros((total, cell), F32)

    def dx_finish(t):
        slot = lax.rem(t, 2)

        def both(off):
            dx_copy(slot, off).wait_send()
            dx_copy(slot, off).wait_recv()
        over(n, both)
        dx = jnp.sum(inbox2[slot].astype(F32), axis=0)
        dx_ref[t] = dx

        @pl.when(second)
        def _():
            relay[t] = (dx + cot[t].astype(F32)).astype(BF)
            g_copy(t).start()

    def da_copy(t):
        slot = lax.rem(t, 2)
        return pltpu.make_async_copy(dabuf.at[slot], da_all.at[t], da_sem.at[slot])

    def backward(k, _):
        t = steps - 1 - k
        slot = lax.rem(t, 2)
        up = rown[...] + cot[t].astype(F32)
        rown[...] = up

        @pl.when(first)
        def _():
            g_copy(t).wait_recv()
            rown[...] = rown[...] + gbuf[t].astype(F32)

        ratio = hown[t] * (1.0 / 3.0)
        dqbuf[t, me] = (rown[...] * (1.0 - ratio * ratio)).astype(BF)
        over(n, lambda off: ag_copy(dqbuf, t, off).start())

        @pl.when(k > 0)
        def _():
            dx_finish(t + 1)

        @pl.when(k > 1)
        def _():
            da_copy(t + 2).wait()

        ag_wait(dqbuf, t)
        escr[...] = jnp.dot(
            dqbuf[t].reshape(total, width), pt[...], preferred_element_type=F32)

        def rows_step(j, _):
            at = pl.ds(pl.multiple_of(j * chunk, chunk), chunk)
            de = escr[at, :]
            i = gates[t, at, :cell].astype(F32)
            f = gates[t, at, cell:2 * cell].astype(F32)
            m = gates[t, at, 2 * cell:3 * cell].astype(F32)
            o = gates[t, at, 3 * cell:].astype(F32)
            c = cells[t + 1, at, :]
            tc = jnp.tanh(c)
            cr = c * (1.0 / 3.0)
            dc = (de * o * (1.0 - tc * tc) + ucell[at, :]) * (1.0 - cr * cr)
            ucell[at, :] = dc * f
            dabuf[slot, at, :cell] = (dc * m * i * (1.0 - i)).astype(BF)
            dabuf[slot, at, cell:2 * cell] = (dc * cells[t, at, :] * f * (1.0 - f)).astype(BF)
            dabuf[slot, at, 2 * cell:3 * cell] = (dc * i * (1.0 - m * m)).astype(BF)
            dabuf[slot, at, 3 * cell:] = (de * tc * o * (1.0 - o)).astype(BF)
            return 0

        lax.fori_loop(0, total // chunk, rows_step, 0)
        r = jnp.dot(dabuf[slot], wht[...], preferred_element_type=F32)
        stage[...] = r.astype(BF).reshape(n, rows, width)
        over(n, lambda off: rs_copy(off).start())
        inbox[me] = stage[me]
        dx = jnp.dot(dabuf[slot], wxt[...], preferred_element_type=F32)
        stage2[slot] = dx.astype(BF).reshape(n, rows, width)
        over(n, lambda off: dx_copy(slot, off).start())
        inbox2[slot, me] = stage2[slot, me]
        da_copy(t).start()
        rs_wait()
        rown[...] = jnp.sum(inbox[...].astype(F32), axis=0)
        return 0

    lax.fori_loop(0, steps, backward, 0)
    dx_finish(0)

    @pl.when(second)
    def _():
        lax.fori_loop(0, steps, lambda t, _: (g_copy(t).wait_send(), 0)[1], 0)

    da_copy(1).wait()
    da_copy(0).wait()
    for at, (buf, dst) in enumerate(((xbuf, x_all), (hbuf.at[pl.ds(0, steps)], h_all),
                                     (ebuf, e_all), (dqbuf, dq_all))):
        pltpu.make_async_copy(buf, dst, st_sem.at[at]).start()
    for at, (buf, dst) in enumerate(((xbuf, x_all), (hbuf.at[pl.ds(0, steps)], h_all),
                                     (ebuf, e_all), (dqbuf, dq_all))):
        pltpu.make_async_copy(buf, dst, st_sem.at[at]).wait()


def lstm_call(n, x, wx, wh, bias, p, wxt, wht, pt, cot, chunk=16):
    steps, _, rows, width = x.shape
    cell = p.shape[0]
    total = n * rows
    sds = jax.ShapeDtypeStruct
    vm = pl.BlockSpec(memory_space=pltpu.VMEM)
    hb = pl.BlockSpec(memory_space=pl.ANY)
    keep = F32 if n <= 8 else BF
    V = pltpu.VMEM
    dma = pltpu.SemaphoreType.DMA
    return pl.pallas_call(
        functools.partial(lstm_kernel, n, chunk),
        out_shape=(
            sds((steps, rows, width), BF), sds((steps, rows, width), F32),
            sds((steps, n, rows, width), BF), sds((steps, n, rows, width), BF),
            sds((steps, total, 4 * cell), BF), sds((steps, total, cell), BF),
            sds((steps, n, rows, width), BF)),
        in_specs=[hb] + [vm] * 8,
        out_specs=(vm, vm, hb, hb, hb, hb, hb),
        scratch_shapes=[
            V((steps, n, rows, width), BF), V((steps + 1, n, rows, width), BF),
            V((steps, n, rows, width), BF), V((steps, total, 4 * cell), keep),
            V((steps + 1, total, cell), F32), V((steps, total, cell), BF),
            V((steps, rows, width), F32), V((total, 4 * cell), F32),
            V((total, cell), F32), V((2, total, 4 * cell), BF), V((total, cell), F32),
            V((n, rows, width), BF), V((n, rows, width), BF),
            V((2, n, rows, width), BF), V((2, n, rows, width), BF),
            V((steps, rows, width), BF), V((steps, rows, width), BF), V((rows, width), F32),
            dma, dma((n,)), dma((n,)), dma((n,)), dma((n,)), dma((n,)), dma((n,)), dma((2, n)), dma((2, n)),
            dma((steps,)), dma((steps,)), dma((steps,)), dma((steps,)), dma((2,)), dma((4,)),
        ],
        compiler_params=pltpu.CompilerParams(
            collective_id=0, has_side_effects=True, vmem_limit_bytes=60 * 1024 * 1024),
        name="relay_lstm",
    )(x, wx, wh, bias, p, wxt, wht, pt, cot)


def exchange(blocks, axis):
    count = lax.axis_size(axis)
    me = lax.axis_index(axis)
    got = jnp.zeros_like(blocks)
    got = lax.dynamic_update_index_in_dim(
        got, lax.dynamic_index_in_dim(blocks, me, 0, keepdims=False), me, 0
    )
    for off in range(1, count):
        sent = lax.dynamic_index_in_dim(blocks, (me + off) % count, 0, keepdims=False)
        came = lax.ppermute(sent, axis, [(i, (i + off) % count) for i in range(count)])
        got = lax.dynamic_update_index_in_dim(got, came, (me - off) % count, 0)
    return got


def encode_forward(ids, weights):
    table_low, conv_low, conv_bias, highway_low, highway_bias, proj_low, proj_bias = weights
    valid_place = conv_masks(FILTERS)[1]
    pooled = jax.nn.logsumexp(conv_response(ids, table_low, conv_low, valid_place)[1], axis=1)
    features = jax.nn.silu(pooled + conv_bias)
    kept = [features]
    mixed = []
    for layer in range(2):
        pre = (
            jnp.dot(features.astype(BF), highway_low[layer], preferred_element_type=F32)
            + highway_bias[layer]
        )
        mixed.append(pre)
        gate = jax.nn.sigmoid(pre[:, FILTERS:])
        features = gate * features + (1.0 - gate) * jax.nn.silu(pre[:, :FILTERS])
        kept.append(features)
    encoded = jnp.dot(features.astype(BF), proj_low, preferred_element_type=F32) + proj_bias
    return encoded, pooled, kept, mixed


def to_columns(value):
    count = lax.axis_size(ALL)
    tokens, columns = value.shape
    split = jnp.transpose(value.reshape(tokens, count, columns // count), (1, 0, 2))
    return lax.all_to_all(split, ALL, 0, 0).reshape(count * tokens, columns // count)


def conv_backward(ids, table_low, conv_low, grad_before):
    weight_mask, valid_place = conv_masks(FILTERS)
    windows, response = conv_response(ids, table_low, conv_low, valid_place)
    share = jax.nn.softmax(response, axis=1)
    grad_response = (grad_before[:, None, :] * share).astype(BF)
    grad_conv = jnp.einsum("bpk,bpf->kf", windows, grad_response, preferred_element_type=F32)
    grad_windows = jnp.einsum("bpf,kf->bpk", grad_response, conv_low, preferred_element_type=F32)
    grad_embedded = jnp.zeros((ids.shape[0], CHARS + KMAX - 1, CDIM), F32)
    for offset in range(KMAX):
        grad_embedded = grad_embedded + jnp.pad(
            grad_windows[:, :, offset * CDIM : (offset + 1) * CDIM],
            ((0, 0), (offset, KMAX - 1 - offset), (0, 0)),
        )
    grad_embedded = grad_embedded[:, :CHARS].astype(BF)
    one_hot = (ids[:, :, None] == jnp.arange(CVOCAB, dtype=jnp.int32)).astype(BF)
    grad_table = jnp.einsum("bpv,bpc->vc", one_hot, grad_embedded, preferred_element_type=F32)
    return grad_conv * weight_mask, grad_table


def local(
    chars,
    lengths,
    char_emb,
    conv_weight,
    conv_bias,
    highway_weight,
    highway_bias,
    proj_weight,
    proj_bias,
    gate_weight,
    gate_bias,
    cell_proj,
    cotangent,
):
    n = lax.axis_size("dp")
    pipe = lax.axis_index("pipe")
    direction = lax.axis_index("dir")
    me = lax.axis_index("dp")
    everyone = lax.axis_size(ALL)
    seqs, steps, char_count = chars.shape
    parts = everyone // n
    quarter = seqs // parts
    tokens = quarter * steps
    width = cell_proj.shape[3]
    cell = cell_proj.shape[2]

    conv_full = lax.all_gather(conv_weight.astype(BF), ("dir", "dp"), axis=1, tiled=True)
    highway_full = lax.all_gather(highway_weight.astype(BF), ("dir", "dp"), axis=2, tiled=True)
    proj_full = lax.all_gather(proj_weight.astype(BF), ("dir", "dp"), axis=0, tiled=True)
    all_lengths = lax.all_gather(lengths, "dp", axis=0, tiled=True)

    in_rows = gate_weight.shape[2]
    gate_low = gate_weight[0, 0].astype(BF).reshape(in_rows, 4, n, cell)
    gate_low = jnp.transpose(gate_low, (2, 0, 1, 3)).reshape(n, in_rows, 4 * cell)
    gate_own = exchange(gate_low, "dp").reshape(n * in_rows, 4 * cell)
    bias_own = lax.dynamic_index_in_dim(
        gate_bias[0, 0].reshape(4, n, cell), me, 1, keepdims=False
    ).reshape(1, 4 * cell)
    cell_low = cell_proj[0, 0].astype(BF)

    def order_matrix(sizes):
        place = jnp.arange(steps, dtype=jnp.int32)[None, :]
        live = place < sizes[:, None]
        order = jnp.where(live & (direction == 1), sizes[:, None] - 1 - place, place)
        return ((order[:, :, None] == place[:, None, :]) & live[:, :, None]).astype(BF)

    own_order = order_matrix(lengths)
    cot = jnp.einsum("rts,rsd->trd", own_order, cotangent[0, 0], preferred_element_type=BF)

    ids = lax.dynamic_slice_in_dim(
        chars, (pipe * lax.axis_size("dir") + direction) * quarter, quarter, 0
    ).reshape(tokens, char_count)
    weight_mask = conv_masks(FILTERS)[0]
    table_low = char_emb.astype(BF)
    conv_low = conv_full * weight_mask.astype(BF)
    encoded, pooled, kept, mixed = encode_forward(
        ids,
        (table_low, conv_low, conv_bias, highway_full, highway_bias, proj_full, proj_bias),
    )
    encoded_all = lax.all_gather(
        encoded.astype(BF).reshape(quarter, steps, width), ("dp", "pipe", "dir"), axis=0, tiled=True
    )
    inputs = jnp.einsum(
        "rts,rsd->trd", order_matrix(all_lengths), encoded_all, preferred_element_type=BF
    ).reshape(steps, n, seqs, width)
    kept_low = [value.astype(BF) for value in kept]
    kept_all = [lax.all_gather(value, ALL, axis=0, tiled=True) for value in kept_low[:2]]
    last_columns = to_columns(kept_low[2])

    out_own, dx_own, x_all, h_all, da_all, e_all, dq_all = lstm_call(
        n,
        inputs,
        gate_own[:width],
        gate_own[width:],
        bias_own,
        cell_low,
        gate_own[:width].T,
        gate_own[width:].T,
        cell_low.T,
        cot,
    )
    activations = jnp.einsum("rts,srd->rtd", own_order, out_own, preferred_element_type=BF)

    total = steps * n * seqs
    da_flat = da_all.reshape(total, 4 * cell)
    grad_gate = jnp.concatenate(
        [
            jnp.einsum(
                "tk,tg->kg", part.reshape(total, width), da_flat, preferred_element_type=F32
            ).astype(BF)
            for part in (x_all, h_all)
        ]
    ).reshape(n, in_rows, 4 * cell)
    grad_gate = exchange(grad_gate, "dp").reshape(n, in_rows, 4, cell)
    grad_gate = jnp.transpose(grad_gate, (1, 2, 0, 3)).reshape(in_rows, 4 * n * cell).astype(F32)
    grad_bias = jnp.sum(da_flat.astype(F32), axis=0).reshape(4, cell)
    grad_bias = jnp.transpose(lax.all_gather(grad_bias, "dp"), (1, 0, 2)).reshape(n, 4 * cell)
    grad_bias = lax.dynamic_index_in_dim(grad_bias, me, 0, keepdims=False)
    grad_cell = jnp.einsum(
        "tc,td->cd",
        e_all.reshape(total, cell),
        dq_all.reshape(total, width),
        preferred_element_type=F32,
    )

    grad_stored = jnp.einsum(
        "rts,srd->rtd", own_order, dx_own.astype(BF), preferred_element_type=F32
    )
    grad_stored = jnp.where(pipe == 1, grad_stored, 0.0).astype(BF)
    grad_encoded = lax.psum_scatter(
        grad_stored, ("pipe", "dir"), scatter_dimension=0, tiled=True
    ).reshape(tokens, width)
    encoded_grads = lax.all_gather(grad_encoded, ALL, axis=0, tiled=True)

    grad_proj_bias = jnp.sum(grad_encoded.astype(F32), axis=0)
    grad_features = jnp.einsum("td,fd->tf", grad_encoded, proj_full, preferred_element_type=F32)
    grad_highway = [None, None]
    grad_highway_bias = [None, None]
    for layer in (1, 0):
        nonlinear = mixed[layer][:, :FILTERS]
        gate = jax.nn.sigmoid(mixed[layer][:, FILTERS:])
        grad_mixed = jnp.concatenate(
            [
                grad_features * (1.0 - gate) * silu_slope(nonlinear),
                grad_features * (kept[layer] - jax.nn.silu(nonlinear)) * gate * (1.0 - gate),
            ],
            axis=1,
        ).astype(BF)
        grad_highway[layer] = jnp.einsum(
            "tf,tg->fg", kept_all[layer], to_columns(grad_mixed), preferred_element_type=F32
        )
        grad_highway_bias[layer] = jnp.sum(grad_mixed.astype(F32), axis=0)
        grad_features = grad_features * gate + jnp.einsum(
            "tg,fg->tf", grad_mixed, highway_full[layer], preferred_element_type=F32
        )
    grad_proj = jnp.einsum("tf,td->fd", last_columns, encoded_grads, preferred_element_type=F32)
    grad_before = grad_features * silu_slope(pooled + conv_bias)
    grad_conv, grad_table = conv_backward(ids, table_low, conv_low, grad_before)

    small = (
        grad_table,
        jnp.sum(grad_before, axis=0),
        jnp.stack(grad_highway_bias),
        grad_proj_bias,
    )
    flat = jnp.concatenate([value.reshape(-1) for value in small])
    share = -(-flat.shape[0] // (everyone * 128)) * 128
    flat = jnp.pad(flat, (0, share * everyone - flat.shape[0])).reshape(everyone, share)
    columns = FILTERS // everyone
    packed = jnp.concatenate(
        [
            jnp.transpose(
                grad_conv.reshape(KMAX * CDIM, everyone, columns), (1, 0, 2)
            ).reshape(everyone, KMAX * CDIM * columns),
            flat,
        ],
        axis=1,
    ).astype(BF)
    summed = jnp.sum(lax.all_to_all(packed, ALL, 0, 0).astype(F32), axis=0)
    grad_conv = summed[: KMAX * CDIM * columns].reshape(KMAX * CDIM, columns)
    shared = lax.all_to_all(
        jnp.broadcast_to(summed[KMAX * CDIM * columns :], (everyone, share)), ALL, 0, 0
    ).reshape(-1)
    small_sums = []
    start = 0
    for value in small:
        small_sums.append(shared[start : start + value.size].reshape(value.shape))
        start += value.size
    return (
        activations[None, None],
        small_sums[0],
        grad_conv,
        small_sums[1],
        jnp.stack(grad_highway),
        small_sums[2],
        grad_proj,
        small_sums[3],
        grad_gate[None, None],
        grad_bias[None, None],
        grad_cell[None, None],
    )


def solution(mesh):
    return jax.shard_map(
        local,
        mesh=mesh,
        in_specs=(
            P("dp", None, None),
            P("dp"),
            P(),
            P(None, ("dir", "dp")),
            P(),
            P(None, None, ("dir", "dp")),
            P(),
            P(("dir", "dp"), None),
            P(),
            P("pipe", "dir", "dp", None),
            P("pipe", "dir", None),
            P("pipe", "dir", "dp", None),
            P("pipe", "dir", "dp", None, None),
        ),
        out_specs=(
            P("pipe", "dir", "dp", None, None),
            P(),
            P(None, ("pipe", "dir", "dp")),
            P(),
            P(None, None, ("pipe", "dir", "dp")),
            P(),
            P(("pipe", "dir", "dp"), None),
            P(),
            P("pipe", "dir", "dp", None),
            P("pipe", "dir", "dp"),
            P("pipe", "dir", "dp", None),
        ),
        check_vma=False,
    )
```

time: 5140 us -> 1630 us (0.32)
  waiting for transfers between devices: 2820 us -> 244 us
  matrix products: 1060 us -> 109 us
  other arithmetic: 602 us -> 54.2 us
  Pallas kernels: 0 us -> 339 us
  local copies, waits for them, and re-layouts: 443 us -> 596 us
    reduce_scatter x7 -> x1, waiting for transfers between devices: 1480 us -> 77.6 us  [local(): lax.psum_scatter(grad_stored, ('pipe', 'dir'), scatter_dimension=0, tiled...]
    dot_general x160 -> x19, matrix products: 1010 us -> 96.8 us  [the longest x2 21.4 us: local(): jnp.einsum('tg,fg->tf', grad_mixed, highway_full[layer], preferred_elemen...]
    all_gather x4 -> x6, waiting for transfers between devices: 811 us -> 119 us  [the longest x1 94.2 us: local(): lax.all_gather(highway_weight.astype(BF), ('dir', 'dp'), axis=2, tiled=True)]
    ppermute x4 -> x14, waiting for transfers between devices: 531 us -> 0.04 us  [exchange(): lax.ppermute(sent, axis, [(i, (i + off) % count) for i in range(count)])]
    dynamic_update_slice x0 -> x16, local copies, waits for them, and re-layouts: none -> 435 us  [the longest x14 381 us: exchange(): got = lax.dynamic_update_index_in_dim(got, came, (me - off) % count, 0)]
    pallas_call x0 -> x1, Pallas kernels: none -> 339 us  [lstm_call(): pl.pallas_call(functools.partial(lstm_kernel, n, chunk), out_shape=(sds((...]
    dynamic_update_slice x224 -> x0, other arithmetic: 162 us -> none  [the longest x192 138 us: lstm_forward(): _, traced = lax.scan(advance, start_value, input_part)]
    cond x72 -> x0, local copies, waits for them, and re-layouts: 157 us -> none  [the longest x2 126 us: local(): lax.cond(first_section & valid_now, run_encoder_back, skip_encoder_back)]
  transfers between devices with their start and end apart: 16 -> 26, of which waited for: 7 -> 6; matrix products, arithmetic and copies ran while one was open for 31% -> 45% of each run, Pallas kernels for 0% -> 0%
where the time goes in v1:
time: 1630 us; the launch traced here: 1610 us
  local copies, waits for them, and re-layouts  596 us (37%)
  Pallas kernels  339 us (21%)
  waiting for transfers between devices  244 us (15%)
  blocking collectives  192 us (12%)
  matrix products  109 us (7%)
  starting transfers between devices  57 us (3%)
  other arithmetic  54.2 us (3%)
  between operations  16.3 us (1%)
    dynamic_update_slice x14, local copies, waits for them, and re-layouts, exchange(): got = lax.dynamic_update_index_in_dim(got, came, (me - off) % count, 0)  381 us
    pallas_call x1, Pallas kernels, lstm_call(): pl.pallas_call(functools.partial(lstm_kernel, n, chunk), out_shape=(sds((...  339 us
    all_gather x1, blocking collectives, local(): lax.all_gather(grad_bias, 'dp')  113 us
    all_gather x1, waiting for transfers between devices, local(): lax.all_gather(highway_weight.astype(BF), ('dir', 'dp'), axis=2, tiled=True)  94.2 us
    reduce_scatter x1, waiting for transfers between devices, local(): lax.psum_scatter(grad_stored, ('pipe', 'dir'), scatter_dimension=0, tiled...  77.6 us
    dynamic_update_slice x2, local copies, waits for them, and re-layouts, exchange(): lax.dynamic_update_index_in_dim(got, lax.dynamic_index_in_dim(blocks, me,...  54.3 us
    broadcast_in_dim x14, local copies, waits for them, and re-layouts, exchange(): got = lax.dynamic_update_index_in_dim(got, came, (me - off) % count, 0)  43.5 us
    all_gather x1, blocking collectives, local(): lax.all_gather(conv_weight.astype(BF), ('dir', 'dp'), axis=1, tiled=True)  43.5 us
  transfers between devices with their start and end apart: 26, of which 6 were waited for; matrix products, arithmetic and copies ran while one was open for 45% of the time, Pallas kernels for 0%

profile of v1, /device:TPU:3, one launch (start us, length us, event | category | flops | bytes accessed | tf_op | source)
XLA Modules:
  0.0 1607.2 jit_solution(6504980378106391951)
XLA Ops:
  26.4 43.5 %all_gather.27 = bf16[112,2048]{1,0:T(8,128)(2,1)} all-gather(bf16[112,128]{1,0:T(8,128)(2,1)S(1)} %convert_element_type.236), channel_id=1, replica_groups=mesh['pipe'=2,'dir'=2,'dp'=8] {'dir','dp'}, dimensions={1}, use_global_device_ids=true | all-gather | bytes 487424 | tf_op jit(solution)/shard_map/all_gather | solution.py:429
  104.5 94.2 %all-gather.7.cloned.1.call-done = bf16[2,2048,4096]{2,1,0:T(8,128)(2,1)} async-done(((bf16[2,2048,256]{2,1,0:T(8,128)(2,1)}), bf16[2,2048,4096]{2,1,0:T(8,128)(2,1)}) %all-gather.7.cloned.1.call-update) | async-done | bytes 33554448 | tf_op jit(solution)/shard_map/all_gather | solution.py:430
  216.2 24.9 %all-gather.9.cloned.1.call-done = bf16[2048,512]{1,0:T(8,128)(2,1)} async-done(((bf16[128,512]{1,0:T(8,128)(2,1)}), bf16[2048,512]{1,0:T(8,128)(2,1)}) %all-gather.9.cloned.1.call-update) | async-done | bytes 2097168 | tf_op jit(solution)/shard_map/all_gather | solution.py:431
  282.9 27.2 %dynamic_update_slice.49 = bf16[8,128,2048]{1,0,2:T(8,128)(2,1)} dynamic-update-slice(bf16[8,128,2048]{1,0,2:T(8,128)(2,1)} %broadcast.300.clone, bf16[1,128,2048]{1,0,2:T(2,128)(2,1)S(1)} %copy.140, s32[]{:T(128)S(6)} %select_n.219, s32[]{:T(128)} %constant.259.clone.1, s32[]{:T(128)} %constant.259.clone.1) | dynamic-update-slice | bytes 1048580 | tf_op jit(solution)/shard_map/jit(dynamic_update_index_in_dim)/dynamic_update_slice | solution.py:346
  311.6 35.0 %all-reduce.9 = s32[128]{0:T(128)S(1)} all-reduce(s32[128]{0:T(128)S(1)} %dynamic-update-slice), channel_id=1, replica_groups=mesh['pipe'=2,'dir'=2,'dp'=8] {'dp'}, use_global_device_ids=true, to_apply=%add.9 | all-reduce | flops 128 | bytes 1024
  385.1 27.2 %dynamic_update_slice.50 = bf16[8,128,2048]{1,0,2:T(8,128)(2,1)} dynamic-update-slice(bf16[8,128,2048]{1,0,2:T(8,128)(2,1)} %dynamic_update_slice.49, bf16[1,128,2048]{1,0,2:T(2,128)(2,1)S(1)} %copy.141, s32[]{:T(128)S(6)} %select_n.223, s32[]{:T(128)} %constant.259.clone.1, s32[]{:T(128)} %constant.259.clone.1) | dynamic-update-slice | bytes 1048580 | tf_op jit(solution)/shard_map/jit(dynamic_update_index_in_dim)/dynamic_update_slice | solution.py:352
  412.3 27.3 %dynamic_update_slice.51 = bf16[8,128,2048]{1,0,2:T(8,128)(2,1)} dynamic-update-slice(bf16[8,128,2048]{1,0,2:T(8,128)(2,1)} %dynamic_update_slice.50, bf16[1,128,2048]{1,0,2:T(2,128)(2,1)} %copy.142, s32[]{:T(128)S(6)} %select_n.227, s32[]{:T(128)} %constant.259.clone.1, s32[]{:T(128)} %constant.259.clone.1) | dynamic-update-slice | bytes 1048580 | tf_op jit(solution)/shard_map/jit(dynamic_update_index_in_dim)/dynamic_update_slice | solution.py:352
  439.6 27.2 %dynamic_update_slice.52 = bf16[8,128,2048]{1,0,2:T(8,128)(2,1)} dynamic-update-slice(bf16[8,128,2048]{1,0,2:T(8,128)(2,1)} %dynamic_update_slice.51, bf16[1,128,2048]{1,0,2:T(2,128)(2,1)} %copy.143, s32[]{:T(128)S(6)} %select_n.231, s32[]{:T(128)} %constant.259.clone.1, s32[]{:T(128)} %constant.259.clone.1) | dynamic-update-slice | bytes 1048580 | tf_op jit(solution)/shard_map/jit(dynamic_update_index_in_dim)/dynamic_update_slice | solution.py:352
  466.8 27.2 %dynamic_update_slice.53 = bf16[8,128,2048]{1,0,2:T(8,128)(2,1)} dynamic-update-slice(bf16[8,128,2048]{1,0,2:T(8,128)(2,1)} %dynamic_update_slice.52, bf16[1,128,2048]{1,0,2:T(2,128)(2,1)} %copy.144, s32[]{:T(128)S(6)} %select_n.235, s32[]{:T(128)} %constant.259.clone.1, s32[]{:T(128)} %constant.259.clone.1) | dynamic-update-slice | bytes 1048580 | tf_op jit(solution)/shard_map/jit(dynamic_update_index_in_dim)/dynamic_update_slice | solution.py:352
  494.1 27.2 %dynamic_update_slice.54 = bf16[8,128,2048]{1,0,2:T(8,128)(2,1)} dynamic-update-slice(bf16[8,128,2048]{1,0,2:T(8,128)(2,1)} %dynamic_update_slice.53, bf16[1,128,2048]{1,0,2:T(2,128)(2,1)S(1)} %copy-done.8, s32[]{:T(128)S(6)} %select_n.239, s32[]{:T(128)} %constant.259.clone.1, s32[]{:T(128)} %constant.259.clone.1) | dynamic-update-slice | bytes 1048580 | tf_op jit(solution)/shard_map/jit(dynamic_update_index_in_dim)/dynamic_update_slice | solution.py:352
  521.2 27.2 %dynamic_update_slice.55 = bf16[8,128,2048]{1,0,2:T(8,128)(2,1)} dynamic-update-slice(bf16[8,128,2048]{1,0,2:T(8,128)(2,1)} %dynamic_update_slice.54, bf16[1,128,2048]{1,0,2:T(2,128)(2,1)} %copy.146, s32[]{:T(128)S(6)} %select_n.243, s32[]{:T(128)} %constant.259.clone.1, s32[]{:T(128)} %constant.259.clone.1) | dynamic-update-slice | bytes 1048580 | tf_op jit(solution)/shard_map/jit(dynamic_update_index_in_dim)/dynamic_update_slice | solution.py:352
  548.4 27.2 %dynamic_update_slice.56 = bf16[8,128,2048]{1,0,2:T(8,128)(2,1)} dynamic-update-slice(bf16[8,128,2048]{1,0,2:T(8,128)(2,1)} %dynamic_update_slice.55, bf16[1,128,2048]{1,0,2:T(2,128)(2,1)} %copy.147, s32[]{:T(128)S(6)} %select_n.247, s32[]{:T(128)} %constant.259.clone.1, s32[]{:T(128)} %constant.259.clone.1) | dynamic-update-slice | bytes 1048580 | tf_op jit(solution)/shard_map/jit(dynamic_update_index_in_dim)/dynamic_update_slice | solution.py:352
  597.5 339.4 %relay_lstm.1 = (bf16[16,16,512]{2,1,0:T(8,128)(2,1)}, f32[16,16,512]{2,1,0:T(8,128)}, bf16[16,8,16,512]{3,2,1,0:T(8,128)(2,1)}, bf16[16,8,16,512]{3,2,1,0:T(8,1...) custom-call(bf16[16,8,16,512]{3,2,1,0:T(8,128)(2,1)} %bitcast.225, ...), custom_call_target="tpu_custom_call" | custom-call | tf_op jit(solution)/shard_map/relay_lstm/pallas_call | solution.py:315
  939.9 77.6 %reduce-scatter.2.cloned.1.call-done = bf16[4,16,512]{2,1,0:T(8,128)(2,1)} async-done(((bf16[16,16,512]{2,1,0:T(8,128)(2,1)}), bf16[4,16,512]{2,1,0:T(8,128)(2,1)}) %reduce-scatter.2.cloned.1.call-update) | async-done | bytes 65552 | tf_op jit(solution)/shard_map/reduce_scatter | solution.py:512
  1159.5 113.0 %all_gather.35 = f32[8,4,512]{2,1,0:T(4,128)S(1)} all-gather(f32[1,4,512]{2,1,0:T(4,128)S(1)} %all_gather_reshape.3), channel_id=1, replica_groups=mesh['pipe'=2,'dir'=2,'dp'=8] {'dp'}, dimensions={0}, use_global_device_ids=true | all-gather | bytes 73728 | tf_op jit(solution)/shard_map/all_gather | solution.py:499
  1286.8 28.1 %all-to-all-done.1 = f32[32,1,512]{2,1,0:T(1,128)S(1)} async-done(((f32[32,1,512]{2,1,0:T(1,128)}), f32[32,1,512]{2,1,0:T(1,128)S(1)}, u32[]{:S(2)}, u32[]{:S(2)}) %all-to-all-start.1) | async-done | bytes 65568 | tf_op jit(solution)/shard_map/all_to_all | solution.py:563
  1323.0 27.2 %dynamic_update_slice.57 = bf16[8,128,2048]{1,0,2:T(8,128)(2,1)} dynamic-update-slice(bf16[8,128,2048]{1,0,2:T(8,128)(2,1)} %broadcast.300, bf16[1,128,2048]{1,0,2:T(2,128)(2,1)S(1)} %copy.183, s32[]{:T(128)S(6)} %select_n.219, s32[]{:T(128)} %constant.259.clone.1, s32[]{:T(128)} %constant.259.clone.1) | dynamic-update-slice | bytes 1048580 | tf_op jit(solution)/shard_map/jit(dynamic_update_index_in_dim)/dynamic_update_slice | solution.py:346
  1371.0 27.2 %dynamic_update_slice.58 = bf16[8,128,2048]{1,0,2:T(8,128)(2,1)} dynamic-update-slice(bf16[8,128,2048]{1,0,2:T(8,128)(2,1)} %dynamic_update_slice.57, bf16[1,128,2048]{1,0,2:T(2,128)(2,1)S(1)} %copy.169, s32[]{:T(128)S(6)} %select_n.223, s32[]{:T(128)} %constant.259.clone.1, s32[]{:T(128)} %constant.259.clone.1) | dynamic-update-slice | bytes 1048580 | tf_op jit(solution)/shard_map/jit(dynamic_update_index_in_dim)/dynamic_update_slice | solution.py:352
  1398.2 27.2 %dynamic_update_slice.59 = bf16[8,128,2048]{1,0,2:T(8,128)(2,1)} dynamic-update-slice(bf16[8,128,2048]{1,0,2:T(8,128)(2,1)} %dynamic_update_slice.58, bf16[1,128,2048]{1,0,2:T(2,128)(2,1)S(1)} %copy.170, s32[]{:T(128)S(6)} %select_n.227, s32[]{:T(128)} %constant.259.clone.1, s32[]{:T(128)} %constant.259.clone.1) | dynamic-update-slice | bytes 1048580 | tf_op jit(solution)/shard_map/jit(dynamic_update_index_in_dim)/dynamic_update_slice | solution.py:352
  1425.4 27.2 %dynamic_update_slice.60 = bf16[8,128,2048]{1,0,2:T(8,128)(2,1)} dynamic-update-slice(bf16[8,128,2048]{1,0,2:T(8,128)(2,1)} %dynamic_update_slice.59, bf16[1,128,2048]{1,0,2:T(2,128)(2,1)S(1)} %copy.171, s32[]{:T(128)S(6)} %select_n.231, s32[]{:T(128)} %constant.259.clone.1, s32[]{:T(128)} %constant.259.clone.1) | dynamic-update-slice | bytes 1048580 | tf_op jit(solution)/shard_map/jit(dynamic_update_index_in_dim)/dynamic_update_slice | solution.py:352
  1452.6 27.2 %dynamic_update_slice.61 = bf16[8,128,2048]{1,0,2:T(8,128)(2,1)} dynamic-update-slice(bf16[8,128,2048]{1,0,2:T(8,128)(2,1)} %dynamic_update_slice.60, bf16[1,128,2048]{1,0,2:T(2,128)(2,1)S(1)} %copy-done.4, s32[]{:T(128)S(6)} %select_n.235, s32[]{:T(128)} %constant.259.clone.1, s32[]{:T(128)} %constant.259.clone.1) | dynamic-update-slice | bytes 1048580 | tf_op jit(solution)/shard_map/jit(dynamic_update_index_in_dim)/dynamic_update_slice | solution.py:352
  1479.9 27.2 %dynamic_update_slice.62 = bf16[8,128,2048]{1,0,2:T(8,128)(2,1)} dynamic-update-slice(bf16[8,128,2048]{1,0,2:T(8,128)(2,1)} %dynamic_update_slice.61, bf16[1,128,2048]{1,0,2:T(2,128)(2,1)S(1)} %copy-done.5, s32[]{:T(128)S(6)} %select_n.239, s32[]{:T(128)} %constant.259.clone.1, s32[]{:T(128)} %constant.259.clone.1) | dynamic-update-slice | bytes 1048580 | tf_op jit(solution)/shard_map/jit(dynamic_update_index_in_dim)/dynamic_update_slice | solution.py:352
  1507.1 27.2 %dynamic_update_slice.63 = bf16[8,128,2048]{1,0,2:T(8,128)(2,1)} dynamic-update-slice(bf16[8,128,2048]{1,0,2:T(8,128)(2,1)} %dynamic_update_slice.62, bf16[1,128,2048]{1,0,2:T(2,128)(2,1)S(1)} %copy-done.6, s32[]{:T(128)S(6)} %select_n.243, s32[]{:T(128)} %constant.259.clone.1, s32[]{:T(128)} %constant.259.clone.1) | dynamic-update-slice | bytes 1048580 | tf_op jit(solution)/shard_map/jit(dynamic_update_index_in_dim)/dynamic_update_slice | solution.py:352
  1534.3 27.2 %dynamic_update_slice.64 = bf16[8,128,2048]{1,0,2:T(8,128)(2,1)} dynamic-update-slice(bf16[8,128,2048]{1,0,2:T(8,128)(2,1)} %dynamic_update_slice.63, bf16[1,128,2048]{1,0,2:T(2,128)(2,1)S(1)} %copy-done.7, s32[]{:T(128)S(6)} %select_n.247, s32[]{:T(128)} %constant.259.clone.1, s32[]{:T(128)} %constant.259.clone.1) | dynamic-update-slice | bytes 1048580 | tf_op jit(solution)/shard_map/jit(dynamic_update_index_in_dim)/dynamic_update_slice | solution.py:352
  (324 shorter events, 399.9 us)
Async XLA Ops:
  7.2 191.5 %all-gather.7.cloned.1.call-start = ((), (), s32[]{:S(2)}) async-start(), calls=%async_computation.6 | async-start | bytes 35651584 | tf_op jit(solution)/shard_map/all_gather | solution.py:430
  11.0 230.0 %all-gather.9.cloned.1.call-start = ((), (), s32[]{:S(2)}) async-start(), calls=%async_computation.7 | async-start | bytes 2228224 | tf_op jit(solution)/shard_map/all_gather | solution.py:431
  11.8 580.6 %all-gather.11.cloned.1.call-start = ((), (), s32[]{:S(2)}) async-start(), calls=%async_computation.8 | async-start | bytes 2162688 | tf_op jit(solution)/shard_map/all_gather | solution.py:462
  243.8 773.6 %reduce-scatter.2.cloned.1.call-start = ((), (), s32[]{:S(2)}) async-start(), calls=%async_computation.9 | async-start | bytes 327680 | tf_op jit(solution)/shard_map/reduce_scatter | solution.py:512
  265.8 80.8 %collective-permute-start = (bf16[128,2048]{1,0:T(8,128)(2,1)}, bf16[128,2048]{1,0:T(8,128)(2,1)}, u32[]{:S(2)}, u32[]{:S(2)}) collective-permute-start(bf16[128,2048]{1,0:T(8,128)(2,1)} %get-tuple-element.81), channel_id=1, source_target_pairs={{0,1},{1,2},{2,3},{3,4},{4,5},{5,6},{6,7},{7,0},{8,9},{9,10},{10,1... | collective-permute-start | bytes 1572872 | tf_op jit(solution)/shard_map/ppermute | solution.py:351
  266.1 80.6 %collective-permute-start.1 = (bf16[128,2048]{1,0:T(8,128)(2,1)}, bf16[128,2048]{1,0:T(8,128)(2,1)}, u32[]{:S(2)}, u32[]{:S(2)}) collective-permute-start(bf16[128,2048]{1,0:T(8,128)(2,1)} %get-tuple-element.80), channel_id=1, source_target_pairs={{0,2},{1,3},{2,4},{3,5},{4,6},{5,7},{6,0},{7,1},{8,10},{9,11},{10,... | collective-permute-start | bytes 1572872 | tf_op jit(solution)/shard_map/ppermute | solution.py:351
  266.3 100.9 %collective-permute-start.2 = (bf16[128,2048]{1,0:T(8,128)(2,1)}, bf16[128,2048]{1,0:T(8,128)(2,1)}, u32[]{:S(2)}, u32[]{:S(2)}) collective-permute-start(bf16[128,2048]{1,0:T(8,128)(2,1)} %get-tuple-element.79), channel_id=1, source_target_pairs={{0,3},{1,4},{2,5},{3,6},{4,7},{5,0},{6,1},{7,2},{8,11},{9,12},{10,... | collective-permute-start | bytes 1572872 | tf_op jit(solution)/shard_map/ppermute | solution.py:351
  269.1 101.8 %collective-permute-start.3 = (bf16[128,2048]{1,0:T(8,128)(2,1)}, bf16[128,2048]{1,0:T(8,128)(2,1)}, u32[]{:S(2)}, u32[]{:S(2)}) collective-permute-start(bf16[128,2048]{1,0:T(8,128)(2,1)} %get-tuple-element.78), channel_id=1, source_target_pairs={{0,4},{1,5},{2,6},{3,7},{4,0},{5,1},{6,2},{7,3},{8,12},{9,13},{10,... | collective-permute-start | bytes 1572872 | tf_op jit(solution)/shard_map/ppermute | solution.py:351
  270.5 103.9 %collective-permute-start.4 = (bf16[128,2048]{1,0:T(8,128)(2,1)}, bf16[128,2048]{1,0:T(8,128)(2,1)}, u32[]{:S(2)}, u32[]{:S(2)}) collective-permute-start(bf16[128,2048]{1,0:T(8,128)(2,1)} %get-tuple-element.77), channel_id=1, source_target_pairs={{0,5},{1,6},{2,7},{3,0},{4,1},{5,2},{6,3},{7,4},{8,13},{9,14},{10,... | collective-permute-start | bytes 1572872 | tf_op jit(solution)/shard_map/ppermute | solution.py:351
  346.6 31.3 %collective-permute-start.5 = (bf16[128,2048]{1,0:T(8,128)(2,1)}, bf16[128,2048]{1,0:T(8,128)(2,1)}, u32[]{:S(2)}, u32[]{:S(2)}) collective-permute-start(bf16[128,2048]{1,0:T(8,128)(2,1)} %get-tuple-element.76), channel_id=1, source_target_pairs={{0,6},{1,7},{2,0},{3,1},{4,2},{5,3},{6,4},{7,5},{8,14},{9,15},{10,... | collective-permute-start | bytes 1572872 | tf_op jit(solution)/shard_map/ppermute | solution.py:351
  346.7 34.8 %collective-permute-start.6 = (bf16[128,2048]{1,0:T(8,128)(2,1)}, bf16[128,2048]{1,0:T(8,128)(2,1)}, u32[]{:S(2)}, u32[]{:S(2)}) collective-permute-start(bf16[128,2048]{1,0:T(8,128)(2,1)} %get-tuple-element.75), channel_id=1, source_target_pairs={{0,7},{1,0},{2,1},{3,2},{4,3},{5,4},{6,5},{7,6},{8,15},{9,8},{10,9... | collective-permute-start | bytes 1572872 | tf_op jit(solution)/shard_map/ppermute | solution.py:351
  939.0 641.9 %all-gather.13.cloned.1.call-start = ((), (), s32[]{:S(2)}) async-start(), calls=%async_computation.10 | async-start | bytes 8650752 | tf_op jit(solution)/shard_map/all_gather | solution.py:469
  939.6 650.3 %all-gather.17.cloned.1.call-start = ((), (), s32[]{:S(2)}) async-start(), calls=%async_computation.12 | async-start | bytes 2162688 | tf_op jit(solution)/shard_map/all_gather | solution.py:515
  1025.1 567.6 %all-gather.15.cloned.1.call-start = ((), (), s32[]{:S(2)}) async-start(), calls=%async_computation.11 | async-start | bytes 8650752 | tf_op jit(solution)/shard_map/all_gather | solution.py:469
  1140.5 134.3 %all-to-all-start.2 = ((bf16[32,64,128]{2,1,0:T(8,128)(2,1)}), bf16[32,64,128]{2,1,0:T(8,128)(2,1)}, u32[]{:S(2)}, u32[]{:S(2)}) async-start(bf16[32,64,128]{2,1,0:T(8,128)(2,1)} %maximum_bitcast_fusion), calls=%async_computation.3 | async-start | bytes 1048576 | tf_op jit(solution)/shard_map/all_to_all | solution.py:380
  1149.3 124.8 %collective-permute-start.7 = (bf16[128,2048]{1,0:T(8,128)(2,1)}, bf16[128,2048]{1,0:T(8,128)(2,1)S(1)}, u32[]{:S(2)}, u32[]{:S(2)}) collective-permute-start(bf16[128,2048]{1,0:T(8,128)(2,1)} %get-tuple-element.71), channel_id=1, source_target_pairs={{0,1},{1,2},{2,3},{3,4},{4,5},{5,6},{6,7},{7,0},{8,9},{9,10},{10,1... | collective-permute-start | bytes 1572872 | tf_op jit(solution)/shard_map/ppermute | solution.py:351
  1150.5 124.2 %collective-permute-start.8 = (bf16[128,2048]{1,0:T(8,128)(2,1)}, bf16[128,2048]{1,0:T(8,128)(2,1)}, u32[]{:S(2)}, u32[]{:S(2)}) collective-permute-start(bf16[128,2048]{1,0:T(8,128)(2,1)} %get-tuple-element.70), channel_id=1, source_target_pairs={{0,2},{1,3},{2,4},{3,5},{4,6},{5,7},{6,0},{7,1},{8,10},{9,11},{10,... | collective-permute-start | bytes 1572872 | tf_op jit(solution)/shard_map/ppermute | solution.py:351
  1151.8 202.5 %collective-permute-start.9 = (bf16[128,2048]{1,0:T(8,128)(2,1)}, bf16[128,2048]{1,0:T(8,128)(2,1)}, u32[]{:S(2)}, u32[]{:S(2)}) collective-permute-start(bf16[128,2048]{1,0:T(8,128)(2,1)} %get-tuple-element.69), channel_id=1, source_target_pairs={{0,3},{1,4},{2,5},{3,6},{4,7},{5,0},{6,1},{7,2},{8,11},{9,12},{10,... | collective-permute-start | bytes 1572872 | tf_op jit(solution)/shard_map/ppermute | solution.py:351
  1154.0 202.7 %collective-permute-start.10 = (bf16[128,2048]{1,0:T(8,128)(2,1)}, bf16[128,2048]{1,0:T(8,128)(2,1)}, u32[]{:S(2)}, u32[]{:S(2)}) collective-permute-start(bf16[128,2048]{1,0:T(8,128)(2,1)} %get-tuple-element.68), channel_id=1, source_target_pairs={{0,4},{1,5},{2,6},{3,7},{4,0},{5,1},{6,2},{7,3},{8,12},{9,13},{10,... | collective-permute-start | bytes 1572872 | tf_op jit(solution)/shard_map/ppermute | solution.py:351
  1155.0 205.2 %collective-permute-start.11 = (bf16[128,2048]{1,0:T(8,128)(2,1)}, bf16[128,2048]{1,0:T(8,128)(2,1)}, u32[]{:S(2)}, u32[]{:S(2)}) collective-permute-start(bf16[128,2048]{1,0:T(8,128)(2,1)} %get-tuple-element.67), channel_id=1, source_target_pairs={{0,5},{1,6},{2,7},{3,0},{4,1},{5,2},{6,3},{7,4},{8,13},{9,14},{10,... | collective-permute-start | bytes 1572872 | tf_op jit(solution)/shard_map/ppermute | solution.py:351
  1274.1 89.7 %collective-permute-start.12 = (bf16[128,2048]{1,0:T(8,128)(2,1)}, bf16[128,2048]{1,0:T(8,128)(2,1)}, u32[]{:S(2)}, u32[]{:S(2)}) collective-permute-start(bf16[128,2048]{1,0:T(8,128)(2,1)} %get-tuple-element.66), channel_id=1, source_target_pairs={{0,6},{1,7},{2,0},{3,1},{4,2},{5,3},{6,4},{7,5},{8,14},{9,15},{10,... | collective-permute-start | bytes 1572872 | tf_op jit(solution)/shard_map/ppermute | solution.py:351
  1274.8 92.6 %collective-permute-start.13 = (bf16[128,2048]{1,0:T(8,128)(2,1)}, bf16[128,2048]{1,0:T(8,128)(2,1)}, u32[]{:S(2)}, u32[]{:S(2)}) collective-permute-start(bf16[128,2048]{1,0:T(8,128)(2,1)} %get-tuple-element.65), channel_id=1, source_target_pairs={{0,7},{1,0},{2,1},{3,2},{4,3},{5,4},{6,5},{7,6},{8,15},{9,8},{10,9... | collective-permute-start | bytes 1572872 | tf_op jit(solution)/shard_map/ppermute | solution.py:351
  1275.4 39.5 %all-to-all-start.1 = ((f32[32,1,512]{2,1,0:T(1,128)}), f32[32,1,512]{2,1,0:T(1,128)S(1)}, u32[]{:S(2)}, u32[]{:S(2)}) async-start(f32[32,1,512]{2,1,0:T(1,128)} %broadcast_in_dim.142), calls=%async_computation.2 | async-start | bytes 131072 | tf_op jit(solution)/shard_map/all_to_all | solution.py:563
  1314.9 277.8 %all-to-all-start.3 = ((bf16[32,64,128]{2,1,0:T(8,128)(2,1)}), bf16[32,64,128]{2,1,0:T(8,128)(2,1)}, u32[]{:S(2)}, u32[]{:S(2)}) async-start(bf16[32,64,128]{2,1,0:T(8,128)(2,1)} %maximum_bitcast_fusion.1), calls=%async_computation.4 | async-start | bytes 1048576 | tf_op jit(solution)/shard_map/all_to_all | solution.py:380
  (61 other events, 2538.4 us)
Sparse Core Ops, SparseCore 0:
  11.2 187.5 all-gather.6
  201.5 39.4 all-gather.8
  244.5 104.4 all-gather.10
  939.2 78.2 reduce-scatter.1
  1020.7 78.9 all-gather.12
  1102.9 106.7 all-gather.16
  1213.1 90.3 all-gather.14

commit v2 on v1

--- a/solution.py
+++ b/solution.py
@@ -339,20 +339,6 @@
     )(x, wx, wh, bias, p, wxt, wht, pt, cot)
 
 
-def exchange(blocks, axis):
-    count = lax.axis_size(axis)
-    me = lax.axis_index(axis)
-    got = jnp.zeros_like(blocks)
-    got = lax.dynamic_update_index_in_dim(
-        got, lax.dynamic_index_in_dim(blocks, me, 0, keepdims=False), me, 0
-    )
-    for off in range(1, count):
-        sent = lax.dynamic_index_in_dim(blocks, (me + off) % count, 0, keepdims=False)
-        came = lax.ppermute(sent, axis, [(i, (i + off) % count) for i in range(count)])
-        got = lax.dynamic_update_index_in_dim(got, came, (me - off) % count, 0)
-    return got
-
-
 def encode_forward(ids, weights):
     table_low, conv_low, conv_bias, highway_low, highway_bias, proj_low, proj_bias = weights
     valid_place = conv_masks(FILTERS)[1]
@@ -429,12 +415,14 @@
     conv_full = lax.all_gather(conv_weight.astype(BF), ("dir", "dp"), axis=1, tiled=True)
     highway_full = lax.all_gather(highway_weight.astype(BF), ("dir", "dp"), axis=2, tiled=True)
     proj_full = lax.all_gather(proj_weight.astype(BF), ("dir", "dp"), axis=0, tiled=True)
-    all_lengths = lax.all_gather(lengths, "dp", axis=0, tiled=True)
+    all_lengths = lax.all_to_all(
+        jnp.broadcast_to(lengths, (n, seqs)), "dp", 0, 0
+    ).reshape(n * seqs)
 
     in_rows = gate_weight.shape[2]
     gate_low = gate_weight[0, 0].astype(BF).reshape(in_rows, 4, n, cell)
     gate_low = jnp.transpose(gate_low, (2, 0, 1, 3)).reshape(n, in_rows, 4 * cell)
-    gate_own = exchange(gate_low, "dp").reshape(n * in_rows, 4 * cell)
+    gate_own = lax.all_to_all(gate_low, "dp", 0, 0).reshape(n * in_rows, 4 * cell)
     bias_own = lax.dynamic_index_in_dim(
         gate_bias[0, 0].reshape(4, n, cell), me, 1, keepdims=False
     ).reshape(1, 4 * cell)
@@ -493,7 +481,7 @@
             for part in (x_all, h_all)
         ]
     ).reshape(n, in_rows, 4 * cell)
-    grad_gate = exchange(grad_gate, "dp").reshape(n, in_rows, 4, cell)
+    grad_gate = lax.all_to_all(grad_gate, "dp", 0, 0).reshape(n, in_rows, 4, cell)
     grad_gate = jnp.transpose(grad_gate, (1, 2, 0, 3)).reshape(in_rows, 4 * n * cell).astype(F32)
     grad_bias = jnp.sum(da_flat.astype(F32), axis=0).reshape(4, cell)
     grad_bias = jnp.transpose(lax.all_gather(grad_bias, "dp"), (1, 0, 2)).reshape(n, 4 * cell)

time: 1630 us -> 1160 us (0.71)
  local copies, waits for them, and re-layouts: 596 us -> 116 us
  waiting for transfers between devices: 244 us -> 299 us
  blocking collectives: 192 us -> 164 us
    dynamic_update_slice x16 -> x0, local copies, waits for them, and re-layouts: 435 us -> none  [the longest x14 381 us: exchange(): got = lax.dynamic_update_index_in_dim(got, came, (me - off) % count, 0)]
    all_gather x1, waiting for transfers between devices: 94.2 us -> 156 us  [local(): lax.all_gather(highway_weight.astype(BF), ('dir', 'dp'), axis=2, tiled=True)]
    broadcast_in_dim x14 -> x1, local copies, waits for them, and re-layouts: 43.5 us -> 0.59 us  [local(): jnp.broadcast_to(lengths, (n, seqs))]
    unnamed x1 -> x0, blocking collectives: 35 us -> none
    all_gather x1, waiting for transfers between devices: 0.01 us -> 32 us  [local(): lax.all_gather(encoded.astype(BF).reshape(quarter, steps, width), ('dp',...]
    ppermute x14 -> x0, starting transfers between devices: 27.3 us -> none  [exchange(): lax.ppermute(sent, axis, [(i, (i + off) % count) for i in range(count)])]
    all_to_all x1, waiting for transfers between devices: 28.1 us -> 1.99 us  [local(): lax.all_to_all(jnp.broadcast_to(summed[KMAX * CDIM * columns:], (everyone...]
  transfers between devices with their start and end apart: 26 -> 15, of which waited for: 6 -> 7; matrix products, arithmetic and copies ran while one was open for 45% -> 22% of each run, Pallas kernels for 0% -> 0%
where the time goes in v2:
time: 1160 us; the launch traced here: 1150 us
  Pallas kernels  344 us (30%)
  waiting for transfers between devices  299 us (26%)
  blocking collectives  164 us (14%)
  local copies, waits for them, and re-layouts  116 us (10%)
  matrix products  112 us (10%)
  other arithmetic  52.7 us (5%)
  starting transfers between devices  46.1 us (4%)
  between operations  15.4 us (1%)
    pallas_call x1, Pallas kernels, lstm_call(): pl.pallas_call(functools.partial(lstm_kernel, n, chunk), out_shape=(sds((...  344 us
    all_gather x1, waiting for transfers between devices, local(): lax.all_gather(highway_weight.astype(BF), ('dir', 'dp'), axis=2, tiled=True)  156 us
    all_gather x1, blocking collectives, local(): lax.all_gather(grad_bias, 'dp')  121 us
    reduce_scatter x1, waiting for transfers between devices, local(): lax.psum_scatter(grad_stored, ('pipe', 'dir'), scatter_dimension=0, tiled...  73.3 us
    all_gather x1, blocking collectives, local(): lax.all_gather(conv_weight.astype(BF), ('dir', 'dp'), axis=1, tiled=True)  42.9 us
    all_gather x1, waiting for transfers between devices, local(): lax.all_gather(encoded.astype(BF).reshape(quarter, steps, width), ('dp',...  32 us
    convert_element_type x3, local copies, waits for them, and re-layouts, local(): jnp.transpose(grad_gate, (1, 2, 0, 3)).reshape(in_rows, 4 * n * cell)  31.6 us
    all_gather x1, waiting for transfers between devices, local(): lax.all_gather(proj_weight.astype(BF), ('dir', 'dp'), axis=0, tiled=True)  26.6 us
  transfers between devices with their start and end apart: 15, of which 7 were waited for; matrix products, arithmetic and copies ran while one was open for 22% of the time, Pallas kernels for 0%

profile of v2, /device:TPU:3, one launch (start us, length us, event | category | flops | bytes accessed | tf_op | source)
XLA Modules:
  0.0 1149.1 jit_solution(9123457250717462736)
XLA Ops:
  20.3 6.7 gather_fusion
  33.1 42.9 %all_gather.24 = bf16[112,2048]{1,0:T(8,128)(2,1)} all-gather(bf16[112,128]{1,0:T(8,128)(2,1)S(1)} %convert_element_type.236), channel_id=1, replica_groups=mesh['pipe'=2,'dir'=2,'dp'=8] {'dir','dp'}, dimensions={1}, use_global_device_ids=true | all-gather | bytes 487424 | tf_op jit(solution)/shard_map/all_gather | solution.py:415
  76.0 6.7 concatenate.50
  82.7 11.8 %select_reduce_fusion = (f32[64,2048]{1,0:T(8,128)S(1)}, f32[64,50,2048]{2,0,1:T(8,128)}) fusion(pred[50,2048]{1,0:T(8,128)(4,1)S(1)} %iota_compare_fusion.7, bf16[64,50,112]{2,0,1:T(8,128)(2,1)S(1)} %concatenate.50, bf16[112,2048]{1,0:T(8,128)(2,1)} %all_gather.24, s32[2048]{0:T(1024)S(1)} %convert_add_fusion, s32[112]{0:T(128)S(1)} %and_select_fusion), kind=kOutput, calls=%fused_computation.5 | convolution fusion | flops 1481900032 | bytes 28025280 | tf_op jit(solution)/shard_map/bpk,kf->bpf/dot_general | solution.py:57
  94.5 15.3 %fusion = (f32[64,2048]{1,0:T(8,128)S(1)}, f32[64,2048]{1,0:T(8,128)S(1)}) fusion(f32[64,50,2048]{2,0,1:T(8,128)} %get-tuple-element.91, f32[64,2048]{1,0:T(8,128)S(1)} %get-tuple-element.90, pred[50,2048]{1,0:T(8,128)(4,1)S(1)} %iota_compare_fusion.7, f32[64,2048]{1,0:T(8,128)S(1)} %is-finite_select_fusion), kind=kLoop, calls=%fused_computation.4 | loop fusion | flops 32505856 | bytes 28413952 | tf_op jit(solution)/shard_map/reduce_sum | solution.py:372
  114.2 7.9 copy.101
  130.2 156.0 %all-gather.7.cloned.1.call-done = bf16[2,2048,4096]{2,1,0:T(8,128)(2,1)} async-done(((bf16[2,2048,256]{2,1,0:T(8,128)(2,1)}), bf16[2,2048,4096]{2,1,0:T(8,128)(2,1)}) %all-gather.7.cloned.1.call-update) | async-done | bytes 33554448 | tf_op jit(solution)/shard_map/all_gather | solution.py:416
  286.2 7.4 fusion.7
  294.8 7.8 fusion.6
  304.0 26.6 %all-gather.9.cloned.1.call-done = bf16[2048,512]{1,0:T(8,128)(2,1)} async-done(((bf16[128,512]{1,0:T(8,128)(2,1)}), bf16[2048,512]{1,0:T(8,128)(2,1)}) %all-gather.9.cloned.1.call-update) | async-done | bytes 2097168 | tf_op jit(solution)/shard_map/all_gather | solution.py:417
  357.2 32.0 %all-gather.11.cloned.1.call-done = bf16[128,16,512]{2,1,0:T(8,128)(2,1)} async-done(((bf16[4,16,512]{2,1,0:T(8,128)(2,1)}), bf16[128,16,512]{2,1,0:T(8,128)(2,1)}) %all-gather.11.cloned.1.call-update) | async-done | bytes 2097168 | tf_op jit(solution)/shard_map/all_gather | solution.py:450
  394.3 343.7 %relay_lstm.1 = (bf16[16,16,512]{2,1,0:T(8,128)(2,1)}, f32[16,16,512]{2,1,0:T(8,128)}, bf16[16,8,16,512]{3,2,1,0:T(8,128)(2,1)}, bf16[16,8,16,512]{3,2,1,0:T(8,1...) custom-call(bf16[16,8,16,512]{3,2,1,0:T(8,128)(2,1)} %bitcast.179, ...), custom_call_target="tpu_custom_call" | custom-call | tf_op jit(solution)/shard_map/relay_lstm/pallas_call | solution.py:315
  740.8 73.3 %reduce-scatter.2.cloned.1.call-done = bf16[4,16,512]{2,1,0:T(8,128)(2,1)} async-done(((bf16[16,16,512]{2,1,0:T(8,128)(2,1)}), bf16[4,16,512]{2,1,0:T(8,128)(2,1)}) %reduce-scatter.2.cloned.1.call-update) | async-done | bytes 65552 | tf_op jit(solution)/shard_map/reduce_scatter | solution.py:500
  826.4 10.4 multiply_convert_fusion.2
  837.6 12.0 %fusion.72 = (bf16[2048]{0:T(1024)(128)(2,1)}, f32[64,2048]{1,0:T(8,128)S(1)}) fusion(f32[2048]{0:T(1024)} %param.19, f32[64,2048]{1,0:T(8,128)S(1)} %get-tuple-element.90, f32[64,2048]{1,0:T(8,128)S(1)} %copy-done.6, bf16[2,2048,4096]{2,1,0:T(8,128)(2,1)} %all-gather.7.cloned.1.call-done, bf16[64,2048]{1,0:T(8,128)(2,1)} %copy-done.21, ...), kind=kOutput, calls=%fused_computation.154 | convolution fusion | flops 1077278720 | bytes 19935232 | tf_op jit(solution)/shard_map/tg,fg->tf/dot_general | solution.py:523
  849.7 12.0 %multiply_convert_fusion = bf16[64,50,2048]{2,0,1:T(8,128)(2,1)S(1)} fusion(f32[64,50,2048]{2,0,1:T(8,128)} %get-tuple-element.91, f32[64,2048]{1,0:T(8,128)S(1)} %get-tuple-element.59, f32[64,2048]{1,0:T(8,128)S(1)} %get-tuple-element.90, f32[64,2048]{1,0:T(8,128)S(1)} %get-tuple-element.95, pred[50,2048]{1,0:T(8,128)(4,1)S(1)} %iota_compare_fusion.7), kind=kLoop, calls=%fused_computation.1 | loop fusion | flops 32768000 | bytes 40996864 | tf_op jit(solution)/shard_map/convert_element_type | solution.py:373
  879.2 6.9 fusion.10
  896.1 8.6 convolution_convert_fusion.1
  914.7 10.0 convolution_convert_fusion
  952.6 121.3 %all_gather.31 = f32[8,4,512]{2,1,0:T(4,128)S(1)} all-gather(f32[1,4,512]{2,1,0:T(4,128)S(1)} %all_gather_reshape.3), channel_id=1, replica_groups=mesh['pipe'=2,'dir'=2,'dp'=8] {'dp'}, dimensions={0}, use_global_device_ids=true | all-gather | bytes 73728 | tf_op jit(solution)/shard_map/all_gather | solution.py:487
  1078.9 10.0 all-to-all-start.5
  1103.1 10.6 reshape.437
  1113.7 11.5 %copy.155 = f32[8,128,4,512]{3,0,2,1:T(8,128)} copy(f32[8,128,4,512]{3,2,1,0:T(4,128)} %reshape.437) | data formatting | bytes 16777216 | tf_op jit(solution)/shard_map/convert_element_type | solution.py:485
  1125.2 9.5 reshape.436
  (251 shorter events, 172.9 us)
Async XLA Ops:
  7.2 328.3 %copy-start = (bf16[1,1,16,16,512]{4,3,2,1,0:T(8,128)(2,1)S(1)}, bf16[1,1,16,16,512]{4,3,2,1,0:T(8,128)(2,1)}, u32[]{:S(2)}) copy-start(bf16[1,1,16,16,512]{4,3,2,1,0:T(8,128)(2,1)} %param.27) | copy-start | bytes 786436
  7.2 279.0 %all-gather.7.cloned.1.call-start = ((), (), s32[]{:S(2)}) async-start(), calls=%async_computation.9 | async-start | bytes 35651584 | tf_op jit(solution)/shard_map/all_gather | solution.py:416
  12.2 109.8 %all-to-all-start = ((s32[8,1,16]{2,1,0:T(1,128)}), s32[8,1,16]{2,1,0:T(1,128)S(1)}, u32[]{:S(2)}, u32[]{:S(2)}) async-start(s32[8,1,16]{2,1,0:T(1,128)} %broadcast_in_dim.56), calls=%async_computation | async-start | bytes 8192 | tf_op jit(solution)/shard_map/all_to_all | solution.py:418
  17.8 312.8 %all-gather.9.cloned.1.call-start = ((), (), s32[]{:S(2)}) async-start(), calls=%async_computation.10 | async-start | bytes 2228224 | tf_op jit(solution)/shard_map/all_gather | solution.py:417
  20.0 62.7 %copy-start.32 = (s32[2048]{0:T(1024)}, s32[2048]{0:T(1024)S(1)}, u32[]{:S(2)}) copy-start(s32[2048]{0:T(1024)S(1)} %convert_add_fusion) | copy-start | bytes 24580
  20.0 62.7 %copy-start.45 = (s32[112]{0:T(128)}, s32[112]{0:T(128)S(1)}, u32[]{:S(2)}) copy-start(s32[112]{0:T(128)S(1)} %and_select_fusion) | copy-start | bytes 1348
  122.7 220.3 %all-to-all-start.1 = ((bf16[8,128,2048]{1,2,0:T(8,128)(2,1)}), bf16[8,128,2048]{1,2,0:T(8,128)(2,1)}, u32[]{:S(2)}, u32[]{:S(2)}) async-start(bf16[8,128,2048]{1,2,0:T(8,128)(2,1)} %bitcast.176), calls=%async_computation.1 | async-start | bytes 8388608 | tf_op jit(solution)/shard_map/all_to_all | solution.py:425
  127.4 261.8 %all-gather.11.cloned.1.call-start = ((), (), s32[]{:S(2)}) async-start(), calls=%async_computation.11 | async-start | bytes 2162688 | tf_op jit(solution)/shard_map/all_gather | solution.py:450
  128.7 164.9 %copy-start.12 = (bf16[64,2048]{1,0:T(8,128)(2,1)}, bf16[64,2048]{1,0:T(8,128)(2,1)S(1)}, u32[]{:S(2)}) copy-start(bf16[64,2048]{1,0:T(8,128)(2,1)S(1)} %get-tuple-element.63) | copy-start | bytes 786436
  304.0 31.3 %copy-start.43 = (s32[16]{0:T(128)S(1)}, s32[16]{0:T(128)}, u32[]{:S(2)}) copy-start(s32[16]{0:T(128)} %param.16) | copy-start | bytes 196
  333.3 480.8 %reduce-scatter.2.cloned.1.call-start = ((), (), s32[]{:S(2)}) async-start(), calls=%async_computation.12 | async-start | bytes 327680 | tf_op jit(solution)/shard_map/reduce_scatter | solution.py:500
  394.3 344.8 %copy-start.30 = (s32[16,16]{1,0:T(8,128)S(1)}, s32[16,16]{1,0:T(8,128)}, u32[]{:S(2)}) copy-start(s32[16,16]{1,0:T(8,128)} %copy-done.29) | copy-start | bytes 3076
  394.3 344.8 %copy-start.39 = (pred[16,16]{1,0:T(8,128)(4,1)S(1)}, pred[16,16]{1,0:T(8,128)(4,1)}, u32[]{:S(2)}) copy-start(pred[16,16]{1,0:T(8,128)(4,1)} %copy-done.38) | copy-start | bytes 772
  738.0 76.1 %copy-start.24 = (s32[4,16,50]{2,1,0:T(8,128)S(1)}, s32[4,16,50]{2,1,0:T(8,128)}, u32[]{:S(2)}) copy-start(s32[4,16,50]{2,1,0:T(8,128)} %copy-done.23) | copy-start | bytes 38404
  740.2 351.2 %all-gather.13.cloned.1.call-start = ((), (), s32[]{:S(2)}) async-start(), calls=%async_computation.13 | async-start | bytes 8650752 | tf_op jit(solution)/shard_map/all_gather | solution.py:457
  740.8 359.6 %all-gather.17.cloned.1.call-start = ((), (), s32[]{:S(2)}) async-start(), calls=%async_computation.15 | async-start | bytes 2162688 | tf_op jit(solution)/shard_map/all_gather | solution.py:503
  816.2 73.8 %all-to-all-start.6 = ((bf16[32,2,2048]{2,1,0:T(2,128)(2,1)}), bf16[32,2,2048]{2,1,0:T(2,128)(2,1)S(1)}, u32[]{:S(2)}, u32[]{:S(2)}) async-start(bf16[32,2,2048]{2,1,0:T(2,128)(2,1)} %reshape.476), calls=%async_computation.7 | async-start | bytes 524288 | tf_op jit(solution)/shard_map/all_to_all | solution.py:366
  822.4 312.3 %all-gather.15.cloned.1.call-start = ((), (), s32[]{:S(2)}) async-start(), calls=%async_computation.14 | async-start | bytes 8650752 | tf_op jit(solution)/shard_map/all_gather | solution.py:457
  889.9 20.6 %all-to-all-start.2 = ((bf16[32,2,3840]{2,1,0:T(2,128)(2,1)}), bf16[32,2,3840]{2,1,0:T(2,128)(2,1)S(1)}, u32[]{:S(2)}, u32[]{:S(2)}) async-start(bf16[32,2,3840]{2,1,0:T(2,128)(2,1)} %reshape.474), calls=%async_computation.3 | async-start | bytes 983040 | tf_op jit(solution)/shard_map/all_to_all | solution.py:549
  910.5 20.9 %all-to-all-start.4 = ((bf16[32,64,128]{2,1,0:T(8,128)(2,1)}), bf16[32,64,128]{2,1,0:T(8,128)(2,1)}, u32[]{:S(2)}, u32[]{:S(2)}) async-start(bf16[32,64,128]{2,1,0:T(8,128)(2,1)} %maximum_bitcast_fusion), calls=%async_computation.5 | async-start | bytes 1048576 | tf_op jit(solution)/shard_map/all_to_all | solution.py:366
  932.1 9.4 all-to-all-start.3
  941.6 137.4 %all-to-all-start.7 = ((bf16[8,128,2048]{2,1,0:T(8,128)(2,1)}), bf16[8,128,2048]{2,1,0:T(8,128)(2,1)}, u32[]{:S(2)}, u32[]{:S(2)}) async-start(bf16[8,128,2048]{2,1,0:T(8,128)(2,1)} %bitcast.177), calls=%async_computation.8 | async-start | bytes 8388608 | tf_op jit(solution)/shard_map/all_to_all | solution.py:484
  947.7 126.3 %copy-start.48 = (bf16[16,128,512]{2,1,0:T(8,128)(2,1)S(1)}, bf16[16,128,512]{2,1,0:T(8,128)(2,1)}, u32[]{:S(2)}) copy-start(bf16[16,128,512]{2,1,0:T(8,128)(2,1)} %get-tuple-element.24) | copy-start | bytes 6291460
  1078.9 55.8 %all-to-all-start.5 = ((bf16[32,64,128]{2,1,0:T(8,128)(2,1)}), bf16[32,64,128]{2,1,0:T(8,128)(2,1)S(1)}, u32[]{:S(2)}, u32[]{:S(2)}) async-start(bf16[32,64,128]{2,1,0:T(8,128)(2,1)} %maximum_bitcast_fusion.1), calls=%async_computation.6 | async-start | bytes 1048576 | tf_op jit(solution)/shard_map/all_to_all | solution.py:366
  (42 other events, 314.4 us)
Sparse Core Ops, SparseCore 0:
  11.1 274.9 all-gather.6
  289.0 41.5 all-gather.8
  334.0 55.1 all-gather.10
  740.3 73.7 reduce-scatter.1
  817.3 79.1 all-gather.12
  899.7 56.9 all-gather.16
  960.2 133.8 all-gather.14

commit v3 on v2

--- a/solution.py
+++ b/solution.py
@@ -69,11 +69,11 @@
 def lstm_kernel(
     n, chunk,
     x_hbm, wx, wh, bias, p, wxt, wht, pt, cot,
-    out_ref, dx_ref, x_all, h_all, da_all, e_all, dq_all,
-    xbuf, hbuf, dqbuf, gates, cells, ebuf, hown, gscr, escr, dabuf, ucell,
+    out_ref, dx_ref, dw_hbm, db_ref, dp_ref,
+    xbuf, hbuf, dqbuf, gates, cells, ebuf, hown, gscr, escr, dabuf, ucell, dwacc,
     stage, inbox, stage2, inbox2, relay, gbuf, rown,
     load_sem, ag_send, ag_recv, dq_send, dq_recv, rs_send, rs_recv, dx_send, dx_recv,
-    x_send, x_recv, g_send, g_recv, da_sem, st_sem,
+    x_send, x_recv, g_send, g_recv, st_sem,
 ):
     steps, _, rows, width = xbuf.shape
     total = n * rows
@@ -206,6 +206,9 @@
 
     rown[...] = jnp.zeros((rows, width), F32)
     ucell[...] = jnp.zeros((total, cell), F32)
+    dwacc[...] = jnp.zeros(dwacc.shape, F32)
+    db_ref[...] = jnp.zeros(db_ref.shape, F32)
+    dp_ref[...] = jnp.zeros(dp_ref.shape, F32)
 
     def dx_finish(t):
         slot = lax.rem(t, 2)
@@ -222,10 +225,6 @@
             relay[t] = (dx + cot[t].astype(F32)).astype(BF)
             g_copy(t).start()
 
-    def da_copy(t):
-        slot = lax.rem(t, 2)
-        return pltpu.make_async_copy(dabuf.at[slot], da_all.at[t], da_sem.at[slot])
-
     def backward(k, _):
         t = steps - 1 - k
         slot = lax.rem(t, 2)
@@ -244,10 +243,6 @@
         @pl.when(k > 0)
         def _():
             dx_finish(t + 1)
-
-        @pl.when(k > 1)
-        def _():
-            da_copy(t + 2).wait()
 
         ag_wait(dqbuf, t)
         escr[...] = jnp.dot(
@@ -265,22 +260,34 @@
             cr = c * (1.0 / 3.0)
             dc = (de * o * (1.0 - tc * tc) + ucell[at, :]) * (1.0 - cr * cr)
             ucell[at, :] = dc * f
-            dabuf[slot, at, :cell] = (dc * m * i * (1.0 - i)).astype(BF)
-            dabuf[slot, at, cell:2 * cell] = (dc * cells[t, at, :] * f * (1.0 - f)).astype(BF)
-            dabuf[slot, at, 2 * cell:3 * cell] = (dc * i * (1.0 - m * m)).astype(BF)
-            dabuf[slot, at, 3 * cell:] = (de * tc * o * (1.0 - o)).astype(BF)
+            for block, value in enumerate((
+                dc * m * i * (1.0 - i),
+                dc * cells[t, at, :] * f * (1.0 - f),
+                dc * i * (1.0 - m * m),
+                de * tc * o * (1.0 - o),
+            )):
+                value = value.astype(BF)
+                where = pl.ds(block * cell, cell)
+                dabuf[0, at, where] = value
+                db_ref[:, where] += jnp.sum(value.astype(F32), axis=0, keepdims=True)
             return 0
 
         lax.fori_loop(0, total // chunk, rows_step, 0)
-        r = jnp.dot(dabuf[slot], wht[...], preferred_element_type=F32)
+        r = jnp.dot(dabuf[0], wht[...], preferred_element_type=F32)
         stage[...] = r.astype(BF).reshape(n, rows, width)
         over(n, lambda off: rs_copy(off).start())
         inbox[me] = stage[me]
-        dx = jnp.dot(dabuf[slot], wxt[...], preferred_element_type=F32)
+        dx = jnp.dot(dabuf[0], wxt[...], preferred_element_type=F32)
         stage2[slot] = dx.astype(BF).reshape(n, rows, width)
         over(n, lambda off: dx_copy(slot, off).start())
         inbox2[slot, me] = stage2[slot, me]
-        da_copy(t).start()
+        for half, buf in enumerate((xbuf, hbuf)):
+            dwacc[pl.ds(half * width, width), :] += lax.dot_general(
+                buf[t].reshape(total, width), dabuf[0], (((0,), (0,)), ((), ())),
+                preferred_element_type=F32)
+        dp_ref[...] += lax.dot_general(
+            ebuf[t], dqbuf[t].reshape(total, width), (((0,), (0,)), ((), ())),
+            preferred_element_type=F32)
         rs_wait()
         rown[...] = jnp.sum(inbox[...].astype(F32), axis=0)
         return 0
@@ -292,14 +299,19 @@
     def _():
         lax.fori_loop(0, steps, lambda t, _: (g_copy(t).wait_send(), 0)[1], 0)
 
-    da_copy(1).wait()
-    da_copy(0).wait()
-    for at, (buf, dst) in enumerate(((xbuf, x_all), (hbuf.at[pl.ds(0, steps)], h_all),
-                                     (ebuf, e_all), (dqbuf, dq_all))):
-        pltpu.make_async_copy(buf, dst, st_sem.at[at]).start()
-    for at, (buf, dst) in enumerate(((xbuf, x_all), (hbuf.at[pl.ds(0, steps)], h_all),
-                                     (ebuf, e_all), (dqbuf, dq_all))):
-        pltpu.make_async_copy(buf, dst, st_sem.at[at]).wait()
+    pieces = 2 * width // total
+
+    def dw_copy(piece):
+        return pltpu.make_async_copy(
+            dabuf.at[piece % 2], dw_hbm.at[pl.ds(piece * total, total)], st_sem.at[piece % 2])
+
+    for piece in range(pieces):
+        if piece > 1:
+            dw_copy(piece - 2).wait()
+        dabuf[piece % 2] = dwacc[pl.ds(piece * total, total), :].astype(BF)
+        dw_copy(piece).start()
+    for piece in range(max(0, pieces - 2), pieces):
+        dw_copy(piece).wait()
 
 
 def lstm_call(n, x, wx, wh, bias, p, wxt, wht, pt, cot, chunk=16):
@@ -316,27 +328,70 @@
         functools.partial(lstm_kernel, n, chunk),
         out_shape=(
             sds((steps, rows, width), BF), sds((steps, rows, width), F32),
-            sds((steps, n, rows, width), BF), sds((steps, n, rows, width), BF),
-            sds((steps, total, 4 * cell), BF), sds((steps, total, cell), BF),
-            sds((steps, n, rows, width), BF)),
+            sds((2 * width, 4 * cell), BF), sds((1, 4 * cell), F32), sds((cell, width), F32)),
         in_specs=[hb] + [vm] * 8,
-        out_specs=(vm, vm, hb, hb, hb, hb, hb),
+        out_specs=(vm, vm, hb, vm, vm),
         scratch_shapes=[
             V((steps, n, rows, width), BF), V((steps + 1, n, rows, width), BF),
             V((steps, n, rows, width), BF), V((steps, total, 4 * cell), keep),
             V((steps + 1, total, cell), F32), V((steps, total, cell), BF),
             V((steps, rows, width), F32), V((total, 4 * cell), F32),
             V((total, cell), F32), V((2, total, 4 * cell), BF), V((total, cell), F32),
+            V((2 * width, 4 * cell), F32),
             V((n, rows, width), BF), V((n, rows, width), BF),
             V((2, n, rows, width), BF), V((2, n, rows, width), BF),
             V((steps, rows, width), BF), V((steps, rows, width), BF), V((rows, width), F32),
             dma, dma((n,)), dma((n,)), dma((n,)), dma((n,)), dma((n,)), dma((n,)), dma((2, n)), dma((2, n)),
-            dma((steps,)), dma((steps,)), dma((steps,)), dma((steps,)), dma((2,)), dma((4,)),
+            dma((steps,)), dma((steps,)), dma((steps,)), dma((steps,)), dma((2,)),
         ],
         compiler_params=pltpu.CompilerParams(
             collective_id=0, has_side_effects=True, vmem_limit_bytes=60 * 1024 * 1024),
+        cost_estimate=pl.CostEstimate(
+            flops=300_000_000_000, bytes_accessed=64 * 1024 * 1024, transcendentals=0),
         name="relay_lstm",
     )(x, wx, wh, bias, p, wxt, wht, pt, cot)
+
+
+def split_cells(weight, n):
+    rows, gates = weight.shape
+    cell = gates // (4 * n)
+
+    def body(src, dst):
+        for k in range(n):
+            dst[k] = src[:, k * cell : (k + 1) * cell].astype(BF)
+
+    return pl.pallas_call(
+        body,
+        grid=(4,),
+        out_shape=jax.ShapeDtypeStruct((n, rows, 4 * cell), BF),
+        in_specs=[pl.BlockSpec((rows, n * cell), lambda b: (0, b))],
+        out_specs=pl.BlockSpec((n, rows, cell), lambda b: (0, 0, b)),
+        cost_estimate=pl.CostEstimate(
+            flops=0, bytes_accessed=6 * rows * gates, transcendentals=0
+        ),
+        name="split_cells",
+    )(weight)
+
+
+def join_cells(blocks):
+    n, rows, gates = blocks.shape
+    cell = gates // 4
+
+    def body(src, dst):
+        for k in range(n):
+            dst[:, k * cell : (k + 1) * cell] = src[k].astype(F32)
+
+    return pl.pallas_call(
+        body,
+        grid=(4,),
+        out_shape=jax.ShapeDtypeStruct((rows, n * gates), F32),
+        in_specs=[pl.BlockSpec((n, rows, cell), lambda b: (0, 0, b))],
+        out_specs=pl.BlockSpec((rows, n * cell), lambda b: (0, b)),
+        cost_estimate=pl.CostEstimate(
+            flops=0, bytes_accessed=6 * n * rows * gates, transcendentals=0
+        ),
+        name="join_cells",
+    )(blocks)
 
 
 def encode_forward(ids, weights):
@@ -412,17 +467,35 @@
     width = cell_proj.shape[3]
     cell = cell_proj.shape[2]
 
-    conv_full = lax.all_gather(conv_weight.astype(BF), ("dir", "dp"), axis=1, tiled=True)
-    highway_full = lax.all_gather(highway_weight.astype(BF), ("dir", "dp"), axis=2, tiled=True)
-    proj_full = lax.all_gather(proj_weight.astype(BF), ("dir", "dp"), axis=0, tiled=True)
+    holders = lax.axis_size(("dir", "dp"))
+    mine = conv_weight.shape[1]
+    conv_full = lax.all_to_all(
+        jnp.broadcast_to(conv_weight.astype(BF), (holders, KMAX * CDIM, mine)), ("dir", "dp"), 0, 0
+    )
+    conv_full = jnp.transpose(conv_full, (1, 0, 2)).reshape(KMAX * CDIM, FILTERS)
+    proj_rows = proj_weight.shape[0]
+    block = highway_weight.shape[2]
+    pieces = width // block
+    proj_blocks = jnp.transpose(proj_weight.reshape(proj_rows, pieces, block), (1, 0, 2))
+    proj_blocks = proj_blocks.reshape(2, pieces * proj_rows // 2, block)
+    gathered = lax.all_gather(
+        jnp.concatenate([highway_weight, proj_blocks], axis=1).astype(BF),
+        ("dir", "dp"),
+        axis=2,
+        tiled=True,
+    )
     all_lengths = lax.all_to_all(
         jnp.broadcast_to(lengths, (n, seqs)), "dp", 0, 0
     ).reshape(n * seqs)
 
     in_rows = gate_weight.shape[2]
-    gate_low = gate_weight[0, 0].astype(BF).reshape(in_rows, 4, n, cell)
-    gate_low = jnp.transpose(gate_low, (2, 0, 1, 3)).reshape(n, in_rows, 4 * cell)
+    gate_low, gathered = lax.optimization_barrier(
+        (split_cells(gate_weight[0, 0], n), gathered)
+    )
     gate_own = lax.all_to_all(gate_low, "dp", 0, 0).reshape(n * in_rows, 4 * cell)
+    highway_full = gathered[:, :FILTERS]
+    proj_full = gathered[:, FILTERS:].reshape(pieces, proj_rows, holders, block)
+    proj_full = jnp.transpose(proj_full, (2, 1, 0, 3)).reshape(FILTERS, width)
     bias_own = lax.dynamic_index_in_dim(
         gate_bias[0, 0].reshape(4, n, cell), me, 1, keepdims=False
     ).reshape(1, 4 * cell)
@@ -450,14 +523,15 @@
     encoded_all = lax.all_gather(
         encoded.astype(BF).reshape(quarter, steps, width), ("dp", "pipe", "dir"), axis=0, tiled=True
     )
+    kept_low = [value.astype(BF) for value in kept]
+    kept_low, encoded_all, gate_own = lax.optimization_barrier((kept_low, encoded_all, gate_own))
+    kept_all = [lax.all_gather(value, ALL, axis=0, tiled=True) for value in kept_low[:2]]
+    last_columns = to_columns(kept_low[2])
     inputs = jnp.einsum(
         "rts,rsd->trd", order_matrix(all_lengths), encoded_all, preferred_element_type=BF
     ).reshape(steps, n, seqs, width)
-    kept_low = [value.astype(BF) for value in kept]
-    kept_all = [lax.all_gather(value, ALL, axis=0, tiled=True) for value in kept_low[:2]]
-    last_columns = to_columns(kept_low[2])
-
-    out_own, dx_own, x_all, h_all, da_all, e_all, dq_all = lstm_call(
+
+    out_own, dx_own, grad_gate, grad_bias, grad_cell = lstm_call(
         n,
         inputs,
         gate_own[:width],
@@ -469,29 +543,16 @@
         cell_low.T,
         cot,
     )
+    dx_own, kept_all, last_columns = lax.optimization_barrier((dx_own, kept_all, last_columns))
     activations = jnp.einsum("rts,srd->rtd", own_order, out_own, preferred_element_type=BF)
 
-    total = steps * n * seqs
-    da_flat = da_all.reshape(total, 4 * cell)
-    grad_gate = jnp.concatenate(
-        [
-            jnp.einsum(
-                "tk,tg->kg", part.reshape(total, width), da_flat, preferred_element_type=F32
-            ).astype(BF)
-            for part in (x_all, h_all)
-        ]
-    ).reshape(n, in_rows, 4 * cell)
-    grad_gate = lax.all_to_all(grad_gate, "dp", 0, 0).reshape(n, in_rows, 4, cell)
-    grad_gate = jnp.transpose(grad_gate, (1, 2, 0, 3)).reshape(in_rows, 4 * n * cell).astype(F32)
-    grad_bias = jnp.sum(da_flat.astype(F32), axis=0).reshape(4, cell)
-    grad_bias = jnp.transpose(lax.all_gather(grad_bias, "dp"), (1, 0, 2)).reshape(n, 4 * cell)
+    grad_gate = grad_gate.reshape(n, 2, in_rows // 2, 4 * cell)
+    gate_halves = [lax.all_to_all(grad_gate[:, half], "dp", 0, 0) for half in range(2)]
+    grad_bias = lax.all_to_all(
+        jnp.broadcast_to(grad_bias, (n, 4 * cell)), "dp", 0, 0
+    ).reshape(n, 4, cell)
+    grad_bias = jnp.transpose(grad_bias, (1, 0, 2)).reshape(n, 4 * cell)
     grad_bias = lax.dynamic_index_in_dim(grad_bias, me, 0, keepdims=False)
-    grad_cell = jnp.einsum(
-        "tc,td->cd",
-        e_all.reshape(total, cell),
-        dq_all.reshape(total, width),
-        preferred_element_type=F32,
-    )
 
     grad_stored = jnp.einsum(
         "rts,srd->rtd", own_order, dx_own.astype(BF), preferred_element_type=F32
@@ -504,7 +565,7 @@
 
     grad_proj_bias = jnp.sum(grad_encoded.astype(F32), axis=0)
     grad_features = jnp.einsum("td,fd->tf", grad_encoded, proj_full, preferred_element_type=F32)
-    grad_highway = [None, None]
+    columns = [None, None]
     grad_highway_bias = [None, None]
     for layer in (1, 0):
         nonlinear = mixed[layer][:, :FILTERS]
@@ -516,16 +577,27 @@
             ],
             axis=1,
         ).astype(BF)
-        grad_highway[layer] = jnp.einsum(
-            "tf,tg->fg", kept_all[layer], to_columns(grad_mixed), preferred_element_type=F32
-        )
+        columns[layer] = to_columns(grad_mixed)
         grad_highway_bias[layer] = jnp.sum(grad_mixed.astype(F32), axis=0)
         grad_features = grad_features * gate + jnp.einsum(
             "tg,fg->tf", grad_mixed, highway_full[layer], preferred_element_type=F32
         )
+        if layer == 1:
+            grad_features, gate_halves[0] = lax.optimization_barrier(
+                (grad_features, gate_halves[0])
+            )
+    grad_features, columns[1] = lax.optimization_barrier((grad_features, columns[1]))
     grad_proj = jnp.einsum("tf,td->fd", last_columns, encoded_grads, preferred_element_type=F32)
     grad_before = grad_features * silu_slope(pooled + conv_bias)
     grad_conv, grad_table = conv_backward(ids, table_low, conv_low, grad_before)
+    grad_conv, gate_halves[1], columns[0] = lax.optimization_barrier(
+        (grad_conv, gate_halves[1], columns[0])
+    )
+    grad_highway = [
+        jnp.einsum("tf,tg->fg", kept_all[layer], columns[layer], preferred_element_type=F32)
+        for layer in range(2)
+    ]
+    grad_gate = join_cells(jnp.concatenate(gate_halves, axis=1))
 
     small = (
         grad_table,

time: 1160 us -> 1070 us (0.922)
  blocking collectives: 164 us -> 0 us
  Pallas kernels: 344 us -> 408 us
  starting transfers between devices: 46.1 us -> 103 us
  matrix products: 112 us -> 89.6 us
  local copies, waits for them, and re-layouts: 116 us -> 94.1 us
    all_gather x2 -> x0, blocking collectives: 164 us -> none  [the longest x1 121 us: local(): lax.all_gather(grad_bias, 'dp')]
    all_to_all x1, waiting for transfers between devices: 0.01 us -> 78.8 us  [local(): lax.all_to_all(gate_low, 'dp', 0, 0).reshape(n * in_rows, 4 * cell)]
    reduce_scatter x1, waiting for transfers between devices: 73.3 us -> 17.8 us  [local(): lax.psum_scatter(grad_stored, ('pipe', 'dir'), scatter_dimension=0, tiled...]
    pallas_call x1, Pallas kernels: 344 us -> 396 us  [lstm_call(): pl.pallas_call(functools.partial(lstm_kernel, n, chunk), out_shape=(sds((...]
    all_gather x2 -> x1, waiting for transfers between devices: 183 us -> 133 us  [local(): lax.all_gather(jnp.concatenate([highway_weight, proj_blocks], axis=1).ast...]
    all_to_all x3, starting transfers between devices: 20.4 us -> 63.4 us  [to_columns(): lax.all_to_all(split, ALL, 0, 0).reshape(count * tokens, columns // count)]
    convert_element_type x4 -> x0, local copies, waits for them, and re-layouts: 39.5 us -> none  [the longest x3 31.6 us: local(): jnp.transpose(grad_gate, (1, 2, 0, 3)).reshape(in_rows, 4 * n * cell)]
    all_to_all x1 -> x4, waiting for transfers between devices: 0.01 us -> 39.3 us  [the longest x2 34.6 us: local(): lax.all_to_all(grad_gate[:, half], 'dp', 0, 0)]
  transfers between devices with their start and end apart: 15 -> 17, of which waited for: 7 -> 10; matrix products, arithmetic and copies ran while one was open for 22% -> 20% of each run, Pallas kernels for 0% -> 39%
where the time goes in v3:
time: 1070 us; the launch traced here: 1060 us
  Pallas kernels  408 us (38%)
  waiting for transfers between devices  295 us (28%)
  starting transfers between devices  103 us (10%)
  local copies, waits for them, and re-layouts  94.1 us (9%)
  matrix products  89.6 us (8%)
  other arithmetic  53.1 us (5%)
  between operations  15.5 us (1%)
    pallas_call x1, Pallas kernels, lstm_call(): pl.pallas_call(functools.partial(lstm_kernel, n, chunk), out_shape=(sds((...  396 us
    all_gather x1, waiting for transfers between devices, local(): lax.all_gather(jnp.concatenate([highway_weight, proj_blocks], axis=1).ast...  133 us
    all_to_all x1, waiting for transfers between devices, local(): lax.all_to_all(gate_low, 'dp', 0, 0).reshape(n * in_rows, 4 * cell)  78.8 us
    all_to_all x3, starting transfers between devices, to_columns(): lax.all_to_all(split, ALL, 0, 0).reshape(count * tokens, columns // count)  63.4 us
    all_to_all x2, waiting for transfers between devices, local(): lax.all_to_all(grad_gate[:, half], 'dp', 0, 0)  34.6 us
  transfers between devices with their start and end apart: 17, of which 10 were waited for; matrix products, arithmetic and copies ran while one was open for 20% of the time, Pallas kernels for 39%

profile of v3, /device:TPU:3, one launch (start us, length us, event | category | flops | bytes accessed | tf_op | source)
XLA Modules:
  0.0 1058.0 jit_solution(4621210972648906175)
XLA Ops:
  13.9 6.5 all-to-all-start
  21.5 6.7 gather_fusion
  40.0 6.6 concatenate.54
  47.6 12.6 %select_reduce_fusion = (f32[64,2048]{1,0:T(8,128)S(1)}, f32[64,50,2048]{2,0,1:T(8,128)}) fusion(pred[50,2048]{1,0:T(8,128)(4,1)S(1)} %iota_compare_fusion.7, bf16[64,50,112]{2,0,1:T(8,128)(2,1)S(1)} %concatenate.54, s32[2048]{0:T(1024)S(1)} %convert_add_fusion, s32[112]{0:T(128)S(1)} %and_select_fusion, bf16[16,112,128]{2,1,0:T(8,128)(2,1)} %all-to-all-done), kind=kOutput, calls=%fused_computation.5 | convolution fusion | flops 1482588160 | bytes 28025280 | tf_op jit(solution)/shard_map/bpk,kf->bpf/dot_general | solution.py:57
  60.2 14.8 %fusion = (f32[64,2048]{1,0:T(8,128)}, f32[64,2048]{1,0:T(8,128)S(1)}) fusion(f32[64,50,2048]{2,0,1:T(8,128)} %get-tuple-element.136, f32[64,2048]{1,0:T(8,128)S(1)} %get-tuple-element.135, pred[50,2048]{1,0:T(8,128)(4,1)S(1)} %iota_compare_fusion.7, f32[64,2048]{1,0:T(8,128)S(1)} %is-finite_select_fusion), kind=kLoop, calls=%fused_computation.4 | loop fusion | flops 32505856 | bytes 28413952 | tf_op jit(solution)/shard_map/reduce_sum | solution.py:427
  76.1 133.3 %all-gather.6.cloned.1.call-done = bf16[2,2176,4096]{2,1,0:T(8,128)(2,1)} async-done(((bf16[2,2176,256]{2,1,0:T(8,128)(2,1)}), bf16[2,2176,4096]{2,1,0:T(8,128)(2,1)}) %all-gather.6.cloned.1.call-update) | async-done | bytes 35651600 | tf_op jit(solution)/shard_map/all_gather | solution.py:481
  220.7 7.4 fusion.14
  229.0 7.7 fusion.17
  238.6 78.8 %all-to-all-done.1 = bf16[8,128,2048]{2,1,0:T(8,128)(2,1)} async-done(((bf16[8,128,2048]{2,1,0:T(8,128)(2,1)}), bf16[8,128,2048]{2,1,0:T(8,128)(2,1)}, u32[]{:S(2)}, u32[]{:S(2)}) %all-to-all-start.1) | async-done | bytes 4194336 | tf_op jit(solution)/shard_map/all_to_all | solution.py:495
  317.4 6.4 copy.167
  323.8 13.5 %all-gather.8.cloned.1.call-done = bf16[128,16,512]{2,1,0:T(8,128)(2,1)} async-done(((bf16[4,16,512]{2,1,0:T(8,128)(2,1)}), bf16[128,16,512]{2,1,0:T(8,128)(2,1)}) %all-gather.8.cloned.1.call-update) | async-done | bytes 2097168 | tf_op jit(solution)/shard_map/all_gather | solution.py:523
  362.2 396.0 %relay_lstm.1 = (bf16[16,16,512]{2,1,0:T(8,128)(2,1)}, f32[16,16,512]{2,1,0:T(8,128)}, bf16[1024,2048]{1,0:T(8,128)(2,1)}, f32[1,2048]{1,0:T(1,128)}, f32[512,512]{1,0:T(8,128)}) custom-call(bf16[16,8,16,512]{3,2,1,0:T(8,128)(2,1)} %bitcast.192, bf16[512,2048]{1,0:T(8,128)(2,1)} %copy.144.wx, bf16[512,2048]{1,0:T(8,128)(2,1)} %copy.145.wh, ...), custom_call_target="tpu_custom_call" | custom-call | flops 299999985664 | bytes 67108864 | tf_op jit(solution)/shard_map/relay_lstm/pallas_call | solution.py:327
  771.5 53.7 %all-to-all-start.3 = ((bf16[32,2,2048]{2,1,0:T(2,128)(2,1)}), bf16[32,2,2048]{2,1,0:T(2,128)(2,1)S(1)}, u32[]{:S(2)}, u32[]{:S(2)}) async-start(bf16[32,2,2048]{2,1,0:T(2,128)(2,1)} %reshape.459), calls=%async_computation.3 | async-start | bytes 524288 | tf_op jit(solution)/shard_map/all_to_all | solution.py:421
  845.9 17.8 %reduce-scatter.2.cloned.1.call-done = bf16[4,16,512]{2,1,0:T(8,128)(2,1)} async-done(((bf16[16,16,512]{2,1,0:T(8,128)(2,1)}), bf16[4,16,512]{2,1,0:T(8,128)(2,1)}) %reduce-scatter.2.cloned.1.call-update) | async-done | bytes 65552 | tf_op jit(solution)/shard_map/reduce_scatter | solution.py:561
  868.2 9.9 fusion.25
  878.1 8.6 all-to-all-done.4
  896.5 9.9 fusion.22
  918.2 11.8 %multiply_convert_fusion = bf16[64,50,2048]{2,0,1:T(8,128)(2,1)S(1)} fusion(f32[64,50,2048]{2,0,1:T(8,128)} %get-tuple-element.136, f32[64,2048]{1,0:T(8,128)S(1)} %copy-done.12, f32[64,2048]{1,0:T(8,128)S(1)} %copy-done.4, f32[64,2048]{1,0:T(8,128)S(1)} %get-tuple-element.105, pred[50,2048]{1,0:T(8,128)(4,1)S(1)} %copy-done.19), kind=kLoop, calls=%fused_computation.1 | loop fusion | flops 32768000 | bytes 40996864 | tf_op jit(solution)/shard_map/convert_element_type | solution.py:428
  939.5 7.0 fusion.94
  946.5 26.0 %all-to-all-done.6 = bf16[8,64,2048]{2,1,0:T(8,128)(2,1)} async-done(((bf16[8,64,2048]{2,1,0:T(8,128)(2,1)}), bf16[8,64,2048]{2,1,0:T(8,128)(2,1)}, u32[]{:S(2)}, u32[]{:S(2)}) %all-to-all-start.6) | async-done | bytes 2097184 | tf_op jit(solution)/shard_map/all_to_all | solution.py:550
  982.9 7.6 fusion.21
  1006.9 6.8 convolution_bitcast_fusion
  1017.8 6.8 convolution_bitcast_fusion.1
  1028.5 6.0 all-to-all-start.9
  (244 shorter events, 180.5 us)
Async XLA Ops:
  7.2 335.7 %copy-start = (bf16[1,1,16,16,512]{4,3,2,1,0:T(8,128)(2,1)S(1)}, bf16[1,1,16,16,512]{4,3,2,1,0:T(8,128)(2,1)}, u32[]{:S(2)}) copy-start(bf16[1,1,16,16,512]{4,3,2,1,0:T(8,128)(2,1)} %param.27) | copy-start | bytes 786436
  7.2 202.2 %all-gather.6.cloned.1.call-start = ((), (), s32[]{:S(2)}) async-start(), calls=%async_computation.12 | async-start | bytes 37879808 | tf_op jit(solution)/shard_map/all_gather | solution.py:481
  13.9 33.7 %all-to-all-start = ((bf16[16,112,128]{2,1,0:T(8,128)(2,1)}), bf16[16,112,128]{2,1,0:T(8,128)(2,1)}, u32[]{:S(2)}, u32[]{:S(2)}) async-start(bf16[16,112,128]{2,1,0:T(8,128)(2,1)} %broadcast_in_dim.60), calls=%async_computation | async-start | bytes 917504 | tf_op jit(solution)/shard_map/all_to_all | solution.py:472
  76.1 144.6 %copy-start.23 = (bf16[64,2048]{1,0:T(8,128)(2,1)}, bf16[64,2048]{1,0:T(8,128)(2,1)S(1)}, u32[]{:S(2)}) copy-start(bf16[64,2048]{1,0:T(8,128)(2,1)S(1)} %get-tuple-element.41) | copy-start | bytes 786436
  76.1 151.9 %copy-start.8 = (f32[64,2048]{1,0:T(8,128)}, f32[64,2048]{1,0:T(8,128)S(1)}, u32[]{:S(2)}) copy-start(f32[64,2048]{1,0:T(8,128)S(1)} %get-tuple-element.109) | copy-start | bytes 1572868
  215.6 101.8 %all-to-all-start.1 = ((bf16[8,128,2048]{2,1,0:T(8,128)(2,1)}), bf16[8,128,2048]{2,1,0:T(8,128)(2,1)}, u32[]{:S(2)}, u32[]{:S(2)}) async-start(bf16[8,128,2048]{2,1,0:T(8,128)(2,1)} %split_cells.1), calls=%async_computation.1 | async-start | bytes 8388608 | tf_op jit(solution)/shard_map/all_to_all | solution.py:495
  220.1 117.1 %all-gather.8.cloned.1.call-start = ((), (), s32[]{:S(2)}) async-start(), calls=%async_computation.13 | async-start | bytes 2162688 | tf_op jit(solution)/shard_map/all_gather | solution.py:523
  238.5 603.2 %all-gather.10.cloned.1.call-start = ((), (), s32[]{:S(2)}) async-start(), calls=%async_computation.14 | async-start | bytes 8650752 | tf_op jit(solution)/shard_map/all_gather | solution.py:528
  317.4 19.9 %copy-start.42 = (s32[16]{0:T(128)S(1)}, s32[16]{0:T(128)}, u32[]{:S(2)}) copy-start(s32[16]{0:T(128)} %param.16) | copy-start | bytes 196
  317.4 24.5 %copy-start.35 = (f32[1,1,16384]{2,1,0:T(1,128)S(1)}, f32[1,1,16384]{2,1,0:T(1,128)}, u32[]{:S(2)}) copy-start(f32[1,1,16384]{2,1,0:T(1,128)} %param.25) | copy-start | bytes 196612
  337.9 9.5 all-to-all-start.2
  341.4 500.3 %all-gather.12.cloned.1.call-start = ((), (), s32[]{:S(2)}) async-start(), calls=%async_computation.15 | async-start | bytes 8650752 | tf_op jit(solution)/shard_map/all_gather | solution.py:528
  362.2 403.1 %copy-start.21 = (bf16[64,2048]{1,0:T(8,128)(2,1)S(1)}, bf16[64,2048]{1,0:T(8,128)(2,1)}, u32[]{:S(2)}) copy-start(bf16[64,2048]{1,0:T(8,128)(2,1)} %copy-done.20) | copy-start | bytes 786436
  759.5 12.0 %all-to-all-start.10 = ((f32[8,1,2048]{2,1,0:T(1,128)}), f32[8,1,2048]{2,1,0:T(1,128)S(1)}, u32[]{:S(2)}, u32[]{:S(2)}) async-start(f32[8,1,2048]{2,1,0:T(1,128)} %broadcast_in_dim.105), calls=%async_computation.11 | async-start | bytes 131072 | tf_op jit(solution)/shard_map/all_to_all | solution.py:551
  771.5 63.3 %all-to-all-start.3 = ((bf16[32,2,2048]{2,1,0:T(2,128)(2,1)}), bf16[32,2,2048]{2,1,0:T(2,128)(2,1)S(1)}, u32[]{:S(2)}, u32[]{:S(2)}) async-start(bf16[32,2,2048]{2,1,0:T(2,128)(2,1)} %reshape.459), calls=%async_computation.3 | async-start | bytes 524288 | tf_op jit(solution)/shard_map/all_to_all | solution.py:421
  834.8 51.9 %all-to-all-start.4 = ((bf16[8,64,2048]{2,1,0:T(8,128)(2,1)}), bf16[8,64,2048]{2,1,0:T(8,128)(2,1)S(1)}, u32[]{:S(2)}, u32[]{:S(2)}) async-start(bf16[8,64,2048]{2,1,0:T(8,128)(2,1)} %get-tuple-element.111), calls=%async_computation.5 | async-start | bytes 4194304 | tf_op jit(solution)/shard_map/all_to_all | solution.py:550
  838.5 25.3 %reduce-scatter.2.cloned.1.call-start = ((), (), s32[]{:S(2)}) async-start(), calls=%async_computation.16 | async-start | bytes 327680 | tf_op jit(solution)/shard_map/reduce_scatter | solution.py:561
  840.1 23.7 %copy-start.17 = (f32[64,2048]{1,0:T(8,128)S(1)}, f32[64,2048]{1,0:T(8,128)}, u32[]{:S(2)}) copy-start(f32[64,2048]{1,0:T(8,128)} %copy-done.16) | copy-start | bytes 1572868
  843.9 203.1 %all-gather.14.cloned.1.call-start = ((), (), s32[]{:S(2)}) async-start(), calls=%async_computation.17 | async-start | bytes 2162688 | tf_op jit(solution)/shard_map/all_gather | solution.py:564
  890.6 21.4 %all-to-all-start.5 = ((bf16[32,64,128]{2,1,0:T(8,128)(2,1)}), bf16[32,64,128]{2,1,0:T(8,128)(2,1)}, u32[]{:S(2)}, u32[]{:S(2)}) async-start(bf16[32,64,128]{2,1,0:T(8,128)(2,1)} %maximum_bitcast_fusion), calls=%async_computation.6 | async-start | bytes 1048576 | tf_op jit(solution)/shard_map/all_to_all | solution.py:421
  912.0 60.4 %all-to-all-start.6 = ((bf16[8,64,2048]{2,1,0:T(8,128)(2,1)}), bf16[8,64,2048]{2,1,0:T(8,128)(2,1)}, u32[]{:S(2)}, u32[]{:S(2)}) async-start(bf16[8,64,2048]{2,1,0:T(8,128)(2,1)} %get-tuple-element.110), calls=%async_computation.7 | async-start | bytes 4194304 | tf_op jit(solution)/shard_map/all_to_all | solution.py:550
  972.5 20.0 %all-to-all-start.7 = ((bf16[32,64,128]{2,1,0:T(8,128)(2,1)}), bf16[32,64,128]{2,1,0:T(8,128)(2,1)}, u32[]{:S(2)}, u32[]{:S(2)}) async-start(bf16[32,64,128]{2,1,0:T(8,128)(2,1)} %maximum_bitcast_fusion.1), calls=%async_computation.8 | async-start | bytes 1048576 | tf_op jit(solution)/shard_map/all_to_all | solution.py:421
  1002.7 21.9 %all-to-all-start.8 = ((bf16[32,2,3840]{2,1,0:T(2,128)(2,1)}), bf16[32,2,3840]{2,1,0:T(2,128)(2,1)}, u32[]{:S(2)}, u32[]{:S(2)}) async-start(bf16[32,2,3840]{2,1,0:T(2,128)(2,1)} %reshape.461), calls=%async_computation.9 | async-start | bytes 983040 | tf_op jit(solution)/shard_map/all_to_all | solution.py:621
  1028.5 15.4 %all-to-all-start.9 = ((f32[32,1,512]{2,1,0:T(1,128)}), f32[32,1,512]{2,1,0:T(1,128)S(1)}, u32[]{:S(2)}, u32[]{:S(2)}) async-start(f32[32,1,512]{2,1,0:T(1,128)} %broadcast_in_dim.103), calls=%async_computation.10 | async-start | bytes 131072 | tf_op jit(solution)/shard_map/all_to_all | solution.py:623
  (40 other events, 283.7 us)
Sparse Core Ops, SparseCore 0:
  12.3 197.0 all-gather.5
  238.6 98.5 all-gather.7
  340.3 89.6 all-gather.9
  432.7 98.5 all-gather.11
  844.0 19.7 reduce-scatter.1
  888.9 78.6 all-gather.13

commit v4 on v3

--- a/solution.py
+++ b/solution.py
@@ -60,7 +60,7 @@
 
 def over(count, step):
     if count <= 9:
-        for off in range(1, count):
+        for off in range(count - 1, 0, -1):
             step(off)
     else:
         lax.fori_loop(1, count, lambda off, _: (step(off), 0)[1], 0)
@@ -68,11 +68,11 @@
 
 def lstm_kernel(
     n, chunk,
-    x_hbm, wx, wh, bias, p, wxt, wht, pt, cot,
+    x_own, wx, wh, bias, p, wxt, wht, pt, cot,
     out_ref, dx_ref, dw_hbm, db_ref, dp_ref,
     xbuf, hbuf, dqbuf, gates, cells, ebuf, hown, gscr, escr, dabuf, ucell, dwacc,
     stage, inbox, stage2, inbox2, relay, gbuf, rown,
-    load_sem, ag_send, ag_recv, dq_send, dq_recv, rs_send, rs_recv, dx_send, dx_recv,
+    in_send, in_recv, ag_send, ag_recv, dq_send, dq_recv, rs_send, rs_recv, dx_send, dx_recv,
     x_send, x_recv, g_send, g_recv, st_sem,
 ):
     steps, _, rows, width = xbuf.shape
@@ -86,7 +86,9 @@
     partner = (1 - pipe, direction, me)
 
     def peer(off):
-        return lax.rem(me + off, n)
+        if n & (n - 1):
+            return lax.rem(me + off, n)
+        return me ^ off
 
     barrier = pltpu.get_barrier_semaphore()
     over(n, lambda off: pl.semaphore_signal(
@@ -95,9 +97,8 @@
 
     @pl.when(first)
     def _():
-        load = pltpu.make_async_copy(x_hbm, xbuf, load_sem)
-        load.start()
-        load.wait()
+        for t in range(steps):
+            xbuf[t, me] = x_own[t]
 
     hbuf[0] = jnp.zeros((n, rows, width), BF)
     cells[0] = jnp.zeros((total, cell), F32)
@@ -134,6 +135,21 @@
             send_sem=g_send.at[t], recv_sem=g_recv.at[t],
             device_id=partner, device_id_type=MESH)
 
+    def in_start(t):
+        over(n, lambda off: pltpu.make_async_remote_copy(
+            src_ref=xbuf.at[t, me], dst_ref=xbuf.at[t, me],
+            send_sem=in_send.at[t], recv_sem=in_recv.at[t],
+            device_id=(pipe, direction, peer(off)), device_id_type=MESH).start())
+
+    def in_wait(sem, t):
+        blocks = xbuf.at[t, pl.ds(0, n - 1)]
+        pltpu.make_async_copy(blocks, blocks, sem.at[t]).wait()
+
+    @pl.when(first)
+    def _():
+        in_start(0)
+        in_start(1)
+
     def ag_wait(buf, slot):
         def both(off):
             ag_copy(buf, slot, off).wait_send()
@@ -150,6 +166,10 @@
         @pl.when(second)
         def _():
             x_copy(t).wait_recv()
+
+        @pl.when(first)
+        def _():
+            in_wait(in_recv, t)
 
         gscr[...] = jnp.dot(
             xbuf[t].reshape(total, width), wx[...], preferred_element_type=F32) + bias[...]
@@ -187,6 +207,11 @@
         stage[...] = q.astype(BF).reshape(n, rows, width)
         over(n, lambda off: rs_copy(off).start())
         inbox[me] = stage[me]
+
+        @pl.when(first & (t + 2 < steps))
+        def _():
+            in_start(t + 2)
+
         rs_wait()
         h = 3.0 * jnp.tanh(jnp.sum(inbox[...].astype(F32), axis=0) * (1.0 / 3.0))
         hown[t] = h
@@ -203,6 +228,7 @@
     def _():
         x_copy(steps - 1).start()
         lax.fori_loop(0, steps, lambda t, _: (x_copy(t).wait_send(), 0)[1], 0)
+        lax.fori_loop(0, steps, lambda t, _: (in_wait(in_send, t), 0)[1], 0)
 
     rown[...] = jnp.zeros((rows, width), F32)
     ucell[...] = jnp.zeros((total, cell), F32)
@@ -315,7 +341,7 @@
 
 
 def lstm_call(n, x, wx, wh, bias, p, wxt, wht, pt, cot, chunk=16):
-    steps, _, rows, width = x.shape
+    steps, rows, width = x.shape
     cell = p.shape[0]
     total = n * rows
     sds = jax.ShapeDtypeStruct
@@ -329,7 +355,7 @@
         out_shape=(
             sds((steps, rows, width), BF), sds((steps, rows, width), F32),
             sds((2 * width, 4 * cell), BF), sds((1, 4 * cell), F32), sds((cell, width), F32)),
-        in_specs=[hb] + [vm] * 8,
+        in_specs=[vm] * 9,
         out_specs=(vm, vm, hb, vm, vm),
         scratch_shapes=[
             V((steps, n, rows, width), BF), V((steps + 1, n, rows, width), BF),
@@ -341,7 +367,7 @@
             V((n, rows, width), BF), V((n, rows, width), BF),
             V((2, n, rows, width), BF), V((2, n, rows, width), BF),
             V((steps, rows, width), BF), V((steps, rows, width), BF), V((rows, width), F32),
-            dma, dma((n,)), dma((n,)), dma((n,)), dma((n,)), dma((n,)), dma((n,)), dma((2, n)), dma((2, n)),
+            dma((steps,)), dma((steps,)), dma((n,)), dma((n,)), dma((n,)), dma((n,)), dma((n,)), dma((n,)), dma((2, n)), dma((2, n)),
             dma((steps,)), dma((steps,)), dma((steps,)), dma((steps,)), dma((2,)),
         ],
         compiler_params=pltpu.CompilerParams(
@@ -394,11 +420,13 @@
     )(blocks)
 
 
-def encode_forward(ids, weights):
-    table_low, conv_low, conv_bias, highway_low, highway_bias, proj_low, proj_bias = weights
+def conv_forward(ids, table_low, conv_low):
     valid_place = conv_masks(FILTERS)[1]
-    pooled = jax.nn.logsumexp(conv_response(ids, table_low, conv_low, valid_place)[1], axis=1)
-    features = jax.nn.silu(pooled + conv_bias)
+    return jax.nn.logsumexp(conv_response(ids, table_low, conv_low, valid_place)[1], axis=1)
+
+
+def encode_forward(features, weights):
+    highway_low, highway_bias, proj_low, proj_bias = weights
     kept = [features]
     mixed = []
     for layer in range(2):
@@ -411,7 +439,7 @@
         features = gate * features + (1.0 - gate) * jax.nn.silu(pre[:, :FILTERS])
         kept.append(features)
     encoded = jnp.dot(features.astype(BF), proj_low, preferred_element_type=F32) + proj_bias
-    return encoded, pooled, kept, mixed
+    return encoded, kept, mixed
 
 
 def to_columns(value):
@@ -484,13 +512,17 @@
         axis=2,
         tiled=True,
     )
-    all_lengths = lax.all_to_all(
-        jnp.broadcast_to(lengths, (n, seqs)), "dp", 0, 0
-    ).reshape(n * seqs)
-
     in_rows = gate_weight.shape[2]
-    gate_low, gathered = lax.optimization_barrier(
-        (split_cells(gate_weight[0, 0], n), gathered)
+    ids = lax.dynamic_slice_in_dim(
+        chars, (pipe * lax.axis_size("dir") + direction) * quarter, quarter, 0
+    ).reshape(tokens, char_count)
+    weight_mask = conv_masks(FILTERS)[0]
+    table_low = char_emb.astype(BF)
+    conv_low = conv_full * weight_mask.astype(BF)
+    pooled = conv_forward(ids, table_low, conv_low)
+    features = jax.nn.silu(pooled + conv_bias)
+    gate_low, gathered, features = lax.optimization_barrier(
+        (split_cells(gate_weight[0, 0], n), gathered, features)
     )
     gate_own = lax.all_to_all(gate_low, "dp", 0, 0).reshape(n * in_rows, 4 * cell)
     highway_full = gathered[:, :FILTERS]
@@ -510,26 +542,16 @@
     own_order = order_matrix(lengths)
     cot = jnp.einsum("rts,rsd->trd", own_order, cotangent[0, 0], preferred_element_type=BF)
 
-    ids = lax.dynamic_slice_in_dim(
-        chars, (pipe * lax.axis_size("dir") + direction) * quarter, quarter, 0
-    ).reshape(tokens, char_count)
-    weight_mask = conv_masks(FILTERS)[0]
-    table_low = char_emb.astype(BF)
-    conv_low = conv_full * weight_mask.astype(BF)
-    encoded, pooled, kept, mixed = encode_forward(
-        ids,
-        (table_low, conv_low, conv_bias, highway_full, highway_bias, proj_full, proj_bias),
-    )
-    encoded_all = lax.all_gather(
-        encoded.astype(BF).reshape(quarter, steps, width), ("dp", "pipe", "dir"), axis=0, tiled=True
+    encoded, kept, mixed = encode_forward(
+        features, (highway_full, highway_bias, proj_full, proj_bias)
+    )
+    encoded_own = lax.all_gather(
+        encoded.astype(BF).reshape(quarter, steps, width), ("pipe", "dir"), axis=0, tiled=True
     )
     kept_low = [value.astype(BF) for value in kept]
-    kept_low, encoded_all, gate_own = lax.optimization_barrier((kept_low, encoded_all, gate_own))
+    kept_low, encoded_own, gate_own = lax.optimization_barrier((kept_low, encoded_own, gate_own))
     kept_all = [lax.all_gather(value, ALL, axis=0, tiled=True) for value in kept_low[:2]]
-    last_columns = to_columns(kept_low[2])
-    inputs = jnp.einsum(
-        "rts,rsd->trd", order_matrix(all_lengths), encoded_all, preferred_element_type=BF
-    ).reshape(steps, n, seqs, width)
+    inputs = jnp.einsum("rts,rsd->trd", own_order, encoded_own, preferred_element_type=BF)
 
     out_own, dx_own, grad_gate, grad_bias, grad_cell = lstm_call(
         n,
@@ -543,24 +565,19 @@
         cell_low.T,
         cot,
     )
-    dx_own, kept_all, last_columns = lax.optimization_barrier((dx_own, kept_all, last_columns))
+    dx_own, kept_all = lax.optimization_barrier((dx_own, kept_all))
     activations = jnp.einsum("rts,srd->rtd", own_order, out_own, preferred_element_type=BF)
 
     grad_gate = grad_gate.reshape(n, 2, in_rows // 2, 4 * cell)
     gate_halves = [lax.all_to_all(grad_gate[:, half], "dp", 0, 0) for half in range(2)]
-    grad_bias = lax.all_to_all(
-        jnp.broadcast_to(grad_bias, (n, 4 * cell)), "dp", 0, 0
-    ).reshape(n, 4, cell)
-    grad_bias = jnp.transpose(grad_bias, (1, 0, 2)).reshape(n, 4 * cell)
-    grad_bias = lax.dynamic_index_in_dim(grad_bias, me, 0, keepdims=False)
-
     grad_stored = jnp.einsum(
         "rts,srd->rtd", own_order, dx_own.astype(BF), preferred_element_type=F32
     )
     grad_stored = jnp.where(pipe == 1, grad_stored, 0.0).astype(BF)
-    grad_encoded = lax.psum_scatter(
-        grad_stored, ("pipe", "dir"), scatter_dimension=0, tiled=True
-    ).reshape(tokens, width)
+    grad_encoded = lax.all_to_all(
+        grad_stored.reshape(parts, tokens, width), ("pipe", "dir"), 0, 0
+    )
+    grad_encoded = jnp.sum(grad_encoded.astype(F32), axis=0).astype(BF)
     encoded_grads = lax.all_gather(grad_encoded, ALL, axis=0, tiled=True)
 
     grad_proj_bias = jnp.sum(grad_encoded.astype(F32), axis=0)
@@ -586,7 +603,16 @@
             grad_features, gate_halves[0] = lax.optimization_barrier(
                 (grad_features, gate_halves[0])
             )
-    grad_features, columns[1] = lax.optimization_barrier((grad_features, columns[1]))
+    grad_features, columns[1], grad_bias = lax.optimization_barrier(
+        (grad_features, columns[1], grad_bias)
+    )
+    grad_bias = lax.all_to_all(
+        jnp.broadcast_to(grad_bias, (n, 4 * cell)), "dp", 0, 0
+    ).reshape(n, 4, cell)
+    grad_bias = jnp.transpose(grad_bias, (1, 0, 2)).reshape(n, 4 * cell)
+    grad_bias = lax.dynamic_index_in_dim(grad_bias, me, 0, keepdims=False)
+
+    last_columns = to_columns(kept_low[2])
     grad_proj = jnp.einsum("tf,td->fd", last_columns, encoded_grads, preferred_element_type=F32)
     grad_before = grad_features * silu_slope(pooled + conv_bias)
     grad_conv, grad_table = conv_backward(ids, table_low, conv_low, grad_before)

time: 1070 us -> 1060 us (level)
  Pallas kernels: 408 us -> 435 us
  waiting for transfers between devices: 295 us -> 276 us
    all_to_all x3, starting transfers between devices: 63.4 us -> 15.1 us  [to_columns(): lax.all_to_all(split, ALL, 0, 0).reshape(count * tokens, columns // count)]
    all_to_all x1, starting transfers between devices: 3.44 us -> 48.8 us  [local(): lax.all_to_all(grad_stored.reshape(parts, tokens, width), ('pipe', 'dir')...]
    pallas_call x1, Pallas kernels: 396 us -> 423 us  [lstm_call(): pl.pallas_call(functools.partial(lstm_kernel, n, chunk), out_shape=(sds((...]
    all_to_all x2, waiting for transfers between devices: 34.6 us -> 58.7 us  [local(): lax.all_to_all(grad_gate[:, half], 'dp', 0, 0)]
    reduce_scatter x1 -> x0, waiting for transfers between devices: 17.8 us -> none  [local(): lax.psum_scatter(grad_stored, ('pipe', 'dir'), scatter_dimension=0, tiled...]
    all_to_all x1, waiting for transfers between devices: 78.8 us -> 63.1 us  [local(): lax.all_to_all(gate_low, 'dp', 0, 0).reshape(n * in_rows, 4 * cell)]
    all_gather x1 -> x0, waiting for transfers between devices: 13.5 us -> none  [local(): lax.all_gather(encoded.astype(BF).reshape(quarter, steps, width), ('dp',...]
  transfers between devices with their start and end apart: 17 -> 15, of which waited for: 10 -> 7; matrix products, arithmetic and copies ran while one was open for 20% -> 19% of each run, Pallas kernels for 39% -> 41%
where the time goes in v4:
time: 1060 us; the launch traced here: 1050 us
  Pallas kernels  435 us (41%)
  waiting for transfers between devices  276 us (26%)
  starting transfers between devices  98.5 us (9%)
  matrix products  83.6 us (8%)
  local copies, waits for them, and re-layouts  83.5 us (8%)
  other arithmetic  52.9 us (5%)
  between operations  15.3 us (1%)
    pallas_call x1, Pallas kernels, lstm_call(): pl.pallas_call(functools.partial(lstm_kernel, n, chunk), out_shape=(sds((...  423 us
    all_gather x1, waiting for transfers between devices, local(): lax.all_gather(jnp.concatenate([highway_weight, proj_blocks], axis=1).ast...  134 us
    all_to_all x1, waiting for transfers between devices, local(): lax.all_to_all(gate_low, 'dp', 0, 0).reshape(n * in_rows, 4 * cell)  63.1 us
    all_to_all x2, waiting for transfers between devices, local(): lax.all_to_all(grad_gate[:, half], 'dp', 0, 0)  58.7 us
    all_to_all x1, starting transfers between devices, local(): lax.all_to_all(grad_stored.reshape(parts, tokens, width), ('pipe', 'dir')...  48.8 us
  transfers between devices with their start and end apart: 15, of which 7 were waited for; matrix products, arithmetic and copies ran while one was open for 19% of the time, Pallas kernels for 41%

profile of v4, /device:TPU:3, one launch (start us, length us, event | category | flops | bytes accessed | tf_op | source)
XLA Modules:
  0.0 1050.6 jit_solution(9024165558877428060)
XLA Ops:
  13.0 6.5 all-to-all-start
  20.6 6.7 gather_fusion
  39.0 6.6 concatenate.55
  45.7 12.6 %select_reduce_fusion = (f32[64,2048]{1,0:T(8,128)S(1)}, f32[64,50,2048]{2,0,1:T(8,128)}) fusion(pred[50,2048]{1,0:T(8,128)(4,1)S(1)} %iota_compare_fusion.6, bf16[64,50,112]{2,0,1:T(8,128)(2,1)S(1)} %concatenate.55, s32[2048]{0:T(1024)S(1)} %convert_add_fusion, s32[112]{0:T(128)S(1)} %and_select_fusion, bf16[16,112,128]{2,1,0:T(8,128)(2,1)} %all-to-all-done), kind=kOutput, calls=%fused_computation.5 | convolution fusion | flops 1482588160 | bytes 28025280 | tf_op jit(solution)/shard_map/bpk,kf->bpf/dot_general | solution.py:57
  58.4 14.8 %fusion = (f32[64,2048]{1,0:T(8,128)}, f32[64,2048]{1,0:T(8,128)S(1)}) fusion(f32[64,50,2048]{2,0,1:T(8,128)} %get-tuple-element.138, f32[64,2048]{1,0:T(8,128)S(1)} %get-tuple-element.137, pred[50,2048]{1,0:T(8,128)(4,1)S(1)} %iota_compare_fusion.6, f32[64,2048]{1,0:T(8,128)S(1)} %is-finite_select_fusion), kind=kLoop, calls=%fused_computation.4 | loop fusion | flops 32505856 | bytes 28413952 | tf_op jit(solution)/shard_map/reduce_sum | solution.py:455
  74.3 134.2 %all-gather.5.cloned.1.call-done = bf16[2,2176,4096]{2,1,0:T(8,128)(2,1)} async-done(((bf16[2,2176,256]{2,1,0:T(8,128)(2,1)}), bf16[2,2176,4096]{2,1,0:T(8,128)(2,1)}) %all-gather.5.cloned.1.call-update) | async-done | bytes 35651600 | tf_op jit(solution)/shard_map/all_gather | solution.py:509
  219.8 7.5 fusion.14
  228.4 7.7 fusion.17
  243.1 63.1 %all-to-all-done.1 = bf16[8,128,2048]{2,1,0:T(8,128)(2,1)} async-done(((bf16[8,128,2048]{2,1,0:T(8,128)(2,1)}), bf16[8,128,2048]{2,1,0:T(8,128)(2,1)}, u32[]{:S(2)}, u32[]{:S(2)}) %all-to-all-start.1) | async-done | bytes 4194336 | tf_op jit(solution)/shard_map/all_to_all | solution.py:527
  306.2 6.4 copy.167
  336.8 423.4 %relay_lstm.1 = (bf16[16,16,512]{2,1,0:T(8,128)(2,1)}, f32[16,16,512]{2,1,0:T(8,128)}, bf16[1024,2048]{1,0:T(8,128)(2,1)}, f32[1,2048]{1,0:T(1,128)}, f32[512,512]{1,0:T(8,128)}) custom-call(bf16[16,16,512]{2,1,0:T(8,128)(2,1)} %bitcast.204, bf16[512,2048]{1,0:T(8,128)(2,1)} %copy.144.wx, bf16[512,2048]{1,0:T(8,128)(2,1)} %copy.145.wh, f32[1,2048]{1,0:T(1,128)} %bitcast.211, ...), custom_call_target="tpu_custom_call" | custom-call | flops 299999985664 | bytes 67108864 | tf_op jit(solution)/shard_map/relay_lstm/pallas_call | solution.py:353
  762.4 48.8 %all-to-all-start.2 = ((bf16[4,64,512]{2,1,0:T(8,128)(2,1)}), bf16[4,64,512]{2,1,0:T(8,128)(2,1)S(1)}, u32[]{:S(2)}, u32[]{:S(2)}) async-start(bf16[4,64,512]{2,1,0:T(8,128)(2,1)} %bitcast.20), calls=%async_computation.2 | async-start | bytes 524288 | tf_op jit(solution)/shard_map/all_to_all | solution.py:577
  831.3 9.9 fusion.25
  841.2 27.7 %all-to-all-done.3 = bf16[8,64,2048]{2,1,0:T(8,128)(2,1)S(1)} async-done(((bf16[8,64,2048]{2,1,0:T(8,128)(2,1)}), bf16[8,64,2048]{2,1,0:T(8,128)(2,1)S(1)}, u32[]{:S(2)}, u32[]{:S(2)}) %all-to-all-start.3) | async-done | bytes 2097184 | tf_op jit(solution)/shard_map/all_to_all | solution.py:572
  872.7 6.1 all-to-all-start.4
  879.8 9.9 fusion.22
  889.7 10.1 all-to-all-done.4
  905.7 15.8 %multiply_convert_fusion = bf16[64,50,2048]{2,0,1:T(8,128)(2,1)} fusion(f32[64,50,2048]{2,0,1:T(8,128)} %get-tuple-element.138, f32[64,2048]{1,0:T(8,128)S(1)} %copy-done.15, f32[64,2048]{1,0:T(8,128)S(1)} %copy-done.4, f32[64,2048]{1,0:T(8,128)S(1)} %get-tuple-element.109, pred[50,2048]{1,0:T(8,128)(4,1)S(1)} %copy-done.22), kind=kLoop, calls=%fused_computation.1 | loop fusion | flops 32768000 | bytes 40996864 | tf_op jit(solution)/shard_map/convert_element_type | solution.py:456
  921.4 31.0 %all-to-all-done.5 = bf16[8,64,2048]{2,1,0:T(8,128)(2,1)S(1)} async-done(((bf16[8,64,2048]{2,1,0:T(8,128)(2,1)}), bf16[8,64,2048]{2,1,0:T(8,128)(2,1)S(1)}, u32[]{:S(2)}, u32[]{:S(2)}) %all-to-all-start.5) | async-done | bytes 2097184 | tf_op jit(solution)/shard_map/all_to_all | solution.py:572
  958.2 7.6 fusion.86
  989.7 6.7 convolution_bitcast_fusion.1
  999.0 6.1 all-to-all-start.7
  1009.2 6.0 join_cells.1
  1015.2 5.9 convolution_bitcast_fusion
  (263 shorter events, 154.2 us)
Async XLA Ops:
  7.2 307.0 %copy-start = (bf16[1,1,16,16,512]{4,3,2,1,0:T(8,128)(2,1)S(1)}, bf16[1,1,16,16,512]{4,3,2,1,0:T(8,128)(2,1)}, u32[]{:S(2)}) copy-start(bf16[1,1,16,16,512]{4,3,2,1,0:T(8,128)(2,1)} %param.27) | copy-start | bytes 786436
  7.2 201.3 %all-gather.5.cloned.1.call-start = ((), (), s32[]{:S(2)}) async-start(), calls=%async_computation.11 | async-start | bytes 37879808 | tf_op jit(solution)/shard_map/all_gather | solution.py:509
  13.0 32.8 %all-to-all-start = ((bf16[16,112,128]{2,1,0:T(8,128)(2,1)}), bf16[16,112,128]{2,1,0:T(8,128)(2,1)}, u32[]{:S(2)}, u32[]{:S(2)}) async-start(bf16[16,112,128]{2,1,0:T(8,128)(2,1)} %broadcast_in_dim.52), calls=%async_computation | async-start | bytes 917504 | tf_op jit(solution)/shard_map/all_to_all | solution.py:500
  74.3 153.0 %copy-start.7 = (f32[64,2048]{1,0:T(8,128)}, f32[64,2048]{1,0:T(8,128)S(1)}, u32[]{:S(2)}) copy-start(f32[64,2048]{1,0:T(8,128)S(1)} %fusion.60) | copy-start | bytes 1572868
  74.3 139.3 %copy-start.53 = (f32[2,4096]{1,0:T(2,128)S(1)}, f32[2,4096]{1,0:T(2,128)}, u32[]{:S(2)}) copy-start(f32[2,4096]{1,0:T(2,128)} %param.21) | copy-start | bytes 98308
  208.5 97.6 %all-to-all-start.1 = ((bf16[8,128,2048]{2,1,0:T(8,128)(2,1)}), bf16[8,128,2048]{2,1,0:T(8,128)(2,1)}, u32[]{:S(2)}, u32[]{:S(2)}) async-start(bf16[8,128,2048]{2,1,0:T(8,128)(2,1)} %split_cells.1), calls=%async_computation.1 | async-start | bytes 8388608 | tf_op jit(solution)/shard_map/all_to_all | solution.py:527
  213.1 547.1 %all-gather.7.cloned.1.call-start = ((), (), s32[]{:S(2)}) async-start(), calls=%async_computation.12 | async-start | bytes 8650752 | tf_op jit(solution)/shard_map/all_gather | solution.py:553
  331.3 431.0 %all-to-all-start.9 = ((bf16[32,2,2048]{2,1,0:T(2,128)(2,1)}), bf16[32,2,2048]{2,1,0:T(2,128)(2,1)}, u32[]{:S(2)}, u32[]{:S(2)}) async-start(bf16[32,2,2048]{2,1,0:T(2,128)(2,1)} %reshape.363), calls=%async_computation.9 | async-start | bytes 524288 | tf_op jit(solution)/shard_map/all_to_all | solution.py:449
  336.0 424.2 %all-gather.9.cloned.1.call-start = ((), (), s32[]{:S(2)}) async-start(), calls=%async_computation.13 | async-start | bytes 8650752 | tf_op jit(solution)/shard_map/all_gather | solution.py:553
  336.7 424.6 %copy-start.44 = (s32[16,16]{1,0:T(8,128)S(1)}, s32[16,16]{1,0:T(8,128)}, u32[]{:S(2)}) copy-start(s32[16,16]{1,0:T(8,128)} %copy-done.43) | copy-start | bytes 3076
  336.8 424.6 %copy-start.52 = (pred[16,16]{1,0:T(8,128)(4,1)S(1)}, pred[16,16]{1,0:T(8,128)(4,1)}, u32[]{:S(2)}) copy-start(pred[16,16]{1,0:T(8,128)(4,1)} %copy-done.51) | copy-start | bytes 772
  762.4 53.6 %all-to-all-start.2 = ((bf16[4,64,512]{2,1,0:T(8,128)(2,1)}), bf16[4,64,512]{2,1,0:T(8,128)(2,1)S(1)}, u32[]{:S(2)}, u32[]{:S(2)}) async-start(bf16[4,64,512]{2,1,0:T(8,128)(2,1)} %bitcast.20), calls=%async_computation.2 | async-start | bytes 524288 | tf_op jit(solution)/shard_map/all_to_all | solution.py:577
  816.0 52.9 %all-to-all-start.3 = ((bf16[8,64,2048]{2,1,0:T(8,128)(2,1)}), bf16[8,64,2048]{2,1,0:T(8,128)(2,1)S(1)}, u32[]{:S(2)}, u32[]{:S(2)}) async-start(bf16[8,64,2048]{2,1,0:T(8,128)(2,1)} %get-tuple-element.113), calls=%async_computation.3 | async-start | bytes 4194304 | tf_op jit(solution)/shard_map/all_to_all | solution.py:572
  819.7 220.2 %all-gather.11.cloned.1.call-start = ((), (), s32[]{:S(2)}) async-start(), calls=%async_computation.14 | async-start | bytes 2162688 | tf_op jit(solution)/shard_map/all_gather | solution.py:581
  831.3 37.6 %copy-start.8 = (f32[64,2048]{1,0:T(8,128)S(1)}, f32[64,2048]{1,0:T(8,128)}, u32[]{:S(2)}) copy-start(f32[64,2048]{1,0:T(8,128)} %copy-done.7) | copy-start | bytes 1572868
  872.7 27.1 %all-to-all-start.4 = ((bf16[32,64,128]{2,1,0:T(8,128)(2,1)}), bf16[32,64,128]{2,1,0:T(8,128)(2,1)S(1)}, u32[]{:S(2)}, u32[]{:S(2)}) async-start(bf16[32,64,128]{2,1,0:T(8,128)(2,1)} %maximum_bitcast_fusion), calls=%async_computation.4 | async-start | bytes 1048576 | tf_op jit(solution)/shard_map/all_to_all | solution.py:449
  900.5 51.9 %all-to-all-start.5 = ((bf16[8,64,2048]{2,1,0:T(8,128)(2,1)}), bf16[8,64,2048]{2,1,0:T(8,128)(2,1)S(1)}, u32[]{:S(2)}, u32[]{:S(2)}) async-start(bf16[8,64,2048]{2,1,0:T(8,128)(2,1)} %get-tuple-element.112), calls=%async_computation.5 | async-start | bytes 4194304 | tf_op jit(solution)/shard_map/all_to_all | solution.py:572
  905.6 52.5 %copy-start.46 = (s32[2048]{0:T(1024)S(1)}, s32[2048]{0:T(1024)}, u32[]{:S(2)}) copy-start(s32[2048]{0:T(1024)} %copy-done.45) | copy-start | bytes 24580
  905.7 52.5 %copy-start.59 = (s32[112]{0:T(128)S(1)}, s32[112]{0:T(128)}, u32[]{:S(2)}) copy-start(s32[112]{0:T(128)} %copy-done.58) | copy-start | bytes 1348
  953.8 19.6 %all-to-all-start.6 = ((bf16[32,64,128]{2,1,0:T(8,128)(2,1)}), bf16[32,64,128]{2,1,0:T(8,128)(2,1)S(1)}, u32[]{:S(2)}, u32[]{:S(2)}) async-start(bf16[32,64,128]{2,1,0:T(8,128)(2,1)} %maximum_bitcast_fusion.1), calls=%async_computation.6 | async-start | bytes 1048576 | tf_op jit(solution)/shard_map/all_to_all | solution.py:449
  986.1 12.9 %all-to-all-start.10 = ((f32[8,1,2048]{2,1,0:T(1,128)}), f32[8,1,2048]{2,1,0:T(1,128)S(1)}, u32[]{:S(2)}, u32[]{:S(2)}) async-start(f32[8,1,2048]{2,1,0:T(1,128)} %broadcast_in_dim.92), calls=%async_computation.10 | async-start | bytes 131072 | tf_op jit(solution)/shard_map/all_to_all | solution.py:609
  999.0 23.9 %all-to-all-start.7 = ((bf16[32,2,3840]{2,1,0:T(2,128)(2,1)}), bf16[32,2,3840]{2,1,0:T(2,128)(2,1)S(1)}, u32[]{:S(2)}, u32[]{:S(2)}) async-start(bf16[32,2,3840]{2,1,0:T(2,128)(2,1)} %reshape.361), calls=%async_computation.7 | async-start | bytes 983040 | tf_op jit(solution)/shard_map/all_to_all | solution.py:647
  1025.0 17.7 %copy-start.28 = (f32[512,512]{1,0:T(8,128)S(1)}, f32[512,512]{1,0:T(8,128)}, u32[]{:S(2)}) copy-start(f32[512,512]{1,0:T(8,128)} %get-tuple-element.59) | copy-start | bytes 3145732
  1025.0 11.9 %all-to-all-start.8 = ((f32[32,1,512]{2,1,0:T(1,128)}), f32[32,1,512]{2,1,0:T(1,128)S(1)}, u32[]{:S(2)}, u32[]{:S(2)}) async-start(f32[32,1,512]{2,1,0:T(1,128)} %broadcast_in_dim.90), calls=%async_computation.8 | async-start | bytes 131072 | tf_op jit(solution)/shard_map/all_to_all | solution.py:649
  (53 other events, 348.5 us)
Sparse Core Ops, SparseCore 0:
  11.5 197.0 all-gather.4
  312.8 104.9 all-gather.6
  420.8 109.5 all-gather.8
  827.1 73.5 all-gather.10

commit v5 on v4

--- a/solution.py
+++ b/solution.py
@@ -26,18 +26,12 @@
     return sig * (1.0 + value * (1.0 - sig))
 
 
-def filter_widths(filter_count):
-    filter_index = jnp.arange(filter_count, dtype=jnp.int32)
-    filter_width = jnp.ones((filter_count,), jnp.int32)
+def conv_masks(filter_index):
+    filter_width = jnp.ones(filter_index.shape, jnp.int32)
     for doubling in range(6):
-        filter_width = filter_width + (filter_index >= filter_count // 64 * (1 << doubling)).astype(
+        filter_width = filter_width + (filter_index >= FILTERS // 64 * (1 << doubling)).astype(
             jnp.int32
         )
-    return filter_width
-
-
-def conv_masks(filter_count):
-    filter_width = filter_widths(filter_count)
     offset_rows = jnp.arange(KMAX * CDIM, dtype=jnp.int32) // CDIM
     weight_mask = (offset_rows[:, None] < filter_width[None, :]).astype(jnp.float32)
     valid_place = jnp.arange(CHARS, dtype=jnp.int32)[:, None] <= CHARS - filter_width[None, :]
@@ -420,26 +414,21 @@
     )(blocks)
 
 
-def conv_forward(ids, table_low, conv_low):
-    valid_place = conv_masks(FILTERS)[1]
+def conv_forward(ids, table_low, conv_low, valid_place):
     return jax.nn.logsumexp(conv_response(ids, table_low, conv_low, valid_place)[1], axis=1)
 
 
-def encode_forward(features, weights):
-    highway_low, highway_bias, proj_low, proj_bias = weights
-    kept = [features]
-    mixed = []
-    for layer in range(2):
-        pre = (
-            jnp.dot(features.astype(BF), highway_low[layer], preferred_element_type=F32)
-            + highway_bias[layer]
-        )
-        mixed.append(pre)
-        gate = jax.nn.sigmoid(pre[:, FILTERS:])
-        features = gate * features + (1.0 - gate) * jax.nn.silu(pre[:, :FILTERS])
-        kept.append(features)
-    encoded = jnp.dot(features.astype(BF), proj_low, preferred_element_type=F32) + proj_bias
-    return encoded, kept, mixed
+def own_half(value, blocks):
+    sub = value.shape[-1] // (2 * blocks)
+    split = value.reshape(*value.shape[:-1], blocks, 2, sub)
+    mine = lax.dynamic_index_in_dim(split, lax.axis_index("pipe"), split.ndim - 2, keepdims=False)
+    return mine.reshape(*value.shape[:-1], blocks * sub)
+
+
+def both_halves(value, blocks):
+    tokens, half = value.shape
+    pair = lax.all_gather(value, "pipe").reshape(2, tokens, blocks, half // blocks)
+    return jnp.transpose(pair, (1, 2, 0, 3)).reshape(tokens, 2 * half)
 
 
 def to_columns(value):
@@ -449,8 +438,8 @@
     return lax.all_to_all(split, ALL, 0, 0).reshape(count * tokens, columns // count)
 
 
-def conv_backward(ids, table_low, conv_low, grad_before):
-    weight_mask, valid_place = conv_masks(FILTERS)
+def conv_backward(ids, table_low, conv_low, masks, grad_before):
+    weight_mask, valid_place = masks
     windows, response = conv_response(ids, table_low, conv_low, valid_place)
     share = jax.nn.softmax(response, axis=1)
     grad_response = (grad_before[:, None, :] * share).astype(BF)
@@ -488,50 +477,39 @@
     direction = lax.axis_index("dir")
     me = lax.axis_index("dp")
     everyone = lax.axis_size(ALL)
+    holders = lax.axis_size(("dir", "dp"))
     seqs, steps, char_count = chars.shape
-    parts = everyone // n
-    quarter = seqs // parts
+    group = seqs // lax.axis_size("dir")
+    quarter = group // 2
+    group_tokens = group * steps
     tokens = quarter * steps
     width = cell_proj.shape[3]
     cell = cell_proj.shape[2]
-
-    holders = lax.axis_size(("dir", "dp"))
-    mine = conv_weight.shape[1]
+    blocks = holders // 2
+    sub = FILTERS // holders
+    half = FILTERS // 2
+    filter_index = (
+        (2 * jnp.arange(blocks, dtype=jnp.int32) + pipe)[:, None] * sub
+        + jnp.arange(sub, dtype=jnp.int32)[None, :]
+    ).reshape(half)
+    masks = conv_masks(filter_index)
+
+    proj_rows = proj_weight.shape[0]
+    pieces = width // sub
+    proj_blocks = jnp.transpose(proj_weight.reshape(proj_rows, pieces, sub), (1, 0, 2))
+    proj_blocks = proj_blocks.reshape(2, pieces * proj_rows // 2, sub)
+    mine = lax.dynamic_slice_in_dim(highway_weight, pipe * sub, sub, 2)
+    gathered = lax.all_gather(
+        jnp.concatenate([mine, proj_blocks], axis=1).astype(BF), ("dir", "dp"), axis=2, tiled=True
+    )
     conv_full = lax.all_to_all(
-        jnp.broadcast_to(conv_weight.astype(BF), (holders, KMAX * CDIM, mine)), ("dir", "dp"), 0, 0
-    )
-    conv_full = jnp.transpose(conv_full, (1, 0, 2)).reshape(KMAX * CDIM, FILTERS)
-    proj_rows = proj_weight.shape[0]
-    block = highway_weight.shape[2]
-    pieces = width // block
-    proj_blocks = jnp.transpose(proj_weight.reshape(proj_rows, pieces, block), (1, 0, 2))
-    proj_blocks = proj_blocks.reshape(2, pieces * proj_rows // 2, block)
-    gathered = lax.all_gather(
-        jnp.concatenate([highway_weight, proj_blocks], axis=1).astype(BF),
-        ("dir", "dp"),
-        axis=2,
-        tiled=True,
-    )
-    in_rows = gate_weight.shape[2]
-    ids = lax.dynamic_slice_in_dim(
-        chars, (pipe * lax.axis_size("dir") + direction) * quarter, quarter, 0
-    ).reshape(tokens, char_count)
-    weight_mask = conv_masks(FILTERS)[0]
-    table_low = char_emb.astype(BF)
-    conv_low = conv_full * weight_mask.astype(BF)
-    pooled = conv_forward(ids, table_low, conv_low)
-    features = jax.nn.silu(pooled + conv_bias)
-    gate_low, gathered, features = lax.optimization_barrier(
-        (split_cells(gate_weight[0, 0], n), gathered, features)
-    )
-    gate_own = lax.all_to_all(gate_low, "dp", 0, 0).reshape(n * in_rows, 4 * cell)
-    highway_full = gathered[:, :FILTERS]
-    proj_full = gathered[:, FILTERS:].reshape(pieces, proj_rows, holders, block)
-    proj_full = jnp.transpose(proj_full, (2, 1, 0, 3)).reshape(FILTERS, width)
-    bias_own = lax.dynamic_index_in_dim(
-        gate_bias[0, 0].reshape(4, n, cell), me, 1, keepdims=False
-    ).reshape(1, 4 * cell)
-    cell_low = cell_proj[0, 0].astype(BF)
+        jnp.broadcast_to(conv_weight.astype(BF), (holders, KMAX * CDIM, sub)), ("dir", "dp"), 0, 0
+    ).reshape(blocks, 2, KMAX * CDIM, sub)
+    conv_low = lax.dynamic_index_in_dim(conv_full, pipe, 1, keepdims=False)
+    conv_low = jnp.transpose(conv_low, (1, 0, 2)).reshape(KMAX * CDIM, half)
+    conv_low = conv_low * masks[0].astype(BF)
+    conv_bias_own = own_half(conv_bias, blocks)
+    highway_bias_own = own_half(highway_bias.reshape(2, 2, FILTERS), blocks).reshape(2, FILTERS)
 
     def order_matrix(sizes):
         place = jnp.arange(steps, dtype=jnp.int32)[None, :]
@@ -542,15 +520,48 @@
     own_order = order_matrix(lengths)
     cot = jnp.einsum("rts,rsd->trd", own_order, cotangent[0, 0], preferred_element_type=BF)
 
-    encoded, kept, mixed = encode_forward(
-        features, (highway_full, highway_bias, proj_full, proj_bias)
-    )
+    ids = lax.dynamic_slice_in_dim(chars, direction * group, group, 0).reshape(
+        group_tokens, char_count
+    )
+    table_low = char_emb.astype(BF)
+    pooled = conv_forward(ids, table_low, conv_low, masks[1])
+    features = jax.nn.silu(pooled + conv_bias_own)
+    features_low = both_halves(features.astype(BF), blocks)
+    in_rows = gate_weight.shape[2]
+    gate_low, gathered, features_low = lax.optimization_barrier(
+        (split_cells(gate_weight[0, 0], n), gathered, features_low)
+    )
+    gate_own = lax.all_to_all(gate_low, "dp", 0, 0).reshape(n * in_rows, 4 * cell)
+    bias_own = lax.dynamic_index_in_dim(
+        gate_bias[0, 0].reshape(4, n, cell), me, 1, keepdims=False
+    ).reshape(1, 4 * cell)
+    cell_low = cell_proj[0, 0].astype(BF)
+    highway_half = gathered[:, :FILTERS]
+    proj_full = gathered[:, FILTERS:].reshape(pieces, proj_rows, holders, sub)
+    proj_full = jnp.transpose(proj_full, (2, 1, 0, 3)).reshape(FILTERS, width)
+
+    kept = [features]
+    kept_low = [features_low]
+    mixed = []
+    for layer in range(2):
+        pre = (
+            jnp.dot(kept_low[layer], highway_half[layer], preferred_element_type=F32)
+            + highway_bias_own[layer]
+        )
+        mixed.append(pre)
+        gate = jax.nn.sigmoid(pre[:, half:])
+        features = gate * features + (1.0 - gate) * jax.nn.silu(pre[:, :half])
+        kept.append(features)
+        kept_low.append(both_halves(features.astype(BF), blocks))
+    own_last = lax.dynamic_slice_in_dim(kept_low[2], pipe * tokens, tokens, 0)
+    encoded = jnp.dot(own_last, proj_full, preferred_element_type=F32) + proj_bias
     encoded_own = lax.all_gather(
-        encoded.astype(BF).reshape(quarter, steps, width), ("pipe", "dir"), axis=0, tiled=True
-    )
-    kept_low = [value.astype(BF) for value in kept]
+        encoded.astype(BF).reshape(quarter, steps, width), ("dir", "pipe"), axis=0, tiled=True
+    )
     kept_low, encoded_own, gate_own = lax.optimization_barrier((kept_low, encoded_own, gate_own))
-    kept_all = [lax.all_gather(value, ALL, axis=0, tiled=True) for value in kept_low[:2]]
+    kept_all = [
+        lax.all_gather(value, ("dir", "dp"), axis=0, tiled=True) for value in kept_low[:2]
+    ]
     inputs = jnp.einsum("rts,rsd->trd", own_order, encoded_own, preferred_element_type=BF)
 
     out_own, dx_own, grad_gate, grad_bias, grad_cell = lstm_call(
@@ -568,25 +579,33 @@
     dx_own, kept_all = lax.optimization_barrier((dx_own, kept_all))
     activations = jnp.einsum("rts,srd->rtd", own_order, out_own, preferred_element_type=BF)
 
-    grad_gate = grad_gate.reshape(n, 2, in_rows // 2, 4 * cell)
-    gate_halves = [lax.all_to_all(grad_gate[:, half], "dp", 0, 0) for half in range(2)]
     grad_stored = jnp.einsum(
         "rts,srd->rtd", own_order, dx_own.astype(BF), preferred_element_type=F32
     )
     grad_stored = jnp.where(pipe == 1, grad_stored, 0.0).astype(BF)
+    grad_stored = grad_stored.reshape(1, -1, group_tokens, width)
     grad_encoded = lax.all_to_all(
-        grad_stored.reshape(parts, tokens, width), ("pipe", "dir"), 0, 0
+        jnp.concatenate([grad_stored, grad_stored]).reshape(-1, group_tokens, width),
+        ("pipe", "dir"),
+        0,
+        0,
     )
     grad_encoded = jnp.sum(grad_encoded.astype(F32), axis=0).astype(BF)
-    encoded_grads = lax.all_gather(grad_encoded, ALL, axis=0, tiled=True)
-
-    grad_proj_bias = jnp.sum(grad_encoded.astype(F32), axis=0)
-    grad_features = jnp.einsum("td,fd->tf", grad_encoded, proj_full, preferred_element_type=F32)
+    grad_encoded, grad_gate = lax.optimization_barrier((grad_encoded, grad_gate))
+    grad_gate = lax.all_to_all(grad_gate.reshape(n, in_rows, 4 * cell), "dp", 0, 0)
+    own_grads = lax.dynamic_slice_in_dim(grad_encoded, pipe * tokens, tokens, 0)
+    encoded_grads = lax.all_gather(own_grads, ALL, axis=0, tiled=True)
+
+    grad_proj_bias = jnp.sum(own_grads.astype(F32), axis=0)
+    proj_half = lax.dynamic_index_in_dim(
+        proj_full.reshape(blocks, 2, sub, width), pipe, 1, keepdims=False
+    ).reshape(half, width)
+    grad_features = jnp.einsum("td,fd->tf", grad_encoded, proj_half, preferred_element_type=F32)
     columns = [None, None]
     grad_highway_bias = [None, None]
     for layer in (1, 0):
-        nonlinear = mixed[layer][:, :FILTERS]
-        gate = jax.nn.sigmoid(mixed[layer][:, FILTERS:])
+        nonlinear = mixed[layer][:, :half]
+        gate = jax.nn.sigmoid(mixed[layer][:, half:])
         grad_mixed = jnp.concatenate(
             [
                 grad_features * (1.0 - gate) * silu_slope(nonlinear),
@@ -594,60 +613,72 @@
             ],
             axis=1,
         ).astype(BF)
-        columns[layer] = to_columns(grad_mixed)
+        columns[layer] = grad_mixed
         grad_highway_bias[layer] = jnp.sum(grad_mixed.astype(F32), axis=0)
-        grad_features = grad_features * gate + jnp.einsum(
-            "tg,fg->tf", grad_mixed, highway_full[layer], preferred_element_type=F32
+        partial = jnp.einsum(
+            "tg,fg->tf", grad_mixed, highway_half[layer], preferred_element_type=F32
+        ).reshape(group_tokens, blocks, 2, sub)
+        sent = lax.dynamic_index_in_dim(partial, 1 - pipe, 2, keepdims=False).astype(BF)
+        came = lax.ppermute(sent, "pipe", [(0, 1), (1, 0)])
+        mine = lax.dynamic_index_in_dim(partial, pipe, 2, keepdims=False)
+        grad_features = grad_features * gate + (mine + came.astype(F32)).reshape(
+            group_tokens, half
         )
-        if layer == 1:
-            grad_features, gate_halves[0] = lax.optimization_barrier(
-                (grad_features, gate_halves[0])
-            )
-    grad_features, columns[1], grad_bias = lax.optimization_barrier(
-        (grad_features, columns[1], grad_bias)
-    )
+    grad_before = grad_features * silu_slope(pooled + conv_bias_own)
+    grad_conv, grad_table = conv_backward(ids, table_low, conv_low, masks, grad_before)
+
+    def spread(value):
+        split = value.reshape(*value.shape[:-1], -1, 1, sub)
+        shown = jnp.arange(2, dtype=jnp.int32)[:, None] == pipe
+        return jnp.where(shown, split, jnp.zeros_like(split)).reshape(*value.shape[:-1], -1)
+
+    grad_conv, grad_gate = lax.optimization_barrier((grad_conv, grad_gate))
+    grad_gate = join_cells(grad_gate)
+    small = (
+        grad_table,
+        spread(jnp.sum(grad_before, axis=0)),
+        spread(jnp.stack(grad_highway_bias)),
+        grad_proj_bias,
+    )
+    flat = jnp.concatenate([value.reshape(-1) for value in small])
+    share = -(-flat.shape[0] // (everyone * 128)) * 128
+    flat = jnp.pad(flat, (0, share * everyone - flat.shape[0])).reshape(everyone, share)
+    cols = FILTERS // everyone
+    packed = jnp.concatenate(
+        [
+            jnp.transpose(
+                spread(grad_conv).reshape(KMAX * CDIM, everyone, cols), (1, 0, 2)
+            ).reshape(everyone, KMAX * CDIM * cols),
+            flat,
+        ],
+        axis=1,
+    ).astype(BF)
+    summed = jnp.sum(lax.all_to_all(packed, ALL, 0, 0).astype(F32), axis=0)
+    grad_conv = summed[: KMAX * CDIM * cols].reshape(KMAX * CDIM, cols)
+    both = jnp.stack(columns, axis=1).reshape(group_tokens, 2, 2, blocks, sub)
+    both = jnp.transpose(both, (2, 3, 0, 1, 4))[:, :, None]
+    shown = (jnp.arange(2, dtype=jnp.int32) == pipe)[None, None, :, None, None, None]
+    both = jnp.where(shown, both, jnp.zeros_like(both))
+    both, summed = lax.optimization_barrier((both, summed))
+    both = lax.all_to_all(both.reshape(everyone, group_tokens, 2 * sub), ALL, 0, 0)
+    parity = lax.rem(lax.axis_index(("dir", "dp")), 2)
+    both = lax.dynamic_index_in_dim(
+        both.reshape(2, holders * group_tokens, 2, sub), parity, 0, keepdims=False
+    )
+    grad_highway = [
+        jnp.einsum("tf,tg->fg", kept_all[layer], both[:, layer], preferred_element_type=F32)
+        for layer in range(2)
+    ]
     grad_bias = lax.all_to_all(
         jnp.broadcast_to(grad_bias, (n, 4 * cell)), "dp", 0, 0
     ).reshape(n, 4, cell)
     grad_bias = jnp.transpose(grad_bias, (1, 0, 2)).reshape(n, 4 * cell)
     grad_bias = lax.dynamic_index_in_dim(grad_bias, me, 0, keepdims=False)
-
-    last_columns = to_columns(kept_low[2])
-    grad_proj = jnp.einsum("tf,td->fd", last_columns, encoded_grads, preferred_element_type=F32)
-    grad_before = grad_features * silu_slope(pooled + conv_bias)
-    grad_conv, grad_table = conv_backward(ids, table_low, conv_low, grad_before)
-    grad_conv, gate_halves[1], columns[0] = lax.optimization_barrier(
-        (grad_conv, gate_halves[1], columns[0])
-    )
-    grad_highway = [
-        jnp.einsum("tf,tg->fg", kept_all[layer], columns[layer], preferred_element_type=F32)
-        for layer in range(2)
-    ]
-    grad_gate = join_cells(jnp.concatenate(gate_halves, axis=1))
-
-    small = (
-        grad_table,
-        jnp.sum(grad_before, axis=0),
-        jnp.stack(grad_highway_bias),
-        grad_proj_bias,
-    )
-    flat = jnp.concatenate([value.reshape(-1) for value in small])
-    share = -(-flat.shape[0] // (everyone * 128)) * 128
-    flat = jnp.pad(flat, (0, share * everyone - flat.shape[0])).reshape(everyone, share)
-    columns = FILTERS // everyone
-    packed = jnp.concatenate(
-        [
-            jnp.transpose(
-                grad_conv.reshape(KMAX * CDIM, everyone, columns), (1, 0, 2)
-            ).reshape(everyone, KMAX * CDIM * columns),
-            flat,
-        ],
-        axis=1,
-    ).astype(BF)
-    summed = jnp.sum(lax.all_to_all(packed, ALL, 0, 0).astype(F32), axis=0)
-    grad_conv = summed[: KMAX * CDIM * columns].reshape(KMAX * CDIM, columns)
+    grad_proj = jnp.einsum(
+        "tf,td->fd", to_columns(own_last), encoded_grads, preferred_element_type=F32
+    )
     shared = lax.all_to_all(
-        jnp.broadcast_to(summed[KMAX * CDIM * columns :], (everyone, share)), ALL, 0, 0
+        jnp.broadcast_to(summed[KMAX * CDIM * cols :], (everyone, share)), ALL, 0, 0
     ).reshape(-1)
     small_sums = []
     start = 0

time: 1060 us -> 1010 us (0.953)
  waiting for transfers between devices: 276 us -> 213 us
  blocking collectives: 5.87 us -> 37.1 us
  matrix products: 83.6 us -> 62.2 us
  Pallas kernels: 435 us -> 452 us
  starting transfers between devices: 98.5 us -> 84.1 us
    all_gather x4, waiting for transfers between devices: 134 us -> 64.1 us  [the longest x1 55.5 us: local(): lax.all_gather(jnp.concatenate([mine, proj_blocks], axis=1).astype(BF), (...]
    all_gather x1 -> x4, blocking collectives: 5.87 us -> 37.1 us  [the longest x3 24.8 us: both_halves(): lax.all_gather(value, 'pipe').reshape(2, tokens, blocks, half // blocks)]
    all_to_all x1, waiting for transfers between devices: 63.1 us -> 43.9 us  [local(): lax.all_to_all(gate_low, 'dp', 0, 0).reshape(n * in_rows, 4 * cell)]
    dot_general x9, matrix products: 54.5 us -> 37.4 us  [the longest x2 11.7 us: local(): jnp.einsum('tg,fg->tf', grad_mixed, highway_half[layer], preferred_elemen...]
    pallas_call x1, Pallas kernels: 423 us -> 440 us  [lstm_call(): pl.pallas_call(functools.partial(lstm_kernel, n, chunk), out_shape=(sds((...]
    all_to_all x1, waiting for transfers between devices: 0.01 us -> 11.9 us  [local(): summed = jnp.sum(lax.all_to_all(packed, ALL, 0, 0).astype(F32), axis=0)]
    all_to_all x3 -> x1, starting transfers between devices: 15.1 us -> 3.51 us  [to_columns(): lax.all_to_all(split, ALL, 0, 0).reshape(count * tokens, columns // count)]
  transfers between devices with their start and end apart: 15 -> 15, of which waited for: 7 -> 11; matrix products, arithmetic and copies ran while one was open for 19% -> 16% of each run, Pallas kernels for 41% -> 45%
where the time goes in v5:
time: 1010 us; the launch traced here: 1000 us
  Pallas kernels  452 us (45%)
  waiting for transfers between devices  213 us (21%)
  local copies, waits for them, and re-layouts  93 us (9%)
  starting transfers between devices  84.1 us (8%)
  matrix products  62.2 us (6%)
  other arithmetic  45.9 us (5%)
  blocking collectives  37.1 us (4%)
  between operations  15.6 us (2%)
    pallas_call x1, Pallas kernels, lstm_call(): pl.pallas_call(functools.partial(lstm_kernel, n, chunk), out_shape=(sds((...  440 us
    all_gather x1, waiting for transfers between devices, local(): lax.all_gather(jnp.concatenate([mine, proj_blocks], axis=1).astype(BF), (...  55.5 us
    all_to_all x1, starting transfers between devices, local(): lax.all_to_all(jnp.concatenate([grad_stored, grad_stored]).reshape(-1, gr...  46 us
    all_to_all x1, waiting for transfers between devices, local(): lax.all_to_all(gate_low, 'dp', 0, 0).reshape(n * in_rows, 4 * cell)  43.9 us
    all_to_all x1, waiting for transfers between devices, local(): lax.all_to_all(grad_gate.reshape(n, in_rows, 4 * cell), 'dp', 0, 0)  43.2 us
    all_to_all x1, waiting for transfers between devices, local(): lax.all_to_all(both.reshape(everyone, group_tokens, 2 * sub), ALL, 0, 0)  27 us
    all_gather x3, blocking collectives, both_halves(): lax.all_gather(value, 'pipe').reshape(2, tokens, blocks, half // blocks)  24.8 us
  transfers between devices with their start and end apart: 15, of which 11 were waited for; matrix products, arithmetic and copies ran while one was open for 16% of the time, Pallas kernels for 45%

profile of v5, /device:TPU:3, one launch (start us, length us, event | category | flops | bytes accessed | tf_op | source)
XLA Modules:
  0.0 1002.7 jit_solution(9871122120316352328)
XLA Ops:
  12.1 6.5 all-to-all-start
  19.4 12.1 %gather_fusion = bf16[6400,16]{1,0:T(8,128)(2,1)S(1)} fusion(bf16[262,16]{1,0:T(8,128)(2,1)S(1)} %copy.250, s32[7168]{0:T(1024)S(1)} %pad_clamp_fusion), kind=kCustom, calls=%fused_computation.clone | custom fusion | bytes 435200 | tf_op jit(solution)/shard_map/jit(_take)/gather | solution.py:49
  40.4 11.0 %select_reduce_fusion = (f32[128,1024]{1,0:T(8,128)S(1)}, f32[128,50,1024]{2,0,1:T(8,128)}) fusion(pred[50,1024]{1,0:T(8,128)(4,1)S(1)} %iota_compare_fusion.6, bf16[128,50,112]{0,2,1:T(8,128)(2,1)S(1)} %slice_dynamic-update-slice_fusion, s32[1024]{0:T(1024)S(1)} %add_bitcast_fusion, s32[112]{0:T(128)S(1)} %and_select_fusion, ...), kind=kOutput, calls=%fused_computation.5 | convolution fusion | flops 1481785344 | bytes 28463620 | tf_op jit(solution)/shard_map/bpk,kf->bpf/dot_general | solution.py:51
  51.5 14.7 %fusion = (f32[128,1024]{1,0:T(8,128)}, f32[128,1024]{1,0:T(8,128)S(1)}) fusion(f32[128,50,1024]{2,0,1:T(8,128)} %get-tuple-element.161, f32[128,1024]{1,0:T(8,128)S(1)} %get-tuple-element.160, pred[50,1024]{1,0:T(8,128)(4,1)S(1)} %iota_compare_fusion.6, f32[128,1024]{1,0:T(8,128)S(1)} %is-finite_select_fusion.1), kind=kLoop, calls=%fused_computation.4 | loop fusion | flops 32505856 | bytes 28362752 | tf_op jit(solution)/shard_map/reduce_sum | solution.py:444
  66.4 8.5 all_gather.32
  75.3 55.5 %all-gather.7.cloned.1.call-done = bf16[2,2304,2048]{2,1,0:T(8,128)(2,1)} async-done(((bf16[2,2304,128]{2,1,0:T(8,128)(2,1)}), bf16[2,2304,2048]{2,1,0:T(8,128)(2,1)}) %all-gather.7.cloned.1.call-update) | async-done | bytes 18874384 | tf_op jit(solution)/shard_map/all_gather | solution.py:502
  141.3 8.6 all-gather
  156.7 7.6 all-gather.1
  172.4 12.3 %all_gather.37 = bf16[16,16,512]{2,1,0:T(8,128)(2,1)S(1)} all-gather(bf16[4,16,512]{2,1,0:T(8,128)(2,1)S(1)} %bitcast.277), channel_id=1, replica_groups=mesh['pipe'=2,'dir'=2,'dp'=8] {'dir','pipe'}, dimensions={0}, use_global_device_ids=true | all-gather | bytes 327680 | tf_op jit(solution)/shard_map/all_gather | solution.py:558
  184.7 43.9 %all-to-all-done.1 = bf16[8,128,2048]{2,1,0:T(8,128)(2,1)} async-done(((bf16[8,128,2048]{2,1,0:T(8,128)(2,1)}), bf16[8,128,2048]{2,1,0:T(8,128)(2,1)}, u32[]{:S(2)}, u32[]{:S(2)}) %all-to-all-start.1) | async-done | bytes 4194336 | tf_op jit(solution)/shard_map/all_to_all | solution.py:534
  228.6 6.5 copy.288
  252.7 440.3 %relay_lstm.1 = (bf16[16,16,512]{2,1,0:T(8,128)(2,1)}, f32[16,16,512]{2,1,0:T(8,128)}, bf16[1024,2048]{1,0:T(8,128)(2,1)}, f32[1,2048]{1,0:T(1,128)}, f32[512,512]{1,0:T(8,128)}) custom-call(bf16[16,16,512]{2,1,0:T(8,128)(2,1)} %bitcast.271, bf16[512,2048]{1,0:T(8,128)(2,1)} %copy.264.wx, bf16[512,2048]{1,0:T(8,128)(2,1)} %copy.265.wh, f32[1,2048]{1,0:T(1,128)} %bitcast.283, ...), custom_call_target="tpu_custom_call" | custom-call | flops 299999985664 | bytes 67108864 | tf_op jit(solution)/shard_map/relay_lstm/pallas_call | solution.py:347
  695.3 46.0 %all-to-all-start.2 = ((bf16[4,128,512]{2,1,0:T(8,128)(2,1)}), bf16[4,128,512]{2,1,0:T(8,128)(2,1)S(1)}, u32[]{:S(2)}, u32[]{:S(2)}) async-start(bf16[4,128,512]{2,1,0:T(8,128)(2,1)} %bitcast.38), calls=%async_computation.2 | async-start | bytes 1048576 | tf_op jit(solution)/shard_map/all_to_all | solution.py:587
  741.3 12.2 %fusion.91 = (bf16[1,2048,2048]{2,1,0:T(8,128)(2,1)}, bf16[1,2048,2048]{2,1,0:T(8,128)(2,1)}) fusion(bf16[2,2304,2048]{2,1,0:T(8,128)(2,1)} %all-gather.7.cloned.1.call-done), kind=kLoop, calls=%fused_computation.174 | loop fusion | bytes 33554432 | tf_op jit(solution)/shard_map/slice | solution.py:548
  761.8 5.9 fusion.37
  798.3 11.7 %multiply_convert_fusion = bf16[128,50,1024]{2,0,1:T(8,128)(2,1)S(1)} fusion(f32[128,50,1024]{2,0,1:T(8,128)} %get-tuple-element.161, f32[128,1024]{1,0:T(8,128)S(1)} %copy-done.19, f32[128,1024]{1,0:T(8,128)S(1)} %copy-done.4, f32[128,1024]{1,0:T(8,128)S(1)} %get-tuple-element.136, pred[50,1024]{1,0:T(8,128)(4,1)S(1)} %copy-done.34), kind=kLoop, calls=%fused_computation.1 | loop fusion | flops 32768000 | bytes 40945664 | tf_op jit(solution)/shard_map/convert_element_type | solution.py:445
  816.9 6.3 fusion.17
  823.1 43.2 %all-to-all-done.3.src = bf16[8,128,2048]{2,1,0:T(8,128)(2,1)} async-done(((bf16[8,128,2048]{2,1,0:T(8,128)(2,1)}), bf16[8,128,2048]{2,1,0:T(8,128)(2,1)}, u32[]{:S(2)}, u32[]{:S(2)}) %all-to-all-start.3) | async-done | bytes 4194336 | tf_op jit(solution)/shard_map/all_to_all | solution.py:595
  878.9 11.9 %all-to-all-done.4 = bf16[32,2,3840]{2,1,0:T(2,128)(2,1)} async-done(((bf16[32,2,3840]{2,1,0:T(2,128)(2,1)}), bf16[32,2,3840]{2,1,0:T(2,128)(2,1)}, u32[]{:S(2)}, u32[]{:S(2)}) %all-to-all-start.4) | async-done | bytes 491552 | tf_op jit(solution)/shard_map/all_to_all | solution.py:656
  898.0 6.5 all-to-all-done.7
  932.5 8.6 all-gather.13.cloned.1.call-done
  943.8 6.0 join_cells.1
  953.7 27.0 %all-to-all-done.6 = bf16[32,128,256]{2,1,0:T(8,128)(2,1)S(1)} async-done(((bf16[32,128,256]{2,1,0:T(8,128)(2,1)}), bf16[32,128,256]{2,1,0:T(8,128)(2,1)S(1)}, u32[]{:S(2)}, u32[]{:S(2)}) %all-to-all-start.6) | async-done | bytes 2097184 | tf_op jit(solution)/shard_map/all_to_all | solution.py:663
  984.8 5.9 convolution_bitcast_fusion
  (294 shorter events, 168.3 us)
Async XLA Ops:
  7.2 229.5 %copy-start = (bf16[1,1,16,16,512]{4,3,2,1,0:T(8,128)(2,1)S(1)}, bf16[1,1,16,16,512]{4,3,2,1,0:T(8,128)(2,1)}, u32[]{:S(2)}) copy-start(bf16[1,1,16,16,512]{4,3,2,1,0:T(8,128)(2,1)} %param.27) | copy-start | bytes 786436
  7.2 123.6 %all-gather.7.cloned.1.call-start = ((), (), s32[]{:S(2)}) async-start(), calls=%async_computation.9 | async-start | bytes 20054016 | tf_op jit(solution)/shard_map/all_gather | solution.py:502
  12.1 28.3 %all-to-all-start = ((bf16[16,112,128]{2,1,0:T(8,128)(2,1)}), bf16[16,112,128]{2,1,0:T(8,128)(2,1)S(1)}, u32[]{:S(2)}, u32[]{:S(2)}) async-start(bf16[16,112,128]{2,1,0:T(8,128)(2,1)} %broadcast_in_dim.202), calls=%async_computation | async-start | bytes 917504 | tf_op jit(solution)/shard_map/all_to_all | solution.py:505
  39.8 100.5 %copy-start.38 = (f32[8,1,128]{2,1,0:T(1,128)}, f32[8,1,128]{2,1,0:T(1,128)S(1)}, u32[]{:S(2)}) copy-start(f32[8,1,128]{2,1,0:T(1,128)S(1)} %constant_dynamic-slice_fusion.7) | copy-start | bytes 12292
  51.4 88.9 %copy-start.3 = (f32[128,1024]{1,0:T(8,128)}, f32[128,1024]{1,0:T(8,128)S(1)}, u32[]{:S(2)}) copy-start(f32[128,1024]{1,0:T(8,128)S(1)} %get-tuple-element.160) | copy-start | bytes 1572868
  66.2 74.2 %copy-start.7 = (f32[128,1024]{1,0:T(8,128)}, f32[128,1024]{1,0:T(8,128)S(1)}, u32[]{:S(2)}) copy-start(f32[128,1024]{1,0:T(8,128)S(1)} %get-tuple-element.132) | copy-start | bytes 1572868
  75.3 60.4 %copy-start.25 = (bf16[128,8,2,128]{0,3,2,1:T(8,128)(2,1)}, bf16[128,8,2,128]{0,3,2,1:T(8,128)(2,1)S(1)}, u32[]{:S(2)}) copy-start(bf16[128,8,2,128]{0,3,2,1:T(8,128)(2,1)S(1)} %copy.255) | copy-start | bytes 1572868
  130.8 97.8 %all-to-all-start.1 = ((bf16[8,128,2048]{2,1,0:T(8,128)(2,1)}), bf16[8,128,2048]{2,1,0:T(8,128)(2,1)}, u32[]{:S(2)}, u32[]{:S(2)}) async-start(bf16[8,128,2048]{2,1,0:T(8,128)(2,1)} %split_cells.1), calls=%async_computation.1 | async-start | bytes 8388608 | tf_op jit(solution)/shard_map/all_to_all | solution.py:534
  135.5 557.5 %all-gather.9.cloned.1.call-start = ((), (), s32[]{:S(2)}) async-start(), calls=%async_computation.10 | async-start | bytes 8912896 | tf_op jit(solution)/shard_map/all_gather | solution.py:563
  141.3 14.0 %copy-start.23 = (f32[128,1024]{1,0:T(8,128)}, f32[128,1024]{1,0:T(8,128)S(1)}, u32[]{:S(2)}) copy-start(f32[128,1024]{1,0:T(8,128)S(1)} %get-tuple-element.140) | copy-start | bytes 1572868
  235.1 458.0 %all-gather.11.cloned.1.call-start = ((), (), s32[]{:S(2)}) async-start(), calls=%async_computation.11 | async-start | bytes 8912896 | tf_op jit(solution)/shard_map/all_gather | solution.py:563
  252.6 441.5 %copy-start.37 = (s32[16,16]{1,0:T(8,128)S(1)}, s32[16,16]{1,0:T(8,128)}, u32[]{:S(2)}) copy-start(s32[16,16]{1,0:T(8,128)} %copy-done.36) | copy-start | bytes 3076
  252.7 441.5 %copy-start.45 = (pred[16,16]{1,0:T(8,128)(4,1)S(1)}, pred[16,16]{1,0:T(8,128)(4,1)}, u32[]{:S(2)}) copy-start(pred[16,16]{1,0:T(8,128)(4,1)} %copy-done.44) | copy-start | bytes 772
  695.3 63.7 %all-to-all-start.2 = ((bf16[4,128,512]{2,1,0:T(8,128)(2,1)}), bf16[4,128,512]{2,1,0:T(8,128)(2,1)S(1)}, u32[]{:S(2)}, u32[]{:S(2)}) async-start(bf16[4,128,512]{2,1,0:T(8,128)(2,1)} %bitcast.38), calls=%async_computation.2 | async-start | bytes 1048576 | tf_op jit(solution)/shard_map/all_to_all | solution.py:587
  768.5 7.6 collective-permute-start
  768.8 97.6 %all-to-all-start.3 = ((bf16[8,128,2048]{2,1,0:T(8,128)(2,1)}), bf16[8,128,2048]{2,1,0:T(8,128)(2,1)}, u32[]{:S(2)}, u32[]{:S(2)}) async-start(bf16[8,128,2048]{2,1,0:T(8,128)(2,1)} %bitcast.231), calls=%async_computation.3 | async-start | bytes 8388608 | tf_op jit(solution)/shard_map/all_to_all | solution.py:595
  787.2 6.5 collective-permute-start.1
  870.5 20.3 %all-to-all-start.4 = ((bf16[32,2,3840]{2,1,0:T(2,128)(2,1)}), bf16[32,2,3840]{2,1,0:T(2,128)(2,1)}, u32[]{:S(2)}, u32[]{:S(2)}) async-start(bf16[32,2,3840]{2,1,0:T(2,128)(2,1)} %reshape.647), calls=%async_computation.4 | async-start | bytes 983040 | tf_op jit(solution)/shard_map/all_to_all | solution.py:656
  876.0 65.1 %all-gather.13.cloned.1.call-start = ((), (), s32[]{:S(2)}) async-start(), calls=%async_computation.12 | async-start | bytes 2162688 | tf_op jit(solution)/shard_map/all_gather | solution.py:597
  878.9 25.7 %copy-start.49 = (f32[1,2048]{1,0:T(1,128)S(1)}, f32[1,2048]{1,0:T(1,128)}, u32[]{:S(2)}) copy-start(f32[1,2048]{1,0:T(1,128)} %get-tuple-element.52) | copy-start | bytes 24580
  890.8 13.8 %all-to-all-start.7 = ((bf16[32,2,2048]{2,1,0:T(2,128)(2,1)}), bf16[32,2,2048]{2,1,0:T(2,128)(2,1)S(1)}, u32[]{:S(2)}, u32[]{:S(2)}) async-start(bf16[32,2,2048]{2,1,0:T(2,128)(2,1)} %reshape.649), calls=%async_computation.7 | async-start | bytes 524288 | tf_op jit(solution)/shard_map/all_to_all | solution.py:438
  905.2 9.2 all-to-all-start.8
  915.1 10.8 %all-to-all-start.5 = ((f32[32,1,512]{2,1,0:T(1,128)}), f32[32,1,512]{2,1,0:T(1,128)S(1)}, u32[]{:S(2)}, u32[]{:S(2)}) async-start(f32[32,1,512]{2,1,0:T(1,128)} %broadcast_in_dim.225), calls=%async_computation.5 | async-start | bytes 131072 | tf_op jit(solution)/shard_map/all_to_all | solution.py:680
  925.9 54.8 %all-to-all-start.6 = ((bf16[32,128,256]{2,1,0:T(8,128)(2,1)}), bf16[32,128,256]{2,1,0:T(8,128)(2,1)S(1)}, u32[]{:S(2)}, u32[]{:S(2)}) async-start(bf16[32,128,256]{2,1,0:T(8,128)(2,1)} %reshape.596), calls=%async_computation.6 | async-start | bytes 4194304 | tf_op jit(solution)/shard_map/all_to_all | solution.py:663
  (49 other events, 339.8 us)
Sparse Core Ops, SparseCore 0:
  11.3 119.4 all-gather.6
  235.2 107.5 all-gather.8
  344.9 116.9 all-gather.10
  880.1 60.9 all-gather.12

commit v6 on v5

--- a/solution.py
+++ b/solution.py
@@ -60,15 +60,14 @@
         lax.fori_loop(1, count, lambda off, _: (step(off), 0)[1], 0)
 
 
-def lstm_kernel(
-    n, chunk,
-    x_own, wx, wh, bias, p, wxt, wht, pt, cot,
-    out_ref, dx_ref, dw_hbm, db_ref, dp_ref,
-    xbuf, hbuf, dqbuf, gates, cells, ebuf, hown, gscr, escr, dabuf, ucell, dwacc,
-    stage, inbox, stage2, inbox2, relay, gbuf, rown,
-    in_send, in_recv, ag_send, ag_recv, dq_send, dq_recv, rs_send, rs_recv, dx_send, dx_recv,
-    x_send, x_recv, g_send, g_recv, st_sem,
-):
+def lstm_kernel(n, chunk, x_own, bias, p, pt, cot, *refs):
+    w_in = refs[:n]
+    out_ref, dx_ref, db_ref, dp_ref = refs[n:n + 4]
+    dw_out = refs[n + 4:2 * n + 4]
+    (xbuf, hbuf, dqbuf, gates, cells, ebuf, hown, gscr, escr, dabuf, ucell, dwacc, w, wt,
+     stage, inbox, stage2, inbox2, relay, gbuf, rown,
+     in_send, in_recv, ag_send, ag_recv, dq_send, dq_recv, rs_send, rs_recv,
+     dx_send, dx_recv, x_send, x_recv, g_send, g_recv, st_sem, w_sem) = refs[2 * n + 4:]
     steps, _, rows, width = xbuf.shape
     total = n * rows
     cell = cells.shape[2]
@@ -89,6 +88,13 @@
         barrier, inc=1, device_id=(pipe, direction, peer(off)), device_id_type=MESH))
     pl.semaphore_signal(barrier, inc=1, device_id=partner, device_id_type=MESH)
 
+    each = 2 * width // n
+    loads = []
+    for off in range(n):
+        at = pl.multiple_of(lax.rem(me + (n - off), n) * each, each)
+        loads.append(pltpu.make_async_copy(w_in[off], w.at[pl.ds(at, each)], w_sem.at[off]))
+        loads[-1].start()
+
     @pl.when(first)
     def _():
         for t in range(steps):
@@ -144,6 +150,11 @@
         in_start(0)
         in_start(1)
 
+    for load in loads:
+        load.wait()
+    for at in range(0, 2 * width, 128):
+        wt[:, at:at + 128] = w[at:at + 128, :].T
+
     def ag_wait(buf, slot):
         def both(off):
             ag_copy(buf, slot, off).wait_send()
@@ -166,7 +177,7 @@
             in_wait(in_recv, t)
 
         gscr[...] = jnp.dot(
-            xbuf[t].reshape(total, width), wx[...], preferred_element_type=F32) + bias[...]
+            xbuf[t].reshape(total, width), w[:width, :], preferred_element_type=F32) + bias[...]
 
         @pl.when(t > 0)
         def _():
@@ -177,7 +188,7 @@
                 x_copy(t - 1).start()
 
         gscr[...] += jnp.dot(
-            hbuf[t].reshape(total, width), wh[...], preferred_element_type=F32)
+            hbuf[t].reshape(total, width), w[width:, :], preferred_element_type=F32)
 
         def rows_step(k, _):
             at = pl.ds(pl.multiple_of(k * chunk, chunk), chunk)
@@ -293,11 +304,11 @@
             return 0
 
         lax.fori_loop(0, total // chunk, rows_step, 0)
-        r = jnp.dot(dabuf[0], wht[...], preferred_element_type=F32)
+        r = jnp.dot(dabuf[0], wt[:, width:], preferred_element_type=F32)
         stage[...] = r.astype(BF).reshape(n, rows, width)
         over(n, lambda off: rs_copy(off).start())
         inbox[me] = stage[me]
-        dx = jnp.dot(dabuf[0], wxt[...], preferred_element_type=F32)
+        dx = jnp.dot(dabuf[0], wt[:, :width], preferred_element_type=F32)
         stage2[slot] = dx.astype(BF).reshape(n, rows, width)
         over(n, lambda off: dx_copy(slot, off).start())
         inbox2[slot, me] = stage2[slot, me]
@@ -319,22 +330,21 @@
     def _():
         lax.fori_loop(0, steps, lambda t, _: (g_copy(t).wait_send(), 0)[1], 0)
 
-    pieces = 2 * width // total
-
-    def dw_copy(piece):
+    def dw_copy(off):
         return pltpu.make_async_copy(
-            dabuf.at[piece % 2], dw_hbm.at[pl.ds(piece * total, total)], st_sem.at[piece % 2])
-
-    for piece in range(pieces):
-        if piece > 1:
-            dw_copy(piece - 2).wait()
-        dabuf[piece % 2] = dwacc[pl.ds(piece * total, total), :].astype(BF)
-        dw_copy(piece).start()
-    for piece in range(max(0, pieces - 2), pieces):
-        dw_copy(piece).wait()
-
-
-def lstm_call(n, x, wx, wh, bias, p, wxt, wht, pt, cot, chunk=16):
+            dabuf.at[off % 2, pl.ds(0, each)], dw_out[off], st_sem.at[off % 2])
+
+    for off in range(n):
+        if off > 1:
+            dw_copy(off - 2).wait()
+        at = pl.multiple_of(lax.rem(me + off, n) * each, each)
+        dabuf[off % 2, :each, :] = dwacc[pl.ds(at, each), :].astype(BF)
+        dw_copy(off).start()
+    for off in range(n - 2, n):
+        dw_copy(off).wait()
+
+
+def lstm_call(n, x, weights, bias, p, pt, cot, chunk=16):
     steps, rows, width = x.shape
     cell = p.shape[0]
     total = n * rows
@@ -348,44 +358,51 @@
         functools.partial(lstm_kernel, n, chunk),
         out_shape=(
             sds((steps, rows, width), BF), sds((steps, rows, width), F32),
-            sds((2 * width, 4 * cell), BF), sds((1, 4 * cell), F32), sds((cell, width), F32)),
-        in_specs=[vm] * 9,
-        out_specs=(vm, vm, hb, vm, vm),
+            sds((1, 4 * cell), F32), sds((cell, width), F32),
+            *[sds((2 * width // n, 4 * cell), BF)] * n),
+        in_specs=[vm] * 5 + [hb] * n,
+        out_specs=[vm] * 4 + [hb] * n,
         scratch_shapes=[
             V((steps, n, rows, width), BF), V((steps + 1, n, rows, width), BF),
             V((steps, n, rows, width), BF), V((steps, total, 4 * cell), keep),
             V((steps + 1, total, cell), F32), V((steps, total, cell), BF),
             V((steps, rows, width), F32), V((total, 4 * cell), F32),
             V((total, cell), F32), V((2, total, 4 * cell), BF), V((total, cell), F32),
-            V((2 * width, 4 * cell), F32),
+            V((2 * width, 4 * cell), F32), V((2 * width, 4 * cell), BF),
+            V((4 * cell, 2 * width), BF),
             V((n, rows, width), BF), V((n, rows, width), BF),
             V((2, n, rows, width), BF), V((2, n, rows, width), BF),
             V((steps, rows, width), BF), V((steps, rows, width), BF), V((rows, width), F32),
             dma((steps,)), dma((steps,)), dma((n,)), dma((n,)), dma((n,)), dma((n,)), dma((n,)), dma((n,)), dma((2, n)), dma((2, n)),
-            dma((steps,)), dma((steps,)), dma((steps,)), dma((steps,)), dma((2,)),
+            dma((steps,)), dma((steps,)), dma((steps,)), dma((steps,)), dma((2,)), dma((n,)),
         ],
         compiler_params=pltpu.CompilerParams(
             collective_id=0, has_side_effects=True, vmem_limit_bytes=60 * 1024 * 1024),
         cost_estimate=pl.CostEstimate(
             flops=300_000_000_000, bytes_accessed=64 * 1024 * 1024, transcendentals=0),
         name="relay_lstm",
-    )(x, wx, wh, bias, p, wxt, wht, pt, cot)
+    )(x, bias, p, pt, cot, *weights)
+
+
+def turned(off, n, sign):
+    return lax.rem(lax.axis_index("dp") + (off if sign > 0 else n - off), n)
 
 
 def split_cells(weight, n):
     rows, gates = weight.shape
     cell = gates // (4 * n)
 
-    def body(src, dst):
-        for k in range(n):
-            dst[k] = src[:, k * cell : (k + 1) * cell].astype(BF)
+    def body(src, *dst):
+        for off in range(n):
+            at = pl.multiple_of(turned(off, n, 1) * cell, cell)
+            dst[off][...] = src[:, pl.ds(at, cell)].astype(BF)
 
     return pl.pallas_call(
         body,
         grid=(4,),
-        out_shape=jax.ShapeDtypeStruct((n, rows, 4 * cell), BF),
+        out_shape=[jax.ShapeDtypeStruct((rows, 4 * cell), BF)] * n,
         in_specs=[pl.BlockSpec((rows, n * cell), lambda b: (0, b))],
-        out_specs=pl.BlockSpec((n, rows, cell), lambda b: (0, 0, b)),
+        out_specs=[pl.BlockSpec((rows, cell), lambda b: (0, b))] * n,
         cost_estimate=pl.CostEstimate(
             flops=0, bytes_accessed=6 * rows * gates, transcendentals=0
         ),
@@ -394,24 +411,35 @@
 
 
 def join_cells(blocks):
-    n, rows, gates = blocks.shape
+    n = len(blocks)
+    rows, gates = blocks[0].shape
     cell = gates // 4
 
-    def body(src, dst):
-        for k in range(n):
-            dst[:, k * cell : (k + 1) * cell] = src[k].astype(F32)
+    def body(*refs):
+        dst = refs[n]
+        for off in range(n):
+            at = pl.multiple_of(turned(off, n, -1) * cell, cell)
+            dst[:, pl.ds(at, cell)] = refs[off][...].astype(F32)
 
     return pl.pallas_call(
         body,
         grid=(4,),
         out_shape=jax.ShapeDtypeStruct((rows, n * gates), F32),
-        in_specs=[pl.BlockSpec((n, rows, cell), lambda b: (0, 0, b))],
+        in_specs=[pl.BlockSpec((rows, cell), lambda b: (0, b))] * n,
         out_specs=pl.BlockSpec((rows, n * cell), lambda b: (0, b)),
         cost_estimate=pl.CostEstimate(
             flops=0, bytes_accessed=6 * n * rows * gates, transcendentals=0
         ),
         name="join_cells",
-    )(blocks)
+    )(*blocks)
+
+
+def exchange(blocks):
+    n = len(blocks)
+    return [blocks[0]] + [
+        lax.ppermute(blocks[off], "dp", [(i, (i + off) % n) for i in range(n)])
+        for off in range(1, n)
+    ]
 
 
 def conv_forward(ids, table_low, conv_low, valid_place):
@@ -429,13 +457,6 @@
     tokens, half = value.shape
     pair = lax.all_gather(value, "pipe").reshape(2, tokens, blocks, half // blocks)
     return jnp.transpose(pair, (1, 2, 0, 3)).reshape(tokens, 2 * half)
-
-
-def to_columns(value):
-    count = lax.axis_size(ALL)
-    tokens, columns = value.shape
-    split = jnp.transpose(value.reshape(tokens, count, columns // count), (1, 0, 2))
-    return lax.all_to_all(split, ALL, 0, 0).reshape(count * tokens, columns // count)
 
 
 def conv_backward(ids, table_low, conv_low, masks, grad_before):
@@ -527,11 +548,10 @@
     pooled = conv_forward(ids, table_low, conv_low, masks[1])
     features = jax.nn.silu(pooled + conv_bias_own)
     features_low = both_halves(features.astype(BF), blocks)
-    in_rows = gate_weight.shape[2]
     gate_low, gathered, features_low = lax.optimization_barrier(
         (split_cells(gate_weight[0, 0], n), gathered, features_low)
     )
-    gate_own = lax.all_to_all(gate_low, "dp", 0, 0).reshape(n * in_rows, 4 * cell)
+    gate_own = exchange(gate_low)
     bias_own = lax.dynamic_index_in_dim(
         gate_bias[0, 0].reshape(4, n, cell), me, 1, keepdims=False
     ).reshape(1, 4 * cell)
@@ -560,22 +580,20 @@
     )
     kept_low, encoded_own, gate_own = lax.optimization_barrier((kept_low, encoded_own, gate_own))
     kept_all = [
-        lax.all_gather(value, ("dir", "dp"), axis=0, tiled=True) for value in kept_low[:2]
+        lax.all_gather(
+            lax.dynamic_slice_in_dim(value, pipe * tokens, tokens, 0),
+            ("dir", "dp"),
+            axis=0,
+            tiled=True,
+        )
+        for value in kept_low[:2]
     ]
     inputs = jnp.einsum("rts,rsd->trd", own_order, encoded_own, preferred_element_type=BF)
 
-    out_own, dx_own, grad_gate, grad_bias, grad_cell = lstm_call(
-        n,
-        inputs,
-        gate_own[:width],
-        gate_own[width:],
-        bias_own,
-        cell_low,
-        gate_own[:width].T,
-        gate_own[width:].T,
-        cell_low.T,
-        cot,
-    )
+    out_own, dx_own, grad_bias, grad_cell, *grad_gate = lstm_call(
+        n, inputs, gate_own, bias_own, cell_low, cell_low.T, cot
+    )
+    grad_gate = exchange(grad_gate)
     dx_own, kept_all = lax.optimization_barrier((dx_own, kept_all))
     activations = jnp.einsum("rts,srd->rtd", own_order, out_own, preferred_element_type=BF)
 
@@ -591,10 +609,8 @@
         0,
     )
     grad_encoded = jnp.sum(grad_encoded.astype(F32), axis=0).astype(BF)
-    grad_encoded, grad_gate = lax.optimization_barrier((grad_encoded, grad_gate))
-    grad_gate = lax.all_to_all(grad_gate.reshape(n, in_rows, 4 * cell), "dp", 0, 0)
     own_grads = lax.dynamic_slice_in_dim(grad_encoded, pipe * tokens, tokens, 0)
-    encoded_grads = lax.all_gather(own_grads, ALL, axis=0, tiled=True)
+    encoded_grads = lax.all_gather(own_grads, ("dir", "dp"), axis=0, tiled=True)
 
     grad_proj_bias = jnp.sum(own_grads.astype(F32), axis=0)
     proj_half = lax.dynamic_index_in_dim(
@@ -617,7 +633,8 @@
         grad_highway_bias[layer] = jnp.sum(grad_mixed.astype(F32), axis=0)
         partial = jnp.einsum(
             "tg,fg->tf", grad_mixed, highway_half[layer], preferred_element_type=F32
-        ).reshape(group_tokens, blocks, 2, sub)
+        )
+        partial = lax.optimization_barrier(partial).reshape(group_tokens, blocks, 2, sub)
         sent = lax.dynamic_index_in_dim(partial, 1 - pipe, 2, keepdims=False).astype(BF)
         came = lax.ppermute(sent, "pipe", [(0, 1), (1, 0)])
         mine = lax.dynamic_index_in_dim(partial, pipe, 2, keepdims=False)
@@ -625,6 +642,7 @@
             group_tokens, half
         )
     grad_before = grad_features * silu_slope(pooled + conv_bias_own)
+    grad_before, grad_gate[1:4] = lax.optimization_barrier((grad_before, grad_gate[1:4]))
     grad_conv, grad_table = conv_backward(ids, table_low, conv_low, masks, grad_before)
 
     def spread(value):
@@ -632,7 +650,18 @@
         shown = jnp.arange(2, dtype=jnp.int32)[:, None] == pipe
         return jnp.where(shown, split, jnp.zeros_like(split)).reshape(*value.shape[:-1], -1)
 
-    grad_conv, grad_gate = lax.optimization_barrier((grad_conv, grad_gate))
+    cols = FILTERS // everyone
+    pair = jnp.stack(columns, axis=1).reshape(2, tokens, 2, 2, blocks, 1, sub)
+    sent = lax.dynamic_index_in_dim(pair, 1 - pipe, 0, keepdims=False)
+    came = lax.ppermute(sent, "pipe", [(0, 1), (1, 0)])
+    mine = lax.dynamic_index_in_dim(pair, pipe, 0, keepdims=False)
+    shown = (jnp.arange(2, dtype=jnp.int32) == pipe)[:, None]
+    pair = jnp.where(shown, mine, came)
+    pair = jnp.transpose(pair, (3, 4, 0, 1, 2, 5)).reshape(holders, tokens, 4 * sub)
+    last = jnp.transpose(own_last.reshape(tokens, 2, holders, cols), (2, 0, 1, 3))
+    pair = jnp.concatenate([pair, last.reshape(holders, tokens, 2 * cols)], axis=2)
+    pair = lax.all_to_all(pair, ("dir", "dp"), 0, 0).reshape(holders * tokens, -1)
+    grad_conv, pair, grad_gate = lax.optimization_barrier((grad_conv, pair, grad_gate))
     grad_gate = join_cells(grad_gate)
     small = (
         grad_table,
@@ -643,42 +672,53 @@
     flat = jnp.concatenate([value.reshape(-1) for value in small])
     share = -(-flat.shape[0] // (everyone * 128)) * 128
     flat = jnp.pad(flat, (0, share * everyone - flat.shape[0])).reshape(everyone, share)
-    cols = FILTERS // everyone
+    mine = jnp.arange(n, dtype=jnp.int32)[None, :, None] == me
+    bias_parts = jnp.where(mine, grad_bias.reshape(4, 1, cell), 0.0).reshape(1, n, 4 * cell)
+    mine = jnp.arange(everyone // n, dtype=jnp.int32) == lax.axis_index(("pipe", "dir"))
+    bias_parts = jnp.where(mine[:, None, None], bias_parts, 0.0).reshape(everyone, 4 * cell)
     packed = jnp.concatenate(
         [
             jnp.transpose(
                 spread(grad_conv).reshape(KMAX * CDIM, everyone, cols), (1, 0, 2)
             ).reshape(everyone, KMAX * CDIM * cols),
             flat,
+            bias_parts,
         ],
         axis=1,
     ).astype(BF)
     summed = jnp.sum(lax.all_to_all(packed, ALL, 0, 0).astype(F32), axis=0)
     grad_conv = summed[: KMAX * CDIM * cols].reshape(KMAX * CDIM, cols)
-    both = jnp.stack(columns, axis=1).reshape(group_tokens, 2, 2, blocks, sub)
-    both = jnp.transpose(both, (2, 3, 0, 1, 4))[:, :, None]
-    shown = (jnp.arange(2, dtype=jnp.int32) == pipe)[None, None, :, None, None, None]
-    both = jnp.where(shown, both, jnp.zeros_like(both))
-    both, summed = lax.optimization_barrier((both, summed))
-    both = lax.all_to_all(both.reshape(everyone, group_tokens, 2 * sub), ALL, 0, 0)
-    parity = lax.rem(lax.axis_index(("dir", "dp")), 2)
-    both = lax.dynamic_index_in_dim(
-        both.reshape(2, holders * group_tokens, 2, sub), parity, 0, keepdims=False
-    )
-    grad_highway = [
-        jnp.einsum("tf,tg->fg", kept_all[layer], both[:, layer], preferred_element_type=F32)
-        for layer in range(2)
-    ]
-    grad_bias = lax.all_to_all(
-        jnp.broadcast_to(grad_bias, (n, 4 * cell)), "dp", 0, 0
-    ).reshape(n, 4, cell)
-    grad_bias = jnp.transpose(grad_bias, (1, 0, 2)).reshape(n, 4 * cell)
-    grad_bias = lax.dynamic_index_in_dim(grad_bias, me, 0, keepdims=False)
-    grad_proj = jnp.einsum(
-        "tf,td->fd", to_columns(own_last), encoded_grads, preferred_element_type=F32
-    )
+    grad_bias = summed[KMAX * CDIM * cols + share :]
+    last = pair[:, 4 * sub :].reshape(holders * tokens, 2, cols)
+    pair = pair[:, : 4 * sub].reshape(holders * tokens, 2, 2, sub)
+
+    def partial_sums(owner):
+        return [
+            jnp.einsum(
+                "tf,tg->fg",
+                kept_all[layer],
+                lax.dynamic_index_in_dim(pair[:, layer], owner, 1, keepdims=False),
+                preferred_element_type=F32,
+            )
+            for layer in range(2)
+        ] + [
+            jnp.einsum(
+                "tf,td->fd",
+                lax.dynamic_index_in_dim(last, owner, 1, keepdims=False),
+                encoded_grads,
+                preferred_element_type=F32,
+            )
+        ]
+
+    sent = jnp.concatenate(
+        [value.astype(BF).reshape(-1, sub) for value in partial_sums(1 - pipe)]
+    )
+    came = lax.ppermute(sent, "pipe", [(0, 1), (1, 0)]).astype(F32)
+    mine = partial_sums(pipe)
+    grad_highway = jnp.stack(mine[:2]) + came[: 2 * FILTERS].reshape(2, FILTERS, sub)
+    grad_proj = mine[2] + came[2 * FILTERS :].reshape(cols, width)
     shared = lax.all_to_all(
-        jnp.broadcast_to(summed[KMAX * CDIM * cols :], (everyone, share)), ALL, 0, 0
+        jnp.broadcast_to(summed[KMAX * CDIM * cols :][:share], (everyone, share)), ALL, 0, 0
     ).reshape(-1)
     small_sums = []
     start = 0
@@ -690,7 +730,7 @@
         small_sums[0],
         grad_conv,
         small_sums[1],
-        jnp.stack(grad_highway),
+        grad_highway,
         small_sums[2],
         grad_proj,
         small_sums[3],

time: 1010 us -> 954 us (0.945)
  waiting for transfers between devices: 213 us -> 99.3 us
  starting transfers between devices: 84.1 us -> 141 us
  Pallas kernels: 452 us -> 430 us
  other arithmetic: 45.9 us -> 60.1 us
    all_to_all x6 -> x2, waiting for transfers between devices: 129 us -> 13.5 us  [the longest x1 13.5 us: local(): lax.all_to_all(pair, ('dir', 'dp'), 0, 0).reshape(holders * tokens, -1)]
    all_to_all x1, starting transfers between devices: 46 us -> 80.5 us  [local(): lax.all_to_all(jnp.concatenate([grad_stored, grad_stored]).reshape(-1, gr...]
    pallas_call x1, Pallas kernels: 440 us -> 418 us  [lstm_call(): pl.pallas_call(functools.partial(lstm_kernel, n, chunk), out_shape=(sds((...]
    ppermute x0 -> x15, waiting for transfers between devices: none -> 21.2 us  [the longest x1 13.2 us: local(): came = lax.ppermute(sent, 'pipe', [(0, 1), (1, 0)]).astype(F32)]
    ppermute x0 -> x15, starting transfers between devices: none -> 17.7 us  [the longest x14 17.6 us: exchange(): lax.ppermute(blocks[off], 'dp', [(i, (i + off) % n) for i in range(n)])]
    slice x4 -> x9, local copies, waits for them, and re-layouts: 18.6 us -> 4.47 us  [the longest x2 1.83 us: local(): pair = pair[:, :4 * sub].reshape(holders * tokens, 2, 2, sub)]
    all_to_all x6 -> x2, starting transfers between devices: 25.3 us -> 13.1 us  [the longest x1 7.26 us: local(): lax.all_to_all(pair, ('dir', 'dp'), 0, 0).reshape(holders * tokens, -1)]
    all_to_all x1, waiting for transfers between devices: 11.9 us -> 0.01 us  [local(): summed = jnp.sum(lax.all_to_all(packed, ALL, 0, 0).astype(F32), axis=0)]
  transfers between devices with their start and end apart: 15 -> 27, of which waited for: 11 -> 7; matrix products, arithmetic and copies ran while one was open for 16% -> 20% of each run, Pallas kernels for 45% -> 46%
where the time goes in v6:
time: 954 us; the launch traced here: 943 us
  Pallas kernels  430 us (45%)
  starting transfers between devices  141 us (15%)
  waiting for transfers between devices  99.3 us (10%)
  local copies, waits for them, and re-layouts  93.3 us (10%)
  matrix products  66.8 us (7%)
  other arithmetic  60.1 us (6%)
  blocking collectives  36.9 us (4%)
  between operations  15.7 us (2%)
    pallas_call x1, Pallas kernels, lstm_call(): pl.pallas_call(functools.partial(lstm_kernel, n, chunk), out_shape=(sds((...  418 us
    all_to_all x1, starting transfers between devices, local(): lax.all_to_all(jnp.concatenate([grad_stored, grad_stored]).reshape(-1, gr...  80.5 us
    all_gather x1, waiting for transfers between devices, local(): lax.all_gather(jnp.concatenate([mine, proj_blocks], axis=1).astype(BF), (...  55.6 us
    all_gather x3, blocking collectives, both_halves(): lax.all_gather(value, 'pipe').reshape(2, tokens, blocks, half // blocks)  22.2 us
    unnamed x159, local copies, waits for them, and re-layouts  20.8 us
  transfers between devices with their start and end apart: 27, of which 7 were waited for; matrix products, arithmetic and copies ran while one was open for 20% of the time, Pallas kernels for 46%

profile of v6, /device:TPU:3, one launch (start us, length us, event | category | flops | bytes accessed | tf_op | source)
XLA Modules:
  0.0 943.4 jit_solution(6635312951921205403)
XLA Ops:
  12.1 6.5 all-to-all-start
  19.2 12.1 %gather_fusion = bf16[6400,16]{1,0:T(8,128)(2,1)S(1)} fusion(bf16[262,16]{1,0:T(8,128)(2,1)S(1)} %copy.232, s32[7168]{0:T(1024)S(1)} %pad_clamp_fusion), kind=kCustom, calls=%fused_computation.clone | custom fusion | bytes 435200 | tf_op jit(solution)/shard_map/jit(_take)/gather | solution.py:49
  33.8 5.9 split_cells.1
  40.3 11.0 %select_reduce_fusion = (f32[128,1024]{1,0:T(8,128)S(1)}, f32[128,50,1024]{2,0,1:T(8,128)}) fusion(pred[50,1024]{1,0:T(8,128)(4,1)S(1)} %iota_compare_fusion.6, bf16[128,50,112]{0,2,1:T(8,128)(2,1)S(1)} %slice_dynamic-update-slice_fusion, s32[1024]{0:T(1024)S(1)} %add_bitcast_fusion, s32[112]{0:T(128)S(1)} %and_select_fusion, ...), kind=kOutput, calls=%fused_computation.5 | convolution fusion | flops 1481785344 | bytes 28463620 | tf_op jit(solution)/shard_map/bpk,kf->bpf/dot_general | solution.py:51
  51.4 14.7 %fusion = (f32[128,1024]{1,0:T(8,128)}, f32[128,1024]{1,0:T(8,128)S(1)}) fusion(f32[128,50,1024]{2,0,1:T(8,128)} %get-tuple-element.224, f32[128,1024]{1,0:T(8,128)S(1)} %get-tuple-element.223, pred[50,1024]{1,0:T(8,128)(4,1)S(1)} %iota_compare_fusion.6, f32[128,1024]{1,0:T(8,128)S(1)} %is-finite_select_fusion.1), kind=kLoop, calls=%fused_computation.4 | loop fusion | flops 32505856 | bytes 28362752 | tf_op jit(solution)/shard_map/reduce_sum | solution.py:465
  66.4 8.5 all_gather.32
  75.2 55.6 %all-gather.7.cloned.1.call-done = bf16[2,2304,2048]{2,1,0:T(8,128)(2,1)} async-done(((bf16[2,2304,128]{2,1,0:T(8,128)(2,1)}), bf16[2,2304,2048]{2,1,0:T(8,128)(2,1)}) %all-gather.7.cloned.1.call-update) | async-done | bytes 18874384 | tf_op jit(solution)/shard_map/all_gather | solution.py:523
  141.3 7.2 all-gather
  154.9 6.4 all-gather.1
  176.1 14.8 %all_gather.37 = bf16[16,16,512]{2,1,0:T(8,128)(2,1)} all-gather(bf16[4,16,512]{2,1,0:T(8,128)(2,1)S(1)} %bitcast.304), channel_id=1, replica_groups=mesh['pipe'=2,'dir'=2,'dp'=8] {'dir','pipe'}, dimensions={0}, use_global_device_ids=true | all-gather | bytes 327680 | tf_op jit(solution)/shard_map/all_gather | solution.py:578
  192.7 6.1 collective-permute-done.6.refs_7_
  220.9 418.4 %relay_lstm.1 = (bf16[16,16,512]{2,1,0:T(8,128)(2,1)}, f32[16,16,512]{2,1,0:T(8,128)}, f32[1,2048]{1,0:T(1,128)}, f32[512,512]{1,0:T(8,128)}, bf16[128,2048]{1,0...) custom-call(bf16[16,16,512]{2,1,0:T(8,128)(2,1)} %bitcast.299, ...), custom_call_target="tpu_custom_call" | custom-call | flops 299999985664 | bytes 67108864 | tf_op jit(solution)/shard_map/relay_lstm/pallas_call | solution.py:357
  648.9 80.5 %all-to-all-start.1 = ((bf16[4,128,512]{2,1,0:T(8,128)(2,1)}), bf16[4,128,512]{2,1,0:T(8,128)(2,1)S(1)}, u32[]{:S(2)}, u32[]{:S(2)}) async-start(bf16[4,128,512]{2,1,0:T(8,128)(2,1)} %bitcast.35), calls=%async_computation.1 | async-start | bytes 1048576 | tf_op jit(solution)/shard_map/all_to_all | solution.py:605
  729.4 8.2 all-gather.13.cloned.1.call-start
  742.3 6.3 fusion.1
  761.6 7.2 fusion.5
  802.4 7.3 all-to-all-start.2
  809.7 11.7 %multiply_convert_fusion = bf16[128,50,1024]{2,0,1:T(8,128)(2,1)S(1)} fusion(f32[128,50,1024]{2,0,1:T(8,128)} %get-tuple-element.224, f32[128,1024]{1,0:T(8,128)S(1)} %copy-done.18, f32[128,1024]{1,0:T(8,128)S(1)} %copy-done.4, f32[128,1024]{1,0:T(8,128)S(1)} %fusion.41, pred[50,1024]{1,0:T(8,128)(4,1)S(1)} %copy-done.36), kind=kLoop, calls=%fused_computation.1 | loop fusion | flops 32768000 | bytes 40945664 | tf_op jit(solution)/shard_map/convert_element_type | solution.py:466
  834.2 6.0 fusion.25
  840.3 13.5 %all-to-all-done.2 = bf16[16,64,640]{2,1,0:T(8,128)(2,1)} async-done(((bf16[16,64,640]{2,1,0:T(8,128)(2,1)}), bf16[16,64,640]{2,1,0:T(8,128)(2,1)}, u32[]{:S(2)}, u32[]{:S(2)}) %all-to-all-start.2) | async-done | bytes 1310752 | tf_op jit(solution)/shard_map/all_to_all | solution.py:663
  863.0 13.2 %all-to-all-start.3 = ((bf16[32,2,4864]{2,1,0:T(2,128)(2,1)}), bf16[32,2,4864]{2,1,0:T(2,128)(2,1)}, u32[]{:S(2)}, u32[]{:S(2)}) async-start(bf16[32,2,4864]{2,1,0:T(2,128)(2,1)} %reshape.675), calls=%async_computation.3 | async-start | bytes 1245184 | tf_op jit(solution)/shard_map/all_to_all | solution.py:689
  883.4 6.1 join_cells.1
  897.3 13.2 %collective-permute-done.17 = bf16[4352,128]{1,0:T(8,128)(2,1)S(1)} collective-permute-done((bf16[4352,128]{1,0:T(8,128)(2,1)}, bf16[4352,128]{1,0:T(8,128)(2,1)S(1)}, u32[]{:S(2)}, u32[]{:S(2)}) %collective-permute-start.17) | collective-permute-done | bytes 1114144 | tf_op jit(solution)/shard_map/ppermute | solution.py:716
  918.8 5.8 all-to-all-start.4
  (368 shorter events, 181.4 us)
Async XLA Ops:
  7.2 123.6 %all-gather.7.cloned.1.call-start = ((), (), s32[]{:S(2)}) async-start(), calls=%async_computation.5 | async-start | bytes 20054016 | tf_op jit(solution)/shard_map/all_gather | solution.py:523
  12.1 28.2 %all-to-all-start = ((bf16[16,112,128]{2,1,0:T(8,128)(2,1)}), bf16[16,112,128]{2,1,0:T(8,128)(2,1)S(1)}, u32[]{:S(2)}, u32[]{:S(2)}) async-start(bf16[16,112,128]{2,1,0:T(8,128)(2,1)} %broadcast_in_dim.261), calls=%async_computation | async-start | bytes 917504 | tf_op jit(solution)/shard_map/all_to_all | solution.py:526
  18.6 628.1 %all-gather.9.cloned.1.call-start = ((), (), s32[]{:S(2)}) async-start(), calls=%async_computation.6 | async-start | bytes 4456448 | tf_op jit(solution)/shard_map/all_gather | solution.py:583
  130.8 38.2 %collective-permute-start = (bf16[128,2048]{1,0:T(8,128)(2,1)}, bf16[128,2048]{1,0:T(8,128)(2,1)}, u32[]{:S(2)}, u32[]{:S(2)}) collective-permute-start(bf16[128,2048]{1,0:T(8,128)(2,1)} %get-tuple-element.81), channel_id=1, source_target_pairs={{0,1},{1,2},{2,3},{3,4},{4,5},{5,6},{6,7},{7,0},{8,9},{9,10},{10,1... | collective-permute-start | bytes 1572872 | tf_op jit(solution)/shard_map/ppermute | solution.py:440
  131.5 39.7 %collective-permute-start.1 = (bf16[128,2048]{1,0:T(8,128)(2,1)}, bf16[128,2048]{1,0:T(8,128)(2,1)}, u32[]{:S(2)}, u32[]{:S(2)}) collective-permute-start(bf16[128,2048]{1,0:T(8,128)(2,1)} %get-tuple-element.82), channel_id=1, source_target_pairs={{0,2},{1,3},{2,4},{3,5},{4,6},{5,7},{6,0},{7,1},{8,10},{9,11},{10,... | collective-permute-start | bytes 1572872 | tf_op jit(solution)/shard_map/ppermute | solution.py:440
  131.5 61.2 %collective-permute-start.2 = (bf16[128,2048]{1,0:T(8,128)(2,1)}, bf16[128,2048]{1,0:T(8,128)(2,1)}, u32[]{:S(2)}, u32[]{:S(2)}) collective-permute-start(bf16[128,2048]{1,0:T(8,128)(2,1)} %get-tuple-element.83), channel_id=1, source_target_pairs={{0,3},{1,4},{2,5},{3,6},{4,7},{5,0},{6,1},{7,2},{8,11},{9,12},{10,... | collective-permute-start | bytes 1572872 | tf_op jit(solution)/shard_map/ppermute | solution.py:440
  133.4 59.4 %collective-permute-start.3 = (bf16[128,2048]{1,0:T(8,128)(2,1)}, bf16[128,2048]{1,0:T(8,128)(2,1)}, u32[]{:S(2)}, u32[]{:S(2)}) collective-permute-start(bf16[128,2048]{1,0:T(8,128)(2,1)} %get-tuple-element.84), channel_id=1, source_target_pairs={{0,4},{1,5},{2,6},{3,7},{4,0},{5,1},{6,2},{7,3},{8,12},{9,13},{10,... | collective-permute-start | bytes 1572872 | tf_op jit(solution)/shard_map/ppermute | solution.py:440
  135.5 57.2 %collective-permute-start.4 = (bf16[128,2048]{1,0:T(8,128)(2,1)}, bf16[128,2048]{1,0:T(8,128)(2,1)}, u32[]{:S(2)}, u32[]{:S(2)}) collective-permute-start(bf16[128,2048]{1,0:T(8,128)(2,1)} %get-tuple-element.85), channel_id=1, source_target_pairs={{0,5},{1,6},{2,7},{3,0},{4,1},{5,2},{6,3},{7,4},{8,13},{9,14},{10,... | collective-permute-start | bytes 1572872 | tf_op jit(solution)/shard_map/ppermute | solution.py:440
  169.1 23.7 %collective-permute-start.5 = (bf16[128,2048]{1,0:T(8,128)(2,1)}, bf16[128,2048]{1,0:T(8,128)(2,1)}, u32[]{:S(2)}, u32[]{:S(2)}) collective-permute-start(bf16[128,2048]{1,0:T(8,128)(2,1)} %get-tuple-element.86), channel_id=1, source_target_pairs={{0,6},{1,7},{2,0},{3,1},{4,2},{5,3},{6,4},{7,5},{8,14},{9,15},{10,... | collective-permute-start | bytes 1572872 | tf_op jit(solution)/shard_map/ppermute | solution.py:440
  171.3 27.6 %collective-permute-start.6 = (bf16[128,2048]{1,0:T(8,128)(2,1)}, bf16[128,2048]{1,0:T(8,128)(2,1)}, u32[]{:S(2)}, u32[]{:S(2)}) collective-permute-start(bf16[128,2048]{1,0:T(8,128)(2,1)} %get-tuple-element.87), channel_id=1, source_target_pairs={{0,7},{1,0},{2,1},{3,2},{4,3},{5,4},{6,5},{7,6},{8,15},{9,8},{10,9... | collective-permute-start | bytes 1572872 | tf_op jit(solution)/shard_map/ppermute | solution.py:440
  201.8 444.9 %all-gather.11.cloned.1.call-start = ((), (), s32[]{:S(2)}) async-start(), calls=%async_computation.7 | async-start | bytes 4456448 | tf_op jit(solution)/shard_map/all_gather | solution.py:583
  641.6 144.7 %collective-permute-start.9 = (bf16[128,2048]{1,0:T(8,128)(2,1)}, bf16[128,2048]{1,0:T(8,128)(2,1)}, u32[]{:S(2)}, u32[]{:S(2)}) collective-permute-start(bf16[128,2048]{1,0:T(8,128)(2,1)} %get-tuple-element.102), channel_id=1, source_target_pairs={{0,1},{1,2},{2,3},{3,4},{4,5},{5,6},{6,7},{7,0},{8,9},{9,10},{10,1... | collective-permute-start | bytes 1572872 | tf_op jit(solution)/shard_map/ppermute | solution.py:440
  642.2 145.3 %collective-permute-start.10 = (bf16[128,2048]{1,0:T(8,128)(2,1)}, bf16[128,2048]{1,0:T(8,128)(2,1)}, u32[]{:S(2)}, u32[]{:S(2)}) collective-permute-start(bf16[128,2048]{1,0:T(8,128)(2,1)} %get-tuple-element.103), channel_id=1, source_target_pairs={{0,2},{1,3},{2,4},{3,5},{4,6},{5,7},{6,0},{7,1},{8,10},{9,11},{10,... | collective-permute-start | bytes 1572872 | tf_op jit(solution)/shard_map/ppermute | solution.py:440
  642.8 146.0 %collective-permute-start.11 = (bf16[128,2048]{1,0:T(8,128)(2,1)}, bf16[128,2048]{1,0:T(8,128)(2,1)}, u32[]{:S(2)}, u32[]{:S(2)}) collective-permute-start(bf16[128,2048]{1,0:T(8,128)(2,1)} %get-tuple-element.104), channel_id=1, source_target_pairs={{0,3},{1,4},{2,5},{3,6},{4,7},{5,0},{6,1},{7,2},{8,11},{9,12},{10,... | collective-permute-start | bytes 1572872 | tf_op jit(solution)/shard_map/ppermute | solution.py:440
  644.0 196.2 %collective-permute-start.13 = (bf16[128,2048]{1,0:T(8,128)(2,1)}, bf16[128,2048]{1,0:T(8,128)(2,1)}, u32[]{:S(2)}, u32[]{:S(2)}) collective-permute-start(bf16[128,2048]{1,0:T(8,128)(2,1)} %get-tuple-element.110), channel_id=1, source_target_pairs={{0,4},{1,5},{2,6},{3,7},{4,0},{5,1},{6,2},{7,3},{8,12},{9,13},{10,... | collective-permute-start | bytes 1572872 | tf_op jit(solution)/shard_map/ppermute | solution.py:440
  648.9 89.6 %all-to-all-start.1 = ((bf16[4,128,512]{2,1,0:T(8,128)(2,1)}), bf16[4,128,512]{2,1,0:T(8,128)(2,1)S(1)}, u32[]{:S(2)}, u32[]{:S(2)}) async-start(bf16[4,128,512]{2,1,0:T(8,128)(2,1)} %bitcast.35), calls=%async_computation.1 | async-start | bytes 1048576 | tf_op jit(solution)/shard_map/all_to_all | solution.py:605
  729.4 127.6 %all-gather.13.cloned.1.call-start = ((), (), s32[]{:S(2)}) async-start(), calls=%async_computation.8 | async-start | bytes 1114112 | tf_op jit(solution)/shard_map/all_gather | solution.py:613
  786.3 54.0 %collective-permute-start.14 = (bf16[128,2048]{1,0:T(8,128)(2,1)}, bf16[128,2048]{1,0:T(8,128)(2,1)}, u32[]{:S(2)}, u32[]{:S(2)}) collective-permute-start(bf16[128,2048]{1,0:T(8,128)(2,1)} %get-tuple-element.111), channel_id=1, source_target_pairs={{0,5},{1,6},{2,7},{3,0},{4,1},{5,2},{6,3},{7,4},{8,13},{9,14},{10,... | collective-permute-start | bytes 1572872 | tf_op jit(solution)/shard_map/ppermute | solution.py:440
  787.5 52.8 %collective-permute-start.15 = (bf16[128,2048]{1,0:T(8,128)(2,1)}, bf16[128,2048]{1,0:T(8,128)(2,1)}, u32[]{:S(2)}, u32[]{:S(2)}) collective-permute-start(bf16[128,2048]{1,0:T(8,128)(2,1)} %get-tuple-element.112), channel_id=1, source_target_pairs={{0,6},{1,7},{2,0},{3,1},{4,2},{5,3},{6,4},{7,5},{8,14},{9,15},{10,... | collective-permute-start | bytes 1572872 | tf_op jit(solution)/shard_map/ppermute | solution.py:440
  788.8 51.4 %collective-permute-start.16 = (bf16[128,2048]{1,0:T(8,128)(2,1)}, bf16[128,2048]{1,0:T(8,128)(2,1)}, u32[]{:S(2)}, u32[]{:S(2)}) collective-permute-start(bf16[128,2048]{1,0:T(8,128)(2,1)} %get-tuple-element.113), channel_id=1, source_target_pairs={{0,7},{1,0},{2,1},{3,2},{4,3},{5,4},{6,5},{7,6},{8,15},{9,8},{10,9... | collective-permute-start | bytes 1572872 | tf_op jit(solution)/shard_map/ppermute | solution.py:440
  802.4 51.4 %all-to-all-start.2 = ((bf16[16,64,640]{2,1,0:T(8,128)(2,1)}), bf16[16,64,640]{2,1,0:T(8,128)(2,1)}, u32[]{:S(2)}, u32[]{:S(2)}) async-start(bf16[16,64,640]{2,1,0:T(8,128)(2,1)} %pad_maximum_fusion), calls=%async_computation.2 | async-start | bytes 2621440 | tf_op jit(solution)/shard_map/all_to_all | solution.py:663
  863.0 47.8 %all-to-all-start.3 = ((bf16[32,2,4864]{2,1,0:T(2,128)(2,1)}), bf16[32,2,4864]{2,1,0:T(2,128)(2,1)}, u32[]{:S(2)}, u32[]{:S(2)}) async-start(bf16[32,2,4864]{2,1,0:T(2,128)(2,1)} %reshape.675), calls=%async_computation.3 | async-start | bytes 1245184 | tf_op jit(solution)/shard_map/all_to_all | solution.py:689
  882.3 28.3 %collective-permute-start.17 = (bf16[4352,128]{1,0:T(8,128)(2,1)}, bf16[4352,128]{1,0:T(8,128)(2,1)S(1)}, u32[]{:S(2)}, u32[]{:S(2)}) collective-permute-start(bf16[4352,128]{1,0:T(8,128)(2,1)} %pad_maximum_fusion.2), channel_id=1, source_target_pairs={{0,16},{16,0},{1,17},{17,1},{2,18},{18,2},{3,19},{19,3},{4,20},{20... | collective-permute-start | bytes 3342344 | tf_op jit(solution)/shard_map/ppermute | solution.py:716
  918.8 13.5 %all-to-all-start.4 = ((f32[32,1,512]{2,1,0:T(1,128)}), f32[32,1,512]{2,1,0:T(1,128)S(1)}, u32[]{:S(2)}, u32[]{:S(2)}) async-start(f32[32,1,512]{2,1,0:T(1,128)} %broadcast_in_dim.302), calls=%async_computation.4 | async-start | bytes 131072 | tf_op jit(solution)/shard_map/all_to_all | solution.py:720
  (75 other events, 2724.7 us)
Sparse Core Ops, SparseCore 0:
  11.3 119.4 all-gather.6
  201.9 90.5 all-gather.8
  294.8 67.2 all-gather.10
  752.0 38.6 all-gather.12

commit v7 on v6

--- a/solution.py
+++ b/solution.py
@@ -73,19 +73,26 @@
     cell = cells.shape[2]
     pipe = lax.axis_index("pipe")
     direction = lax.axis_index("dir")
-    me = lax.axis_index("dp")
-    first = pipe == 1
-    second = pipe == 0
-    partner = (1 - pipe, direction, me)
+    place = lax.axis_index("dp")
+    wing = n // 2
+    first = place >= wing
+    second = place < wing
+    me = pipe * wing + lax.rem(place, wing)
+    base = place - lax.rem(place, wing)
+    partner = (pipe, direction, lax.rem(place + wing, n))
 
     def peer(off):
         if n & (n - 1):
             return lax.rem(me + off, n)
         return me ^ off
 
+    def at_peer(off):
+        rank = peer(off)
+        return (lax.div(rank, wing), direction, base + lax.rem(rank, wing))
+
     barrier = pltpu.get_barrier_semaphore()
     over(n, lambda off: pl.semaphore_signal(
-        barrier, inc=1, device_id=(pipe, direction, peer(off)), device_id_type=MESH))
+        barrier, inc=1, device_id=at_peer(off), device_id_type=MESH))
     pl.semaphore_signal(barrier, inc=1, device_id=partner, device_id_type=MESH)
 
     each = 2 * width // n
@@ -109,23 +116,23 @@
         return pltpu.make_async_remote_copy(
             src_ref=buf.at[slot, me], dst_ref=buf.at[slot, me],
             send_sem=out.at[off], recv_sem=into.at[off],
-            device_id=(pipe, direction, peer(off)), device_id_type=MESH)
+            device_id=at_peer(off), device_id_type=MESH)
 
     def rs_copy(off):
         return pltpu.make_async_remote_copy(
             src_ref=stage.at[peer(off)], dst_ref=inbox.at[me],
             send_sem=rs_send.at[off], recv_sem=rs_recv.at[off],
-            device_id=(pipe, direction, peer(off)), device_id_type=MESH)
+            device_id=at_peer(off), device_id_type=MESH)
 
     def dx_copy(slot, off):
         return pltpu.make_async_remote_copy(
             src_ref=stage2.at[slot, peer(off)], dst_ref=inbox2.at[slot, me],
             send_sem=dx_send.at[slot, off], recv_sem=dx_recv.at[slot, off],
-            device_id=(pipe, direction, peer(off)), device_id_type=MESH)
+            device_id=at_peer(off), device_id_type=MESH)
 
     def x_copy(t):
         return pltpu.make_async_remote_copy(
-            src_ref=hbuf.at[t + 1], dst_ref=xbuf.at[t],
+            src_ref=hbuf.at[t + 1, me], dst_ref=xbuf.at[t, me],
             send_sem=x_send.at[t], recv_sem=x_recv.at[t],
             device_id=partner, device_id_type=MESH)
 
@@ -139,7 +146,7 @@
         over(n, lambda off: pltpu.make_async_remote_copy(
             src_ref=xbuf.at[t, me], dst_ref=xbuf.at[t, me],
             send_sem=in_send.at[t], recv_sem=in_recv.at[t],
-            device_id=(pipe, direction, peer(off)), device_id_type=MESH).start())
+            device_id=at_peer(off), device_id_type=MESH).start())
 
     def in_wait(sem, t):
         blocks = xbuf.at[t, pl.ds(0, n - 1)]
@@ -149,6 +156,11 @@
     def _():
         in_start(0)
         in_start(1)
+
+    @pl.when(second)
+    def _():
+        x_copy(0).wait_recv()
+        in_start(0)
 
     for load in loads:
         load.wait()
@@ -168,24 +180,13 @@
         over(n, both)
 
     def forward(t, _):
-        @pl.when(second)
-        def _():
-            x_copy(t).wait_recv()
-
-        @pl.when(first)
-        def _():
-            in_wait(in_recv, t)
-
+        in_wait(in_recv, t)
         gscr[...] = jnp.dot(
             xbuf[t].reshape(total, width), w[:width, :], preferred_element_type=F32) + bias[...]
 
         @pl.when(t > 0)
         def _():
             ag_wait(hbuf, t)
-
-            @pl.when(first)
-            def _():
-                x_copy(t - 1).start()
 
         gscr[...] += jnp.dot(
             hbuf[t].reshape(total, width), w[width:, :], preferred_element_type=F32)
@@ -217,11 +218,21 @@
         def _():
             in_start(t + 2)
 
+        @pl.when(second & (t + 1 < steps))
+        def _():
+            x_copy(t + 1).wait_recv()
+            in_start(t + 1)
+
         rs_wait()
         h = 3.0 * jnp.tanh(jnp.sum(inbox[...].astype(F32), axis=0) * (1.0 / 3.0))
         hown[t] = h
         hbuf[t + 1, me] = h.astype(BF)
         over(n, lambda off: ag_copy(hbuf, t + 1, off).start())
+
+        @pl.when(first)
+        def _():
+            x_copy(t).start()
+
         add = jnp.where(second, 1.0, 0.0)
         out_ref[t] = (h + add * xbuf[t, me].astype(F32)).astype(BF)
         return 0
@@ -229,11 +240,11 @@
     lax.fori_loop(0, steps, forward, 0)
     ag_wait(hbuf, steps)
 
+    lax.fori_loop(0, steps, lambda t, _: (in_wait(in_send, t), 0)[1], 0)
+
     @pl.when(first)
     def _():
-        x_copy(steps - 1).start()
         lax.fori_loop(0, steps, lambda t, _: (x_copy(t).wait_send(), 0)[1], 0)
-        lax.fori_loop(0, steps, lambda t, _: (in_wait(in_send, t), 0)[1], 0)
 
     rown[...] = jnp.zeros((rows, width), F32)
     ucell[...] = jnp.zeros((total, cell), F32)
@@ -434,12 +445,23 @@
     )(*blocks)
 
 
-def exchange(blocks):
-    n = len(blocks)
-    return [blocks[0]] + [
-        lax.ppermute(blocks[off], "dp", [(i, (i + off) % n) for i in range(n)])
-        for off in range(1, n)
-    ]
+def rank_pairs(n, off, layers=(0, 1)):
+    wing = n // 2
+    pairs = []
+    for layer in layers:
+        for j in range(n):
+            rank = (j + off) % n
+            pairs.append((layer * n + j, rank // wing * n + layer * wing + rank % wing))
+    return pairs
+
+
+def to_ranks(value, off):
+    return lax.ppermute(value, ("pipe", "dp"), rank_pairs(lax.axis_size("dp"), off))
+
+
+def from_ranks(value, off, layers=(0, 1)):
+    pairs = rank_pairs(lax.axis_size("dp"), -off, layers)
+    return lax.ppermute(value, ("pipe", "dp"), [(there, here) for here, there in pairs])
 
 
 def conv_forward(ids, table_low, conv_low, valid_place):
@@ -548,14 +570,19 @@
     pooled = conv_forward(ids, table_low, conv_low, masks[1])
     features = jax.nn.silu(pooled + conv_bias_own)
     features_low = both_halves(features.astype(BF), blocks)
-    gate_low, gathered, features_low = lax.optimization_barrier(
-        (split_cells(gate_weight[0, 0], n), gathered, features_low)
-    )
-    gate_own = exchange(gate_low)
     bias_own = lax.dynamic_index_in_dim(
         gate_bias[0, 0].reshape(4, n, cell), me, 1, keepdims=False
     ).reshape(1, 4 * cell)
-    cell_low = cell_proj[0, 0].astype(BF)
+    bias_own = to_ranks(bias_own, 0)
+    moved = to_ranks(
+        jnp.concatenate([cell_proj[0, 0].astype(BF), cot.reshape(steps * seqs, width)]), 0
+    )
+    gate_low, gathered, features_low, bias_own, moved = lax.optimization_barrier(
+        (split_cells(gate_weight[0, 0], n), gathered, features_low, bias_own, moved)
+    )
+    cell_low = moved[:cell]
+    cot = moved[cell:].reshape(steps, seqs, width)
+    gate_own = [to_ranks(block, off) for off, block in enumerate(gate_low)]
     highway_half = gathered[:, :FILTERS]
     proj_full = gathered[:, FILTERS:].reshape(pieces, proj_rows, holders, sub)
     proj_full = jnp.transpose(proj_full, (2, 1, 0, 3)).reshape(FILTERS, width)
@@ -589,16 +616,22 @@
         for value in kept_low[:2]
     ]
     inputs = jnp.einsum("rts,rsd->trd", own_order, encoded_own, preferred_element_type=BF)
+    wing = n // 2
+    inputs = lax.ppermute(
+        inputs,
+        ("pipe", "dp"),
+        [(k, wing + k) for k in range(wing)] + [(n + k, n + k) for k in range(wing, n)],
+    )
 
     out_own, dx_own, grad_bias, grad_cell, *grad_gate = lstm_call(
         n, inputs, gate_own, bias_own, cell_low, cell_low.T, cot
     )
-    grad_gate = exchange(grad_gate)
+    dx_own = from_ranks(dx_own.astype(BF), 0, (1,))
+    grad_gate = [from_ranks(block, off) for off, block in enumerate(grad_gate)]
     dx_own, kept_all = lax.optimization_barrier((dx_own, kept_all))
-    activations = jnp.einsum("rts,srd->rtd", own_order, out_own, preferred_element_type=BF)
 
     grad_stored = jnp.einsum(
-        "rts,srd->rtd", own_order, dx_own.astype(BF), preferred_element_type=F32
+        "rts,srd->rtd", own_order, dx_own, preferred_element_type=F32
     )
     grad_stored = jnp.where(pipe == 1, grad_stored, 0.0).astype(BF)
     grad_stored = grad_stored.reshape(1, -1, group_tokens, width)
@@ -642,7 +675,7 @@
             group_tokens, half
         )
     grad_before = grad_features * silu_slope(pooled + conv_bias_own)
-    grad_before, grad_gate[1:4] = lax.optimization_barrier((grad_before, grad_gate[1:4]))
+    grad_before, grad_gate[1:5] = lax.optimization_barrier((grad_before, grad_gate[1:5]))
     grad_conv, grad_table = conv_backward(ids, table_low, conv_low, masks, grad_before)
 
     def spread(value):
@@ -672,9 +705,11 @@
     flat = jnp.concatenate([value.reshape(-1) for value in small])
     share = -(-flat.shape[0] // (everyone * 128)) * 128
     flat = jnp.pad(flat, (0, share * everyone - flat.shape[0])).reshape(everyone, share)
-    mine = jnp.arange(n, dtype=jnp.int32)[None, :, None] == me
+    rank = pipe * wing + lax.rem(me, wing)
+    mine = jnp.arange(n, dtype=jnp.int32)[None, :, None] == rank
     bias_parts = jnp.where(mine, grad_bias.reshape(4, 1, cell), 0.0).reshape(1, n, 4 * cell)
-    mine = jnp.arange(everyone // n, dtype=jnp.int32) == lax.axis_index(("pipe", "dir"))
+    layer = lax.div(me, wing) * lax.axis_size("dir") + direction
+    mine = jnp.arange(everyone // n, dtype=jnp.int32) == layer
     bias_parts = jnp.where(mine[:, None, None], bias_parts, 0.0).reshape(everyone, 4 * cell)
     packed = jnp.concatenate(
         [
@@ -687,6 +722,11 @@
         axis=1,
     ).astype(BF)
     summed = jnp.sum(lax.all_to_all(packed, ALL, 0, 0).astype(F32), axis=0)
+    out_own = from_ranks(out_own, 0)
+    grad_cell = from_ranks(grad_cell.astype(BF), 0)
+    summed, out_own, grad_cell = lax.optimization_barrier((summed, out_own, grad_cell))
+    activations = jnp.einsum("rts,srd->rtd", own_order, out_own, preferred_element_type=BF)
+    grad_cell = grad_cell.astype(F32)
     grad_conv = summed[: KMAX * CDIM * cols].reshape(KMAX * CDIM, cols)
     grad_bias = summed[KMAX * CDIM * cols + share :]
     last = pair[:, 4 * sub :].reshape(holders * tokens, 2, cols)

time: 954 us -> 1050 us (1.10)
  Pallas kernels: 430 us -> 319 us
  waiting for transfers between devices: 99.3 us -> 184 us
  starting transfers between devices: 141 us -> 214 us
  blocking collectives: 36.9 us -> 93.3 us
    pallas_call x1, Pallas kernels: 418 us -> 307 us  [lstm_call(): pl.pallas_call(functools.partial(lstm_kernel, n, chunk), out_shape=(sds((...]
    ppermute x14 -> x22, waiting for transfers between devices: 7.94 us -> 91.5 us  [the longest x10 55.5 us: to_ranks(): lax.ppermute(value, ('pipe', 'dp'), rank_pairs(lax.axis_size('dp'), off))]
    ppermute x14 -> x22, starting transfers between devices: 17.6 us -> 87.5 us  [the longest x11 45.6 us: from_ranks(): lax.ppermute(value, ('pipe', 'dp'), [(there, here) for here, there in pai...]
    all_gather x3, blocking collectives: 22.2 us -> 55.6 us  [both_halves(): lax.all_gather(value, 'pipe').reshape(2, tokens, blocks, half // blocks)]
    all_gather x1, blocking collectives: 14.8 us -> 37.7 us  [local(): lax.all_gather(encoded.astype(BF).reshape(quarter, steps, width), ('dir',...]
    all_to_all x1, waiting for transfers between devices: 13.5 us -> 0.01 us  [local(): lax.all_to_all(pair, ('dir', 'dp'), 0, 0).reshape(holders * tokens, -1)]
    ppermute x1, starting transfers between devices: 0.08 us -> 12.6 us  [local(): came = lax.ppermute(sent, 'pipe', [(0, 1), (1, 0)]).astype(F32)]
    all_gather x1, waiting for transfers between devices: 55.6 us -> 67.7 us  [local(): lax.all_gather(jnp.concatenate([mine, proj_blocks], axis=1).astype(BF), (...]
  transfers between devices with their start and end apart: 27 -> 35, of which waited for: 7 -> 10; matrix products, arithmetic and copies ran while one was open for 20% -> 18% of each run, Pallas kernels for 46% -> 31%
where the time goes in v7:
time: 1050 us; the launch traced here: 1030 us
  Pallas kernels  319 us (30%)
  starting transfers between devices  214 us (20%)
  waiting for transfers between devices  184 us (18%)
  blocking collectives  93.3 us (9%)
  local copies, waits for them, and re-layouts  86.2 us (8%)
  matrix products  65.3 us (6%)
  other arithmetic  56.8 us (5%)
  between operations  16 us (2%)
    pallas_call x1, Pallas kernels, lstm_call(): pl.pallas_call(functools.partial(lstm_kernel, n, chunk), out_shape=(sds((...  307 us
    all_to_all x1, starting transfers between devices, local(): lax.all_to_all(jnp.concatenate([grad_stored, grad_stored]).reshape(-1, gr...  78.5 us
    all_gather x1, waiting for transfers between devices, local(): lax.all_gather(jnp.concatenate([mine, proj_blocks], axis=1).astype(BF), (...  67.7 us
    all_gather x3, blocking collectives, both_halves(): lax.all_gather(value, 'pipe').reshape(2, tokens, blocks, half // blocks)  55.6 us
    ppermute x10, waiting for transfers between devices, to_ranks(): lax.ppermute(value, ('pipe', 'dp'), rank_pairs(lax.axis_size('dp'), off))  55.5 us
    ppermute x11, starting transfers between devices, from_ranks(): lax.ppermute(value, ('pipe', 'dp'), [(there, here) for here, there in pai...  45.6 us
    ppermute x10, starting transfers between devices, to_ranks(): lax.ppermute(value, ('pipe', 'dp'), rank_pairs(lax.axis_size('dp'), off))  40.5 us
    all_gather x1, blocking collectives, local(): lax.all_gather(encoded.astype(BF).reshape(quarter, steps, width), ('dir',...  37.7 us
  transfers between devices with their start and end apart: 35, of which 10 were waited for; matrix products, arithmetic and copies ran while one was open for 18% of the time, Pallas kernels for 31%

profile of v7, /device:TPU:3, one launch (start us, length us, event | category | flops | bytes accessed | tf_op | source)
XLA Modules:
  0.0 1034.3 jit_solution(3049529319365474052)
XLA Ops:
  29.9 12.1 %gather_fusion = bf16[6400,16]{1,0:T(8,128)(2,1)S(1)} fusion(bf16[262,16]{1,0:T(8,128)(2,1)S(1)} %copy.242, s32[7168]{0:T(1024)S(1)} %pad_clamp_fusion), kind=kCustom, calls=%fused_computation.clone | custom fusion | bytes 435200 | tf_op jit(solution)/shard_map/jit(_take)/gather | solution.py:49
  51.1 11.2 %select_reduce_fusion = (f32[128,1024]{1,0:T(8,128)S(1)}, f32[128,50,1024]{2,0,1:T(8,128)}) fusion(pred[50,1024]{1,0:T(8,128)(4,1)S(1)} %iota_compare_fusion.6, bf16[128,50,112]{0,2,1:T(8,128)(2,1)S(1)} %slice_dynamic-update-slice_fusion, s32[1024]{0:T(1024)S(1)} %add_bitcast_fusion, s32[112]{0:T(128)S(1)} %and_select_fusion, ...), kind=kOutput, calls=%fused_computation.5 | convolution fusion | flops 1481785344 | bytes 28463620 | tf_op jit(solution)/shard_map/bpk,kf->bpf/dot_general | solution.py:51
  62.4 14.8 %fusion = (f32[128,1024]{1,0:T(8,128)}, f32[128,1024]{1,0:T(8,128)S(1)}) fusion(f32[128,50,1024]{2,0,1:T(8,128)} %get-tuple-element.238, f32[128,1024]{1,0:T(8,128)S(1)} %get-tuple-element.237, pred[50,1024]{1,0:T(8,128)(4,1)S(1)} %iota_compare_fusion.6, f32[128,1024]{1,0:T(8,128)S(1)} %is-finite_select_fusion.1), kind=kLoop, calls=%fused_computation.4 | loop fusion | flops 32505856 | bytes 28362752 | tf_op jit(solution)/shard_map/reduce_sum | solution.py:487
  77.4 15.4 %all_gather.32 = bf16[2,128,1024]{2,1,0:T(8,128)(2,1)S(1)} all-gather(bf16[1,128,1024]{2,1,0:T(8,128)(2,1)S(1)} %multiply_convert_fusion.5), channel_id=1, replica_groups=mesh['pipe'=2,'dir'=2,'dp'=8] {'pipe'}, dimensions={0}, use_global_device_ids=true | all-gather | bytes 786432 | tf_op jit(solution)/shard_map/all_gather | solution.py:480
  93.2 67.7 %all-gather.7.cloned.1.call-done = bf16[2,2304,2048]{2,1,0:T(8,128)(2,1)} async-done(((bf16[2,2304,128]{2,1,0:T(8,128)(2,1)}), bf16[2,2304,2048]{2,1,0:T(8,128)(2,1)}) %all-gather.7.cloned.1.call-update) | async-done | bytes 18874384 | tf_op jit(solution)/shard_map/all_gather | solution.py:545
  176.9 31.8 %all-gather = bf16[256,1024]{1,0:T(8,128)(2,1)S(1)} all-gather(bf16[128,1024]{1,0:T(8,128)(2,1)S(1)} %get-tuple-element.212), channel_id=2, replica_groups=mesh['pipe'=2,'dir'=2,'dp'=8] {'pipe'}, dimensions={0}, use_global_device_ids=true | all-gather | bytes 786432 | tf_op jit(solution)/shard_map/all_gather | solution.py:480
  215.1 8.4 all-gather.1
  234.4 19.3 %collective-permute-start.7 = (bf16[128,2048]{1,0:T(8,128)(2,1)}, bf16[128,2048]{1,0:T(8,128)(2,1)}, u32[]{:S(2)}, u32[]{:S(2)}) collective-permute-start(bf16[128,2048]{1,0:T(8,128)(2,1)} %get-tuple-element.91), channel_id=1, source_target_pairs={{0,17},{1,18},{2,19},{3,0},{4,1},{5,2},{6,3},{7,16},{16,21},{17,22... | collective-permute-start | bytes 1572872 | tf_op jit(solution)/shard_map/ppermute | solution.py:459
  259.5 37.7 %all_gather.37 = bf16[16,16,512]{2,1,0:T(8,128)(2,1)S(1)} all-gather(bf16[4,16,512]{2,1,0:T(8,128)(2,1)S(1)} %bitcast.303), channel_id=1, replica_groups=mesh['pipe'=2,'dir'=2,'dp'=8] {'dir','pipe'}, dimensions={0}, use_global_device_ids=true | all-gather | bytes 327680 | tf_op jit(solution)/shard_map/all_gather | solution.py:605
  297.2 52.4 %collective-permute-done.9.refs_7_ = bf16[128,2048]{1,0:T(8,128)(2,1)} collective-permute-done((bf16[128,2048]{1,0:T(8,128)(2,1)}, bf16[128,2048]{1,0:T(8,128)(2,1)}, u32[]{:S(2)}, u32[]{:S(2)}) %collective-permute-start.9) | collective-permute-done | bytes 524320 | tf_op jit(solution)/shard_map/ppermute | solution.py:459
  367.1 306.9 %relay_lstm.1 = (bf16[16,16,512]{2,1,0:T(8,128)(2,1)}, f32[16,16,512]{2,1,0:T(8,128)}, f32[1,2048]{1,0:T(1,128)}, f32[512,512]{1,0:T(8,128)}, bf16[128,2048]{1,0...) custom-call(bf16[16,16,512]{2,1,0:T(8,128)(2,1)} %collective-permute, ...), custom_call_target="tpu_custom_call" | custom-call | flops 299999985664 | bytes 67108864 | tf_op jit(solution)/shard_map/relay_lstm/pallas_call | solution.py:368
  682.4 15.1 %collective-permute-start.14 = (bf16[128,2048]{1,0:T(8,128)(2,1)}, bf16[128,2048]{1,0:T(8,128)(2,1)}, u32[]{:S(2)}, u32[]{:S(2)}) collective-permute-start(bf16[128,2048]{1,0:T(8,128)(2,1)} %get-tuple-element.109), channel_id=1, source_target_pairs={{19,0},{0,1},{1,2},{2,3},{3,4},{16,5},{17,6},{18,7},{23,16},{4,17}... | collective-permute-start | bytes 1572872 | tf_op jit(solution)/shard_map/ppermute | solution.py:464
  701.9 78.5 %all-to-all-start.1 = ((bf16[4,128,512]{2,1,0:T(8,128)(2,1)}), bf16[4,128,512]{2,1,0:T(8,128)(2,1)S(1)}, u32[]{:S(2)}, u32[]{:S(2)}) async-start(bf16[4,128,512]{2,1,0:T(8,128)(2,1)} %bitcast.36), calls=%async_computation.1 | async-start | bytes 1048576 | tf_op jit(solution)/shard_map/all_to_all | solution.py:638
  781.3 7.8 all-to-all-done.1
  791.4 6.3 fusion.1
  809.5 7.2 fusion.5
  833.1 10.4 %collective-permute-start.23 = (bf16[16,16,512]{2,1,0:T(8,128)(2,1)}, bf16[16,16,512]{2,1,0:T(8,128)(2,1)}, u32[]{:S(2)}, u32[]{:S(2)}) collective-permute-start(bf16[16,16,512]{2,1,0:T(8,128)(2,1)} %get-tuple-element.124), channel_id=1, source_target_pairs={{0,0},{1,1},{2,2},{3,3},{16,4},{17,5},{18,6},{19,7},{4,16},{5,17},... | collective-permute-start | bytes 786440 | tf_op jit(solution)/shard_map/ppermute | solution.py:464
  851.5 6.8 collective-permute-start.22
  865.4 16.4 %all-to-all-start.2 = ((bf16[16,64,640]{2,1,0:T(8,128)(2,1)}), bf16[16,64,640]{2,1,0:T(8,128)(2,1)}, u32[]{:S(2)}, u32[]{:S(2)}) async-start(bf16[16,64,640]{2,1,0:T(8,128)(2,1)} %pad_maximum_fusion), calls=%async_computation.2 | async-start | bytes 2621440 | tf_op jit(solution)/shard_map/all_to_all | solution.py:696
  881.9 11.7 %multiply_convert_fusion = bf16[128,50,1024]{2,0,1:T(8,128)(2,1)S(1)} fusion(f32[128,50,1024]{2,0,1:T(8,128)} %get-tuple-element.238, f32[128,1024]{1,0:T(8,128)S(1)} %copy-done.19, f32[128,1024]{1,0:T(8,128)S(1)} %copy-done.4, f32[128,1024]{1,0:T(8,128)S(1)} %fusion.41, pred[50,1024]{1,0:T(8,128)(4,1)S(1)} %copy-done.39), kind=kLoop, calls=%fused_computation.1 | loop fusion | flops 32768000 | bytes 40945664 | tf_op jit(solution)/shard_map/convert_element_type | solution.py:488
  917.6 32.7 %collective-permute-done.22.refs_7_ = bf16[128,2048]{1,0:T(8,128)(2,1)} collective-permute-done((bf16[128,2048]{1,0:T(8,128)(2,1)}, bf16[128,2048]{1,0:T(8,128)(2,1)}, u32[]{:S(2)}, u32[]{:S(2)}) %collective-permute-start.22) | collective-permute-done | bytes 524320 | tf_op jit(solution)/shard_map/ppermute | solution.py:464
  964.0 12.6 %collective-permute-start.25 = (bf16[4352,128]{1,0:T(8,128)(2,1)}, bf16[4352,128]{1,0:T(8,128)(2,1)S(1)}, u32[]{:S(2)}, u32[]{:S(2)}) collective-permute-start(bf16[4352,128]{1,0:T(8,128)(2,1)} %pad_maximum_fusion.2), channel_id=1, source_target_pairs={{0,16},{16,0},{1,17},{17,1},{2,18},{18,2},{3,19},{19,3},{4,20},{20... | collective-permute-start | bytes 3342344 | tf_op jit(solution)/shard_map/ppermute | solution.py:756
  996.7 9.1 collective-permute-done.25
  1011.9 6.3 all-to-all-start.4
  (384 shorter events, 219.9 us)
Async XLA Ops:
  7.2 153.7 %all-gather.7.cloned.1.call-start = ((), (), s32[]{:S(2)}) async-start(), calls=%async_computation.5 | async-start | bytes 20054016 | tf_op jit(solution)/shard_map/all_gather | solution.py:545
  12.6 80.6 %collective-permute-start = (f32[1,2048]{1,0:T(1,128)S(1)}, f32[1,2048]{1,0:T(1,128)S(1)}, u32[]{:S(2)}, u32[]{:S(2)}) collective-permute-start(f32[1,2048]{1,0:T(1,128)S(1)} %bitcast.309), channel_id=1, source_target_pairs={{0,0},{1,1},{2,2},{3,3},{4,16},{5,17},{6,18},{7,19},{16,4},{17,5},... | collective-permute-start | bytes 24584 | tf_op jit(solution)/shard_map/ppermute | solution.py:459
  22.4 677.3 %all-gather.9.cloned.1.call-start = ((), (), s32[]{:S(2)}) async-start(), calls=%async_computation.6 | async-start | bytes 4456448 | tf_op jit(solution)/shard_map/all_gather | solution.py:610
  24.4 68.8 %collective-permute-start.1 = (bf16[768,512]{0,1:T(8,128)(2,1)}, bf16[768,512]{0,1:T(8,128)(2,1)}, u32[]{:S(2)}, u32[]{:S(2)}) collective-permute-start(bf16[768,512]{0,1:T(8,128)(2,1)} %pad_maximum_fusion.3), channel_id=1, source_target_pairs={{0,0},{1,1},{2,2},{3,3},{4,16},{5,17},{6,18},{7,19},{16,4},{17,5},... | collective-permute-start | bytes 2359304 | tf_op jit(solution)/shard_map/ppermute | solution.py:459
  160.9 73.5 %collective-permute-start.2 = (bf16[128,2048]{1,0:T(8,128)(2,1)}, bf16[128,2048]{1,0:T(8,128)(2,1)}, u32[]{:S(2)}, u32[]{:S(2)}) collective-permute-start(bf16[128,2048]{1,0:T(8,128)(2,1)} %get-tuple-element.86), channel_id=1, source_target_pairs={{0,0},{1,1},{2,2},{3,3},{4,16},{5,17},{6,18},{7,19},{16,4},{17,5},... | collective-permute-start | bytes 1572872 | tf_op jit(solution)/shard_map/ppermute | solution.py:459
  164.8 88.9 %collective-permute-start.3 = (bf16[128,2048]{1,0:T(8,128)(2,1)}, bf16[128,2048]{1,0:T(8,128)(2,1)}, u32[]{:S(2)}, u32[]{:S(2)}) collective-permute-start(bf16[128,2048]{1,0:T(8,128)(2,1)} %get-tuple-element.87), channel_id=1, source_target_pairs={{0,1},{1,2},{2,3},{3,16},{4,17},{5,18},{6,19},{7,0},{16,5},{17,6},... | collective-permute-start | bytes 1572872 | tf_op jit(solution)/shard_map/ppermute | solution.py:459
  167.0 86.7 %collective-permute-start.4 = (bf16[128,2048]{1,0:T(8,128)(2,1)}, bf16[128,2048]{1,0:T(8,128)(2,1)}, u32[]{:S(2)}, u32[]{:S(2)}) collective-permute-start(bf16[128,2048]{1,0:T(8,128)(2,1)} %get-tuple-element.88), channel_id=1, source_target_pairs={{0,2},{1,3},{2,16},{3,17},{4,18},{5,19},{6,0},{7,1},{16,6},{17,7},... | collective-permute-start | bytes 1572872 | tf_op jit(solution)/shard_map/ppermute | solution.py:459
  168.2 128.9 %collective-permute-start.5 = (bf16[128,2048]{1,0:T(8,128)(2,1)}, bf16[128,2048]{1,0:T(8,128)(2,1)}, u32[]{:S(2)}, u32[]{:S(2)}) collective-permute-start(bf16[128,2048]{1,0:T(8,128)(2,1)} %get-tuple-element.89), channel_id=1, source_target_pairs={{0,3},{1,16},{2,17},{3,18},{4,19},{5,0},{6,1},{7,2},{16,7},{17,20}... | collective-permute-start | bytes 1572872 | tf_op jit(solution)/shard_map/ppermute | solution.py:459
  171.6 125.5 %collective-permute-start.6 = (bf16[128,2048]{1,0:T(8,128)(2,1)}, bf16[128,2048]{1,0:T(8,128)(2,1)}, u32[]{:S(2)}, u32[]{:S(2)}) collective-permute-start(bf16[128,2048]{1,0:T(8,128)(2,1)} %get-tuple-element.90), channel_id=1, source_target_pairs={{0,16},{1,17},{2,18},{3,19},{4,0},{5,1},{6,2},{7,3},{16,20},{17,21... | collective-permute-start | bytes 1572872 | tf_op jit(solution)/shard_map/ppermute | solution.py:459
  253.7 95.9 %collective-permute-start.9 = (bf16[128,2048]{1,0:T(8,128)(2,1)}, bf16[128,2048]{1,0:T(8,128)(2,1)}, u32[]{:S(2)}, u32[]{:S(2)}) collective-permute-start(bf16[128,2048]{1,0:T(8,128)(2,1)} %get-tuple-element.93), channel_id=1, source_target_pairs={{0,19},{1,0},{2,1},{3,2},{4,3},{5,16},{6,17},{7,18},{16,23},{17,4}... | collective-permute-start | bytes 1572872 | tf_op jit(solution)/shard_map/ppermute | solution.py:459
  352.5 347.2 %all-gather.11.cloned.1.call-start = ((), (), s32[]{:S(2)}) async-start(), calls=%async_computation.7 | async-start | bytes 4456448 | tf_op jit(solution)/shard_map/all_gather | solution.py:610
  682.4 150.7 %collective-permute-start.14 = (bf16[128,2048]{1,0:T(8,128)(2,1)}, bf16[128,2048]{1,0:T(8,128)(2,1)}, u32[]{:S(2)}, u32[]{:S(2)}) collective-permute-start(bf16[128,2048]{1,0:T(8,128)(2,1)} %get-tuple-element.109), channel_id=1, source_target_pairs={{19,0},{0,1},{1,2},{2,3},{3,4},{16,5},{17,6},{18,7},{23,16},{4,17}... | collective-permute-start | bytes 1572872 | tf_op jit(solution)/shard_map/ppermute | solution.py:464
  697.4 146.0 %collective-permute-start.15 = (bf16[128,2048]{1,0:T(8,128)(2,1)}, bf16[128,2048]{1,0:T(8,128)(2,1)}, u32[]{:S(2)}, u32[]{:S(2)}) collective-permute-start(bf16[128,2048]{1,0:T(8,128)(2,1)} %get-tuple-element.110), channel_id=1, source_target_pairs={{18,0},{19,1},{0,2},{1,3},{2,4},{3,5},{16,6},{17,7},{22,16},{23,17... | collective-permute-start | bytes 1572872 | tf_op jit(solution)/shard_map/ppermute | solution.py:464
  697.4 148.0 %collective-permute-start.16 = (bf16[128,2048]{1,0:T(8,128)(2,1)}, bf16[128,2048]{1,0:T(8,128)(2,1)}, u32[]{:S(2)}, u32[]{:S(2)}) collective-permute-start(bf16[128,2048]{1,0:T(8,128)(2,1)} %get-tuple-element.111), channel_id=1, source_target_pairs={{17,0},{18,1},{19,2},{0,3},{1,4},{2,5},{3,6},{16,7},{21,16},{22,17... | collective-permute-start | bytes 1572872 | tf_op jit(solution)/shard_map/ppermute | solution.py:464
  699.7 145.8 %collective-permute-start.17 = (bf16[128,2048]{1,0:T(8,128)(2,1)}, bf16[128,2048]{1,0:T(8,128)(2,1)}, u32[]{:S(2)}, u32[]{:S(2)}) collective-permute-start(bf16[128,2048]{1,0:T(8,128)(2,1)} %get-tuple-element.112), channel_id=1, source_target_pairs={{16,0},{17,1},{18,2},{19,3},{0,4},{1,5},{2,6},{3,7},{20,16},{21,17... | collective-permute-start | bytes 1572872 | tf_op jit(solution)/shard_map/ppermute | solution.py:464
  701.9 87.3 %all-to-all-start.1 = ((bf16[4,128,512]{2,1,0:T(8,128)(2,1)}), bf16[4,128,512]{2,1,0:T(8,128)(2,1)S(1)}, u32[]{:S(2)}, u32[]{:S(2)}) async-start(bf16[4,128,512]{2,1,0:T(8,128)(2,1)} %bitcast.36), calls=%async_computation.1 | async-start | bytes 1048576 | tf_op jit(solution)/shard_map/all_to_all | solution.py:638
  780.3 174.1 %all-gather.13.cloned.1.call-start = ((), (), s32[]{:S(2)}) async-start(), calls=%async_computation.8 | async-start | bytes 1114112 | tf_op jit(solution)/shard_map/all_gather | solution.py:646
  833.1 176.8 %collective-permute-start.23 = (bf16[16,16,512]{2,1,0:T(8,128)(2,1)}, bf16[16,16,512]{2,1,0:T(8,128)(2,1)}, u32[]{:S(2)}, u32[]{:S(2)}) collective-permute-start(bf16[16,16,512]{2,1,0:T(8,128)(2,1)} %get-tuple-element.124), channel_id=1, source_target_pairs={{0,0},{1,1},{2,2},{3,3},{16,4},{17,5},{18,6},{19,7},{4,16},{5,17},... | collective-permute-start | bytes 786440 | tf_op jit(solution)/shard_map/ppermute | solution.py:464
  843.5 72.2 %collective-permute-start.19 = (bf16[128,2048]{1,0:T(8,128)(2,1)}, bf16[128,2048]{1,0:T(8,128)(2,1)}, u32[]{:S(2)}, u32[]{:S(2)}) collective-permute-start(bf16[128,2048]{1,0:T(8,128)(2,1)} %get-tuple-element.114), channel_id=1, source_target_pairs={{0,0},{1,1},{2,2},{3,3},{16,4},{17,5},{18,6},{19,7},{4,16},{5,17},... | collective-permute-start | bytes 1572872 | tf_op jit(solution)/shard_map/ppermute | solution.py:464
  845.4 72.2 %collective-permute-start.20 = (bf16[128,2048]{1,0:T(8,128)(2,1)}, bf16[128,2048]{1,0:T(8,128)(2,1)}, u32[]{:S(2)}, u32[]{:S(2)}) collective-permute-start(bf16[128,2048]{1,0:T(8,128)(2,1)} %get-tuple-element.119), channel_id=1, source_target_pairs={{3,0},{16,1},{17,2},{18,3},{19,4},{0,5},{1,6},{2,7},{7,16},{20,17}... | collective-permute-start | bytes 1572872 | tf_op jit(solution)/shard_map/ppermute | solution.py:464
  845.5 72.1 %collective-permute-start.21 = (bf16[128,2048]{1,0:T(8,128)(2,1)}, bf16[128,2048]{1,0:T(8,128)(2,1)}, u32[]{:S(2)}, u32[]{:S(2)}) collective-permute-start(bf16[128,2048]{1,0:T(8,128)(2,1)} %get-tuple-element.120), channel_id=1, source_target_pairs={{2,0},{3,1},{16,2},{17,3},{18,4},{19,5},{0,6},{1,7},{6,16},{7,17},... | collective-permute-start | bytes 1572872 | tf_op jit(solution)/shard_map/ppermute | solution.py:464
  851.5 98.8 %collective-permute-start.22 = (bf16[128,2048]{1,0:T(8,128)(2,1)}, bf16[128,2048]{1,0:T(8,128)(2,1)}, u32[]{:S(2)}, u32[]{:S(2)}) collective-permute-start(bf16[128,2048]{1,0:T(8,128)(2,1)} %get-tuple-element.121), channel_id=1, source_target_pairs={{1,0},{2,1},{3,2},{16,3},{17,4},{18,5},{19,6},{0,7},{5,16},{6,17},... | collective-permute-start | bytes 1572872 | tf_op jit(solution)/shard_map/ppermute | solution.py:464
  865.4 84.9 %all-to-all-start.2 = ((bf16[16,64,640]{2,1,0:T(8,128)(2,1)}), bf16[16,64,640]{2,1,0:T(8,128)(2,1)}, u32[]{:S(2)}, u32[]{:S(2)}) async-start(bf16[16,64,640]{2,1,0:T(8,128)(2,1)} %pad_maximum_fusion), calls=%async_computation.2 | async-start | bytes 2621440 | tf_op jit(solution)/shard_map/all_to_all | solution.py:696
  915.7 94.2 %collective-permute-start.24 = (bf16[512,512]{1,0:T(8,128)(2,1)}, bf16[512,512]{1,0:T(8,128)(2,1)}, u32[]{:S(2)}, u32[]{:S(2)}) collective-permute-start(bf16[512,512]{1,0:T(8,128)(2,1)} %convert_element_type.262), channel_id=1, source_target_pairs={{0,0},{1,1},{2,2},{3,3},{16,4},{17,5},{18,6},{19,7},{4,16},{5,17},... | collective-permute-start | bytes 1572872 | tf_op jit(solution)/shard_map/ppermute | solution.py:464
  (80 other events, 2864.4 us)
Sparse Core Ops, SparseCore 0:
  11.3 149.5 all-gather.6
  352.7 63.8 all-gather.8
  418.8 62.2 all-gather.10
  801.1 50.5 all-gather.12

commit v8 on v7

--- a/solution.py
+++ b/solution.py
@@ -60,14 +60,13 @@
         lax.fori_loop(1, count, lambda off, _: (step(off), 0)[1], 0)
 
 
-def lstm_kernel(n, chunk, x_own, bias, p, pt, cot, *refs):
-    w_in = refs[:n]
-    out_ref, dx_ref, db_ref, dp_ref = refs[n:n + 4]
-    dw_out = refs[n + 4:2 * n + 4]
+def lstm_kernel(n, chunk, x_own, bias, p, pt, cot, w_in, *refs):
+    out_ref, dx_ref, db_ref, dp_ref = refs[:4]
+    dw_out = refs[4:n + 4]
     (xbuf, hbuf, dqbuf, gates, cells, ebuf, hown, gscr, escr, dabuf, ucell, dwacc, w, wt,
      stage, inbox, stage2, inbox2, relay, gbuf, rown,
      in_send, in_recv, ag_send, ag_recv, dq_send, dq_recv, rs_send, rs_recv,
-     dx_send, dx_recv, x_send, x_recv, g_send, g_recv, st_sem, w_sem) = refs[2 * n + 4:]
+     dx_send, dx_recv, x_send, x_recv, g_send, g_recv, st_sem, w_sem) = refs[n + 4:]
     steps, _, rows, width = xbuf.shape
     total = n * rows
     cell = cells.shape[2]
@@ -96,11 +95,8 @@
     pl.semaphore_signal(barrier, inc=1, device_id=partner, device_id_type=MESH)
 
     each = 2 * width // n
-    loads = []
-    for off in range(n):
-        at = pl.multiple_of(lax.rem(me + (n - off), n) * each, each)
-        loads.append(pltpu.make_async_copy(w_in[off], w.at[pl.ds(at, each)], w_sem.at[off]))
-        loads[-1].start()
+    load = pltpu.make_async_copy(w_in, w, w_sem)
+    load.start()
 
     @pl.when(first)
     def _():
@@ -162,8 +158,7 @@
         x_copy(0).wait_recv()
         in_start(0)
 
-    for load in loads:
-        load.wait()
+    load.wait()
     for at in range(0, 2 * width, 128):
         wt[:, at:at + 128] = w[at:at + 128, :].T
 
@@ -348,7 +343,7 @@
     for off in range(n):
         if off > 1:
             dw_copy(off - 2).wait()
-        at = pl.multiple_of(lax.rem(me + off, n) * each, each)
+        at = pl.multiple_of(lax.rem(place + off, n) * each, each)
         dabuf[off % 2, :each, :] = dwacc[pl.ds(at, each), :].astype(BF)
         dw_copy(off).start()
     for off in range(n - 2, n):
@@ -371,7 +366,7 @@
             sds((steps, rows, width), BF), sds((steps, rows, width), F32),
             sds((1, 4 * cell), F32), sds((cell, width), F32),
             *[sds((2 * width // n, 4 * cell), BF)] * n),
-        in_specs=[vm] * 5 + [hb] * n,
+        in_specs=[vm] * 5 + [hb],
         out_specs=[vm] * 4 + [hb] * n,
         scratch_shapes=[
             V((steps, n, rows, width), BF), V((steps + 1, n, rows, width), BF),
@@ -385,35 +380,34 @@
             V((2, n, rows, width), BF), V((2, n, rows, width), BF),
             V((steps, rows, width), BF), V((steps, rows, width), BF), V((rows, width), F32),
             dma((steps,)), dma((steps,)), dma((n,)), dma((n,)), dma((n,)), dma((n,)), dma((n,)), dma((n,)), dma((2, n)), dma((2, n)),
-            dma((steps,)), dma((steps,)), dma((steps,)), dma((steps,)), dma((2,)), dma((n,)),
+            dma((steps,)), dma((steps,)), dma((steps,)), dma((steps,)), dma((2,)), dma,
         ],
         compiler_params=pltpu.CompilerParams(
             collective_id=0, has_side_effects=True, vmem_limit_bytes=60 * 1024 * 1024),
         cost_estimate=pl.CostEstimate(
             flops=300_000_000_000, bytes_accessed=64 * 1024 * 1024, transcendentals=0),
         name="relay_lstm",
-    )(x, bias, p, pt, cot, *weights)
-
-
-def turned(off, n, sign):
-    return lax.rem(lax.axis_index("dp") + (off if sign > 0 else n - off), n)
+    )(x, bias, p, pt, cot, weights)
 
 
 def split_cells(weight, n):
     rows, gates = weight.shape
     cell = gates // (4 * n)
-
-    def body(src, *dst):
-        for off in range(n):
-            at = pl.multiple_of(turned(off, n, 1) * cell, cell)
-            dst[off][...] = src[:, pl.ds(at, cell)].astype(BF)
+    wing = n // 2
+
+    def body(src, keep, give):
+        pipe = lax.axis_index("pipe")
+        for k in range(wing):
+            for dst, side in ((keep, pipe), (give, 1 - pipe)):
+                at = pl.multiple_of((side * wing + k) * cell, cell)
+                dst[k] = src[:, pl.ds(at, cell)].astype(BF)
 
     return pl.pallas_call(
         body,
         grid=(4,),
-        out_shape=[jax.ShapeDtypeStruct((rows, 4 * cell), BF)] * n,
+        out_shape=[jax.ShapeDtypeStruct((wing, rows, 4 * cell), BF)] * 2,
         in_specs=[pl.BlockSpec((rows, n * cell), lambda b: (0, b))],
-        out_specs=[pl.BlockSpec((rows, cell), lambda b: (0, b))] * n,
+        out_specs=[pl.BlockSpec((wing, rows, cell), lambda b: (0, 0, b))] * 2,
         cost_estimate=pl.CostEstimate(
             flops=0, bytes_accessed=6 * rows * gates, transcendentals=0
         ),
@@ -421,28 +415,80 @@
     )(weight)
 
 
-def join_cells(blocks):
+def sort_blocks(blocks):
     n = len(blocks)
-    rows, gates = blocks[0].shape
+    wing = n // 2
+
+    def body(*refs):
+        src, (keep, give, sems) = refs[:n], refs[n:]
+        pipe = lax.axis_index("pipe")
+        for off in range(n):
+            place = lax.rem(lax.axis_index("dp") + (n - off), n)
+            stays = lax.div(place, wing) == pipe
+
+            @pl.when(stays)
+            def _():
+                pltpu.make_async_copy(
+                    src[off], keep.at[lax.rem(place, wing)], sems.at[off]
+                ).start()
+
+            @pl.when(jnp.logical_not(stays))
+            def _():
+                pltpu.make_async_copy(
+                    src[off], give.at[lax.rem(place, wing)], sems.at[off]
+                ).start()
+
+        for off in range(n):
+            pltpu.make_async_copy(src[off], keep.at[0], sems.at[off]).wait()
+
+    return pl.pallas_call(
+        body,
+        out_shape=[jax.ShapeDtypeStruct((wing, *blocks[0].shape), BF)] * 2,
+        in_specs=[pl.BlockSpec(memory_space=pl.ANY)] * n,
+        out_specs=[pl.BlockSpec(memory_space=pl.ANY)] * 2,
+        scratch_shapes=[pltpu.SemaphoreType.DMA((n,))],
+        cost_estimate=pl.CostEstimate(
+            flops=0, bytes_accessed=4 * n * blocks[0].size, transcendentals=0
+        ),
+        name="sort_blocks",
+    )(*blocks)
+
+
+def join_cells(keep, came):
+    wing, rows, gates = keep.shape
     cell = gates // 4
-
-    def body(*refs):
-        dst = refs[n]
-        for off in range(n):
-            at = pl.multiple_of(turned(off, n, -1) * cell, cell)
-            dst[:, pl.ds(at, cell)] = refs[off][...].astype(F32)
+    n = 2 * wing
+
+    def body(keep, came, dst):
+        pipe = lax.axis_index("pipe")
+        for k in range(wing):
+            for src, side in ((keep, pipe), (came, 1 - pipe)):
+                at = pl.multiple_of((side * wing + k) * cell, cell)
+                dst[:, pl.ds(at, cell)] = src[k].astype(F32)
 
     return pl.pallas_call(
         body,
         grid=(4,),
         out_shape=jax.ShapeDtypeStruct((rows, n * gates), F32),
-        in_specs=[pl.BlockSpec((rows, cell), lambda b: (0, b))] * n,
+        in_specs=[pl.BlockSpec((wing, rows, cell), lambda b: (0, 0, b))] * 2,
         out_specs=pl.BlockSpec((rows, n * cell), lambda b: (0, b)),
         cost_estimate=pl.CostEstimate(
             flops=0, bytes_accessed=6 * n * rows * gates, transcendentals=0
         ),
         name="join_cells",
-    )(*blocks)
+    )(keep, came)
+
+
+def swap_pipes(value):
+    return lax.ppermute(value, "pipe", [(0, 1), (1, 0)])
+
+
+def exchange(blocks):
+    n = len(blocks)
+    return [blocks[0]] + [
+        lax.ppermute(blocks[off], "dp", [(i, (i + off) % n) for i in range(n)])
+        for off in range(1, n)
+    ]
 
 
 def rank_pairs(n, off, layers=(0, 1)):
@@ -577,12 +623,20 @@
     moved = to_ranks(
         jnp.concatenate([cell_proj[0, 0].astype(BF), cot.reshape(steps * seqs, width)]), 0
     )
+    gate_kept, gate_given = split_cells(gate_weight[0, 0], n)
+    gate_came = swap_pipes(gate_given)
+    gate_low = jnp.concatenate(
+        [
+            jnp.where(pipe == 0, gate_kept, gate_came),
+            jnp.where(pipe == 0, gate_came, gate_kept),
+        ]
+    )
     gate_low, gathered, features_low, bias_own, moved = lax.optimization_barrier(
-        (split_cells(gate_weight[0, 0], n), gathered, features_low, bias_own, moved)
+        (gate_low, gathered, features_low, bias_own, moved)
     )
     cell_low = moved[:cell]
     cot = moved[cell:].reshape(steps, seqs, width)
-    gate_own = [to_ranks(block, off) for off, block in enumerate(gate_low)]
+    gate_own = lax.all_to_all(gate_low, "dp", 0, 0).reshape(2 * width, 4 * cell)
     highway_half = gathered[:, :FILTERS]
     proj_full = gathered[:, FILTERS:].reshape(pieces, proj_rows, holders, sub)
     proj_full = jnp.transpose(proj_full, (2, 1, 0, 3)).reshape(FILTERS, width)
@@ -627,7 +681,7 @@
         n, inputs, gate_own, bias_own, cell_low, cell_low.T, cot
     )
     dx_own = from_ranks(dx_own.astype(BF), 0, (1,))
-    grad_gate = [from_ranks(block, off) for off, block in enumerate(grad_gate)]
+    grad_gate = exchange(grad_gate)
     dx_own, kept_all = lax.optimization_barrier((dx_own, kept_all))
 
     grad_stored = jnp.einsum(
@@ -695,7 +749,9 @@
     pair = jnp.concatenate([pair, last.reshape(holders, tokens, 2 * cols)], axis=2)
     pair = lax.all_to_all(pair, ("dir", "dp"), 0, 0).reshape(holders * tokens, -1)
     grad_conv, pair, grad_gate = lax.optimization_barrier((grad_conv, pair, grad_gate))
-    grad_gate = join_cells(grad_gate)
+    gate_kept, gate_given = sort_blocks(grad_gate)
+    gate_came = swap_pipes(gate_given)
+    grad_gate = join_cells(gate_kept, gate_came)
     small = (
         grad_table,
         spread(jnp.sum(grad_before, axis=0)),

time: 1050 us -> 1080 us (1.029)
  Pallas kernels: 319 us -> 447 us
  waiting for transfers between devices: 184 us -> 132 us
  blocking collectives: 93.3 us -> 55 us
  starting transfers between devices: 214 us -> 202 us
    pallas_call x1 -> x2, Pallas kernels: 5.97 us -> 134 us  [the longest x1 128 us: sort_blocks(): pl.pallas_call(body, out_shape=[jax.ShapeDtypeStruct((wing, *blocks[0].sh...]
    ppermute x10 -> x2, waiting for transfers between devices: 55.5 us -> 0.01 us  [to_ranks(): lax.ppermute(value, ('pipe', 'dp'), rank_pairs(lax.axis_size('dp'), off))]
    all_to_all x0 -> x1, waiting for transfers between devices: none -> 40 us  [local(): gate_own = lax.all_to_all(gate_low, 'dp', 0, 0).reshape(2 * width, 4 * cell)]
    ppermute x11 -> x3, starting transfers between devices: 45.6 us -> 8.37 us  [from_ranks(): lax.ppermute(value, ('pipe', 'dp'), [(there, here) for here, there in pai...]
    ppermute x11 -> x3, waiting for transfers between devices: 36 us -> 0.01 us  [from_ranks(): lax.ppermute(value, ('pipe', 'dp'), [(there, here) for here, there in pai...]
    ppermute x10 -> x2, starting transfers between devices: 40.5 us -> 9.07 us  [to_ranks(): lax.ppermute(value, ('pipe', 'dp'), rank_pairs(lax.axis_size('dp'), off))]
    all_to_all x1, waiting for transfers between devices: 1.91 us -> 27.4 us  [local(): lax.all_to_all(jnp.broadcast_to(summed[KMAX * CDIM * cols:][:share], (eve...]
    all_gather x1, blocking collectives: 37.7 us -> 12.3 us  [local(): lax.all_gather(encoded.astype(BF).reshape(quarter, steps, width), ('dir',...]
  transfers between devices with their start and end apart: 35 -> 29, of which waited for: 10 -> 6; matrix products, arithmetic and copies ran while one was open for 18% -> 19% of each run, Pallas kernels for 31% -> 41%
where the time goes in v8:
time: 1080 us; the launch traced here: 1070 us
  Pallas kernels  447 us (41%)
  starting transfers between devices  202 us (19%)
  waiting for transfers between devices  132 us (12%)
  local copies, waits for them, and re-layouts  86.2 us (8%)
  matrix products  65.4 us (6%)
  other arithmetic  61.7 us (6%)
  blocking collectives  55 us (5%)
  between operations  15.6 us (1%)
    pallas_call x1, Pallas kernels, lstm_call(): pl.pallas_call(functools.partial(lstm_kernel, n, chunk), out_shape=(sds((...  307 us
    pallas_call x1, Pallas kernels, sort_blocks(): pl.pallas_call(body, out_shape=[jax.ShapeDtypeStruct((wing, *blocks[0].sh...  128 us
    all_to_all x1, starting transfers between devices, local(): lax.all_to_all(jnp.concatenate([grad_stored, grad_stored]).reshape(-1, gr...  78.9 us
    all_gather x1, waiting for transfers between devices, local(): lax.all_gather(jnp.concatenate([mine, proj_blocks], axis=1).astype(BF), (...  48.3 us
    all_gather x3, blocking collectives, both_halves(): lax.all_gather(value, 'pipe').reshape(2, tokens, blocks, half // blocks)  42.7 us
    all_to_all x1, waiting for transfers between devices, local(): gate_own = lax.all_to_all(gate_low, 'dp', 0, 0).reshape(2 * width, 4 * cell)  40 us
    all_to_all x1, waiting for transfers between devices, local(): lax.all_to_all(jnp.broadcast_to(summed[KMAX * CDIM * cols:][:share], (eve...  27.4 us
    ppermute x1, starting transfers between devices, local(): came = lax.ppermute(sent, 'pipe', [(0, 1), (1, 0)]).astype(F32)  25.3 us
  transfers between devices with their start and end apart: 29, of which 6 were waited for; matrix products, arithmetic and copies ran while one was open for 19% of the time, Pallas kernels for 41%

profile of v8, /device:TPU:3, one launch (start us, length us, event | category | flops | bytes accessed | tf_op | source)
XLA Modules:
  0.0 1065.3 jit_solution(655638518968468377)
XLA Ops:
  39.1 12.1 %gather_fusion = bf16[6400,16]{1,0:T(8,128)(2,1)S(1)} fusion(bf16[262,16]{1,0:T(8,128)(2,1)S(1)} %copy.242, s32[7168]{0:T(1024)S(1)} %pad_clamp_fusion), kind=kCustom, calls=%fused_computation.clone | custom fusion | bytes 435200 | tf_op jit(solution)/shard_map/jit(_take)/gather | solution.py:49
  54.3 11.2 %select_reduce_fusion = (f32[128,1024]{1,0:T(8,128)S(1)}, f32[128,50,1024]{2,0,1:T(8,128)}) fusion(pred[50,1024]{1,0:T(8,128)(4,1)S(1)} %iota_compare_fusion.6, bf16[128,50,112]{0,2,1:T(8,128)(2,1)S(1)} %slice_dynamic-update-slice_fusion, s32[1024]{0:T(1024)S(1)} %add_bitcast_fusion, s32[112]{0:T(128)S(1)} %and_select_fusion, ...), kind=kOutput, calls=%fused_computation.5 | convolution fusion | flops 1481785344 | bytes 28463620 | tf_op jit(solution)/shard_map/bpk,kf->bpf/dot_general | solution.py:51
  65.6 14.8 %fusion = (f32[128,1024]{1,0:T(8,128)}, f32[128,1024]{1,0:T(8,128)S(1)}) fusion(f32[128,50,1024]{2,0,1:T(8,128)} %get-tuple-element.204, f32[128,1024]{1,0:T(8,128)S(1)} %get-tuple-element.203, pred[50,1024]{1,0:T(8,128)(4,1)S(1)} %iota_compare_fusion.6, f32[128,1024]{1,0:T(8,128)S(1)} %is-finite_select_fusion.1), kind=kLoop, calls=%fused_computation.4 | loop fusion | flops 32505856 | bytes 28362752 | tf_op jit(solution)/shard_map/reduce_sum | solution.py:533
  80.6 26.5 %all_gather.32 = bf16[2,128,1024]{2,1,0:T(8,128)(2,1)S(1)} all-gather(bf16[1,128,1024]{2,1,0:T(8,128)(2,1)S(1)} %multiply_convert_fusion.5), channel_id=1, replica_groups=mesh['pipe'=2,'dir'=2,'dp'=8] {'pipe'}, dimensions={0}, use_global_device_ids=true | all-gather | bytes 786432 | tf_op jit(solution)/shard_map/all_gather | solution.py:526
  112.6 48.3 %all-gather.7.cloned.1.call-done = bf16[2,2304,2048]{2,1,0:T(8,128)(2,1)} async-done(((bf16[2,2304,128]{2,1,0:T(8,128)(2,1)}), bf16[2,2304,2048]{2,1,0:T(8,128)(2,1)}) %all-gather.7.cloned.1.call-update) | async-done | bytes 18874384 | tf_op jit(solution)/shard_map/all_gather | solution.py:591
  171.4 8.4 all-gather
  186.3 7.8 all-gather.1
  206.3 12.3 %all_gather.37 = bf16[16,16,512]{2,1,0:T(8,128)(2,1)S(1)} all-gather(bf16[4,16,512]{2,1,0:T(8,128)(2,1)S(1)} %bitcast.304), channel_id=1, replica_groups=mesh['pipe'=2,'dir'=2,'dp'=8] {'dir','pipe'}, dimensions={0}, use_global_device_ids=true | all-gather | bytes 327680 | tf_op jit(solution)/shard_map/all_gather | solution.py:659
  218.6 40.0 %all-to-all-done.1 = bf16[8,128,2048]{2,1,0:T(8,128)(2,1)} async-done(((bf16[8,128,2048]{2,1,0:T(8,128)(2,1)}), bf16[8,128,2048]{2,1,0:T(8,128)(2,1)}, u32[]{:S(2)}, u32[]{:S(2)}) %all-to-all-start.1) | async-done | bytes 4194336 | tf_op jit(solution)/shard_map/all_to_all | solution.py:639
  276.0 307.4 %relay_lstm.1 = (bf16[16,16,512]{2,1,0:T(8,128)(2,1)}, f32[16,16,512]{2,1,0:T(8,128)}, f32[1,2048]{1,0:T(1,128)}, f32[512,512]{1,0:T(8,128)}, bf16[128,2048]{1,0...) custom-call(bf16[16,16,512]{2,1,0:T(8,128)(2,1)} %collective-permute, ...), custom_call_target="tpu_custom_call" | custom-call | flops 299999985664 | bytes 67108864 | tf_op jit(solution)/shard_map/relay_lstm/pallas_call | solution.py:363
  593.2 13.2 %collective-permute-start.9 = (bf16[128,2048]{1,0:T(8,128)(2,1)}, bf16[128,2048]{1,0:T(8,128)(2,1)}, u32[]{:S(2)}, u32[]{:S(2)}) collective-permute-start(bf16[128,2048]{1,0:T(8,128)(2,1)} %get-tuple-element.73), channel_id=1, source_target_pairs={{0,3},{1,4},{2,5},{3,6},{4,7},{5,0},{6,1},{7,2},{8,11},{9,12},{10,... | collective-permute-start | bytes 1572872 | tf_op jit(solution)/shard_map/ppermute | solution.py:489
  608.5 78.9 %all-to-all-start.2 = ((bf16[4,128,512]{2,1,0:T(8,128)(2,1)}), bf16[4,128,512]{2,1,0:T(8,128)(2,1)S(1)}, u32[]{:S(2)}, u32[]{:S(2)}) async-start(bf16[4,128,512]{2,1,0:T(8,128)(2,1)} %bitcast.37), calls=%async_computation.2 | async-start | bytes 1048576 | tf_op jit(solution)/shard_map/all_to_all | solution.py:692
  688.1 6.3 all-to-all-done.2
  696.7 6.3 fusion.1
  714.6 7.3 fusion.5
  758.9 21.7 %all-to-all-start.3 = ((bf16[16,64,640]{2,1,0:T(8,128)(2,1)}), bf16[16,64,640]{2,1,0:T(8,128)(2,1)}, u32[]{:S(2)}, u32[]{:S(2)}) async-start(bf16[16,64,640]{2,1,0:T(8,128)(2,1)} %pad_maximum_fusion.1), calls=%async_computation.3 | async-start | bytes 2621440 | tf_op jit(solution)/shard_map/all_to_all | solution.py:750
  780.7 11.7 %multiply_convert_fusion = bf16[128,50,1024]{2,0,1:T(8,128)(2,1)S(1)} fusion(f32[128,50,1024]{2,0,1:T(8,128)} %get-tuple-element.204, f32[128,1024]{1,0:T(8,128)S(1)} %copy-done.19, f32[128,1024]{1,0:T(8,128)S(1)} %copy-done.4, f32[128,1024]{1,0:T(8,128)S(1)} %fusion.41, pred[50,1024]{1,0:T(8,128)(4,1)S(1)} %copy-done.40), kind=kLoop, calls=%fused_computation.1 | loop fusion | flops 32768000 | bytes 40945664 | tf_op jit(solution)/shard_map/convert_element_type | solution.py:534
  805.2 6.0 fusion.25
  830.6 25.3 %collective-permute-start.17 = (bf16[4352,128]{1,0:T(8,128)(2,1)}, bf16[4352,128]{1,0:T(8,128)(2,1)S(1)}, u32[]{:S(2)}, u32[]{:S(2)}) collective-permute-start(bf16[4352,128]{1,0:T(8,128)(2,1)} %pad_maximum_fusion.3), channel_id=1, source_target_pairs={{0,16},{16,0},{1,17},{17,1},{2,18},{18,2},{3,19},{19,3},{4,20},{20... | collective-permute-start | bytes 3342344 | tf_op jit(solution)/shard_map/ppermute | solution.py:812
  858.6 13.1 %all-to-all-start.4 = ((bf16[32,2,4864]{2,1,0:T(2,128)(2,1)}), bf16[32,2,4864]{2,1,0:T(2,128)(2,1)S(1)}, u32[]{:S(2)}, u32[]{:S(2)}) async-start(bf16[32,2,4864]{2,1,0:T(2,128)(2,1)} %reshape.688), calls=%async_computation.4 | async-start | bytes 1245184 | tf_op jit(solution)/shard_map/all_to_all | solution.py:780
  871.7 128.2 %sort_blocks.1 = (bf16[4,128,2048]{2,1,0:T(8,128)(2,1)}, bf16[4,128,2048]{2,1,0:T(8,128)(2,1)}) custom-call(bf16[128,2048]{1,0:T(8,128)(2,1)} %get-tuple-element.93.refs_0_, bf16[128,2048]{1,0:T(8,128)(2,1)} %collective-permute-done.7.refs_1_, bf16[128,2048]{1,0:T(8,128)(2,1)} %collective-permute-done.8.refs_2_, ...), custom_call_target="tpu_custom_call" | custom-call | bytes 8388608 | tf_op jit(solution)/shard_map/sort_blocks/pallas_call | solution.py:444
  1011.7 6.3 all-to-all-start.5
  1022.1 27.4 %all-to-all-done.5 = f32[32,1,512]{2,1,0:T(1,128)S(1)} async-done(((f32[32,1,512]{2,1,0:T(1,128)}), f32[32,1,512]{2,1,0:T(1,128)S(1)}, u32[]{:S(2)}, u32[]{:S(2)}) %all-to-all-start.5) | async-done | bytes 65568 | tf_op jit(solution)/shard_map/all_to_all | solution.py:816
  1052.6 6.0 join_cells.1
  (377 shorter events, 203.0 us)
Async XLA Ops:
  7.2 153.7 %all-gather.7.cloned.1.call-start = ((), (), s32[]{:S(2)}) async-start(), calls=%async_computation.6 | async-start | bytes 20054016 | tf_op jit(solution)/shard_map/all_gather | solution.py:591
  12.6 100.0 %collective-permute-start.1 = (f32[1,2048]{1,0:T(1,128)S(1)}, f32[1,2048]{1,0:T(1,128)S(1)}, u32[]{:S(2)}, u32[]{:S(2)}) collective-permute-start(f32[1,2048]{1,0:T(1,128)S(1)} %bitcast.310), channel_id=1, source_target_pairs={{0,0},{1,1},{2,2},{3,3},{4,16},{5,17},{6,18},{7,19},{16,4},{17,5},... | collective-permute-start | bytes 24584 | tf_op jit(solution)/shard_map/ppermute | solution.py:505
  17.6 36.6 %all-to-all-start = ((bf16[16,112,128]{2,1,0:T(8,128)(2,1)}), bf16[16,112,128]{2,1,0:T(8,128)(2,1)S(1)}, u32[]{:S(2)}, u32[]{:S(2)}) async-start(bf16[16,112,128]{2,1,0:T(8,128)(2,1)} %broadcast_in_dim.267), calls=%async_computation | async-start | bytes 917504 | tf_op jit(solution)/shard_map/all_to_all | solution.py:594
  24.3 88.2 %collective-permute-start.2 = (bf16[768,512]{0,1:T(8,128)(2,1)}, bf16[768,512]{0,1:T(8,128)(2,1)}, u32[]{:S(2)}, u32[]{:S(2)}) collective-permute-start(bf16[768,512]{0,1:T(8,128)(2,1)} %pad_maximum_fusion.4), channel_id=1, source_target_pairs={{0,0},{1,1},{2,2},{3,3},{4,16},{5,17},{6,18},{7,19},{16,4},{17,5},... | collective-permute-start | bytes 2359304 | tf_op jit(solution)/shard_map/ppermute | solution.py:505
  35.0 72.4 %collective-permute-start = (bf16[4,128,2048]{2,1,0:T(8,128)(2,1)}, bf16[4,128,2048]{2,1,0:T(8,128)(2,1)}, u32[]{:S(2)}, u32[]{:S(2)}) collective-permute-start(bf16[4,128,2048]{2,1,0:T(8,128)(2,1)} %get-tuple-element.59), channel_id=1, source_target_pairs={{0,16},{16,0},{1,17},{17,1},{2,18},{18,2},{3,19},{19,3},{4,20},{20... | collective-permute-start | bytes 6291464 | tf_op jit(solution)/shard_map/ppermute | solution.py:483
  160.9 97.8 %all-to-all-start.1 = ((bf16[8,128,2048]{2,1,0:T(8,128)(2,1)}), bf16[8,128,2048]{2,1,0:T(8,128)(2,1)}, u32[]{:S(2)}, u32[]{:S(2)}) async-start(bf16[8,128,2048]{2,1,0:T(8,128)(2,1)} %pad_maximum_fusion), calls=%async_computation.1 | async-start | bytes 8388608 | tf_op jit(solution)/shard_map/all_to_all | solution.py:639
  165.6 440.8 %all-gather.9.cloned.1.call-start = ((), (), s32[]{:S(2)}) async-start(), calls=%async_computation.7 | async-start | bytes 4456448 | tf_op jit(solution)/shard_map/all_gather | solution.py:664
  261.6 344.8 %all-gather.11.cloned.1.call-start = ((), (), s32[]{:S(2)}) async-start(), calls=%async_computation.8 | async-start | bytes 4456448 | tf_op jit(solution)/shard_map/all_gather | solution.py:664
  591.7 146.5 %collective-permute-start.7 = (bf16[128,2048]{1,0:T(8,128)(2,1)}, bf16[128,2048]{1,0:T(8,128)(2,1)}, u32[]{:S(2)}, u32[]{:S(2)}) collective-permute-start(bf16[128,2048]{1,0:T(8,128)(2,1)} %get-tuple-element.71), channel_id=1, source_target_pairs={{0,1},{1,2},{2,3},{3,4},{4,5},{5,6},{6,7},{7,0},{8,9},{9,10},{10,1... | collective-permute-start | bytes 1572872 | tf_op jit(solution)/shard_map/ppermute | solution.py:489
  592.4 150.6 %collective-permute-start.8 = (bf16[128,2048]{1,0:T(8,128)(2,1)}, bf16[128,2048]{1,0:T(8,128)(2,1)}, u32[]{:S(2)}, u32[]{:S(2)}) collective-permute-start(bf16[128,2048]{1,0:T(8,128)(2,1)} %get-tuple-element.72), channel_id=1, source_target_pairs={{0,2},{1,3},{2,4},{3,5},{4,6},{5,7},{6,0},{7,1},{8,10},{9,11},{10,... | collective-permute-start | bytes 1572872 | tf_op jit(solution)/shard_map/ppermute | solution.py:489
  593.2 152.2 %collective-permute-start.9 = (bf16[128,2048]{1,0:T(8,128)(2,1)}, bf16[128,2048]{1,0:T(8,128)(2,1)}, u32[]{:S(2)}, u32[]{:S(2)}) collective-permute-start(bf16[128,2048]{1,0:T(8,128)(2,1)} %get-tuple-element.73), channel_id=1, source_target_pairs={{0,3},{1,4},{2,5},{3,6},{4,7},{5,0},{6,1},{7,2},{8,11},{9,12},{10,... | collective-permute-start | bytes 1572872 | tf_op jit(solution)/shard_map/ppermute | solution.py:489
  606.3 143.9 %collective-permute-start.10 = (bf16[128,2048]{1,0:T(8,128)(2,1)}, bf16[128,2048]{1,0:T(8,128)(2,1)}, u32[]{:S(2)}, u32[]{:S(2)}) collective-permute-start(bf16[128,2048]{1,0:T(8,128)(2,1)} %get-tuple-element.74), channel_id=1, source_target_pairs={{0,4},{1,5},{2,6},{3,7},{4,0},{5,1},{6,2},{7,3},{8,12},{9,13},{10,... | collective-permute-start | bytes 1572872 | tf_op jit(solution)/shard_map/ppermute | solution.py:489
  608.5 85.9 %all-to-all-start.2 = ((bf16[4,128,512]{2,1,0:T(8,128)(2,1)}), bf16[4,128,512]{2,1,0:T(8,128)(2,1)S(1)}, u32[]{:S(2)}, u32[]{:S(2)}) async-start(bf16[4,128,512]{2,1,0:T(8,128)(2,1)} %bitcast.37), calls=%async_computation.2 | async-start | bytes 1048576 | tf_op jit(solution)/shard_map/all_to_all | solution.py:692
  687.4 133.7 %all-gather.13.cloned.1.call-start = ((), (), s32[]{:S(2)}) async-start(), calls=%async_computation.9 | async-start | bytes 1114112 | tf_op jit(solution)/shard_map/all_gather | solution.py:700
  738.3 271.3 %collective-permute-start.15 = (bf16[16,16,512]{2,1,0:T(8,128)(2,1)}, bf16[16,16,512]{2,1,0:T(8,128)(2,1)}, u32[]{:S(2)}, u32[]{:S(2)}) collective-permute-start(bf16[16,16,512]{2,1,0:T(8,128)(2,1)} %get-tuple-element.86), channel_id=1, source_target_pairs={{0,0},{1,1},{2,2},{3,3},{16,4},{17,5},{18,6},{19,7},{4,16},{5,17},... | collective-permute-start | bytes 786440 | tf_op jit(solution)/shard_map/ppermute | solution.py:510
  743.1 266.6 %collective-permute-start.16 = (bf16[512,512]{1,0:T(8,128)(2,1)}, bf16[512,512]{1,0:T(8,128)(2,1)}, u32[]{:S(2)}, u32[]{:S(2)}) collective-permute-start(bf16[512,512]{1,0:T(8,128)(2,1)} %convert_element_type.262), channel_id=1, source_target_pairs={{0,0},{1,1},{2,2},{3,3},{16,4},{17,5},{18,6},{19,7},{4,16},{5,17},... | collective-permute-start | bytes 1572872 | tf_op jit(solution)/shard_map/ppermute | solution.py:510
  745.4 65.8 %collective-permute-start.12 = (bf16[128,2048]{1,0:T(8,128)(2,1)}, bf16[128,2048]{1,0:T(8,128)(2,1)}, u32[]{:S(2)}, u32[]{:S(2)}) collective-permute-start(bf16[128,2048]{1,0:T(8,128)(2,1)} %get-tuple-element.81), channel_id=1, source_target_pairs={{0,5},{1,6},{2,7},{3,0},{4,1},{5,2},{6,3},{7,4},{8,13},{9,14},{10,... | collective-permute-start | bytes 1572872 | tf_op jit(solution)/shard_map/ppermute | solution.py:489
  750.2 61.0 %collective-permute-start.13 = (bf16[128,2048]{1,0:T(8,128)(2,1)}, bf16[128,2048]{1,0:T(8,128)(2,1)}, u32[]{:S(2)}, u32[]{:S(2)}) collective-permute-start(bf16[128,2048]{1,0:T(8,128)(2,1)} %get-tuple-element.82), channel_id=1, source_target_pairs={{0,6},{1,7},{2,0},{3,1},{4,2},{5,3},{6,4},{7,5},{8,14},{9,15},{10,... | collective-permute-start | bytes 1572872 | tf_op jit(solution)/shard_map/ppermute | solution.py:489
  750.3 61.0 %collective-permute-start.14 = (bf16[128,2048]{1,0:T(8,128)(2,1)}, bf16[128,2048]{1,0:T(8,128)(2,1)}, u32[]{:S(2)}, u32[]{:S(2)}) collective-permute-start(bf16[128,2048]{1,0:T(8,128)(2,1)} %get-tuple-element.83), channel_id=1, source_target_pairs={{0,7},{1,0},{2,1},{3,2},{4,3},{5,4},{6,5},{7,6},{8,15},{9,8},{10,9... | collective-permute-start | bytes 1572872 | tf_op jit(solution)/shard_map/ppermute | solution.py:489
  758.9 58.0 %all-to-all-start.3 = ((bf16[16,64,640]{2,1,0:T(8,128)(2,1)}), bf16[16,64,640]{2,1,0:T(8,128)(2,1)}, u32[]{:S(2)}, u32[]{:S(2)}) async-start(bf16[16,64,640]{2,1,0:T(8,128)(2,1)} %pad_maximum_fusion.1), calls=%async_computation.3 | async-start | bytes 2621440 | tf_op jit(solution)/shard_map/all_to_all | solution.py:750
  830.6 174.8 %collective-permute-start.17 = (bf16[4352,128]{1,0:T(8,128)(2,1)}, bf16[4352,128]{1,0:T(8,128)(2,1)S(1)}, u32[]{:S(2)}, u32[]{:S(2)}) collective-permute-start(bf16[4352,128]{1,0:T(8,128)(2,1)} %pad_maximum_fusion.3), channel_id=1, source_target_pairs={{0,16},{16,0},{1,17},{17,1},{2,18},{18,2},{3,19},{19,3},{4,20},{20... | collective-permute-start | bytes 3342344 | tf_op jit(solution)/shard_map/ppermute | solution.py:812
  858.6 149.3 %all-to-all-start.4 = ((bf16[32,2,4864]{2,1,0:T(2,128)(2,1)}), bf16[32,2,4864]{2,1,0:T(2,128)(2,1)S(1)}, u32[]{:S(2)}, u32[]{:S(2)}) async-start(bf16[32,2,4864]{2,1,0:T(2,128)(2,1)} %reshape.688), calls=%async_computation.4 | async-start | bytes 1245184 | tf_op jit(solution)/shard_map/all_to_all | solution.py:780
  1000.0 52.6 %collective-permute-start.18 = (bf16[4,128,2048]{2,1,0:T(8,128)(2,1)}, bf16[4,128,2048]{2,1,0:T(8,128)(2,1)}, u32[]{:S(2)}, u32[]{:S(2)}) collective-permute-start(bf16[4,128,2048]{2,1,0:T(8,128)(2,1)} %get-tuple-element.102), channel_id=1, source_target_pairs={{0,16},{16,0},{1,17},{17,1},{2,18},{18,2},{3,19},{19,3},{4,20},{20... | collective-permute-start | bytes 6291464 | tf_op jit(solution)/shard_map/ppermute | solution.py:483
  1011.7 37.8 %all-to-all-start.5 = ((f32[32,1,512]{2,1,0:T(1,128)}), f32[32,1,512]{2,1,0:T(1,128)S(1)}, u32[]{:S(2)}, u32[]{:S(2)}) async-start(f32[32,1,512]{2,1,0:T(1,128)} %broadcast_in_dim.305), calls=%async_computation.5 | async-start | bytes 131072 | tf_op jit(solution)/shard_map/all_to_all | solution.py:816
  (75 other events, 2338.6 us)
Sparse Core Ops, SparseCore 0:
  11.3 149.5 all-gather.6
  261.7 60.6 all-gather.8
  324.7 65.9 all-gather.10
  706.8 38.6 all-gather.12

commit v9 on v8

--- a/solution.py
+++ b/solution.py
@@ -419,8 +419,11 @@
     n = len(blocks)
     wing = n // 2
 
+    rows, gates = blocks[0].shape
+    cell = gates // 4
+
     def body(*refs):
-        src, (keep, give, sems) = refs[:n], refs[n:]
+        src, (keep, give) = refs[:n], refs[n:]
         pipe = lax.axis_index("pipe")
         for off in range(n):
             place = lax.rem(lax.axis_index("dp") + (n - off), n)
@@ -428,25 +431,18 @@
 
             @pl.when(stays)
             def _():
-                pltpu.make_async_copy(
-                    src[off], keep.at[lax.rem(place, wing)], sems.at[off]
-                ).start()
+                keep[lax.rem(place, wing)] = src[off][...]
 
             @pl.when(jnp.logical_not(stays))
             def _():
-                pltpu.make_async_copy(
-                    src[off], give.at[lax.rem(place, wing)], sems.at[off]
-                ).start()
-
-        for off in range(n):
-            pltpu.make_async_copy(src[off], keep.at[0], sems.at[off]).wait()
+                give[lax.rem(place, wing)] = src[off][...]
 
     return pl.pallas_call(
         body,
-        out_shape=[jax.ShapeDtypeStruct((wing, *blocks[0].shape), BF)] * 2,
-        in_specs=[pl.BlockSpec(memory_space=pl.ANY)] * n,
-        out_specs=[pl.BlockSpec(memory_space=pl.ANY)] * 2,
-        scratch_shapes=[pltpu.SemaphoreType.DMA((n,))],
+        grid=(4,),
+        out_shape=[jax.ShapeDtypeStruct((wing, rows, gates), BF)] * 2,
+        in_specs=[pl.BlockSpec((rows, cell), lambda b: (0, b))] * n,
+        out_specs=[pl.BlockSpec((wing, rows, cell), lambda b: (0, 0, b))] * 2,
         cost_estimate=pl.CostEstimate(
             flops=0, bytes_accessed=4 * n * blocks[0].size, transcendentals=0
         ),
@@ -619,10 +615,7 @@
     bias_own = lax.dynamic_index_in_dim(
         gate_bias[0, 0].reshape(4, n, cell), me, 1, keepdims=False
     ).reshape(1, 4 * cell)
-    bias_own = to_ranks(bias_own, 0)
-    moved = to_ranks(
-        jnp.concatenate([cell_proj[0, 0].astype(BF), cot.reshape(steps * seqs, width)]), 0
-    )
+    moved = jnp.concatenate([cell_proj[0, 0].astype(BF), cot.reshape(steps * seqs, width)])
     gate_kept, gate_given = split_cells(gate_weight[0, 0], n)
     gate_came = swap_pipes(gate_given)
     gate_low = jnp.concatenate(
@@ -634,8 +627,8 @@
     gate_low, gathered, features_low, bias_own, moved = lax.optimization_barrier(
         (gate_low, gathered, features_low, bias_own, moved)
     )
-    cell_low = moved[:cell]
-    cot = moved[cell:].reshape(steps, seqs, width)
+    bias_own = to_ranks(bias_own, 0)
+    moved = to_ranks(moved, 0)
     gate_own = lax.all_to_all(gate_low, "dp", 0, 0).reshape(2 * width, 4 * cell)
     highway_half = gathered[:, :FILTERS]
     proj_full = gathered[:, FILTERS:].reshape(pieces, proj_rows, holders, sub)
@@ -659,7 +652,18 @@
     encoded_own = lax.all_gather(
         encoded.astype(BF).reshape(quarter, steps, width), ("dir", "pipe"), axis=0, tiled=True
     )
-    kept_low, encoded_own, gate_own = lax.optimization_barrier((kept_low, encoded_own, gate_own))
+    inputs = jnp.einsum("rts,rsd->trd", own_order, encoded_own, preferred_element_type=BF)
+    wing = n // 2
+    inputs = lax.ppermute(
+        inputs,
+        ("pipe", "dp"),
+        [(k, wing + k) for k in range(wing)] + [(n + k, n + k) for k in range(wing, n)],
+    )
+    kept_low, gate_own, inputs, moved, bias_own = lax.optimization_barrier(
+        (kept_low, gate_own, inputs, moved, bias_own)
+    )
+    cell_low = moved[:cell]
+    cot = moved[cell:].reshape(steps, seqs, width)
     kept_all = [
         lax.all_gather(
             lax.dynamic_slice_in_dim(value, pipe * tokens, tokens, 0),
@@ -669,13 +673,6 @@
         )
         for value in kept_low[:2]
     ]
-    inputs = jnp.einsum("rts,rsd->trd", own_order, encoded_own, preferred_element_type=BF)
-    wing = n // 2
-    inputs = lax.ppermute(
-        inputs,
-        ("pipe", "dp"),
-        [(k, wing + k) for k in range(wing)] + [(n + k, n + k) for k in range(wing, n)],
-    )
 
     out_own, dx_own, grad_bias, grad_cell, *grad_gate = lstm_call(
         n, inputs, gate_own, bias_own, cell_low, cell_low.T, cot
@@ -748,7 +745,9 @@
     last = jnp.transpose(own_last.reshape(tokens, 2, holders, cols), (2, 0, 1, 3))
     pair = jnp.concatenate([pair, last.reshape(holders, tokens, 2 * cols)], axis=2)
     pair = lax.all_to_all(pair, ("dir", "dp"), 0, 0).reshape(holders * tokens, -1)
-    grad_conv, pair, grad_gate = lax.optimization_barrier((grad_conv, pair, grad_gate))
+    grad_conv, pair, grad_gate, out_own, grad_cell = lax.optimization_barrier(
+        (grad_conv, pair, grad_gate, out_own, grad_cell)
+    )
     gate_kept, gate_given = sort_blocks(grad_gate)
     gate_came = swap_pipes(gate_given)
     grad_gate = join_cells(gate_kept, gate_came)

time: 1080 us -> 953 us (0.88)
  Pallas kernels: 447 us -> 314 us
  waiting for transfers between devices: 132 us -> 185 us
  starting transfers between devices: 202 us -> 178 us
  blocking collectives: 55 us -> 39 us
    pallas_call x1, Pallas kernels: 128 us -> 5.04 us  [sort_blocks(): pl.pallas_call(body, grid=(4,), out_shape=[jax.ShapeDtypeStruct((wing, ro...]
    ppermute x2, waiting for transfers between devices: 0.01 us -> 64.1 us  [to_ranks(): lax.ppermute(value, ('pipe', 'dp'), rank_pairs(lax.axis_size('dp'), off))]
    all_to_all x1, waiting for transfers between devices: 40 us -> 0.01 us  [local(): gate_own = lax.all_to_all(gate_low, 'dp', 0, 0).reshape(2 * width, 4 * cell)]
    ppermute x1, starting transfers between devices: 25.3 us -> 0.01 us  [local(): came = lax.ppermute(sent, 'pipe', [(0, 1), (1, 0)]).astype(F32)]
    all_gather x3, blocking collectives: 42.7 us -> 27.2 us  [both_halves(): lax.all_gather(value, 'pipe').reshape(2, tokens, blocks, half // blocks)]
    ppermute x3, waiting for transfers between devices: 0.01 us -> 12.8 us  [from_ranks(): lax.ppermute(value, ('pipe', 'dp'), [(there, here) for here, there in pai...]
  transfers between devices with their start and end apart: 29 -> 29, of which waited for: 6 -> 10; matrix products, arithmetic and copies ran while one was open for 19% -> 21% of each run, Pallas kernels for 41% -> 33%
where the time goes in v9:
time: 953 us; the launch traced here: 943 us
  Pallas kernels  314 us (33%)
  waiting for transfers between devices  185 us (19%)
  starting transfers between devices  178 us (19%)
  local copies, waits for them, and re-layouts  84.6 us (9%)
  matrix products  65.1 us (7%)
  other arithmetic  61.7 us (6%)
  blocking collectives  39 us (4%)
  between operations  15.6 us (2%)
    pallas_call x1, Pallas kernels, lstm_call(): pl.pallas_call(functools.partial(lstm_kernel, n, chunk), out_shape=(sds((...  297 us
    all_to_all x1, starting transfers between devices, local(): lax.all_to_all(jnp.concatenate([grad_stored, grad_stored]).reshape(-1, gr...  75.4 us
    ppermute x2, waiting for transfers between devices, to_ranks(): lax.ppermute(value, ('pipe', 'dp'), rank_pairs(lax.axis_size('dp'), off))  64.1 us
    all_gather x1, waiting for transfers between devices, local(): lax.all_gather(jnp.concatenate([mine, proj_blocks], axis=1).astype(BF), (...  46 us
    all_to_all x1, waiting for transfers between devices, local(): lax.all_to_all(jnp.broadcast_to(summed[KMAX * CDIM * cols:][:share], (eve...  34.2 us
    all_gather x3, blocking collectives, both_halves(): lax.all_gather(value, 'pipe').reshape(2, tokens, blocks, half // blocks)  27.2 us
    all_to_all x1, starting transfers between devices, local(): lax.all_to_all(pair, ('dir', 'dp'), 0, 0).reshape(holders * tokens, -1)  26.6 us
    ppermute x7, starting transfers between devices, exchange(): lax.ppermute(blocks[off], 'dp', [(i, (i + off) % n) for i in range(n)])  20.8 us
  transfers between devices with their start and end apart: 29, of which 10 were waited for; matrix products, arithmetic and copies ran while one was open for 21% of the time, Pallas kernels for 33%

profile of v9, /device:TPU:3, one launch (start us, length us, event | category | flops | bytes accessed | tf_op | source)
XLA Modules:
  0.0 943.0 jit_solution(10238282806315790580)
XLA Ops:
  12.0 6.5 all-to-all-start
  18.6 6.2 split_cells.1
  27.0 12.1 %gather_fusion = bf16[6400,16]{1,0:T(8,128)(2,1)S(1)} fusion(bf16[262,16]{1,0:T(8,128)(2,1)S(1)} %copy.242, s32[7168]{0:T(1024)S(1)} %pad_clamp_fusion), kind=kCustom, calls=%fused_computation.clone | custom fusion | bytes 435200 | tf_op jit(solution)/shard_map/jit(_take)/gather | solution.py:49
  45.5 10.8 %select_reduce_fusion = (f32[128,1024]{1,0:T(8,128)S(1)}, f32[128,50,1024]{2,0,1:T(8,128)}) fusion(pred[50,1024]{1,0:T(8,128)(4,1)S(1)} %iota_compare_fusion.6, bf16[128,50,112]{0,2,1:T(8,128)(2,1)S(1)} %slice_dynamic-update-slice_fusion, s32[1024]{0:T(1024)S(1)} %add_bitcast_fusion, s32[112]{0:T(128)S(1)} %and_select_fusion, ...), kind=kOutput, calls=%fused_computation.5 | convolution fusion | flops 1481785344 | bytes 28463620 | tf_op jit(solution)/shard_map/bpk,kf->bpf/dot_general | solution.py:51
  56.3 14.6 %fusion = (f32[128,1024]{1,0:T(8,128)}, f32[128,1024]{1,0:T(8,128)S(1)}) fusion(f32[128,50,1024]{2,0,1:T(8,128)} %get-tuple-element.212, f32[128,1024]{1,0:T(8,128)S(1)} %get-tuple-element.211, pred[50,1024]{1,0:T(8,128)(4,1)S(1)} %iota_compare_fusion.6, f32[128,1024]{1,0:T(8,128)S(1)} %is-finite_select_fusion.1), kind=kLoop, calls=%fused_computation.4 | loop fusion | flops 32505856 | bytes 28362752 | tf_op jit(solution)/shard_map/reduce_sum | solution.py:529
  71.2 8.2 all_gather.32
  84.8 46.0 %all-gather.7.cloned.1.call-done = bf16[2,2304,2048]{2,1,0:T(8,128)(2,1)} async-done(((bf16[2,2304,128]{2,1,0:T(8,128)(2,1)}), bf16[2,2304,2048]{2,1,0:T(8,128)(2,1)}) %all-gather.7.cloned.1.call-update) | async-done | bytes 18874384 | tf_op jit(solution)/shard_map/all_gather | solution.py:587
  145.5 10.8 %all-gather = bf16[256,1024]{1,0:T(8,128)(2,1)S(1)} all-gather(bf16[128,1024]{1,0:T(8,128)(2,1)S(1)} %get-tuple-element.184), channel_id=2, replica_groups=mesh['pipe'=2,'dir'=2,'dp'=8] {'pipe'}, dimensions={0}, use_global_device_ids=true | all-gather | bytes 786432 | tf_op jit(solution)/shard_map/all_gather | solution.py:522
  162.8 8.1 all-gather.1
  180.7 11.9 %all_gather.37 = bf16[16,16,512]{2,1,0:T(8,128)(2,1)S(1)} all-gather(bf16[4,16,512]{2,1,0:T(8,128)(2,1)S(1)} %bitcast.305), channel_id=1, replica_groups=mesh['pipe'=2,'dir'=2,'dp'=8] {'dir','pipe'}, dimensions={0}, use_global_device_ids=true | all-gather | bytes 327680 | tf_op jit(solution)/shard_map/all_gather | solution.py:652
  198.5 64.1 %collective-permute-done.3.bias = f32[1,2048]{1,0:T(1,128)S(1)} collective-permute-done((f32[1,2048]{1,0:T(1,128)S(1)}, f32[1,2048]{1,0:T(1,128)S(1)}, u32[]{:S(2)}, u32[]{:S(2)}) %collective-permute-start.3) | collective-permute-done | bytes 8224 | tf_op jit(solution)/shard_map/ppermute | solution.py:501
  278.3 296.9 %relay_lstm.1 = (bf16[16,16,512]{2,1,0:T(8,128)(2,1)}, f32[16,16,512]{2,1,0:T(8,128)}, f32[1,2048]{1,0:T(1,128)}, f32[512,512]{1,0:T(8,128)}, bf16[128,2048]{1,0...) custom-call(bf16[16,16,512]{2,1,0:T(8,128)(2,1)} %copy-done.66, ...), custom_call_target="tpu_custom_call" | custom-call | flops 299999985664 | bytes 67108864 | tf_op jit(solution)/shard_map/relay_lstm/pallas_call | solution.py:363
  582.9 13.1 %collective-permute-start.9 = (bf16[128,2048]{1,0:T(8,128)(2,1)}, bf16[128,2048]{1,0:T(8,128)(2,1)}, u32[]{:S(2)}, u32[]{:S(2)}) collective-permute-start(bf16[128,2048]{1,0:T(8,128)(2,1)} %get-tuple-element.79), channel_id=1, source_target_pairs={{0,3},{1,4},{2,5},{3,6},{4,7},{5,0},{6,1},{7,2},{8,11},{9,12},{10,... | collective-permute-start | bytes 1572872 | tf_op jit(solution)/shard_map/ppermute | solution.py:485
  599.8 75.4 %all-to-all-start.2 = ((bf16[4,128,512]{2,1,0:T(8,128)(2,1)}), bf16[4,128,512]{2,1,0:T(8,128)(2,1)S(1)}, u32[]{:S(2)}, u32[]{:S(2)}) async-start(bf16[4,128,512]{2,1,0:T(8,128)(2,1)} %bitcast.37), calls=%async_computation.2 | async-start | bytes 1048576 | tf_op jit(solution)/shard_map/all_to_all | solution.py:689
  676.0 6.3 all-to-all-done.2
  684.5 6.3 fusion.1
  702.5 7.2 fusion.5
  742.7 26.6 %all-to-all-start.3 = ((bf16[16,64,640]{2,1,0:T(8,128)(2,1)}), bf16[16,64,640]{2,1,0:T(8,128)(2,1)}, u32[]{:S(2)}, u32[]{:S(2)}) async-start(bf16[16,64,640]{2,1,0:T(8,128)(2,1)} %pad_maximum_fusion.1), calls=%async_computation.3 | async-start | bytes 2621440 | tf_op jit(solution)/shard_map/all_to_all | solution.py:747
  769.3 11.8 %multiply_convert_fusion = bf16[128,50,1024]{2,0,1:T(8,128)(2,1)S(1)} fusion(f32[128,50,1024]{2,0,1:T(8,128)} %get-tuple-element.212, f32[128,1024]{1,0:T(8,128)S(1)} %copy-done.19, f32[128,1024]{1,0:T(8,128)S(1)} %copy-done.4, f32[128,1024]{1,0:T(8,128)S(1)} %fusion.41, pred[50,1024]{1,0:T(8,128)(4,1)S(1)} %copy-done.39), kind=kLoop, calls=%fused_computation.1 | loop fusion | flops 32768000 | bytes 40945664 | tf_op jit(solution)/shard_map/convert_element_type | solution.py:530
  800.0 8.1 all-to-all-done.3
  814.0 8.8 collective-permute-start.15
  833.0 10.2 %all-to-all-start.4 = ((bf16[32,2,4864]{2,1,0:T(2,128)(2,1)}), bf16[32,2,4864]{2,1,0:T(2,128)(2,1)S(1)}, u32[]{:S(2)}, u32[]{:S(2)}) async-start(bf16[32,2,4864]{2,1,0:T(2,128)(2,1)} %reshape.688), calls=%async_computation.4 | async-start | bytes 1245184 | tf_op jit(solution)/shard_map/all_to_all | solution.py:779
  870.9 11.2 %collective-permute-done.16 = bf16[512,512]{1,0:T(8,128)(2,1)} collective-permute-done((bf16[512,512]{1,0:T(8,128)(2,1)}, bf16[512,512]{1,0:T(8,128)(2,1)}, u32[]{:S(2)}, u32[]{:S(2)}) %collective-permute-start.16) | collective-permute-done | bytes 524320 | tf_op jit(solution)/shard_map/ppermute | solution.py:506
  892.9 34.2 %all-to-all-done.5 = f32[32,1,512]{2,1,0:T(1,128)S(1)} async-done(((f32[32,1,512]{2,1,0:T(1,128)}), f32[32,1,512]{2,1,0:T(1,128)S(1)}, u32[]{:S(2)}, u32[]{:S(2)}) %all-to-all-start.5) | async-done | bytes 65568 | tf_op jit(solution)/shard_map/all_to_all | solution.py:815
  (377 shorter events, 211.9 us)
Async XLA Ops:
  7.2 123.6 %all-gather.7.cloned.1.call-start = ((), (), s32[]{:S(2)}) async-start(), calls=%async_computation.6 | async-start | bytes 20054016 | tf_op jit(solution)/shard_map/all_gather | solution.py:587
  12.0 33.4 %all-to-all-start = ((bf16[16,112,128]{2,1,0:T(8,128)(2,1)}), bf16[16,112,128]{2,1,0:T(8,128)(2,1)S(1)}, u32[]{:S(2)}, u32[]{:S(2)}) async-start(bf16[16,112,128]{2,1,0:T(8,128)(2,1)} %broadcast_in_dim.267), calls=%async_computation | async-start | bytes 917504 | tf_op jit(solution)/shard_map/all_to_all | solution.py:590
  24.8 54.9 %collective-permute-start = (bf16[4,128,2048]{2,1,0:T(8,128)(2,1)}, bf16[4,128,2048]{2,1,0:T(8,128)(2,1)}, u32[]{:S(2)}, u32[]{:S(2)}) collective-permute-start(bf16[4,128,2048]{2,1,0:T(8,128)(2,1)} %get-tuple-element.63), channel_id=1, source_target_pairs={{0,16},{16,0},{1,17},{17,1},{2,18},{18,2},{3,19},{19,3},{4,20},{20... | collective-permute-start | bytes 6291464 | tf_op jit(solution)/shard_map/ppermute | solution.py:479
  130.8 132.6 %all-to-all-start.1 = ((bf16[8,128,2048]{2,1,0:T(8,128)(2,1)}), bf16[8,128,2048]{2,1,0:T(8,128)(2,1)}, u32[]{:S(2)}, u32[]{:S(2)}) async-start(bf16[8,128,2048]{2,1,0:T(8,128)(2,1)} %pad_maximum_fusion), calls=%async_computation.1 | async-start | bytes 8388608 | tf_op jit(solution)/shard_map/all_to_all | solution.py:632
  135.5 462.2 %all-gather.9.cloned.1.call-start = ((), (), s32[]{:S(2)}) async-start(), calls=%async_computation.7 | async-start | bytes 4456448 | tf_op jit(solution)/shard_map/all_gather | solution.py:668
  135.6 127.7 %collective-permute-start.2 = (bf16[768,512]{0,1:T(8,128)(2,1)}, bf16[768,512]{0,1:T(8,128)(2,1)}, u32[]{:S(2)}, u32[]{:S(2)}) collective-permute-start(bf16[768,512]{0,1:T(8,128)(2,1)} %pad_maximum_fusion.4), channel_id=1, source_target_pairs={{0,0},{1,1},{2,2},{3,3},{4,16},{5,17},{6,18},{7,19},{16,4},{17,5},... | collective-permute-start | bytes 2359304 | tf_op jit(solution)/shard_map/ppermute | solution.py:501
  193.0 69.6 %collective-permute-start.1 = (bf16[16,16,512]{2,1,0:T(8,128)(2,1)S(1)}, bf16[16,16,512]{2,1,0:T(8,128)(2,1)S(1)}, u32[]{:S(2)}, u32[]{:S(2)}) collective-permute-start(bf16[16,16,512]{2,1,0:T(8,128)(2,1)S(1)} %bitcast.300), channel_id=1, source_target_pairs={{0,4},{1,5},{2,6},{3,7},{20,20},{21,21},{22,22},{23,23},{8,12},{9,... | collective-permute-start | bytes 786440 | tf_op jit(solution)/shard_map/ppermute | solution.py:657
  193.7 68.9 %collective-permute-start.3 = (f32[1,2048]{1,0:T(1,128)S(1)}, f32[1,2048]{1,0:T(1,128)S(1)}, u32[]{:S(2)}, u32[]{:S(2)}) collective-permute-start(f32[1,2048]{1,0:T(1,128)S(1)} %bitcast.311), channel_id=1, source_target_pairs={{0,0},{1,1},{2,2},{3,3},{4,16},{5,17},{6,18},{7,19},{16,4},{17,5},... | collective-permute-start | bytes 24584 | tf_op jit(solution)/shard_map/ppermute | solution.py:501
  266.3 331.4 %all-gather.11.cloned.1.call-start = ((), (), s32[]{:S(2)}) async-start(), calls=%async_computation.8 | async-start | bytes 4456448 | tf_op jit(solution)/shard_map/all_gather | solution.py:668
  581.5 144.6 %collective-permute-start.7 = (bf16[128,2048]{1,0:T(8,128)(2,1)}, bf16[128,2048]{1,0:T(8,128)(2,1)}, u32[]{:S(2)}, u32[]{:S(2)}) collective-permute-start(bf16[128,2048]{1,0:T(8,128)(2,1)} %get-tuple-element.77), channel_id=1, source_target_pairs={{0,1},{1,2},{2,3},{3,4},{4,5},{5,6},{6,7},{7,0},{8,9},{9,10},{10,1... | collective-permute-start | bytes 1572872 | tf_op jit(solution)/shard_map/ppermute | solution.py:485
  582.2 146.9 %collective-permute-start.8 = (bf16[128,2048]{1,0:T(8,128)(2,1)}, bf16[128,2048]{1,0:T(8,128)(2,1)}, u32[]{:S(2)}, u32[]{:S(2)}) collective-permute-start(bf16[128,2048]{1,0:T(8,128)(2,1)} %get-tuple-element.78), channel_id=1, source_target_pairs={{0,2},{1,3},{2,4},{3,5},{4,6},{5,7},{6,0},{7,1},{8,10},{9,11},{10,... | collective-permute-start | bytes 1572872 | tf_op jit(solution)/shard_map/ppermute | solution.py:485
  582.9 147.5 %collective-permute-start.9 = (bf16[128,2048]{1,0:T(8,128)(2,1)}, bf16[128,2048]{1,0:T(8,128)(2,1)}, u32[]{:S(2)}, u32[]{:S(2)}) collective-permute-start(bf16[128,2048]{1,0:T(8,128)(2,1)} %get-tuple-element.79), channel_id=1, source_target_pairs={{0,3},{1,4},{2,5},{3,6},{4,7},{5,0},{6,1},{7,2},{8,11},{9,12},{10,... | collective-permute-start | bytes 1572872 | tf_op jit(solution)/shard_map/ppermute | solution.py:485
  596.0 136.3 %collective-permute-start.10 = (bf16[128,2048]{1,0:T(8,128)(2,1)}, bf16[128,2048]{1,0:T(8,128)(2,1)}, u32[]{:S(2)}, u32[]{:S(2)}) collective-permute-start(bf16[128,2048]{1,0:T(8,128)(2,1)} %get-tuple-element.80), channel_id=1, source_target_pairs={{0,4},{1,5},{2,6},{3,7},{4,0},{5,1},{6,2},{7,3},{8,12},{9,13},{10,... | collective-permute-start | bytes 1572872 | tf_op jit(solution)/shard_map/ppermute | solution.py:485
  599.8 82.5 %all-to-all-start.2 = ((bf16[4,128,512]{2,1,0:T(8,128)(2,1)}), bf16[4,128,512]{2,1,0:T(8,128)(2,1)S(1)}, u32[]{:S(2)}, u32[]{:S(2)}) async-start(bf16[4,128,512]{2,1,0:T(8,128)(2,1)} %bitcast.37), calls=%async_computation.2 | async-start | bytes 1048576 | tf_op jit(solution)/shard_map/all_to_all | solution.py:689
  675.2 136.8 %all-gather.13.cloned.1.call-start = ((), (), s32[]{:S(2)}) async-start(), calls=%async_computation.9 | async-start | bytes 1114112 | tf_op jit(solution)/shard_map/all_gather | solution.py:697
  726.1 73.9 %collective-permute-start.12 = (bf16[128,2048]{1,0:T(8,128)(2,1)}, bf16[128,2048]{1,0:T(8,128)(2,1)}, u32[]{:S(2)}, u32[]{:S(2)}) collective-permute-start(bf16[128,2048]{1,0:T(8,128)(2,1)} %get-tuple-element.87), channel_id=1, source_target_pairs={{0,5},{1,6},{2,7},{3,0},{4,1},{5,2},{6,3},{7,4},{8,13},{9,14},{10,... | collective-permute-start | bytes 1572872 | tf_op jit(solution)/shard_map/ppermute | solution.py:485
  729.1 70.9 %collective-permute-start.13 = (bf16[128,2048]{1,0:T(8,128)(2,1)}, bf16[128,2048]{1,0:T(8,128)(2,1)}, u32[]{:S(2)}, u32[]{:S(2)}) collective-permute-start(bf16[128,2048]{1,0:T(8,128)(2,1)} %get-tuple-element.88), channel_id=1, source_target_pairs={{0,6},{1,7},{2,0},{3,1},{4,2},{5,3},{6,4},{7,5},{8,14},{9,15},{10,... | collective-permute-start | bytes 1572872 | tf_op jit(solution)/shard_map/ppermute | solution.py:485
  730.4 69.6 %collective-permute-start.14 = (bf16[128,2048]{1,0:T(8,128)(2,1)}, bf16[128,2048]{1,0:T(8,128)(2,1)}, u32[]{:S(2)}, u32[]{:S(2)}) collective-permute-start(bf16[128,2048]{1,0:T(8,128)(2,1)} %get-tuple-element.89), channel_id=1, source_target_pairs={{0,7},{1,0},{2,1},{3,2},{4,3},{5,4},{6,5},{7,6},{8,15},{9,8},{10,9... | collective-permute-start | bytes 1572872 | tf_op jit(solution)/shard_map/ppermute | solution.py:485
  742.7 65.4 %all-to-all-start.3 = ((bf16[16,64,640]{2,1,0:T(8,128)(2,1)}), bf16[16,64,640]{2,1,0:T(8,128)(2,1)}, u32[]{:S(2)}, u32[]{:S(2)}) async-start(bf16[16,64,640]{2,1,0:T(8,128)(2,1)} %pad_maximum_fusion.1), calls=%async_computation.3 | async-start | bytes 2621440 | tf_op jit(solution)/shard_map/all_to_all | solution.py:747
  814.0 56.9 %collective-permute-start.15 = (bf16[16,16,512]{2,1,0:T(8,128)(2,1)}, bf16[16,16,512]{2,1,0:T(8,128)(2,1)}, u32[]{:S(2)}, u32[]{:S(2)}) collective-permute-start(bf16[16,16,512]{2,1,0:T(8,128)(2,1)} %get-tuple-element.94), channel_id=1, source_target_pairs={{0,0},{1,1},{2,2},{3,3},{16,4},{17,5},{18,6},{19,7},{4,16},{5,17},... | collective-permute-start | bytes 786440 | tf_op jit(solution)/shard_map/ppermute | solution.py:506
  833.0 36.1 %all-to-all-start.4 = ((bf16[32,2,4864]{2,1,0:T(2,128)(2,1)}), bf16[32,2,4864]{2,1,0:T(2,128)(2,1)S(1)}, u32[]{:S(2)}, u32[]{:S(2)}) async-start(bf16[32,2,4864]{2,1,0:T(2,128)(2,1)} %reshape.688), calls=%async_computation.4 | async-start | bytes 1245184 | tf_op jit(solution)/shard_map/all_to_all | solution.py:779
  845.3 36.8 %collective-permute-start.16 = (bf16[512,512]{1,0:T(8,128)(2,1)}, bf16[512,512]{1,0:T(8,128)(2,1)}, u32[]{:S(2)}, u32[]{:S(2)}) collective-permute-start(bf16[512,512]{1,0:T(8,128)(2,1)} %convert_element_type.262), channel_id=1, source_target_pairs={{0,0},{1,1},{2,2},{3,3},{16,4},{17,5},{18,6},{19,7},{4,16},{5,17},... | collective-permute-start | bytes 1572872 | tf_op jit(solution)/shard_map/ppermute | solution.py:506
  854.5 75.8 %collective-permute-start.18 = (bf16[4,128,2048]{2,1,0:T(8,128)(2,1)}, bf16[4,128,2048]{2,1,0:T(8,128)(2,1)}, u32[]{:S(2)}, u32[]{:S(2)}) collective-permute-start(bf16[4,128,2048]{2,1,0:T(8,128)(2,1)} %get-tuple-element.110), channel_id=1, source_target_pairs={{0,16},{16,0},{1,17},{17,1},{2,18},{18,2},{3,19},{19,3},{4,20},{20... | collective-permute-start | bytes 6291464 | tf_op jit(solution)/shard_map/ppermute | solution.py:479
  884.1 43.0 %all-to-all-start.5 = ((f32[32,1,512]{2,1,0:T(1,128)}), f32[32,1,512]{2,1,0:T(1,128)S(1)}, u32[]{:S(2)}, u32[]{:S(2)}) async-start(f32[32,1,512]{2,1,0:T(1,128)} %broadcast_in_dim.305), calls=%async_computation.5 | async-start | bytes 131072 | tf_op jit(solution)/shard_map/all_to_all | solution.py:815
  (75 other events, 1996.5 us)
Sparse Core Ops, SparseCore 0:
  11.3 119.4 all-gather.6
  266.4 56.7 all-gather.8
  325.4 63.7 all-gather.10
  694.6 93.0 all-gather.12

commit v10 on v9

--- a/solution.py
+++ b/solution.py
@@ -624,11 +624,21 @@
             jnp.where(pipe == 0, gate_came, gate_kept),
         ]
     )
-    gate_low, gathered, features_low, bias_own, moved = lax.optimization_barrier(
-        (gate_low, gathered, features_low, bias_own, moved)
+    direct, local_part = moved[: moved.shape[0] // 2], moved[moved.shape[0] // 2 :]
+    swapped = swap_pipes(local_part)
+    gate_low, gathered, features_low, bias_own, direct, swapped = lax.optimization_barrier(
+        (gate_low, gathered, features_low, bias_own, direct, swapped)
     )
     bias_own = to_ranks(bias_own, 0)
-    moved = to_ranks(moved, 0)
+    wing = n // 2
+    swapped = lax.ppermute(
+        swapped,
+        ("pipe", "dp"),
+        [(k, wing + k) for k in range(wing)] + [(n + wing + k, n + k) for k in range(wing)],
+    )
+    moved = jnp.concatenate(
+        [to_ranks(direct, 0), jnp.where(lax.div(me, wing) == pipe, local_part, swapped)]
+    )
     gate_own = lax.all_to_all(gate_low, "dp", 0, 0).reshape(2 * width, 4 * cell)
     highway_half = gathered[:, :FILTERS]
     proj_full = gathered[:, FILTERS:].reshape(pieces, proj_rows, holders, sub)
@@ -653,7 +663,6 @@
         encoded.astype(BF).reshape(quarter, steps, width), ("dir", "pipe"), axis=0, tiled=True
     )
     inputs = jnp.einsum("rts,rsd->trd", own_order, encoded_own, preferred_element_type=BF)
-    wing = n // 2
     inputs = lax.ppermute(
         inputs,
         ("pipe", "dp"),
@@ -749,8 +758,8 @@
         (grad_conv, pair, grad_gate, out_own, grad_cell)
     )
     gate_kept, gate_given = sort_blocks(grad_gate)
+    gate_given, pair = lax.optimization_barrier((gate_given, pair))
     gate_came = swap_pipes(gate_given)
-    grad_gate = join_cells(gate_kept, gate_came)
     small = (
         grad_table,
         spread(jnp.sum(grad_before, axis=0)),
@@ -779,7 +788,10 @@
     summed = jnp.sum(lax.all_to_all(packed, ALL, 0, 0).astype(F32), axis=0)
     out_own = from_ranks(out_own, 0)
     grad_cell = from_ranks(grad_cell.astype(BF), 0)
-    summed, out_own, grad_cell = lax.optimization_barrier((summed, out_own, grad_cell))
+    summed, out_own, grad_cell, gate_came = lax.optimization_barrier(
+        (summed, out_own, grad_cell, gate_came)
+    )
+    grad_gate = join_cells(gate_kept, gate_came)
     activations = jnp.einsum("rts,srd->rtd", own_order, out_own, preferred_element_type=BF)
     grad_cell = grad_cell.astype(F32)
     grad_conv = summed[: KMAX * CDIM * cols].reshape(KMAX * CDIM, cols)

time: 953 us -> 955 us (level)
  local copies, waits for them, and re-layouts: 84.6 us -> 72.3 us
    ppermute x2, waiting for transfers between devices: 64.1 us -> 0.01 us  [to_ranks(): lax.ppermute(value, ('pipe', 'dp'), rank_pairs(lax.axis_size('dp'), off))]
    all_to_all x1, waiting for transfers between devices: 5.49 us -> 64.7 us  [local(): summed = jnp.sum(lax.all_to_all(packed, ALL, 0, 0).astype(F32), axis=0)]
    ppermute x0 -> x1, waiting for transfers between devices: none -> 49.9 us  [local(): lax.ppermute(swapped, ('pipe', 'dp'), [(k, wing + k) for k in range(wing)...]
    all_to_all x1, waiting for transfers between devices: 34.2 us -> 0.01 us  [local(): lax.all_to_all(jnp.broadcast_to(summed[KMAX * CDIM * cols:][:share], (eve...]
    ppermute x3, waiting for transfers between devices: 12.8 us -> 1.13 us  [from_ranks(): lax.ppermute(value, ('pipe', 'dp'), [(there, here) for here, there in pai...]
  transfers between devices with their start and end apart: 29 -> 31, of which waited for: 10 -> 9; matrix products, arithmetic and copies ran while one was open for 21% -> 20% of each run, Pallas kernels for 33% -> 34%
where the time goes in v10:
time: 955 us; the launch traced here: 944 us
  Pallas kernels  322 us (34%)
  waiting for transfers between devices  183 us (19%)
  starting transfers between devices  176 us (18%)
  local copies, waits for them, and re-layouts  72.3 us (8%)
  other arithmetic  67.9 us (7%)
  matrix products  67.3 us (7%)
  blocking collectives  40.4 us (4%)
  between operations  15.6 us (2%)
    pallas_call x1, Pallas kernels, lstm_call(): pl.pallas_call(functools.partial(lstm_kernel, n, chunk), out_shape=(sds((...  305 us
    all_to_all x1, starting transfers between devices, local(): lax.all_to_all(jnp.concatenate([grad_stored, grad_stored]).reshape(-1, gr...  76 us
    all_to_all x1, waiting for transfers between devices, local(): summed = jnp.sum(lax.all_to_all(packed, ALL, 0, 0).astype(F32), axis=0)  64.7 us
    ppermute x1, waiting for transfers between devices, local(): lax.ppermute(swapped, ('pipe', 'dp'), [(k, wing + k) for k in range(wing)...  49.9 us
    all_gather x1, waiting for transfers between devices, local(): lax.all_gather(jnp.concatenate([mine, proj_blocks], axis=1).astype(BF), (...  43.5 us
    all_gather x3, blocking collectives, both_halves(): lax.all_gather(value, 'pipe').reshape(2, tokens, blocks, half // blocks)  27.1 us
    all_to_all x1, starting transfers between devices, local(): lax.all_to_all(pair, ('dir', 'dp'), 0, 0).reshape(holders * tokens, -1)  26.1 us
    ppermute x7, starting transfers between devices, exchange(): lax.ppermute(blocks[off], 'dp', [(i, (i + off) % n) for i in range(n)])  21.3 us
  transfers between devices with their start and end apart: 31, of which 9 were waited for; matrix products, arithmetic and copies ran while one was open for 20% of the time, Pallas kernels for 34%

profile of v10, /device:TPU:3, one launch (start us, length us, event | category | flops | bytes accessed | tf_op | source)
XLA Modules:
  0.0 944.4 jit_solution(5715349642127904862)
XLA Ops:
  12.1 6.5 all-to-all-start
  29.6 12.1 %gather_fusion = bf16[6400,16]{1,0:T(8,128)(2,1)S(1)} fusion(bf16[262,16]{1,0:T(8,128)(2,1)S(1)} %copy.242, s32[7168]{0:T(1024)S(1)} %pad_clamp_fusion), kind=kCustom, calls=%fused_computation.clone | custom fusion | bytes 435200 | tf_op jit(solution)/shard_map/jit(_take)/gather | solution.py:49
  45.8 10.8 %select_reduce_fusion = (f32[128,1024]{1,0:T(8,128)S(1)}, f32[128,50,1024]{2,0,1:T(8,128)}) fusion(pred[50,1024]{1,0:T(8,128)(4,1)S(1)} %iota_compare_fusion.6, bf16[128,50,112]{0,2,1:T(8,128)(2,1)S(1)} %slice_dynamic-update-slice_fusion, s32[1024]{0:T(1024)S(1)} %add_bitcast_fusion, s32[112]{0:T(128)S(1)} %and_select_fusion, ...), kind=kOutput, calls=%fused_computation.5 | convolution fusion | flops 1481785344 | bytes 28463620 | tf_op jit(solution)/shard_map/bpk,kf->bpf/dot_general | solution.py:51
  56.6 14.6 %fusion = (f32[128,1024]{1,0:T(8,128)}, f32[128,1024]{1,0:T(8,128)S(1)}) fusion(f32[128,50,1024]{2,0,1:T(8,128)} %get-tuple-element.220, f32[128,1024]{1,0:T(8,128)S(1)} %get-tuple-element.219, pred[50,1024]{1,0:T(8,128)(4,1)S(1)} %iota_compare_fusion.6, f32[128,1024]{1,0:T(8,128)S(1)} %is-finite_select_fusion.1), kind=kLoop, calls=%fused_computation.4 | loop fusion | flops 32505856 | bytes 28362752 | tf_op jit(solution)/shard_map/reduce_sum | solution.py:529
  71.5 10.5 %all_gather.32 = bf16[2,128,1024]{2,1,0:T(8,128)(2,1)S(1)} all-gather(bf16[1,128,1024]{2,1,0:T(8,128)(2,1)S(1)} %multiply_convert_fusion.5), channel_id=1, replica_groups=mesh['pipe'=2,'dir'=2,'dp'=8] {'pipe'}, dimensions={0}, use_global_device_ids=true | all-gather | bytes 786432 | tf_op jit(solution)/shard_map/all_gather | solution.py:522
  87.3 43.5 %all-gather.7.cloned.1.call-done = bf16[2,2304,2048]{2,1,0:T(8,128)(2,1)} async-done(((bf16[2,2304,128]{2,1,0:T(8,128)(2,1)}), bf16[2,2304,2048]{2,1,0:T(8,128)(2,1)}) %all-gather.7.cloned.1.call-update) | async-done | bytes 18874384 | tf_op jit(solution)/shard_map/all_gather | solution.py:587
  149.8 9.8 %all-gather = bf16[256,1024]{1,0:T(8,128)(2,1)S(1)} all-gather(bf16[128,1024]{1,0:T(8,128)(2,1)S(1)} %get-tuple-element.192), channel_id=2, replica_groups=mesh['pipe'=2,'dir'=2,'dp'=8] {'pipe'}, dimensions={0}, use_global_device_ids=true | all-gather | bytes 786432 | tf_op jit(solution)/shard_map/all_gather | solution.py:522
  166.3 6.8 all-gather.1
  181.1 13.3 %all_gather.37 = bf16[16,16,512]{2,1,0:T(8,128)(2,1)S(1)} all-gather(bf16[4,16,512]{2,1,0:T(8,128)(2,1)S(1)} %bitcast.307), channel_id=1, replica_groups=mesh['pipe'=2,'dir'=2,'dp'=8] {'dir','pipe'}, dimensions={0}, use_global_device_ids=true | all-gather | bytes 327680 | tf_op jit(solution)/shard_map/all_gather | solution.py:662
  195.5 49.9 %collective-permute-done.4 = bf16[384,512]{0,1:T(8,128)(2,1)} collective-permute-done((bf16[384,512]{0,1:T(8,128)(2,1)}, bf16[384,512]{0,1:T(8,128)(2,1)}, u32[]{:S(2)}, u32[]{:S(2)}) %collective-permute-start.4) | collective-permute-done | bytes 393248 | tf_op jit(solution)/shard_map/ppermute | solution.py:634
  261.8 305.0 %relay_lstm.1 = (bf16[16,16,512]{2,1,0:T(8,128)(2,1)}, f32[16,16,512]{2,1,0:T(8,128)}, f32[1,2048]{1,0:T(1,128)}, f32[512,512]{1,0:T(8,128)}, bf16[128,2048]{1,0...) custom-call(bf16[16,16,512]{2,1,0:T(8,128)(2,1)} %copy-done.68, ...), custom_call_target="tpu_custom_call" | custom-call | flops 299999985664 | bytes 67108864 | tf_op jit(solution)/shard_map/relay_lstm/pallas_call | solution.py:363
  574.6 13.5 %collective-permute-start.11 = (bf16[128,2048]{1,0:T(8,128)(2,1)}, bf16[128,2048]{1,0:T(8,128)(2,1)}, u32[]{:S(2)}, u32[]{:S(2)}) collective-permute-start(bf16[128,2048]{1,0:T(8,128)(2,1)} %get-tuple-element.84), channel_id=1, source_target_pairs={{0,3},{1,4},{2,5},{3,6},{4,7},{5,0},{6,1},{7,2},{8,11},{9,12},{10,... | collective-permute-start | bytes 1572872 | tf_op jit(solution)/shard_map/ppermute | solution.py:485
  591.3 76.0 %all-to-all-start.2 = ((bf16[4,128,512]{2,1,0:T(8,128)(2,1)}), bf16[4,128,512]{2,1,0:T(8,128)(2,1)S(1)}, u32[]{:S(2)}, u32[]{:S(2)}) async-start(bf16[4,128,512]{2,1,0:T(8,128)(2,1)} %bitcast.38), calls=%async_computation.2 | async-start | bytes 1048576 | tf_op jit(solution)/shard_map/all_to_all | solution.py:698
  668.1 6.3 all-to-all-done.2
  676.6 6.3 fusion.1
  694.5 7.2 fusion.5
  733.5 26.1 %all-to-all-start.3 = ((bf16[16,64,640]{2,1,0:T(8,128)(2,1)}), bf16[16,64,640]{2,1,0:T(8,128)(2,1)S(1)}, u32[]{:S(2)}, u32[]{:S(2)}) async-start(bf16[16,64,640]{2,1,0:T(8,128)(2,1)} %pad_maximum_fusion.1), calls=%async_computation.3 | async-start | bytes 2621440 | tf_op jit(solution)/shard_map/all_to_all | solution.py:756
  759.6 15.8 %multiply_convert_fusion = bf16[128,50,1024]{2,0,1:T(8,128)(2,1)} fusion(f32[128,50,1024]{2,0,1:T(8,128)} %get-tuple-element.220, f32[128,1024]{1,0:T(8,128)S(1)} %copy-done.17, f32[128,1024]{1,0:T(8,128)S(1)} %copy-done.3, f32[128,1024]{1,0:T(8,128)S(1)} %fusion.41, pred[50,1024]{1,0:T(8,128)(4,1)S(1)} %copy-done.38), kind=kLoop, calls=%fused_computation.1 | loop fusion | flops 32768000 | bytes 40945664 | tf_op jit(solution)/shard_map/convert_element_type | solution.py:530
  775.5 7.3 fusion.109
  786.0 6.0 fusion.25
  792.1 8.8 all-to-all-done.3
  806.2 8.1 collective-permute-start.17
  829.0 9.9 %all-to-all-start.4 = ((bf16[32,2,4864]{2,1,0:T(2,128)(2,1)}), bf16[32,2,4864]{2,1,0:T(2,128)(2,1)S(1)}, u32[]{:S(2)}, u32[]{:S(2)}) async-start(bf16[32,2,4864]{2,1,0:T(2,128)(2,1)} %reshape.689), calls=%async_computation.4 | async-start | bytes 1245184 | tf_op jit(solution)/shard_map/all_to_all | solution.py:788
  853.6 64.7 %all-to-all-done.4 = bf16[32,2,4864]{2,1,0:T(2,128)(2,1)S(1)} async-done(((bf16[32,2,4864]{2,1,0:T(2,128)(2,1)}), bf16[32,2,4864]{2,1,0:T(2,128)(2,1)S(1)}, u32[]{:S(2)}, u32[]{:S(2)}) %all-to-all-start.4) | async-done | bytes 622624 | tf_op jit(solution)/shard_map/all_to_all | solution.py:788
  (388 shorter events, 190.0 us)
Async XLA Ops:
  7.2 123.6 %all-gather.7.cloned.1.call-start = ((), (), s32[]{:S(2)}) async-start(), calls=%async_computation.6 | async-start | bytes 20054016 | tf_op jit(solution)/shard_map/all_gather | solution.py:587
  20.4 67.0 %collective-permute-start.1 = (bf16[384,512]{0,1:T(8,128)(2,1)}, bf16[384,512]{0,1:T(8,128)(2,1)}, u32[]{:S(2)}, u32[]{:S(2)}) collective-permute-start(bf16[384,512]{0,1:T(8,128)(2,1)} %pad_maximum_fusion.9), channel_id=1, source_target_pairs={{0,16},{16,0},{1,17},{17,1},{2,18},{18,2},{3,19},{19,3},{4,20},{20... | collective-permute-start | bytes 1179656 | tf_op jit(solution)/shard_map/ppermute | solution.py:479
  26.6 55.7 %collective-permute-start = (bf16[4,128,2048]{2,1,0:T(8,128)(2,1)}, bf16[4,128,2048]{2,1,0:T(8,128)(2,1)}, u32[]{:S(2)}, u32[]{:S(2)}) collective-permute-start(bf16[4,128,2048]{2,1,0:T(8,128)(2,1)} %get-tuple-element.67), channel_id=1, source_target_pairs={{0,16},{16,0},{1,17},{17,1},{2,18},{18,2},{3,19},{19,3},{4,20},{20... | collective-permute-start | bytes 6291464 | tf_op jit(solution)/shard_map/ppermute | solution.py:479
  130.8 116.8 %all-to-all-start.1 = ((bf16[8,128,2048]{2,1,0:T(8,128)(2,1)}), bf16[8,128,2048]{2,1,0:T(8,128)(2,1)}, u32[]{:S(2)}, u32[]{:S(2)}) async-start(bf16[8,128,2048]{2,1,0:T(8,128)(2,1)} %pad_maximum_fusion), calls=%async_computation.1 | async-start | bytes 8388608 | tf_op jit(solution)/shard_map/all_to_all | solution.py:642
  135.5 453.7 %all-gather.9.cloned.1.call-start = ((), (), s32[]{:S(2)}) async-start(), calls=%async_computation.7 | async-start | bytes 4456448 | tf_op jit(solution)/shard_map/all_gather | solution.py:677
  135.7 111.9 %collective-permute-start.5 = (f32[1,2048]{1,0:T(1,128)S(1)}, f32[1,2048]{1,0:T(1,128)S(1)}, u32[]{:S(2)}, u32[]{:S(2)}) collective-permute-start(f32[1,2048]{1,0:T(1,128)S(1)} %bitcast.313), channel_id=1, source_target_pairs={{0,0},{1,1},{2,2},{3,3},{4,16},{5,17},{6,18},{7,19},{16,4},{17,5},... | collective-permute-start | bytes 24584 | tf_op jit(solution)/shard_map/ppermute | solution.py:501
  139.7 106.7 %collective-permute-start.3 = (bf16[384,512]{0,1:T(8,128)(2,1)}, bf16[384,512]{0,1:T(8,128)(2,1)}, u32[]{:S(2)}, u32[]{:S(2)}) collective-permute-start(bf16[384,512]{0,1:T(8,128)(2,1)} %slice_bitcast_fusion), channel_id=1, source_target_pairs={{0,0},{1,1},{2,2},{3,3},{4,16},{5,17},{6,18},{7,19},{16,4},{17,5},... | collective-permute-start | bytes 1179656 | tf_op jit(solution)/shard_map/ppermute | solution.py:501
  142.8 102.7 %collective-permute-start.4 = (bf16[384,512]{0,1:T(8,128)(2,1)}, bf16[384,512]{0,1:T(8,128)(2,1)}, u32[]{:S(2)}, u32[]{:S(2)}) collective-permute-start(bf16[384,512]{0,1:T(8,128)(2,1)} %collective-permute-done.1), channel_id=1, source_target_pairs={{0,4},{1,5},{2,6},{3,7},{20,16},{21,17},{22,18},{23,19},{8,12},{9,... | collective-permute-start | bytes 1179656 | tf_op jit(solution)/shard_map/ppermute | solution.py:634
  194.8 52.8 %collective-permute-start.2 = (bf16[16,16,512]{2,1,0:T(8,128)(2,1)S(1)}, bf16[16,16,512]{2,1,0:T(8,128)(2,1)S(1)}, u32[]{:S(2)}, u32[]{:S(2)}) collective-permute-start(bf16[16,16,512]{2,1,0:T(8,128)(2,1)S(1)} %bitcast.302), channel_id=1, source_target_pairs={{0,4},{1,5},{2,6},{3,7},{20,20},{21,21},{22,22},{23,23},{8,12},{9,... | collective-permute-start | bytes 786440 | tf_op jit(solution)/shard_map/ppermute | solution.py:666
  251.7 337.5 %all-gather.11.cloned.1.call-start = ((), (), s32[]{:S(2)}) async-start(), calls=%async_computation.8 | async-start | bytes 4456448 | tf_op jit(solution)/shard_map/all_gather | solution.py:677
  573.0 145.7 %collective-permute-start.9 = (bf16[128,2048]{1,0:T(8,128)(2,1)}, bf16[128,2048]{1,0:T(8,128)(2,1)}, u32[]{:S(2)}, u32[]{:S(2)}) collective-permute-start(bf16[128,2048]{1,0:T(8,128)(2,1)} %get-tuple-element.82), channel_id=1, source_target_pairs={{0,1},{1,2},{2,3},{3,4},{4,5},{5,6},{6,7},{7,0},{8,9},{9,10},{10,1... | collective-permute-start | bytes 1572872 | tf_op jit(solution)/shard_map/ppermute | solution.py:485
  573.9 147.8 %collective-permute-start.10 = (bf16[128,2048]{1,0:T(8,128)(2,1)}, bf16[128,2048]{1,0:T(8,128)(2,1)}, u32[]{:S(2)}, u32[]{:S(2)}) collective-permute-start(bf16[128,2048]{1,0:T(8,128)(2,1)} %get-tuple-element.83), channel_id=1, source_target_pairs={{0,2},{1,3},{2,4},{3,5},{4,6},{5,7},{6,0},{7,1},{8,10},{9,11},{10,... | collective-permute-start | bytes 1572872 | tf_op jit(solution)/shard_map/ppermute | solution.py:485
  574.6 148.3 %collective-permute-start.11 = (bf16[128,2048]{1,0:T(8,128)(2,1)}, bf16[128,2048]{1,0:T(8,128)(2,1)}, u32[]{:S(2)}, u32[]{:S(2)}) collective-permute-start(bf16[128,2048]{1,0:T(8,128)(2,1)} %get-tuple-element.84), channel_id=1, source_target_pairs={{0,3},{1,4},{2,5},{3,6},{4,7},{5,0},{6,1},{7,2},{8,11},{9,12},{10,... | collective-permute-start | bytes 1572872 | tf_op jit(solution)/shard_map/ppermute | solution.py:485
  588.1 136.9 %collective-permute-start.12 = (bf16[128,2048]{1,0:T(8,128)(2,1)}, bf16[128,2048]{1,0:T(8,128)(2,1)}, u32[]{:S(2)}, u32[]{:S(2)}) collective-permute-start(bf16[128,2048]{1,0:T(8,128)(2,1)} %get-tuple-element.85), channel_id=1, source_target_pairs={{0,4},{1,5},{2,6},{3,7},{4,0},{5,1},{6,2},{7,3},{8,12},{9,13},{10,... | collective-permute-start | bytes 1572872 | tf_op jit(solution)/shard_map/ppermute | solution.py:485
  591.3 83.1 %all-to-all-start.2 = ((bf16[4,128,512]{2,1,0:T(8,128)(2,1)}), bf16[4,128,512]{2,1,0:T(8,128)(2,1)S(1)}, u32[]{:S(2)}, u32[]{:S(2)}) async-start(bf16[4,128,512]{2,1,0:T(8,128)(2,1)} %bitcast.38), calls=%async_computation.2 | async-start | bytes 1048576 | tf_op jit(solution)/shard_map/all_to_all | solution.py:698
  667.3 149.5 %all-gather.13.cloned.1.call-start = ((), (), s32[]{:S(2)}) async-start(), calls=%async_computation.9 | async-start | bytes 1114112 | tf_op jit(solution)/shard_map/all_gather | solution.py:706
  718.7 73.4 %collective-permute-start.14 = (bf16[128,2048]{1,0:T(8,128)(2,1)}, bf16[128,2048]{1,0:T(8,128)(2,1)}, u32[]{:S(2)}, u32[]{:S(2)}) collective-permute-start(bf16[128,2048]{1,0:T(8,128)(2,1)} %get-tuple-element.92), channel_id=1, source_target_pairs={{0,5},{1,6},{2,7},{3,0},{4,1},{5,2},{6,3},{7,4},{8,13},{9,14},{10,... | collective-permute-start | bytes 1572872 | tf_op jit(solution)/shard_map/ppermute | solution.py:485
  721.7 70.4 %collective-permute-start.15 = (bf16[128,2048]{1,0:T(8,128)(2,1)}, bf16[128,2048]{1,0:T(8,128)(2,1)}, u32[]{:S(2)}, u32[]{:S(2)}) collective-permute-start(bf16[128,2048]{1,0:T(8,128)(2,1)} %get-tuple-element.93), channel_id=1, source_target_pairs={{0,6},{1,7},{2,0},{3,1},{4,2},{5,3},{6,4},{7,5},{8,14},{9,15},{10,... | collective-permute-start | bytes 1572872 | tf_op jit(solution)/shard_map/ppermute | solution.py:485
  722.9 69.2 %collective-permute-start.16 = (bf16[128,2048]{1,0:T(8,128)(2,1)}, bf16[128,2048]{1,0:T(8,128)(2,1)}, u32[]{:S(2)}, u32[]{:S(2)}) collective-permute-start(bf16[128,2048]{1,0:T(8,128)(2,1)} %get-tuple-element.94), channel_id=1, source_target_pairs={{0,7},{1,0},{2,1},{3,2},{4,3},{5,4},{6,5},{7,6},{8,15},{9,8},{10,9... | collective-permute-start | bytes 1572872 | tf_op jit(solution)/shard_map/ppermute | solution.py:485
  733.5 67.4 %all-to-all-start.3 = ((bf16[16,64,640]{2,1,0:T(8,128)(2,1)}), bf16[16,64,640]{2,1,0:T(8,128)(2,1)S(1)}, u32[]{:S(2)}, u32[]{:S(2)}) async-start(bf16[16,64,640]{2,1,0:T(8,128)(2,1)} %pad_maximum_fusion.1), calls=%async_computation.3 | async-start | bytes 2621440 | tf_op jit(solution)/shard_map/all_to_all | solution.py:756
  806.2 113.8 %collective-permute-start.17 = (bf16[16,16,512]{2,1,0:T(8,128)(2,1)}, bf16[16,16,512]{2,1,0:T(8,128)(2,1)S(1)}, u32[]{:S(2)}, u32[]{:S(2)}) collective-permute-start(bf16[16,16,512]{2,1,0:T(8,128)(2,1)} %get-tuple-element.99), channel_id=1, source_target_pairs={{0,0},{1,1},{2,2},{3,3},{16,4},{17,5},{18,6},{19,7},{4,16},{5,17},... | collective-permute-start | bytes 786440 | tf_op jit(solution)/shard_map/ppermute | solution.py:506
  824.9 95.2 %collective-permute-start.19 = (bf16[4,128,2048]{2,1,0:T(8,128)(2,1)}, bf16[4,128,2048]{2,1,0:T(8,128)(2,1)}, u32[]{:S(2)}, u32[]{:S(2)}) collective-permute-start(bf16[4,128,2048]{2,1,0:T(8,128)(2,1)} %get-tuple-element.111), channel_id=1, source_target_pairs={{0,16},{16,0},{1,17},{17,1},{2,18},{18,2},{3,19},{19,3},{4,20},{20... | collective-permute-start | bytes 6291464 | tf_op jit(solution)/shard_map/ppermute | solution.py:479
  829.0 89.3 %all-to-all-start.4 = ((bf16[32,2,4864]{2,1,0:T(2,128)(2,1)}), bf16[32,2,4864]{2,1,0:T(2,128)(2,1)S(1)}, u32[]{:S(2)}, u32[]{:S(2)}) async-start(bf16[32,2,4864]{2,1,0:T(2,128)(2,1)} %reshape.689), calls=%async_computation.4 | async-start | bytes 1245184 | tf_op jit(solution)/shard_map/all_to_all | solution.py:788
  841.1 79.0 %collective-permute-start.18 = (bf16[512,512]{1,0:T(8,128)(2,1)}, bf16[512,512]{1,0:T(8,128)(2,1)}, u32[]{:S(2)}, u32[]{:S(2)}) collective-permute-start(bf16[512,512]{1,0:T(8,128)(2,1)} %convert_element_type.262), channel_id=1, source_target_pairs={{0,0},{1,1},{2,2},{3,3},{16,4},{17,5},{18,6},{19,7},{4,16},{5,17},... | collective-permute-start | bytes 1572872 | tf_op jit(solution)/shard_map/ppermute | solution.py:506
  (79 other events, 1974.1 us)
Sparse Core Ops, SparseCore 0:
  11.3 119.4 all-gather.6
  251.8 66.1 all-gather.8
  320.2 62.0 all-gather.10
  687.3 93.8 all-gather.12

commit v11 on v10

--- a/solution.py
+++ b/solution.py
@@ -343,7 +343,7 @@
     for off in range(n):
         if off > 1:
             dw_copy(off - 2).wait()
-        at = pl.multiple_of(lax.rem(place + off, n) * each, each)
+        at = pl.multiple_of(lax.rem(me + off, n) * each, each)
         dabuf[off % 2, :each, :] = dwacc[pl.ds(at, each), :].astype(BF)
         dw_copy(off).start()
     for off in range(n - 2, n):
@@ -415,76 +415,32 @@
     )(weight)
 
 
-def sort_blocks(blocks):
+def join_cells(blocks):
     n = len(blocks)
-    wing = n // 2
-
     rows, gates = blocks[0].shape
     cell = gates // 4
 
     def body(*refs):
-        src, (keep, give) = refs[:n], refs[n:]
-        pipe = lax.axis_index("pipe")
+        dst = refs[n]
         for off in range(n):
-            place = lax.rem(lax.axis_index("dp") + (n - off), n)
-            stays = lax.div(place, wing) == pipe
-
-            @pl.when(stays)
-            def _():
-                keep[lax.rem(place, wing)] = src[off][...]
-
-            @pl.when(jnp.logical_not(stays))
-            def _():
-                give[lax.rem(place, wing)] = src[off][...]
-
-    return pl.pallas_call(
-        body,
-        grid=(4,),
-        out_shape=[jax.ShapeDtypeStruct((wing, rows, gates), BF)] * 2,
-        in_specs=[pl.BlockSpec((rows, cell), lambda b: (0, b))] * n,
-        out_specs=[pl.BlockSpec((wing, rows, cell), lambda b: (0, 0, b))] * 2,
-        cost_estimate=pl.CostEstimate(
-            flops=0, bytes_accessed=4 * n * blocks[0].size, transcendentals=0
-        ),
-        name="sort_blocks",
-    )(*blocks)
-
-
-def join_cells(keep, came):
-    wing, rows, gates = keep.shape
-    cell = gates // 4
-    n = 2 * wing
-
-    def body(keep, came, dst):
-        pipe = lax.axis_index("pipe")
-        for k in range(wing):
-            for src, side in ((keep, pipe), (came, 1 - pipe)):
-                at = pl.multiple_of((side * wing + k) * cell, cell)
-                dst[:, pl.ds(at, cell)] = src[k].astype(F32)
+            rank = lax.rem(lax.axis_index("dp") + (n - off), n)
+            dst[:, pl.ds(pl.multiple_of(rank * cell, cell), cell)] = refs[off][...].astype(F32)
 
     return pl.pallas_call(
         body,
         grid=(4,),
         out_shape=jax.ShapeDtypeStruct((rows, n * gates), F32),
-        in_specs=[pl.BlockSpec((wing, rows, cell), lambda b: (0, 0, b))] * 2,
+        in_specs=[pl.BlockSpec((rows, cell), lambda b: (0, b))] * n,
         out_specs=pl.BlockSpec((rows, n * cell), lambda b: (0, b)),
         cost_estimate=pl.CostEstimate(
             flops=0, bytes_accessed=6 * n * rows * gates, transcendentals=0
         ),
         name="join_cells",
-    )(keep, came)
+    )(*blocks)
 
 
 def swap_pipes(value):
     return lax.ppermute(value, "pipe", [(0, 1), (1, 0)])
-
-
-def exchange(blocks):
-    n = len(blocks)
-    return [blocks[0]] + [
-        lax.ppermute(blocks[off], "dp", [(i, (i + off) % n) for i in range(n)])
-        for off in range(1, n)
-    ]
 
 
 def rank_pairs(n, off, layers=(0, 1)):
@@ -687,7 +643,7 @@
         n, inputs, gate_own, bias_own, cell_low, cell_low.T, cot
     )
     dx_own = from_ranks(dx_own.astype(BF), 0, (1,))
-    grad_gate = exchange(grad_gate)
+    grad_gate = [from_ranks(block, off) for off, block in enumerate(grad_gate)]
     dx_own, kept_all = lax.optimization_barrier((dx_own, kept_all))
 
     grad_stored = jnp.einsum(
@@ -754,12 +710,9 @@
     last = jnp.transpose(own_last.reshape(tokens, 2, holders, cols), (2, 0, 1, 3))
     pair = jnp.concatenate([pair, last.reshape(holders, tokens, 2 * cols)], axis=2)
     pair = lax.all_to_all(pair, ("dir", "dp"), 0, 0).reshape(holders * tokens, -1)
-    grad_conv, pair, grad_gate, out_own, grad_cell = lax.optimization_barrier(
-        (grad_conv, pair, grad_gate, out_own, grad_cell)
-    )
-    gate_kept, gate_given = sort_blocks(grad_gate)
-    gate_given, pair = lax.optimization_barrier((gate_given, pair))
-    gate_came = swap_pipes(gate_given)
+    grad_conv, pair, out_own, grad_cell = lax.optimization_barrier(
+        (grad_conv, pair, out_own, grad_cell)
+    )
     small = (
         grad_table,
         spread(jnp.sum(grad_before, axis=0)),
@@ -788,10 +741,8 @@
     summed = jnp.sum(lax.all_to_all(packed, ALL, 0, 0).astype(F32), axis=0)
     out_own = from_ranks(out_own, 0)
     grad_cell = from_ranks(grad_cell.astype(BF), 0)
-    summed, out_own, grad_cell, gate_came = lax.optimization_barrier(
-        (summed, out_own, grad_cell, gate_came)
-    )
-    grad_gate = join_cells(gate_kept, gate_came)
+    summed, grad_gate = lax.optimization_barrier((summed, grad_gate))
+    grad_gate = join_cells(grad_gate)
     activations = jnp.einsum("rts,srd->rtd", own_order, out_own, preferred_element_type=BF)
     grad_cell = grad_cell.astype(F32)
     grad_conv = summed[: KMAX * CDIM * cols].reshape(KMAX * CDIM, cols)

time: 955 us -> 943 us (0.987)
  waiting for transfers between devices: 183 us -> 161 us
  local copies, waits for them, and re-layouts: 72.3 us -> 88.6 us
    all_to_all x1, waiting for transfers between devices: 64.7 us -> 0.01 us  [local(): summed = jnp.sum(lax.all_to_all(packed, ALL, 0, 0).astype(F32), axis=0)]
    ppermute x3 -> x11, waiting for transfers between devices: 1.13 us -> 55.3 us  [from_ranks(): lax.ppermute(value, ('pipe', 'dp'), [(there, here) for here, there in pai...]
    ppermute x3 -> x11, starting transfers between devices: 13.4 us -> 35 us  [from_ranks(): lax.ppermute(value, ('pipe', 'dp'), [(there, here) for here, there in pai...]
    ppermute x7 -> x0, starting transfers between devices: 21.3 us -> none  [exchange(): lax.ppermute(blocks[off], 'dp', [(i, (i + off) % n) for i in range(n)])]
    unnamed x158 -> x170, local copies, waits for them, and re-layouts: 8.08 us -> 18.8 us
  transfers between devices with their start and end apart: 31 -> 31, of which waited for: 9 -> 9; matrix products, arithmetic and copies ran while one was open for 20% -> 21% of each run, Pallas kernels for 34% -> 34%
where the time goes in v11:
time: 943 us; the launch traced here: 933 us
  Pallas kernels  319 us (34%)
  starting transfers between devices  176 us (19%)
  waiting for transfers between devices  161 us (17%)
  local copies, waits for them, and re-layouts  88.6 us (9%)
  other arithmetic  66.6 us (7%)
  matrix products  65.3 us (7%)
  blocking collectives  40.4 us (4%)
  between operations  15.7 us (2%)
    pallas_call x1, Pallas kernels, lstm_call(): pl.pallas_call(functools.partial(lstm_kernel, n, chunk), out_shape=(sds((...  307 us
    all_to_all x1, starting transfers between devices, local(): lax.all_to_all(jnp.concatenate([grad_stored, grad_stored]).reshape(-1, gr...  77.3 us
    ppermute x11, waiting for transfers between devices, from_ranks(): lax.ppermute(value, ('pipe', 'dp'), [(there, here) for here, there in pai...  55.3 us
    ppermute x1, waiting for transfers between devices, local(): lax.ppermute(swapped, ('pipe', 'dp'), [(k, wing + k) for k in range(wing)...  50 us
    all_gather x1, waiting for transfers between devices, local(): lax.all_gather(jnp.concatenate([mine, proj_blocks], axis=1).astype(BF), (...  43.5 us
    ppermute x11, starting transfers between devices, from_ranks(): lax.ppermute(value, ('pipe', 'dp'), [(there, here) for here, there in pai...  35 us
    all_gather x3, blocking collectives, both_halves(): lax.all_gather(value, 'pipe').reshape(2, tokens, blocks, half // blocks)  27.1 us
    all_to_all x1, starting transfers between devices, local(): lax.all_to_all(pair, ('dir', 'dp'), 0, 0).reshape(holders * tokens, -1)  23.1 us
  transfers between devices with their start and end apart: 31, of which 9 were waited for; matrix products, arithmetic and copies ran while one was open for 21% of the time, Pallas kernels for 34%

profile of v11, /device:TPU:3, one launch (start us, length us, event | category | flops | bytes accessed | tf_op | source)
XLA Modules:
  0.0 932.8 jit_solution(8890613761821519015)
XLA Ops:
  12.1 6.5 all-to-all-start
  29.6 12.1 %gather_fusion = bf16[6400,16]{1,0:T(8,128)(2,1)S(1)} fusion(bf16[262,16]{1,0:T(8,128)(2,1)S(1)} %copy.242, s32[7168]{0:T(1024)S(1)} %pad_clamp_fusion), kind=kCustom, calls=%fused_computation.clone | custom fusion | bytes 435200 | tf_op jit(solution)/shard_map/jit(_take)/gather | solution.py:49
  45.8 10.7 %select_reduce_fusion = (f32[128,1024]{1,0:T(8,128)S(1)}, f32[128,50,1024]{2,0,1:T(8,128)}) fusion(pred[50,1024]{1,0:T(8,128)(4,1)S(1)} %iota_compare_fusion.6, bf16[128,50,112]{0,2,1:T(8,128)(2,1)S(1)} %slice_dynamic-update-slice_fusion, s32[1024]{0:T(1024)S(1)} %add_bitcast_fusion, s32[112]{0:T(128)S(1)} %and_select_fusion, ...), kind=kOutput, calls=%fused_computation.5 | convolution fusion | flops 1481785344 | bytes 28463620 | tf_op jit(solution)/shard_map/bpk,kf->bpf/dot_general | solution.py:51
  56.6 14.6 %exponential_reduce_fusion = (f32[128,1024]{1,0:T(8,128)S(1)}, f32[128,1024]{1,0:T(8,128)}) fusion(f32[128,50,1024]{2,0,1:T(8,128)} %get-tuple-element.206, f32[128,1024]{1,0:T(8,128)S(1)} %is-finite_select_fusion.1, pred[50,1024]{1,0:T(8,128)(4,1)S(1)} %iota_compare_fusion.6, f32[128,1024]{1,0:T(8,128)S(1)} %get-tuple-element.205), kind=kLoop, calls=%fused_computation.3 | loop fusion | flops 32505856 | bytes 28362752 | tf_op jit(solution)/shard_map/reduce_sum | solution.py:466
  71.4 10.5 %all_gather.32 = bf16[2,128,1024]{2,1,0:T(8,128)(2,1)S(1)} all-gather(bf16[1,128,1024]{2,1,0:T(8,128)(2,1)S(1)} %multiply_convert_fusion.5), channel_id=1, replica_groups=mesh['pipe'=2,'dir'=2,'dp'=8] {'pipe'}, dimensions={0}, use_global_device_ids=true | all-gather | bytes 786432 | tf_op jit(solution)/shard_map/all_gather | solution.py:478
  87.4 43.5 %all-gather.7.cloned.1.call-done = bf16[2,2304,2048]{2,1,0:T(8,128)(2,1)} async-done(((bf16[2,2304,128]{2,1,0:T(8,128)(2,1)}), bf16[2,2304,2048]{2,1,0:T(8,128)(2,1)}) %all-gather.7.cloned.1.call-update) | async-done | bytes 18874384 | tf_op jit(solution)/shard_map/all_gather | solution.py:543
  149.8 9.8 %all-gather = bf16[256,1024]{1,0:T(8,128)(2,1)S(1)} all-gather(bf16[128,1024]{1,0:T(8,128)(2,1)S(1)} %get-tuple-element.178), channel_id=2, replica_groups=mesh['pipe'=2,'dir'=2,'dp'=8] {'pipe'}, dimensions={0}, use_global_device_ids=true | all-gather | bytes 786432 | tf_op jit(solution)/shard_map/all_gather | solution.py:478
  166.3 6.8 all-gather.1
  181.1 13.3 %all_gather.37 = bf16[16,16,512]{2,1,0:T(8,128)(2,1)S(1)} all-gather(bf16[4,16,512]{2,1,0:T(8,128)(2,1)S(1)} %bitcast.305), channel_id=1, replica_groups=mesh['pipe'=2,'dir'=2,'dp'=8] {'dir','pipe'}, dimensions={0}, use_global_device_ids=true | all-gather | bytes 327680 | tf_op jit(solution)/shard_map/all_gather | solution.py:618
  195.5 50.0 %collective-permute-done.4 = bf16[384,512]{0,1:T(8,128)(2,1)} collective-permute-done((bf16[384,512]{0,1:T(8,128)(2,1)}, bf16[384,512]{0,1:T(8,128)(2,1)}, u32[]{:S(2)}, u32[]{:S(2)}) %collective-permute-start.4) | collective-permute-done | bytes 393248 | tf_op jit(solution)/shard_map/ppermute | solution.py:590
  261.8 306.7 %relay_lstm.1 = (bf16[16,16,512]{2,1,0:T(8,128)(2,1)}, f32[16,16,512]{2,1,0:T(8,128)}, f32[1,2048]{1,0:T(1,128)}, f32[512,512]{1,0:T(8,128)}, bf16[128,2048]{1,0...) custom-call(bf16[16,16,512]{2,1,0:T(8,128)(2,1)} %copy-done.74, ...), custom_call_target="tpu_custom_call" | custom-call | flops 299999985664 | bytes 67108864 | tf_op jit(solution)/shard_map/relay_lstm/pallas_call | solution.py:363
  575.4 14.3 %collective-permute-start.9 = (bf16[128,2048]{1,0:T(8,128)(2,1)}, bf16[128,2048]{1,0:T(8,128)(2,1)}, u32[]{:S(2)}, u32[]{:S(2)}) collective-permute-start(bf16[128,2048]{1,0:T(8,128)(2,1)} %get-tuple-element.75), channel_id=1, source_target_pairs={{19,0},{0,1},{1,2},{2,3},{3,4},{16,5},{17,6},{18,7},{23,16},{4,17}... | collective-permute-start | bytes 1572872 | tf_op jit(solution)/shard_map/ppermute | solution.py:462
  593.9 77.3 %all-to-all-start.2 = ((bf16[4,128,512]{2,1,0:T(8,128)(2,1)}), bf16[4,128,512]{2,1,0:T(8,128)(2,1)S(1)}, u32[]{:S(2)}, u32[]{:S(2)}) async-start(bf16[4,128,512]{2,1,0:T(8,128)(2,1)} %bitcast.38), calls=%async_computation.2 | async-start | bytes 1048576 | tf_op jit(solution)/shard_map/all_to_all | solution.py:654
  672.1 8.3 all-to-all-done.2
  684.1 6.3 fusion.1
  704.0 7.2 fusion.5
  728.9 10.1 %collective-permute-start.15 = (bf16[128,2048]{1,0:T(8,128)(2,1)}, bf16[128,2048]{1,0:T(8,128)(2,1)}, u32[]{:S(2)}, u32[]{:S(2)}) collective-permute-start(bf16[128,2048]{1,0:T(8,128)(2,1)} %get-tuple-element.85), channel_id=1, source_target_pairs={{0,0},{1,1},{2,2},{3,3},{16,4},{17,5},{18,6},{19,7},{4,16},{5,17},... | collective-permute-start | bytes 1572872 | tf_op jit(solution)/shard_map/ppermute | solution.py:462
  746.2 23.1 %all-to-all-start.3 = ((bf16[16,64,640]{2,1,0:T(8,128)(2,1)}), bf16[16,64,640]{2,1,0:T(8,128)(2,1)}, u32[]{:S(2)}, u32[]{:S(2)}) async-start(bf16[16,64,640]{2,1,0:T(8,128)(2,1)} %pad_maximum_fusion.1), calls=%async_computation.3 | async-start | bytes 2621440 | tf_op jit(solution)/shard_map/all_to_all | solution.py:712
  769.4 11.7 %multiply_convert_fusion = bf16[128,50,1024]{2,0,1:T(8,128)(2,1)S(1)} fusion(f32[128,50,1024]{2,0,1:T(8,128)} %get-tuple-element.206, f32[128,1024]{1,0:T(8,128)S(1)} %copy-done.19, f32[128,1024]{1,0:T(8,128)S(1)} %copy-done.4, f32[128,1024]{1,0:T(8,128)S(1)} %fusion.41, pred[50,1024]{1,0:T(8,128)(4,1)S(1)} %copy-done.39), kind=kLoop, calls=%fused_computation.1 | loop fusion | flops 32768000 | bytes 40945664 | tf_op jit(solution)/shard_map/convert_element_type | solution.py:486
  809.1 7.2 all-to-all-start.4
  835.5 19.4 %collective-permute-done.14 = bf16[16,16,512]{2,1,0:T(8,128)(2,1)S(1)} collective-permute-done((bf16[16,16,512]{2,1,0:T(8,128)(2,1)S(1)}, bf16[16,16,512]{2,1,0:T(8,128)(2,1)S(1)}, u32[]{:S(2)}, u32[]{:S(2)}) %collective-permute-start.14) | collective-permute-done | bytes 262176 | tf_op jit(solution)/shard_map/ppermute | solution.py:462
  855.9 21.5 %collective-permute-done.20 = bf16[512,512]{1,0:T(8,128)(2,1)S(1)} collective-permute-done((bf16[512,512]{1,0:T(8,128)(2,1)S(1)}, bf16[512,512]{1,0:T(8,128)(2,1)S(1)}, u32[]{:S(2)}, u32[]{:S(2)}) %collective-permute-start.20) | collective-permute-done | bytes 524320 | tf_op jit(solution)/shard_map/ppermute | solution.py:462
  886.1 14.3 %collective-permute-done.18.refs_7_ = bf16[128,2048]{1,0:T(8,128)(2,1)} collective-permute-done((bf16[128,2048]{1,0:T(8,128)(2,1)}, bf16[128,2048]{1,0:T(8,128)(2,1)}, u32[]{:S(2)}, u32[]{:S(2)}) %collective-permute-start.18) | collective-permute-done | bytes 524320 | tf_op jit(solution)/shard_map/ppermute | solution.py:462
  901.2 9.0 all-to-all-start.5
  (399 shorter events, 202.7 us)
Async XLA Ops:
  7.2 123.6 %all-gather.7.cloned.1.call-start = ((), (), s32[]{:S(2)}) async-start(), calls=%async_computation.6 | async-start | bytes 20054016 | tf_op jit(solution)/shard_map/all_gather | solution.py:543
  12.1 33.7 %all-to-all-start = ((bf16[16,112,128]{2,1,0:T(8,128)(2,1)}), bf16[16,112,128]{2,1,0:T(8,128)(2,1)S(1)}, u32[]{:S(2)}, u32[]{:S(2)}) async-start(bf16[16,112,128]{2,1,0:T(8,128)(2,1)} %broadcast_in_dim.264), calls=%async_computation | async-start | bytes 917504 | tf_op jit(solution)/shard_map/all_to_all | solution.py:546
  20.4 67.0 %collective-permute-start.1 = (bf16[384,512]{0,1:T(8,128)(2,1)}, bf16[384,512]{0,1:T(8,128)(2,1)}, u32[]{:S(2)}, u32[]{:S(2)}) collective-permute-start(bf16[384,512]{0,1:T(8,128)(2,1)} %pad_maximum_fusion.9), channel_id=1, source_target_pairs={{0,16},{16,0},{1,17},{17,1},{2,18},{18,2},{3,19},{19,3},{4,20},{20... | collective-permute-start | bytes 1179656 | tf_op jit(solution)/shard_map/ppermute | solution.py:443
  26.6 55.7 %collective-permute-start = (bf16[4,128,2048]{2,1,0:T(8,128)(2,1)}, bf16[4,128,2048]{2,1,0:T(8,128)(2,1)}, u32[]{:S(2)}, u32[]{:S(2)}) collective-permute-start(bf16[4,128,2048]{2,1,0:T(8,128)(2,1)} %get-tuple-element.60), channel_id=1, source_target_pairs={{0,16},{16,0},{1,17},{17,1},{2,18},{18,2},{3,19},{19,3},{4,20},{20... | collective-permute-start | bytes 6291464 | tf_op jit(solution)/shard_map/ppermute | solution.py:443
  130.8 116.8 %all-to-all-start.1 = ((bf16[8,128,2048]{2,1,0:T(8,128)(2,1)}), bf16[8,128,2048]{2,1,0:T(8,128)(2,1)}, u32[]{:S(2)}, u32[]{:S(2)}) async-start(bf16[8,128,2048]{2,1,0:T(8,128)(2,1)} %pad_maximum_fusion), calls=%async_computation.1 | async-start | bytes 8388608 | tf_op jit(solution)/shard_map/all_to_all | solution.py:598
  135.5 456.2 %all-gather.9.cloned.1.call-start = ((), (), s32[]{:S(2)}) async-start(), calls=%async_computation.7 | async-start | bytes 4456448 | tf_op jit(solution)/shard_map/all_gather | solution.py:633
  135.7 111.9 %collective-permute-start.5 = (f32[1,2048]{1,0:T(1,128)S(1)}, f32[1,2048]{1,0:T(1,128)S(1)}, u32[]{:S(2)}, u32[]{:S(2)}) collective-permute-start(f32[1,2048]{1,0:T(1,128)S(1)} %bitcast.311), channel_id=1, source_target_pairs={{0,0},{1,1},{2,2},{3,3},{4,16},{5,17},{6,18},{7,19},{16,4},{17,5},... | collective-permute-start | bytes 24584 | tf_op jit(solution)/shard_map/ppermute | solution.py:457
  139.8 106.7 %collective-permute-start.3 = (bf16[384,512]{0,1:T(8,128)(2,1)}, bf16[384,512]{0,1:T(8,128)(2,1)}, u32[]{:S(2)}, u32[]{:S(2)}) collective-permute-start(bf16[384,512]{0,1:T(8,128)(2,1)} %slice_bitcast_fusion), channel_id=1, source_target_pairs={{0,0},{1,1},{2,2},{3,3},{4,16},{5,17},{6,18},{7,19},{16,4},{17,5},... | collective-permute-start | bytes 1179656 | tf_op jit(solution)/shard_map/ppermute | solution.py:457
  142.8 102.7 %collective-permute-start.4 = (bf16[384,512]{0,1:T(8,128)(2,1)}, bf16[384,512]{0,1:T(8,128)(2,1)}, u32[]{:S(2)}, u32[]{:S(2)}) collective-permute-start(bf16[384,512]{0,1:T(8,128)(2,1)} %collective-permute-done.1), channel_id=1, source_target_pairs={{0,4},{1,5},{2,6},{3,7},{20,16},{21,17},{22,18},{23,19},{8,12},{9,... | collective-permute-start | bytes 1179656 | tf_op jit(solution)/shard_map/ppermute | solution.py:590
  194.8 52.8 %collective-permute-start.2 = (bf16[16,16,512]{2,1,0:T(8,128)(2,1)S(1)}, bf16[16,16,512]{2,1,0:T(8,128)(2,1)S(1)}, u32[]{:S(2)}, u32[]{:S(2)}) collective-permute-start(bf16[16,16,512]{2,1,0:T(8,128)(2,1)S(1)} %bitcast.300), channel_id=1, source_target_pairs={{0,4},{1,5},{2,6},{3,7},{20,20},{21,21},{22,22},{23,23},{8,12},{9,... | collective-permute-start | bytes 786440 | tf_op jit(solution)/shard_map/ppermute | solution.py:622
  251.8 340.0 %all-gather.11.cloned.1.call-start = ((), (), s32[]{:S(2)}) async-start(), calls=%async_computation.8 | async-start | bytes 4456448 | tf_op jit(solution)/shard_map/all_gather | solution.py:633
  575.4 153.5 %collective-permute-start.9 = (bf16[128,2048]{1,0:T(8,128)(2,1)}, bf16[128,2048]{1,0:T(8,128)(2,1)}, u32[]{:S(2)}, u32[]{:S(2)}) collective-permute-start(bf16[128,2048]{1,0:T(8,128)(2,1)} %get-tuple-element.75), channel_id=1, source_target_pairs={{19,0},{0,1},{1,2},{2,3},{3,4},{16,5},{17,6},{18,7},{23,16},{4,17}... | collective-permute-start | bytes 1572872 | tf_op jit(solution)/shard_map/ppermute | solution.py:462
  589.7 149.3 %collective-permute-start.10 = (bf16[128,2048]{1,0:T(8,128)(2,1)}, bf16[128,2048]{1,0:T(8,128)(2,1)}, u32[]{:S(2)}, u32[]{:S(2)}) collective-permute-start(bf16[128,2048]{1,0:T(8,128)(2,1)} %get-tuple-element.76), channel_id=1, source_target_pairs={{18,0},{19,1},{0,2},{1,3},{2,4},{3,5},{16,6},{17,7},{22,16},{23,17... | collective-permute-start | bytes 1572872 | tf_op jit(solution)/shard_map/ppermute | solution.py:462
  589.7 149.4 %collective-permute-start.11 = (bf16[128,2048]{1,0:T(8,128)(2,1)}, bf16[128,2048]{1,0:T(8,128)(2,1)}, u32[]{:S(2)}, u32[]{:S(2)}) collective-permute-start(bf16[128,2048]{1,0:T(8,128)(2,1)} %get-tuple-element.77), channel_id=1, source_target_pairs={{17,0},{18,1},{19,2},{0,3},{1,4},{2,5},{3,6},{16,7},{21,16},{22,17... | collective-permute-start | bytes 1572872 | tf_op jit(solution)/shard_map/ppermute | solution.py:462
  591.7 147.4 %collective-permute-start.12 = (bf16[128,2048]{1,0:T(8,128)(2,1)}, bf16[128,2048]{1,0:T(8,128)(2,1)}, u32[]{:S(2)}, u32[]{:S(2)}) collective-permute-start(bf16[128,2048]{1,0:T(8,128)(2,1)} %get-tuple-element.78), channel_id=1, source_target_pairs={{16,0},{17,1},{18,2},{19,3},{0,4},{1,5},{2,6},{3,7},{20,16},{21,17... | collective-permute-start | bytes 1572872 | tf_op jit(solution)/shard_map/ppermute | solution.py:462
  593.9 86.5 %all-to-all-start.2 = ((bf16[4,128,512]{2,1,0:T(8,128)(2,1)}), bf16[4,128,512]{2,1,0:T(8,128)(2,1)S(1)}, u32[]{:S(2)}, u32[]{:S(2)}) async-start(bf16[4,128,512]{2,1,0:T(8,128)(2,1)} %bitcast.38), calls=%async_computation.2 | async-start | bytes 1048576 | tf_op jit(solution)/shard_map/all_to_all | solution.py:654
  671.2 132.0 %all-gather.13.cloned.1.call-start = ((), (), s32[]{:S(2)}) async-start(), calls=%async_computation.9 | async-start | bytes 1114112 | tf_op jit(solution)/shard_map/all_gather | solution.py:662
  728.9 157.3 %collective-permute-start.15 = (bf16[128,2048]{1,0:T(8,128)(2,1)}, bf16[128,2048]{1,0:T(8,128)(2,1)}, u32[]{:S(2)}, u32[]{:S(2)}) collective-permute-start(bf16[128,2048]{1,0:T(8,128)(2,1)} %get-tuple-element.85), channel_id=1, source_target_pairs={{0,0},{1,1},{2,2},{3,3},{16,4},{17,5},{18,6},{19,7},{4,16},{5,17},... | collective-permute-start | bytes 1572872 | tf_op jit(solution)/shard_map/ppermute | solution.py:462
  739.0 147.1 %collective-permute-start.16 = (bf16[128,2048]{1,0:T(8,128)(2,1)}, bf16[128,2048]{1,0:T(8,128)(2,1)}, u32[]{:S(2)}, u32[]{:S(2)}) collective-permute-start(bf16[128,2048]{1,0:T(8,128)(2,1)} %get-tuple-element.90), channel_id=1, source_target_pairs={{3,0},{16,1},{17,2},{18,3},{19,4},{0,5},{1,6},{2,7},{7,16},{20,17}... | collective-permute-start | bytes 1572872 | tf_op jit(solution)/shard_map/ppermute | solution.py:462
  746.2 53.7 %all-to-all-start.3 = ((bf16[16,64,640]{2,1,0:T(8,128)(2,1)}), bf16[16,64,640]{2,1,0:T(8,128)(2,1)}, u32[]{:S(2)}, u32[]{:S(2)}) async-start(bf16[16,64,640]{2,1,0:T(8,128)(2,1)} %pad_maximum_fusion.1), calls=%async_computation.3 | async-start | bytes 2621440 | tf_op jit(solution)/shard_map/all_to_all | solution.py:712
  809.1 69.5 %all-to-all-start.4 = ((bf16[32,2,4864]{2,1,0:T(2,128)(2,1)}), bf16[32,2,4864]{2,1,0:T(2,128)(2,1)}, u32[]{:S(2)}, u32[]{:S(2)}) async-start(bf16[32,2,4864]{2,1,0:T(2,128)(2,1)} %reshape.689), calls=%async_computation.4 | async-start | bytes 1245184 | tf_op jit(solution)/shard_map/all_to_all | solution.py:741
  821.5 57.0 %collective-permute-start.19 = (bf16[4352,128]{1,0:T(8,128)(2,1)S(1)}, bf16[4352,128]{1,0:T(8,128)(2,1)S(1)}, u32[]{:S(2)}, u32[]{:S(2)}) collective-permute-start(bf16[4352,128]{1,0:T(8,128)(2,1)S(1)} %pad_maximum_fusion.3), channel_id=1, source_target_pairs={{0,16},{16,0},{1,17},{17,1},{2,18},{18,2},{3,19},{19,3},{4,20},{20... | collective-permute-start | bytes 3342344 | tf_op jit(solution)/shard_map/ppermute | solution.py:774
  829.1 48.3 %collective-permute-start.20 = (bf16[512,512]{1,0:T(8,128)(2,1)S(1)}, bf16[512,512]{1,0:T(8,128)(2,1)S(1)}, u32[]{:S(2)}, u32[]{:S(2)}) collective-permute-start(bf16[512,512]{1,0:T(8,128)(2,1)S(1)} %convert_element_type.266), channel_id=1, source_target_pairs={{0,0},{1,1},{2,2},{3,3},{16,4},{17,5},{18,6},{19,7},{4,16},{5,17},... | collective-permute-start | bytes 1572872 | tf_op jit(solution)/shard_map/ppermute | solution.py:462
  854.9 31.3 %collective-permute-start.17 = (bf16[128,2048]{1,0:T(8,128)(2,1)}, bf16[128,2048]{1,0:T(8,128)(2,1)}, u32[]{:S(2)}, u32[]{:S(2)}) collective-permute-start(bf16[128,2048]{1,0:T(8,128)(2,1)} %get-tuple-element.91), channel_id=1, source_target_pairs={{2,0},{3,1},{16,2},{17,3},{18,4},{19,5},{0,6},{1,7},{6,16},{7,17},... | collective-permute-start | bytes 1572872 | tf_op jit(solution)/shard_map/ppermute | solution.py:462
  (85 other events, 2027.0 us)
Sparse Core Ops, SparseCore 0:
  11.4 119.4 all-gather.6
  251.9 66.0 all-gather.8
  320.2 62.2 all-gather.10
  694.4 50.1 all-gather.12

commit v12 on v11

--- a/solution.py
+++ b/solution.py
@@ -710,8 +710,8 @@
     last = jnp.transpose(own_last.reshape(tokens, 2, holders, cols), (2, 0, 1, 3))
     pair = jnp.concatenate([pair, last.reshape(holders, tokens, 2 * cols)], axis=2)
     pair = lax.all_to_all(pair, ("dir", "dp"), 0, 0).reshape(holders * tokens, -1)
-    grad_conv, pair, out_own, grad_cell = lax.optimization_barrier(
-        (grad_conv, pair, out_own, grad_cell)
+    grad_conv, pair, out_own, grad_cell, grad_gate[5:] = lax.optimization_barrier(
+        (grad_conv, pair, out_own, grad_cell, grad_gate[5:])
     )
     small = (
         grad_table,

time: 943 us -> 947 us (level)
  starting transfers between devices: 176 us -> 206 us
  waiting for transfers between devices: 161 us -> 136 us
    ppermute x11, waiting for transfers between devices: 55.3 us -> 29.6 us  [from_ranks(): lax.ppermute(value, ('pipe', 'dp'), [(there, here) for here, there in pai...]
    all_to_all x1, starting transfers between devices: 23.1 us -> 47.5 us  [local(): lax.all_to_all(pair, ('dir', 'dp'), 0, 0).reshape(holders * tokens, -1)]
    ppermute x11, starting transfers between devices: 35 us -> 44.9 us  [from_ranks(): lax.ppermute(value, ('pipe', 'dp'), [(there, here) for here, there in pai...]
  transfers between devices with their start and end apart: 31 -> 31, of which waited for: 9 -> 7; matrix products, arithmetic and copies ran while one was open for 21% -> 21% of each run, Pallas kernels for 34% -> 34%
where the time goes in v12:
time: 947 us; the launch traced here: 937 us
  Pallas kernels  319 us (34%)
  starting transfers between devices  206 us (22%)
  waiting for transfers between devices  136 us (14%)
  local copies, waits for them, and re-layouts  88.7 us (9%)
  other arithmetic  66.6 us (7%)
  matrix products  65.3 us (7%)
  blocking collectives  40.4 us (4%)
  between operations  15.7 us (2%)
    pallas_call x1, Pallas kernels, lstm_call(): pl.pallas_call(functools.partial(lstm_kernel, n, chunk), out_shape=(sds((...  307 us
    all_to_all x1, starting transfers between devices, local(): lax.all_to_all(jnp.concatenate([grad_stored, grad_stored]).reshape(-1, gr...  77.5 us
    ppermute x1, waiting for transfers between devices, local(): lax.ppermute(swapped, ('pipe', 'dp'), [(k, wing + k) for k in range(wing)...  50 us
    all_to_all x1, starting transfers between devices, local(): lax.all_to_all(pair, ('dir', 'dp'), 0, 0).reshape(holders * tokens, -1)  47.5 us
    ppermute x11, starting transfers between devices, from_ranks(): lax.ppermute(value, ('pipe', 'dp'), [(there, here) for here, there in pai...  44.9 us
    all_gather x1, waiting for transfers between devices, local(): lax.all_gather(jnp.concatenate([mine, proj_blocks], axis=1).astype(BF), (...  43.5 us
    ppermute x11, waiting for transfers between devices, from_ranks(): lax.ppermute(value, ('pipe', 'dp'), [(there, here) for here, there in pai...  29.6 us
    all_gather x3, blocking collectives, both_halves(): lax.all_gather(value, 'pipe').reshape(2, tokens, blocks, half // blocks)  27.1 us
  transfers between devices with their start and end apart: 31, of which 7 were waited for; matrix products, arithmetic and copies ran while one was open for 21% of the time, Pallas kernels for 34%

profile of v12, /device:TPU:3, one launch (start us, length us, event | category | flops | bytes accessed | tf_op | source)
XLA Modules:
  0.0 937.2 jit_solution(826071120968590234)
XLA Ops:
  12.1 6.5 all-to-all-start
  29.6 12.1 %gather_fusion = bf16[6400,16]{1,0:T(8,128)(2,1)S(1)} fusion(bf16[262,16]{1,0:T(8,128)(2,1)S(1)} %copy.242, s32[7168]{0:T(1024)S(1)} %pad_clamp_fusion), kind=kCustom, calls=%fused_computation.clone | custom fusion | bytes 435200 | tf_op jit(solution)/shard_map/jit(_take)/gather | solution.py:49
  45.8 10.7 %select_reduce_fusion = (f32[128,1024]{1,0:T(8,128)S(1)}, f32[128,50,1024]{2,0,1:T(8,128)}) fusion(pred[50,1024]{1,0:T(8,128)(4,1)S(1)} %iota_compare_fusion.6, bf16[128,50,112]{0,2,1:T(8,128)(2,1)S(1)} %slice_dynamic-update-slice_fusion, s32[1024]{0:T(1024)S(1)} %add_bitcast_fusion, s32[112]{0:T(128)S(1)} %and_select_fusion, ...), kind=kOutput, calls=%fused_computation.5 | convolution fusion | flops 1481785344 | bytes 28463620 | tf_op jit(solution)/shard_map/bpk,kf->bpf/dot_general | solution.py:51
  56.6 14.6 %exponential_reduce_fusion = (f32[128,1024]{1,0:T(8,128)S(1)}, f32[128,1024]{1,0:T(8,128)}) fusion(f32[128,50,1024]{2,0,1:T(8,128)} %get-tuple-element.212, f32[128,1024]{1,0:T(8,128)S(1)} %is-finite_select_fusion.1, pred[50,1024]{1,0:T(8,128)(4,1)S(1)} %iota_compare_fusion.6, f32[128,1024]{1,0:T(8,128)S(1)} %get-tuple-element.211), kind=kLoop, calls=%fused_computation.3 | loop fusion | flops 32505856 | bytes 28362752 | tf_op jit(solution)/shard_map/reduce_sum | solution.py:466
  71.5 10.5 %all_gather.32 = bf16[2,128,1024]{2,1,0:T(8,128)(2,1)S(1)} all-gather(bf16[1,128,1024]{2,1,0:T(8,128)(2,1)S(1)} %multiply_convert_fusion.5), channel_id=1, replica_groups=mesh['pipe'=2,'dir'=2,'dp'=8] {'pipe'}, dimensions={0}, use_global_device_ids=true | all-gather | bytes 786432 | tf_op jit(solution)/shard_map/all_gather | solution.py:478
  87.4 43.5 %all-gather.7.cloned.1.call-done = bf16[2,2304,2048]{2,1,0:T(8,128)(2,1)} async-done(((bf16[2,2304,128]{2,1,0:T(8,128)(2,1)}), bf16[2,2304,2048]{2,1,0:T(8,128)(2,1)}) %all-gather.7.cloned.1.call-update) | async-done | bytes 18874384 | tf_op jit(solution)/shard_map/all_gather | solution.py:543
  149.8 9.8 %all-gather = bf16[256,1024]{1,0:T(8,128)(2,1)S(1)} all-gather(bf16[128,1024]{1,0:T(8,128)(2,1)S(1)} %get-tuple-element.184), channel_id=2, replica_groups=mesh['pipe'=2,'dir'=2,'dp'=8] {'pipe'}, dimensions={0}, use_global_device_ids=true | all-gather | bytes 786432 | tf_op jit(solution)/shard_map/all_gather | solution.py:478
  166.3 6.8 all-gather.1
  181.1 13.3 %all_gather.37 = bf16[16,16,512]{2,1,0:T(8,128)(2,1)S(1)} all-gather(bf16[4,16,512]{2,1,0:T(8,128)(2,1)S(1)} %bitcast.305), channel_id=1, replica_groups=mesh['pipe'=2,'dir'=2,'dp'=8] {'dir','pipe'}, dimensions={0}, use_global_device_ids=true | all-gather | bytes 327680 | tf_op jit(solution)/shard_map/all_gather | solution.py:618
  195.5 50.0 %collective-permute-done.4 = bf16[384,512]{0,1:T(8,128)(2,1)} collective-permute-done((bf16[384,512]{0,1:T(8,128)(2,1)}, bf16[384,512]{0,1:T(8,128)(2,1)}, u32[]{:S(2)}, u32[]{:S(2)}) %collective-permute-start.4) | collective-permute-done | bytes 393248 | tf_op jit(solution)/shard_map/ppermute | solution.py:590
  261.8 306.6 %relay_lstm.1 = (bf16[16,16,512]{2,1,0:T(8,128)(2,1)}, f32[16,16,512]{2,1,0:T(8,128)}, f32[1,2048]{1,0:T(1,128)}, f32[512,512]{1,0:T(8,128)}, bf16[128,2048]{1,0...) custom-call(bf16[16,16,512]{2,1,0:T(8,128)(2,1)} %copy-done.74, ...), custom_call_target="tpu_custom_call" | custom-call | flops 299999985664 | bytes 67108864 | tf_op jit(solution)/shard_map/relay_lstm/pallas_call | solution.py:363
  575.3 14.9 %collective-permute-start.9 = (bf16[128,2048]{1,0:T(8,128)(2,1)}, bf16[128,2048]{1,0:T(8,128)(2,1)}, u32[]{:S(2)}, u32[]{:S(2)}) collective-permute-start(bf16[128,2048]{1,0:T(8,128)(2,1)} %get-tuple-element.78), channel_id=1, source_target_pairs={{19,0},{0,1},{1,2},{2,3},{3,4},{16,5},{17,6},{18,7},{23,16},{4,17}... | collective-permute-start | bytes 1572872 | tf_op jit(solution)/shard_map/ppermute | solution.py:462
  594.4 77.5 %all-to-all-start.2 = ((bf16[4,128,512]{2,1,0:T(8,128)(2,1)}), bf16[4,128,512]{2,1,0:T(8,128)(2,1)S(1)}, u32[]{:S(2)}, u32[]{:S(2)}) async-start(bf16[4,128,512]{2,1,0:T(8,128)(2,1)} %bitcast.38), calls=%async_computation.2 | async-start | bytes 1048576 | tf_op jit(solution)/shard_map/all_to_all | solution.py:654
  672.7 8.2 all-to-all-done.2
  684.7 6.3 fusion.1
  704.6 7.2 fusion.5
  729.6 8.8 collective-permute-start.15
  738.4 8.7 collective-permute-start.16
  756.1 47.5 %all-to-all-start.3 = ((bf16[16,64,640]{2,1,0:T(8,128)(2,1)}), bf16[16,64,640]{2,1,0:T(8,128)(2,1)}, u32[]{:S(2)}, u32[]{:S(2)}) async-start(bf16[16,64,640]{2,1,0:T(8,128)(2,1)} %pad_maximum_fusion.1), calls=%async_computation.3 | async-start | bytes 2621440 | tf_op jit(solution)/shard_map/all_to_all | solution.py:712
  803.7 11.7 %multiply_convert_fusion = bf16[128,50,1024]{2,0,1:T(8,128)(2,1)S(1)} fusion(f32[128,50,1024]{2,0,1:T(8,128)} %get-tuple-element.212, f32[128,1024]{1,0:T(8,128)S(1)} %copy-done.19, f32[128,1024]{1,0:T(8,128)S(1)} %copy-done.4, f32[128,1024]{1,0:T(8,128)S(1)} %fusion.41, pred[50,1024]{1,0:T(8,128)(4,1)S(1)} %copy-done.39), kind=kLoop, calls=%fused_computation.1 | loop fusion | flops 32768000 | bytes 40945664 | tf_op jit(solution)/shard_map/convert_element_type | solution.py:486
  828.2 6.0 fusion.25
  843.5 7.2 all-to-all-start.4
  869.8 19.4 %collective-permute-done.17 = bf16[16,16,512]{2,1,0:T(8,128)(2,1)S(1)} collective-permute-done((bf16[16,16,512]{2,1,0:T(8,128)(2,1)S(1)}, bf16[16,16,512]{2,1,0:T(8,128)(2,1)S(1)}, u32[]{:S(2)}, u32[]{:S(2)}) %collective-permute-start.17) | collective-permute-done | bytes 262176 | tf_op jit(solution)/shard_map/ppermute | solution.py:462
  890.2 10.2 %collective-permute-done.20 = bf16[512,512]{1,0:T(8,128)(2,1)S(1)} collective-permute-done((bf16[512,512]{1,0:T(8,128)(2,1)S(1)}, bf16[512,512]{1,0:T(8,128)(2,1)S(1)}, u32[]{:S(2)}, u32[]{:S(2)}) %collective-permute-start.20) | collective-permute-done | bytes 524320 | tf_op jit(solution)/shard_map/ppermute | solution.py:462
  (399 shorter events, 203.4 us)
Async XLA Ops:
  7.2 123.6 %all-gather.7.cloned.1.call-start = ((), (), s32[]{:S(2)}) async-start(), calls=%async_computation.6 | async-start | bytes 20054016 | tf_op jit(solution)/shard_map/all_gather | solution.py:543
  20.4 67.0 %collective-permute-start.1 = (bf16[384,512]{0,1:T(8,128)(2,1)}, bf16[384,512]{0,1:T(8,128)(2,1)}, u32[]{:S(2)}, u32[]{:S(2)}) collective-permute-start(bf16[384,512]{0,1:T(8,128)(2,1)} %pad_maximum_fusion.9), channel_id=1, source_target_pairs={{0,16},{16,0},{1,17},{17,1},{2,18},{18,2},{3,19},{19,3},{4,20},{20... | collective-permute-start | bytes 1179656 | tf_op jit(solution)/shard_map/ppermute | solution.py:443
  26.6 55.7 %collective-permute-start = (bf16[4,128,2048]{2,1,0:T(8,128)(2,1)}, bf16[4,128,2048]{2,1,0:T(8,128)(2,1)}, u32[]{:S(2)}, u32[]{:S(2)}) collective-permute-start(bf16[4,128,2048]{2,1,0:T(8,128)(2,1)} %get-tuple-element.63), channel_id=1, source_target_pairs={{0,16},{16,0},{1,17},{17,1},{2,18},{18,2},{3,19},{19,3},{4,20},{20... | collective-permute-start | bytes 6291464 | tf_op jit(solution)/shard_map/ppermute | solution.py:443
  130.8 116.8 %all-to-all-start.1 = ((bf16[8,128,2048]{2,1,0:T(8,128)(2,1)}), bf16[8,128,2048]{2,1,0:T(8,128)(2,1)}, u32[]{:S(2)}, u32[]{:S(2)}) async-start(bf16[8,128,2048]{2,1,0:T(8,128)(2,1)} %pad_maximum_fusion), calls=%async_computation.1 | async-start | bytes 8388608 | tf_op jit(solution)/shard_map/all_to_all | solution.py:598
  135.5 456.7 %all-gather.9.cloned.1.call-start = ((), (), s32[]{:S(2)}) async-start(), calls=%async_computation.7 | async-start | bytes 4456448 | tf_op jit(solution)/shard_map/all_gather | solution.py:633
  135.7 111.9 %collective-permute-start.5 = (f32[1,2048]{1,0:T(1,128)S(1)}, f32[1,2048]{1,0:T(1,128)S(1)}, u32[]{:S(2)}, u32[]{:S(2)}) collective-permute-start(f32[1,2048]{1,0:T(1,128)S(1)} %bitcast.311), channel_id=1, source_target_pairs={{0,0},{1,1},{2,2},{3,3},{4,16},{5,17},{6,18},{7,19},{16,4},{17,5},... | collective-permute-start | bytes 24584 | tf_op jit(solution)/shard_map/ppermute | solution.py:457
  139.8 106.7 %collective-permute-start.3 = (bf16[384,512]{0,1:T(8,128)(2,1)}, bf16[384,512]{0,1:T(8,128)(2,1)}, u32[]{:S(2)}, u32[]{:S(2)}) collective-permute-start(bf16[384,512]{0,1:T(8,128)(2,1)} %slice_bitcast_fusion), channel_id=1, source_target_pairs={{0,0},{1,1},{2,2},{3,3},{4,16},{5,17},{6,18},{7,19},{16,4},{17,5},... | collective-permute-start | bytes 1179656 | tf_op jit(solution)/shard_map/ppermute | solution.py:457
  142.8 102.7 %collective-permute-start.4 = (bf16[384,512]{0,1:T(8,128)(2,1)}, bf16[384,512]{0,1:T(8,128)(2,1)}, u32[]{:S(2)}, u32[]{:S(2)}) collective-permute-start(bf16[384,512]{0,1:T(8,128)(2,1)} %collective-permute-done.1), channel_id=1, source_target_pairs={{0,4},{1,5},{2,6},{3,7},{20,16},{21,17},{22,18},{23,19},{8,12},{9,... | collective-permute-start | bytes 1179656 | tf_op jit(solution)/shard_map/ppermute | solution.py:590
  194.8 52.8 %collective-permute-start.2 = (bf16[16,16,512]{2,1,0:T(8,128)(2,1)S(1)}, bf16[16,16,512]{2,1,0:T(8,128)(2,1)S(1)}, u32[]{:S(2)}, u32[]{:S(2)}) collective-permute-start(bf16[16,16,512]{2,1,0:T(8,128)(2,1)S(1)} %bitcast.300), channel_id=1, source_target_pairs={{0,4},{1,5},{2,6},{3,7},{20,20},{21,21},{22,22},{23,23},{8,12},{9,... | collective-permute-start | bytes 786440 | tf_op jit(solution)/shard_map/ppermute | solution.py:622
  251.8 340.5 %all-gather.11.cloned.1.call-start = ((), (), s32[]{:S(2)}) async-start(), calls=%async_computation.8 | async-start | bytes 4456448 | tf_op jit(solution)/shard_map/all_gather | solution.py:633
  575.3 154.1 %collective-permute-start.9 = (bf16[128,2048]{1,0:T(8,128)(2,1)}, bf16[128,2048]{1,0:T(8,128)(2,1)}, u32[]{:S(2)}, u32[]{:S(2)}) collective-permute-start(bf16[128,2048]{1,0:T(8,128)(2,1)} %get-tuple-element.78), channel_id=1, source_target_pairs={{19,0},{0,1},{1,2},{2,3},{3,4},{16,5},{17,6},{18,7},{23,16},{4,17}... | collective-permute-start | bytes 1572872 | tf_op jit(solution)/shard_map/ppermute | solution.py:462
  590.2 139.3 %collective-permute-start.10 = (bf16[128,2048]{1,0:T(8,128)(2,1)}, bf16[128,2048]{1,0:T(8,128)(2,1)}, u32[]{:S(2)}, u32[]{:S(2)}) collective-permute-start(bf16[128,2048]{1,0:T(8,128)(2,1)} %get-tuple-element.79), channel_id=1, source_target_pairs={{18,0},{19,1},{0,2},{1,3},{2,4},{3,5},{16,6},{17,7},{22,16},{23,17... | collective-permute-start | bytes 1572872 | tf_op jit(solution)/shard_map/ppermute | solution.py:462
  590.2 148.1 %collective-permute-start.11 = (bf16[128,2048]{1,0:T(8,128)(2,1)}, bf16[128,2048]{1,0:T(8,128)(2,1)}, u32[]{:S(2)}, u32[]{:S(2)}) collective-permute-start(bf16[128,2048]{1,0:T(8,128)(2,1)} %get-tuple-element.80), channel_id=1, source_target_pairs={{17,0},{18,1},{19,2},{0,3},{1,4},{2,5},{3,6},{16,7},{21,16},{22,17... | collective-permute-start | bytes 1572872 | tf_op jit(solution)/shard_map/ppermute | solution.py:462
  592.2 154.8 %collective-permute-start.12 = (bf16[128,2048]{1,0:T(8,128)(2,1)}, bf16[128,2048]{1,0:T(8,128)(2,1)}, u32[]{:S(2)}, u32[]{:S(2)}) collective-permute-start(bf16[128,2048]{1,0:T(8,128)(2,1)} %get-tuple-element.81), channel_id=1, source_target_pairs={{16,0},{17,1},{18,2},{19,3},{0,4},{1,5},{2,6},{3,7},{20,16},{21,17... | collective-permute-start | bytes 1572872 | tf_op jit(solution)/shard_map/ppermute | solution.py:462
  594.4 86.6 %all-to-all-start.2 = ((bf16[4,128,512]{2,1,0:T(8,128)(2,1)}), bf16[4,128,512]{2,1,0:T(8,128)(2,1)S(1)}, u32[]{:S(2)}, u32[]{:S(2)}) async-start(bf16[4,128,512]{2,1,0:T(8,128)(2,1)} %bitcast.38), calls=%async_computation.2 | async-start | bytes 1048576 | tf_op jit(solution)/shard_map/all_to_all | solution.py:654
  671.9 165.7 %all-gather.13.cloned.1.call-start = ((), (), s32[]{:S(2)}) async-start(), calls=%async_computation.9 | async-start | bytes 1114112 | tf_op jit(solution)/shard_map/all_gather | solution.py:662
  729.5 104.8 %collective-permute-start.14 = (bf16[128,2048]{1,0:T(8,128)(2,1)}, bf16[128,2048]{1,0:T(8,128)(2,1)}, u32[]{:S(2)}, u32[]{:S(2)}) collective-permute-start(bf16[128,2048]{1,0:T(8,128)(2,1)} %get-tuple-element.85), channel_id=1, source_target_pairs={{3,0},{16,1},{17,2},{18,3},{19,4},{0,5},{1,6},{2,7},{7,16},{20,17}... | collective-permute-start | bytes 1572872 | tf_op jit(solution)/shard_map/ppermute | solution.py:462
  729.6 104.7 %collective-permute-start.15 = (bf16[128,2048]{1,0:T(8,128)(2,1)}, bf16[128,2048]{1,0:T(8,128)(2,1)}, u32[]{:S(2)}, u32[]{:S(2)}) collective-permute-start(bf16[128,2048]{1,0:T(8,128)(2,1)} %get-tuple-element.86), channel_id=1, source_target_pairs={{2,0},{3,1},{16,2},{17,3},{18,4},{19,5},{0,6},{1,7},{6,16},{7,17},... | collective-permute-start | bytes 1572872 | tf_op jit(solution)/shard_map/ppermute | solution.py:462
  738.4 95.9 %collective-permute-start.16 = (bf16[128,2048]{1,0:T(8,128)(2,1)}, bf16[128,2048]{1,0:T(8,128)(2,1)}, u32[]{:S(2)}, u32[]{:S(2)}) collective-permute-start(bf16[128,2048]{1,0:T(8,128)(2,1)} %get-tuple-element.87), channel_id=1, source_target_pairs={{1,0},{2,1},{3,2},{16,3},{17,4},{18,5},{19,6},{0,7},{5,16},{6,17},... | collective-permute-start | bytes 1572872 | tf_op jit(solution)/shard_map/ppermute | solution.py:462
  747.0 162.1 %collective-permute-start.18 = (bf16[128,2048]{1,0:T(8,128)(2,1)}, bf16[128,2048]{1,0:T(8,128)(2,1)}, u32[]{:S(2)}, u32[]{:S(2)}) collective-permute-start(bf16[128,2048]{1,0:T(8,128)(2,1)} %get-tuple-element.91), channel_id=1, source_target_pairs={{0,0},{1,1},{2,2},{3,3},{16,4},{17,5},{18,6},{19,7},{4,16},{5,17},... | collective-permute-start | bytes 1572872 | tf_op jit(solution)/shard_map/ppermute | solution.py:462
  756.1 78.2 %all-to-all-start.3 = ((bf16[16,64,640]{2,1,0:T(8,128)(2,1)}), bf16[16,64,640]{2,1,0:T(8,128)(2,1)}, u32[]{:S(2)}, u32[]{:S(2)}) async-start(bf16[16,64,640]{2,1,0:T(8,128)(2,1)} %pad_maximum_fusion.1), calls=%async_computation.3 | async-start | bytes 2621440 | tf_op jit(solution)/shard_map/all_to_all | solution.py:712
  843.5 58.2 %all-to-all-start.4 = ((bf16[32,2,4864]{2,1,0:T(2,128)(2,1)}), bf16[32,2,4864]{2,1,0:T(2,128)(2,1)}, u32[]{:S(2)}, u32[]{:S(2)}) async-start(bf16[32,2,4864]{2,1,0:T(2,128)(2,1)} %reshape.689), calls=%async_computation.4 | async-start | bytes 1245184 | tf_op jit(solution)/shard_map/all_to_all | solution.py:741
  855.9 45.7 %collective-permute-start.19 = (bf16[4352,128]{1,0:T(8,128)(2,1)S(1)}, bf16[4352,128]{1,0:T(8,128)(2,1)S(1)}, u32[]{:S(2)}, u32[]{:S(2)}) collective-permute-start(bf16[4352,128]{1,0:T(8,128)(2,1)S(1)} %pad_maximum_fusion.3), channel_id=1, source_target_pairs={{0,16},{16,0},{1,17},{17,1},{2,18},{18,2},{3,19},{19,3},{4,20},{20... | collective-permute-start | bytes 3342344 | tf_op jit(solution)/shard_map/ppermute | solution.py:774
  863.5 37.0 %collective-permute-start.20 = (bf16[512,512]{1,0:T(8,128)(2,1)S(1)}, bf16[512,512]{1,0:T(8,128)(2,1)S(1)}, u32[]{:S(2)}, u32[]{:S(2)}) collective-permute-start(bf16[512,512]{1,0:T(8,128)(2,1)S(1)} %convert_element_type.266), channel_id=1, source_target_pairs={{0,0},{1,1},{2,2},{3,3},{16,4},{17,5},{18,6},{19,7},{4,16},{5,17},... | collective-permute-start | bytes 1572872 | tf_op jit(solution)/shard_map/ppermute | solution.py:462
  (85 other events, 2110.5 us)
Sparse Core Ops, SparseCore 0:
  11.4 119.4 all-gather.6
  251.9 66.0 all-gather.8
  320.2 63.2 all-gather.10
  695.0 50.4 all-gather.12

commit v13 on v11

--- a/solution.py
+++ b/solution.py
@@ -62,11 +62,11 @@
 
 def lstm_kernel(n, chunk, x_own, bias, p, pt, cot, w_in, *refs):
     out_ref, dx_ref, db_ref, dp_ref = refs[:4]
-    dw_out = refs[4:n + 4]
+    gate_out = refs[4]
     (xbuf, hbuf, dqbuf, gates, cells, ebuf, hown, gscr, escr, dabuf, ucell, dwacc, w, wt,
      stage, inbox, stage2, inbox2, relay, gbuf, rown,
      in_send, in_recv, ag_send, ag_recv, dq_send, dq_recv, rs_send, rs_recv,
-     dx_send, dx_recv, x_send, x_recv, g_send, g_recv, st_sem, w_sem) = refs[n + 4:]
+     dx_send, dx_recv, x_send, x_recv, g_send, g_recv, row_send, row_recv, w_sem) = refs[5:]
     steps, _, rows, width = xbuf.shape
     total = n * rows
     cell = cells.shape[2]
@@ -90,9 +90,15 @@
         return (lax.div(rank, wing), direction, base + lax.rem(rank, wing))
 
     barrier = pltpu.get_barrier_semaphore()
-    over(n, lambda off: pl.semaphore_signal(
-        barrier, inc=1, device_id=at_peer(off), device_id_type=MESH))
-    pl.semaphore_signal(barrier, inc=1, device_id=partner, device_id_type=MESH)
+
+    def greet(side, off):
+        pl.semaphore_signal(
+            barrier, inc=1, device_id=(side, direction, lax.rem(place + off, n)),
+            device_id_type=MESH)
+
+    over(n, lambda off: greet(pipe, off))
+    over(n, lambda off: greet(1 - pipe, off))
+    greet(1 - pipe, 0)
 
     each = 2 * width // n
     load = pltpu.make_async_copy(w_in, w, w_sem)
@@ -105,7 +111,7 @@
 
     hbuf[0] = jnp.zeros((n, rows, width), BF)
     cells[0] = jnp.zeros((total, cell), F32)
-    pl.semaphore_wait(barrier, n)
+    pl.semaphore_wait(barrier, 2 * n - 1)
 
     def ag_copy(buf, slot, off):
         out, into = (ag_send, ag_recv) if buf is hbuf else (dq_send, dq_recv)
@@ -336,18 +342,55 @@
     def _():
         lax.fori_loop(0, steps, lambda t, _: (g_copy(t).wait_send(), 0)[1], 0)
 
-    def dw_copy(off):
+    layer = lax.div(place, wing)
+    at_home = layer == pipe
+
+    def row_copy(row, rank):
+        return pltpu.make_async_remote_copy(
+            src_ref=w.at[pl.ds(pl.multiple_of(row * each, each), each)],
+            dst_ref=gate_out.at[rank], send_sem=row_send.at[row], recv_sem=row_recv.at[rank],
+            device_id=(layer, direction, row), device_id_type=MESH)
+
+    def own_copy():
         return pltpu.make_async_copy(
-            dabuf.at[off % 2, pl.ds(0, each)], dw_out[off], st_sem.at[off % 2])
-
-    for off in range(n):
-        if off > 1:
-            dw_copy(off - 2).wait()
-        at = pl.multiple_of(lax.rem(me + off, n) * each, each)
-        dabuf[off % 2, :each, :] = dwacc[pl.ds(at, each), :].astype(BF)
-        dw_copy(off).start()
-    for off in range(n - 2, n):
-        dw_copy(off).wait()
+            w.at[pl.ds(pl.multiple_of(place * each, each), each)], gate_out.at[me], w_sem)
+
+    def send_row(off, _):
+        row = lax.rem(me + off, n)
+        at = pl.ds(pl.multiple_of(row * each, each), each)
+        w[at, :] = dwacc[at, :].astype(BF)
+        mine = at_home & (row == place)
+
+        @pl.when(mine)
+        def _():
+            own_copy().start()
+
+        @pl.when(jnp.logical_not(mine))
+        def _():
+            row_copy(row, me).start()
+        return 0
+
+    def end_row(row, _):
+        mine = at_home & (row == place)
+
+        @pl.when(mine)
+        def _():
+            own_copy().wait()
+
+        @pl.when(jnp.logical_not(mine))
+        def _():
+            row_copy(row, me).wait_send()
+        return 0
+
+    def end_rank(rank, _):
+        @pl.when(jnp.logical_not(at_home & (rank == me)))
+        def _():
+            row_copy(0, rank).wait_recv()
+        return 0
+
+    lax.fori_loop(0, n, send_row, 0)
+    lax.fori_loop(0, n, end_row, 0)
+    lax.fori_loop(0, n, end_rank, 0)
 
 
 def lstm_call(n, x, weights, bias, p, pt, cot, chunk=16):
@@ -365,9 +408,9 @@
         out_shape=(
             sds((steps, rows, width), BF), sds((steps, rows, width), F32),
             sds((1, 4 * cell), F32), sds((cell, width), F32),
-            *[sds((2 * width // n, 4 * cell), BF)] * n),
+            sds((n, 2 * width // n, 4 * cell), BF)),
         in_specs=[vm] * 5 + [hb],
-        out_specs=[vm] * 4 + [hb] * n,
+        out_specs=[vm] * 4 + [hb],
         scratch_shapes=[
             V((steps, n, rows, width), BF), V((steps + 1, n, rows, width), BF),
             V((steps, n, rows, width), BF), V((steps, total, 4 * cell), keep),
@@ -380,7 +423,7 @@
             V((2, n, rows, width), BF), V((2, n, rows, width), BF),
             V((steps, rows, width), BF), V((steps, rows, width), BF), V((rows, width), F32),
             dma((steps,)), dma((steps,)), dma((n,)), dma((n,)), dma((n,)), dma((n,)), dma((n,)), dma((n,)), dma((2, n)), dma((2, n)),
-            dma((steps,)), dma((steps,)), dma((steps,)), dma((steps,)), dma((2,)), dma,
+            dma((steps,)), dma((steps,)), dma((steps,)), dma((steps,)), dma((n,)), dma((n,)), dma,
         ],
         compiler_params=pltpu.CompilerParams(
             collective_id=0, has_side_effects=True, vmem_limit_bytes=60 * 1024 * 1024),
@@ -416,27 +459,24 @@
 
 
 def join_cells(blocks):
-    n = len(blocks)
-    rows, gates = blocks[0].shape
+    n, rows, gates = blocks.shape
     cell = gates // 4
 
-    def body(*refs):
-        dst = refs[n]
-        for off in range(n):
-            rank = lax.rem(lax.axis_index("dp") + (n - off), n)
-            dst[:, pl.ds(pl.multiple_of(rank * cell, cell), cell)] = refs[off][...].astype(F32)
+    def body(src, dst):
+        for k in range(n):
+            dst[:, k * cell : (k + 1) * cell] = src[k].astype(F32)
 
     return pl.pallas_call(
         body,
         grid=(4,),
         out_shape=jax.ShapeDtypeStruct((rows, n * gates), F32),
-        in_specs=[pl.BlockSpec((rows, cell), lambda b: (0, b))] * n,
+        in_specs=[pl.BlockSpec((n, rows, cell), lambda b: (0, 0, b))],
         out_specs=pl.BlockSpec((rows, n * cell), lambda b: (0, b)),
         cost_estimate=pl.CostEstimate(
             flops=0, bytes_accessed=6 * n * rows * gates, transcendentals=0
         ),
         name="join_cells",
-    )(*blocks)
+    )(blocks)
 
 
 def swap_pipes(value):
@@ -639,11 +679,10 @@
         for value in kept_low[:2]
     ]
 
-    out_own, dx_own, grad_bias, grad_cell, *grad_gate = lstm_call(
+    out_own, dx_own, grad_bias, grad_cell, grad_gate = lstm_call(
         n, inputs, gate_own, bias_own, cell_low, cell_low.T, cot
     )
     dx_own = from_ranks(dx_own.astype(BF), 0, (1,))
-    grad_gate = [from_ranks(block, off) for off, block in enumerate(grad_gate)]
     dx_own, kept_all = lax.optimization_barrier((dx_own, kept_all))
 
     grad_stored = jnp.einsum(
@@ -691,7 +730,6 @@
             group_tokens, half
         )
     grad_before = grad_features * silu_slope(pooled + conv_bias_own)
-    grad_before, grad_gate[1:5] = lax.optimization_barrier((grad_before, grad_gate[1:5]))
     grad_conv, grad_table = conv_backward(ids, table_low, conv_low, masks, grad_before)
 
     def spread(value):
@@ -741,7 +779,6 @@
     summed = jnp.sum(lax.all_to_all(packed, ALL, 0, 0).astype(F32), axis=0)
     out_own = from_ranks(out_own, 0)
     grad_cell = from_ranks(grad_cell.astype(BF), 0)
-    summed, grad_gate = lax.optimization_barrier((summed, grad_gate))
     grad_gate = join_cells(grad_gate)
     activations = jnp.einsum("rts,srd->rtd", own_order, out_own, preferred_element_type=BF)
     grad_cell = grad_cell.astype(F32)

time: 943 us -> 987 us (1.047)
  Pallas kernels: 319 us -> 389 us
  waiting for transfers between devices: 161 us -> 145 us
    pallas_call x1, Pallas kernels: 307 us -> 377 us  [lstm_call(): pl.pallas_call(functools.partial(lstm_kernel, n, chunk), out_shape=(sds((...]
    ppermute x11 -> x3, starting transfers between devices: 35 us -> 8.49 us  [from_ranks(): lax.ppermute(value, ('pipe', 'dp'), [(there, here) for here, there in pai...]
    ppermute x11 -> x3, waiting for transfers between devices: 55.3 us -> 29.6 us  [from_ranks(): lax.ppermute(value, ('pipe', 'dp'), [(there, here) for here, there in pai...]
    all_to_all x1, starting transfers between devices: 77.3 us -> 101 us  [local(): lax.all_to_all(jnp.concatenate([grad_stored, grad_stored]).reshape(-1, gr...]
  transfers between devices with their start and end apart: 31 -> 23, of which waited for: 9 -> 8; matrix products, arithmetic and copies ran while one was open for 21% -> 18% of each run, Pallas kernels for 34% -> 40%
where the time goes in v13:
time: 987 us; the launch traced here: 976 us
  Pallas kernels  389 us (39%)
  starting transfers between devices  171 us (17%)
  waiting for transfers between devices  145 us (15%)
  local copies, waits for them, and re-layouts  83.2 us (8%)
  other arithmetic  65.7 us (7%)
  matrix products  65.4 us (7%)
  blocking collectives  40.5 us (4%)
  between operations  15.6 us (2%)
    pallas_call x1, Pallas kernels, lstm_call(): pl.pallas_call(functools.partial(lstm_kernel, n, chunk), out_shape=(sds((...  377 us
    all_to_all x1, starting transfers between devices, local(): lax.all_to_all(jnp.concatenate([grad_stored, grad_stored]).reshape(-1, gr...  101 us
    ppermute x1, waiting for transfers between devices, local(): lax.ppermute(swapped, ('pipe', 'dp'), [(k, wing + k) for k in range(wing)...  49.9 us
    all_gather x1, waiting for transfers between devices, local(): lax.all_gather(jnp.concatenate([mine, proj_blocks], axis=1).astype(BF), (...  43.4 us
    ppermute x3, waiting for transfers between devices, from_ranks(): lax.ppermute(value, ('pipe', 'dp'), [(there, here) for here, there in pai...  29.6 us
    all_gather x3, blocking collectives, both_halves(): lax.all_gather(value, 'pipe').reshape(2, tokens, blocks, half // blocks)  27.2 us
    all_to_all x1, starting transfers between devices, local(): lax.all_to_all(pair, ('dir', 'dp'), 0, 0).reshape(holders * tokens, -1)  26.4 us
  transfers between devices with their start and end apart: 23, of which 8 were waited for; matrix products, arithmetic and copies ran while one was open for 18% of the time, Pallas kernels for 40%

profile of v13, /device:TPU:3, one launch (start us, length us, event | category | flops | bytes accessed | tf_op | source)
XLA Modules:
  0.0 976.0 jit_solution(10911306480325093308)
XLA Ops:
  12.1 6.5 all-to-all-start
  20.7 5.9 split_cells.1
  29.6 12.1 %gather_fusion = bf16[6400,16]{1,0:T(8,128)(2,1)S(1)} fusion(bf16[262,16]{1,0:T(8,128)(2,1)S(1)} %copy.242, s32[7168]{0:T(1024)S(1)} %pad_clamp_fusion), kind=kCustom, calls=%fused_computation.clone | custom fusion | bytes 435200 | tf_op jit(solution)/shard_map/jit(_take)/gather | solution.py:49
  45.8 10.7 %select_reduce_fusion = (f32[128,1024]{1,0:T(8,128)S(1)}, f32[128,50,1024]{2,0,1:T(8,128)}) fusion(pred[50,1024]{1,0:T(8,128)(4,1)S(1)} %iota_compare_fusion.6, bf16[128,50,112]{0,2,1:T(8,128)(2,1)S(1)} %slice_dynamic-update-slice_fusion, s32[1024]{0:T(1024)S(1)} %add_bitcast_fusion, s32[112]{0:T(128)S(1)} %and_select_fusion, ...), kind=kOutput, calls=%fused_computation.5 | convolution fusion | flops 1481785344 | bytes 28463620 | tf_op jit(solution)/shard_map/bpk,kf->bpf/dot_general | solution.py:51
  56.6 14.6 %exponential_reduce_fusion = (f32[128,1024]{1,0:T(8,128)S(1)}, f32[128,1024]{1,0:T(8,128)}) fusion(f32[128,50,1024]{2,0,1:T(8,128)} %get-tuple-element.166, f32[128,1024]{1,0:T(8,128)S(1)} %is-finite_select_fusion.1, pred[50,1024]{1,0:T(8,128)(4,1)S(1)} %iota_compare_fusion.6, f32[128,1024]{1,0:T(8,128)S(1)} %get-tuple-element.165), kind=kLoop, calls=%fused_computation.3 | loop fusion | flops 32505856 | bytes 28362752 | tf_op jit(solution)/shard_map/reduce_sum | solution.py:506
  71.4 10.5 %all_gather.32 = bf16[2,128,1024]{2,1,0:T(8,128)(2,1)S(1)} all-gather(bf16[1,128,1024]{2,1,0:T(8,128)(2,1)S(1)} %multiply_convert_fusion.5), channel_id=1, replica_groups=mesh['pipe'=2,'dir'=2,'dp'=8] {'pipe'}, dimensions={0}, use_global_device_ids=true | all-gather | bytes 786432 | tf_op jit(solution)/shard_map/all_gather | solution.py:518
  87.4 43.4 %all-gather.7.cloned.1.call-done = bf16[2,2304,2048]{2,1,0:T(8,128)(2,1)} async-done(((bf16[2,2304,128]{2,1,0:T(8,128)(2,1)}), bf16[2,2304,2048]{2,1,0:T(8,128)(2,1)}) %all-gather.7.cloned.1.call-update) | async-done | bytes 18874384 | tf_op jit(solution)/shard_map/all_gather | solution.py:583
  149.7 9.9 %all-gather = bf16[256,1024]{1,0:T(8,128)(2,1)S(1)} all-gather(bf16[128,1024]{1,0:T(8,128)(2,1)S(1)} %get-tuple-element.138), channel_id=2, replica_groups=mesh['pipe'=2,'dir'=2,'dp'=8] {'pipe'}, dimensions={0}, use_global_device_ids=true | all-gather | bytes 786432 | tf_op jit(solution)/shard_map/all_gather | solution.py:518
  166.3 6.8 all-gather.1
  181.1 13.3 %all_gather.37 = bf16[16,16,512]{2,1,0:T(8,128)(2,1)S(1)} all-gather(bf16[4,16,512]{2,1,0:T(8,128)(2,1)S(1)} %bitcast.308), channel_id=1, replica_groups=mesh['pipe'=2,'dir'=2,'dp'=8] {'dir','pipe'}, dimensions={0}, use_global_device_ids=true | all-gather | bytes 327680 | tf_op jit(solution)/shard_map/all_gather | solution.py:658
  195.5 49.9 %collective-permute-done.4 = bf16[384,512]{0,1:T(8,128)(2,1)} collective-permute-done((bf16[384,512]{0,1:T(8,128)(2,1)}, bf16[384,512]{0,1:T(8,128)(2,1)}, u32[]{:S(2)}, u32[]{:S(2)}) %collective-permute-start.4) | collective-permute-done | bytes 393248 | tf_op jit(solution)/shard_map/ppermute | solution.py:630
  261.7 377.4 %relay_lstm.1 = (bf16[16,16,512]{2,1,0:T(8,128)(2,1)}, f32[16,16,512]{2,1,0:T(8,128)}, f32[1,2048]{1,0:T(1,128)}, f32[512,512]{1,0:T(8,128)}, bf16[8,128,2048]{2,1,0:T(8,128)(2,1)}) custom-call(bf16[16,16,512]{2,1,0:T(8,128)(2,1)} %copy-done.75, f32[1,2048]{1,0:T(1,128)} %copy-done.76, bf16[512,512]{1,0:T(8,128)(2,1)} %copy.258.p, ...), custom_call_target="tpu_custom_call" | custom-call | flops 299999985664 | bytes 67108864 | tf_op jit(solution)/shard_map/relay_lstm/pallas_call | solution.py:406
  645.8 6.0 join_cells.1
  654.1 101.1 %all-to-all-start.2 = ((bf16[4,128,512]{2,1,0:T(8,128)(2,1)}), bf16[4,128,512]{2,1,0:T(8,128)(2,1)S(1)}, u32[]{:S(2)}, u32[]{:S(2)}) async-start(bf16[4,128,512]{2,1,0:T(8,128)(2,1)} %bitcast.38), calls=%async_computation.2 | async-start | bytes 1048576 | tf_op jit(solution)/shard_map/all_to_all | solution.py:693
  756.1 6.1 all-to-all-done.2
  766.0 6.3 fusion.1
  785.5 7.2 fusion.5
  811.1 7.3 collective-permute-done.9
  823.6 26.4 %all-to-all-start.3 = ((bf16[16,64,640]{2,1,0:T(8,128)(2,1)}), bf16[16,64,640]{2,1,0:T(8,128)(2,1)S(1)}, u32[]{:S(2)}, u32[]{:S(2)}) async-start(bf16[16,64,640]{2,1,0:T(8,128)(2,1)} %pad_maximum_fusion.1), calls=%async_computation.3 | async-start | bytes 2621440 | tf_op jit(solution)/shard_map/all_to_all | solution.py:750
  850.0 11.7 %multiply_convert_fusion = bf16[128,50,1024]{2,0,1:T(8,128)(2,1)S(1)} fusion(f32[128,50,1024]{2,0,1:T(8,128)} %get-tuple-element.166, f32[128,1024]{1,0:T(8,128)S(1)} %copy-done.18, f32[128,1024]{1,0:T(8,128)S(1)} %copy-done.4, f32[128,1024]{1,0:T(8,128)S(1)} %copy-done.19, pred[50,1024]{1,0:T(8,128)(4,1)S(1)} %copy-done.40), kind=kLoop, calls=%fused_computation.1 | loop fusion | flops 32768000 | bytes 40945664 | tf_op jit(solution)/shard_map/convert_element_type | solution.py:526
  869.1 6.0 fusion.25
  875.2 5.3 all-to-all-done.3
  913.8 19.4 %collective-permute-done.10 = bf16[16,16,512]{2,1,0:T(8,128)(2,1)S(1)} collective-permute-done((bf16[16,16,512]{2,1,0:T(8,128)(2,1)S(1)}, bf16[16,16,512]{2,1,0:T(8,128)(2,1)S(1)}, u32[]{:S(2)}, u32[]{:S(2)}) %collective-permute-start.10) | collective-permute-done | bytes 262176 | tf_op jit(solution)/shard_map/ppermute | solution.py:502
  934.2 10.2 %collective-permute-done.12 = bf16[512,512]{1,0:T(8,128)(2,1)S(1)} collective-permute-done((bf16[512,512]{1,0:T(8,128)(2,1)S(1)}, bf16[512,512]{1,0:T(8,128)(2,1)S(1)}, u32[]{:S(2)}, u32[]{:S(2)}) %collective-permute-start.12) | collective-permute-done | bytes 524320 | tf_op jit(solution)/shard_map/ppermute | solution.py:502
  (384 shorter events, 186.2 us)
Async XLA Ops:
  7.2 123.6 %all-gather.7.cloned.1.call-start = ((), (), s32[]{:S(2)}) async-start(), calls=%async_computation.6 | async-start | bytes 20054016 | tf_op jit(solution)/shard_map/all_gather | solution.py:583
  12.1 33.7 %all-to-all-start = ((bf16[16,112,128]{2,1,0:T(8,128)(2,1)}), bf16[16,112,128]{2,1,0:T(8,128)(2,1)S(1)}, u32[]{:S(2)}, u32[]{:S(2)}) async-start(bf16[16,112,128]{2,1,0:T(8,128)(2,1)} %broadcast_in_dim.264), calls=%async_computation | async-start | bytes 917504 | tf_op jit(solution)/shard_map/all_to_all | solution.py:586
  20.4 67.0 %collective-permute-start.1 = (bf16[384,512]{0,1:T(8,128)(2,1)}, bf16[384,512]{0,1:T(8,128)(2,1)}, u32[]{:S(2)}, u32[]{:S(2)}) collective-permute-start(bf16[384,512]{0,1:T(8,128)(2,1)} %pad_maximum_fusion.9), channel_id=1, source_target_pairs={{0,16},{16,0},{1,17},{17,1},{2,18},{18,2},{3,19},{19,3},{4,20},{20... | collective-permute-start | bytes 1179656 | tf_op jit(solution)/shard_map/ppermute | solution.py:483
  26.6 55.7 %collective-permute-start = (bf16[4,128,2048]{2,1,0:T(8,128)(2,1)}, bf16[4,128,2048]{2,1,0:T(8,128)(2,1)}, u32[]{:S(2)}, u32[]{:S(2)}) collective-permute-start(bf16[4,128,2048]{2,1,0:T(8,128)(2,1)} %get-tuple-element.39), channel_id=1, source_target_pairs={{0,16},{16,0},{1,17},{17,1},{2,18},{18,2},{3,19},{19,3},{4,20},{20... | collective-permute-start | bytes 6291464 | tf_op jit(solution)/shard_map/ppermute | solution.py:483
  130.8 116.8 %all-to-all-start.1 = ((bf16[8,128,2048]{2,1,0:T(8,128)(2,1)}), bf16[8,128,2048]{2,1,0:T(8,128)(2,1)}, u32[]{:S(2)}, u32[]{:S(2)}) async-start(bf16[8,128,2048]{2,1,0:T(8,128)(2,1)} %pad_maximum_fusion), calls=%async_computation.1 | async-start | bytes 8388608 | tf_op jit(solution)/shard_map/all_to_all | solution.py:638
  135.5 516.3 %all-gather.9.cloned.1.call-start = ((), (), s32[]{:S(2)}) async-start(), calls=%async_computation.7 | async-start | bytes 4456448 | tf_op jit(solution)/shard_map/all_gather | solution.py:673
  135.6 111.9 %collective-permute-start.5 = (f32[1,2048]{1,0:T(1,128)S(1)}, f32[1,2048]{1,0:T(1,128)S(1)}, u32[]{:S(2)}, u32[]{:S(2)}) collective-permute-start(f32[1,2048]{1,0:T(1,128)S(1)} %bitcast.313), channel_id=1, source_target_pairs={{0,0},{1,1},{2,2},{3,3},{4,16},{5,17},{6,18},{7,19},{16,4},{17,5},... | collective-permute-start | bytes 24584 | tf_op jit(solution)/shard_map/ppermute | solution.py:497
  139.7 106.7 %collective-permute-start.3 = (bf16[384,512]{0,1:T(8,128)(2,1)}, bf16[384,512]{0,1:T(8,128)(2,1)}, u32[]{:S(2)}, u32[]{:S(2)}) collective-permute-start(bf16[384,512]{0,1:T(8,128)(2,1)} %slice_bitcast_fusion), channel_id=1, source_target_pairs={{0,0},{1,1},{2,2},{3,3},{4,16},{5,17},{6,18},{7,19},{16,4},{17,5},... | collective-permute-start | bytes 1179656 | tf_op jit(solution)/shard_map/ppermute | solution.py:497
  142.7 102.7 %collective-permute-start.4 = (bf16[384,512]{0,1:T(8,128)(2,1)}, bf16[384,512]{0,1:T(8,128)(2,1)}, u32[]{:S(2)}, u32[]{:S(2)}) collective-permute-start(bf16[384,512]{0,1:T(8,128)(2,1)} %collective-permute-done.1), channel_id=1, source_target_pairs={{0,4},{1,5},{2,6},{3,7},{20,16},{21,17},{22,18},{23,19},{8,12},{9,... | collective-permute-start | bytes 1179656 | tf_op jit(solution)/shard_map/ppermute | solution.py:630
  194.8 52.8 %collective-permute-start.2 = (bf16[16,16,512]{2,1,0:T(8,128)(2,1)S(1)}, bf16[16,16,512]{2,1,0:T(8,128)(2,1)S(1)}, u32[]{:S(2)}, u32[]{:S(2)}) collective-permute-start(bf16[16,16,512]{2,1,0:T(8,128)(2,1)S(1)} %bitcast.303), channel_id=1, source_target_pairs={{0,4},{1,5},{2,6},{3,7},{20,20},{21,21},{22,22},{23,23},{8,12},{9,... | collective-permute-start | bytes 786440 | tf_op jit(solution)/shard_map/ppermute | solution.py:662
  251.7 400.1 %all-gather.11.cloned.1.call-start = ((), (), s32[]{:S(2)}) async-start(), calls=%async_computation.8 | async-start | bytes 4456448 | tf_op jit(solution)/shard_map/all_gather | solution.py:673
  261.7 379.9 %copy-start.13 = (bf16[16,128,4,128]{1,3,2,0:T(8,128)(2,1)S(1)}, bf16[16,128,4,128]{1,3,2,0:T(8,128)(2,1)}, u32[]{:S(2)}) copy-start(bf16[16,128,4,128]{1,3,2,0:T(8,128)(2,1)} %copy.262) | copy-start | bytes 6291460
  640.3 11.5 %collective-permute-start.6 = (bf16[16,16,512]{2,1,0:T(8,128)(2,1)S(1)}, bf16[16,16,512]{2,1,0:T(8,128)(2,1)}, u32[]{:S(2)}, u32[]{:S(2)}) collective-permute-start(bf16[16,16,512]{2,1,0:T(8,128)(2,1)S(1)} %convert_element_type.247), channel_id=1, source_target_pairs={{4,16},{5,17},{6,18},{7,19},{20,20},{21,21},{22,22},{23,23},{12,24... | collective-permute-start | bytes 786440 | tf_op jit(solution)/shard_map/ppermute | solution.py:502
  654.1 108.1 %all-to-all-start.2 = ((bf16[4,128,512]{2,1,0:T(8,128)(2,1)}), bf16[4,128,512]{2,1,0:T(8,128)(2,1)S(1)}, u32[]{:S(2)}, u32[]{:S(2)}) async-start(bf16[4,128,512]{2,1,0:T(8,128)(2,1)} %bitcast.38), calls=%async_computation.2 | async-start | bytes 1048576 | tf_op jit(solution)/shard_map/all_to_all | solution.py:693
  755.2 128.2 %all-gather.13.cloned.1.call-start = ((), (), s32[]{:S(2)}) async-start(), calls=%async_computation.9 | async-start | bytes 1114112 | tf_op jit(solution)/shard_map/all_gather | solution.py:701
  774.1 7.3 collective-permute-start.7
  800.7 8.1 collective-permute-start.8
  807.0 11.4 %collective-permute-start.9 = (bf16[64,2,2,8,1,128]{5,3,2,1,0,4:T(8,128)(2,1)}, bf16[64,2,2,8,1,128]{5,3,2,1,0,4:T(8,128)(2,1)S(1)}, u32[]{:S(2)}, u32[]{:S(2)}) collective-permute-start(bf16[64,2,2,8,1,128]{5,3,2,1,0,4:T(8,128)(2,1)} %get-tuple-element.155), channel_id=1, source_target_pairs={{0,16},{16,0},{1,17},{17,1},{2,18},{18,2},{3,19},{19,3},{4,20},{20... | collective-permute-start | bytes 1572872 | tf_op jit(solution)/shard_map/ppermute | solution.py:743
  823.6 56.9 %all-to-all-start.3 = ((bf16[16,64,640]{2,1,0:T(8,128)(2,1)}), bf16[16,64,640]{2,1,0:T(8,128)(2,1)S(1)}, u32[]{:S(2)}, u32[]{:S(2)}) async-start(bf16[16,64,640]{2,1,0:T(8,128)(2,1)} %pad_maximum_fusion.1), calls=%async_computation.3 | async-start | bytes 2621440 | tf_op jit(solution)/shard_map/all_to_all | solution.py:750
  889.4 56.3 %all-to-all-start.4 = ((bf16[32,2,4864]{2,1,0:T(2,128)(2,1)}), bf16[32,2,4864]{2,1,0:T(2,128)(2,1)}, u32[]{:S(2)}, u32[]{:S(2)}) async-start(bf16[32,2,4864]{2,1,0:T(2,128)(2,1)} %reshape.689), calls=%async_computation.4 | async-start | bytes 1245184 | tf_op jit(solution)/shard_map/all_to_all | solution.py:779
  899.8 45.7 %collective-permute-start.11 = (bf16[4352,128]{1,0:T(8,128)(2,1)S(1)}, bf16[4352,128]{1,0:T(8,128)(2,1)S(1)}, u32[]{:S(2)}, u32[]{:S(2)}) collective-permute-start(bf16[4352,128]{1,0:T(8,128)(2,1)S(1)} %pad_maximum_fusion.3), channel_id=1, source_target_pairs={{0,16},{16,0},{1,17},{17,1},{2,18},{18,2},{3,19},{19,3},{4,20},{20... | collective-permute-start | bytes 3342344 | tf_op jit(solution)/shard_map/ppermute | solution.py:811
  903.2 30.0 %collective-permute-start.10 = (bf16[16,16,512]{2,1,0:T(8,128)(2,1)S(1)}, bf16[16,16,512]{2,1,0:T(8,128)(2,1)S(1)}, u32[]{:S(2)}, u32[]{:S(2)}) collective-permute-start(bf16[16,16,512]{2,1,0:T(8,128)(2,1)S(1)} %copy-done.74), channel_id=1, source_target_pairs={{0,0},{1,1},{2,2},{3,3},{16,4},{17,5},{18,6},{19,7},{4,16},{5,17},... | collective-permute-start | bytes 786440 | tf_op jit(solution)/shard_map/ppermute | solution.py:502
  907.5 36.9 %collective-permute-start.12 = (bf16[512,512]{1,0:T(8,128)(2,1)S(1)}, bf16[512,512]{1,0:T(8,128)(2,1)S(1)}, u32[]{:S(2)}, u32[]{:S(2)}) collective-permute-start(bf16[512,512]{1,0:T(8,128)(2,1)S(1)} %convert_element_type.266), channel_id=1, source_target_pairs={{0,0},{1,1},{2,2},{3,3},{16,4},{17,5},{18,6},{19,7},{4,16},{5,17},... | collective-permute-start | bytes 1572872 | tf_op jit(solution)/shard_map/ppermute | solution.py:502
  953.8 12.4 %all-to-all-start.5 = ((f32[32,1,512]{2,1,0:T(1,128)}), f32[32,1,512]{2,1,0:T(1,128)S(1)}, u32[]{:S(2)}, u32[]{:S(2)}) async-start(f32[32,1,512]{2,1,0:T(1,128)} %broadcast_in_dim.305), calls=%async_computation.5 | async-start | bytes 131072 | tf_op jit(solution)/shard_map/all_to_all | solution.py:815
  (78 other events, 1651.3 us)
Sparse Core Ops, SparseCore 0:
  11.3 119.4 all-gather.6
  251.8 65.9 all-gather.8
  320.0 62.7 all-gather.10
  776.5 57.1 all-gather.12

commit v14 on v11

--- a/solution.py
+++ b/solution.py
@@ -582,8 +582,8 @@
     )
     direct, local_part = moved[: moved.shape[0] // 2], moved[moved.shape[0] // 2 :]
     swapped = swap_pipes(local_part)
-    gate_low, gathered, features_low, bias_own, direct, swapped = lax.optimization_barrier(
-        (gate_low, gathered, features_low, bias_own, direct, swapped)
+    gathered, features_low, bias_own, direct, swapped = lax.optimization_barrier(
+        (gathered, features_low, bias_own, direct, swapped)
     )
     bias_own = to_ranks(bias_own, 0)
     wing = n // 2

time: 943 us -> 980 us (1.039)
  starting transfers between devices: 176 us -> 202 us
    ppermute x1, waiting for transfers between devices: 50 us -> 0.01 us  [local(): lax.ppermute(swapped, ('pipe', 'dp'), [(k, wing + k) for k in range(wing)...]
    ppermute x2, waiting for transfers between devices: 0.01 us -> 29.5 us  [swap_pipes(): return lax.ppermute(value, 'pipe', [(0, 1), (1, 0)])]
    ppermute x2, starting transfers between devices: 7.08 us -> 32.4 us  [to_ranks(): lax.ppermute(value, ('pipe', 'dp'), rank_pairs(lax.axis_size('dp'), off))]
    all_gather x1, waiting for transfers between devices: 43.5 us -> 66.9 us  [local(): lax.all_gather(jnp.concatenate([mine, proj_blocks], axis=1).astype(BF), (...]
  transfers between devices with their start and end apart: 31 -> 31, of which waited for: 9 -> 9; matrix products, arithmetic and copies ran while one was open for 21% -> 21% of each run, Pallas kernels for 34% -> 33%
where the time goes in v14:
time: 980 us; the launch traced here: 968 us
  Pallas kernels  319 us (33%)
  starting transfers between devices  202 us (21%)
  waiting for transfers between devices  164 us (17%)
  local copies, waits for them, and re-layouts  89.2 us (9%)
  other arithmetic  65.7 us (7%)
  matrix products  65.4 us (7%)
  blocking collectives  46.8 us (5%)
  between operations  15.8 us (2%)
    pallas_call x1, Pallas kernels, lstm_call(): pl.pallas_call(functools.partial(lstm_kernel, n, chunk), out_shape=(sds((...  307 us
    all_to_all x1, starting transfers between devices, local(): lax.all_to_all(jnp.concatenate([grad_stored, grad_stored]).reshape(-1, gr...  76.8 us
    all_gather x1, waiting for transfers between devices, local(): lax.all_gather(jnp.concatenate([mine, proj_blocks], axis=1).astype(BF), (...  66.9 us
    ppermute x11, waiting for transfers between devices, from_ranks(): lax.ppermute(value, ('pipe', 'dp'), [(there, here) for here, there in pai...  55.3 us
    all_gather x3, blocking collectives, both_halves(): lax.all_gather(value, 'pipe').reshape(2, tokens, blocks, half // blocks)  35.3 us
    ppermute x11, starting transfers between devices, from_ranks(): lax.ppermute(value, ('pipe', 'dp'), [(there, here) for here, there in pai...  35.2 us
    ppermute x2, starting transfers between devices, to_ranks(): lax.ppermute(value, ('pipe', 'dp'), rank_pairs(lax.axis_size('dp'), off))  32.4 us
    ppermute x2, waiting for transfers between devices, swap_pipes(): return lax.ppermute(value, 'pipe', [(0, 1), (1, 0)])  29.5 us
  transfers between devices with their start and end apart: 31, of which 9 were waited for; matrix products, arithmetic and copies ran while one was open for 21% of the time, Pallas kernels for 33%

profile of v14, /device:TPU:3, one launch (start us, length us, event | category | flops | bytes accessed | tf_op | source)
XLA Modules:
  0.0 967.7 jit_solution(13385341463162712179)
XLA Ops:
  12.1 6.5 all-to-all-start
  29.1 12.1 %gather_fusion = bf16[6400,16]{1,0:T(8,128)(2,1)S(1)} fusion(bf16[262,16]{1,0:T(8,128)(2,1)S(1)} %copy.242, s32[7168]{0:T(1024)S(1)} %pad_clamp_fusion), kind=kCustom, calls=%fused_computation.clone | custom fusion | bytes 435200 | tf_op jit(solution)/shard_map/jit(_take)/gather | solution.py:49
  46.0 29.5 %collective-permute-done.1 = bf16[4,128,2048]{2,1,0:T(8,128)(2,1)} collective-permute-done((bf16[4,128,2048]{2,1,0:T(8,128)(2,1)}, bf16[4,128,2048]{2,1,0:T(8,128)(2,1)}, u32[]{:S(2)}, u32[]{:S(2)}) %collective-permute-start.1) | collective-permute-done | bytes 2097184 | tf_op jit(solution)/shard_map/ppermute | solution.py:443
  85.5 10.8 %select_reduce_fusion = (f32[128,1024]{1,0:T(8,128)S(1)}, f32[128,50,1024]{2,0,1:T(8,128)}) fusion(pred[50,1024]{1,0:T(8,128)(4,1)S(1)} %iota_compare_fusion.6, bf16[128,50,112]{0,2,1:T(8,128)(2,1)S(1)} %slice_dynamic-update-slice_fusion, s32[1024]{0:T(1024)S(1)} %add_bitcast_fusion, s32[112]{0:T(128)S(1)} %and_select_fusion, ...), kind=kOutput, calls=%fused_computation.5 | convolution fusion | flops 1481785344 | bytes 28463620 | tf_op jit(solution)/shard_map/bpk,kf->bpf/dot_general | solution.py:51
  96.4 14.5 %exponential_reduce_fusion = (f32[128,1024]{1,0:T(8,128)S(1)}, f32[128,1024]{1,0:T(8,128)}) fusion(f32[128,50,1024]{2,0,1:T(8,128)} %get-tuple-element.204, f32[128,1024]{1,0:T(8,128)S(1)} %is-finite_select_fusion.1, pred[50,1024]{1,0:T(8,128)(4,1)S(1)} %iota_compare_fusion.6, f32[128,1024]{1,0:T(8,128)S(1)} %get-tuple-element.203), kind=kLoop, calls=%fused_computation.3 | loop fusion | flops 32505856 | bytes 28362752 | tf_op jit(solution)/shard_map/reduce_sum | solution.py:466
  111.2 7.1 all_gather.32
  118.7 66.9 %all-gather.7.cloned.1.call-done = bf16[2,2304,2048]{2,1,0:T(8,128)(2,1)} async-done(((bf16[2,2304,128]{2,1,0:T(8,128)(2,1)}), bf16[2,2304,2048]{2,1,0:T(8,128)(2,1)}) %all-gather.7.cloned.1.call-update) | async-done | bytes 18874384 | tf_op jit(solution)/shard_map/all_gather | solution.py:543
  185.6 30.5 %collective-permute-start.5 = (f32[1,2048]{1,0:T(1,128)}, f32[1,2048]{1,0:T(1,128)S(1)}, u32[]{:S(2)}, u32[]{:S(2)}) collective-permute-start(f32[1,2048]{1,0:T(1,128)} %bitcast.95), channel_id=1, source_target_pairs={{0,0},{1,1},{2,2},{3,3},{4,16},{5,17},{6,18},{7,19},{16,4},{17,5},... | collective-permute-start | bytes 24584 | tf_op jit(solution)/shard_map/ppermute | solution.py:457
  225.0 20.0 %all-gather = bf16[256,1024]{1,0:T(8,128)(2,1)S(1)} all-gather(bf16[128,1024]{1,0:T(8,128)(2,1)S(1)} %get-tuple-element.176), channel_id=2, replica_groups=mesh['pipe'=2,'dir'=2,'dp'=8] {'pipe'}, dimensions={0}, use_global_device_ids=true | all-gather | bytes 786432 | tf_op jit(solution)/shard_map/all_gather | solution.py:478
  251.7 8.2 all-gather.1
  267.9 11.4 %all_gather.37 = bf16[16,16,512]{2,1,0:T(8,128)(2,1)S(1)} all-gather(bf16[4,16,512]{2,1,0:T(8,128)(2,1)S(1)} %bitcast.305), channel_id=1, replica_groups=mesh['pipe'=2,'dir'=2,'dp'=8] {'dir','pipe'}, dimensions={0}, use_global_device_ids=true | all-gather | bytes 327680 | tf_op jit(solution)/shard_map/all_gather | solution.py:618
  296.8 307.3 %relay_lstm.1 = (bf16[16,16,512]{2,1,0:T(8,128)(2,1)}, f32[16,16,512]{2,1,0:T(8,128)}, f32[1,2048]{1,0:T(1,128)}, f32[512,512]{1,0:T(8,128)}, bf16[128,2048]{1,0...) custom-call(bf16[16,16,512]{2,1,0:T(8,128)(2,1)} %copy-done.76, ...), custom_call_target="tpu_custom_call" | custom-call | flops 299999985664 | bytes 67108864 | tf_op jit(solution)/shard_map/relay_lstm/pallas_call | solution.py:363
  611.0 14.2 %collective-permute-start.9 = (bf16[128,2048]{1,0:T(8,128)(2,1)}, bf16[128,2048]{1,0:T(8,128)(2,1)}, u32[]{:S(2)}, u32[]{:S(2)}) collective-permute-start(bf16[128,2048]{1,0:T(8,128)(2,1)} %get-tuple-element.73), channel_id=1, source_target_pairs={{19,0},{0,1},{1,2},{2,3},{3,4},{16,5},{17,6},{18,7},{23,16},{4,17}... | collective-permute-start | bytes 1572872 | tf_op jit(solution)/shard_map/ppermute | solution.py:462
  629.6 76.8 %all-to-all-start.2 = ((bf16[4,128,512]{2,1,0:T(8,128)(2,1)}), bf16[4,128,512]{2,1,0:T(8,128)(2,1)S(1)}, u32[]{:S(2)}, u32[]{:S(2)}) async-start(bf16[4,128,512]{2,1,0:T(8,128)(2,1)} %bitcast.38), calls=%async_computation.2 | async-start | bytes 1048576 | tf_op jit(solution)/shard_map/all_to_all | solution.py:654
  707.3 8.0 all-to-all-done.2
  738.9 7.2 fusion.5
  763.8 10.2 %collective-permute-start.15 = (bf16[128,2048]{1,0:T(8,128)(2,1)}, bf16[128,2048]{1,0:T(8,128)(2,1)}, u32[]{:S(2)}, u32[]{:S(2)}) collective-permute-start(bf16[128,2048]{1,0:T(8,128)(2,1)} %get-tuple-element.83), channel_id=1, source_target_pairs={{0,0},{1,1},{2,2},{3,3},{16,4},{17,5},{18,6},{19,7},{4,16},{5,17},... | collective-permute-start | bytes 1572872 | tf_op jit(solution)/shard_map/ppermute | solution.py:462
  781.3 23.1 %all-to-all-start.3 = ((bf16[16,64,640]{2,1,0:T(8,128)(2,1)}), bf16[16,64,640]{2,1,0:T(8,128)(2,1)}, u32[]{:S(2)}, u32[]{:S(2)}) async-start(bf16[16,64,640]{2,1,0:T(8,128)(2,1)} %pad_maximum_fusion.1), calls=%async_computation.3 | async-start | bytes 2621440 | tf_op jit(solution)/shard_map/all_to_all | solution.py:712
  804.4 11.7 %multiply_convert_fusion = bf16[128,50,1024]{2,0,1:T(8,128)(2,1)S(1)} fusion(f32[128,50,1024]{2,0,1:T(8,128)} %get-tuple-element.204, f32[128,1024]{1,0:T(8,128)S(1)} %copy-done.19, f32[128,1024]{1,0:T(8,128)S(1)} %copy-done.4, f32[128,1024]{1,0:T(8,128)S(1)} %fusion.41, pred[50,1024]{1,0:T(8,128)(4,1)S(1)} %copy-done.41), kind=kLoop, calls=%fused_computation.1 | loop fusion | flops 32768000 | bytes 40945664 | tf_op jit(solution)/shard_map/convert_element_type | solution.py:486
  844.1 7.2 all-to-all-start.4
  870.5 19.4 %collective-permute-done.14 = bf16[16,16,512]{2,1,0:T(8,128)(2,1)S(1)} collective-permute-done((bf16[16,16,512]{2,1,0:T(8,128)(2,1)S(1)}, bf16[16,16,512]{2,1,0:T(8,128)(2,1)S(1)}, u32[]{:S(2)}, u32[]{:S(2)}) %collective-permute-start.14) | collective-permute-done | bytes 262176 | tf_op jit(solution)/shard_map/ppermute | solution.py:462
  890.9 21.5 %collective-permute-done.20 = bf16[512,512]{1,0:T(8,128)(2,1)S(1)} collective-permute-done((bf16[512,512]{1,0:T(8,128)(2,1)S(1)}, bf16[512,512]{1,0:T(8,128)(2,1)S(1)}, u32[]{:S(2)}, u32[]{:S(2)}) %collective-permute-start.20) | collective-permute-done | bytes 524320 | tf_op jit(solution)/shard_map/ppermute | solution.py:462
  921.1 14.3 %collective-permute-done.18.refs_7_ = bf16[128,2048]{1,0:T(8,128)(2,1)} collective-permute-done((bf16[128,2048]{1,0:T(8,128)(2,1)}, bf16[128,2048]{1,0:T(8,128)(2,1)}, u32[]{:S(2)}, u32[]{:S(2)}) %collective-permute-start.18) | collective-permute-done | bytes 524320 | tf_op jit(solution)/shard_map/ppermute | solution.py:462
  936.1 9.0 all-to-all-start.5
  (403 shorter events, 204.3 us)
Async XLA Ops:
  7.2 178.4 %all-gather.7.cloned.1.call-start = ((), (), s32[]{:S(2)}) async-start(), calls=%async_computation.6 | async-start | bytes 20054016 | tf_op jit(solution)/shard_map/all_gather | solution.py:543
  12.1 68.3 %all-to-all-start = ((bf16[16,112,128]{2,1,0:T(8,128)(2,1)}), bf16[16,112,128]{2,1,0:T(8,128)(2,1)S(1)}, u32[]{:S(2)}, u32[]{:S(2)}) async-start(bf16[16,112,128]{2,1,0:T(8,128)(2,1)} %broadcast_in_dim.264), calls=%async_computation | async-start | bytes 917504 | tf_op jit(solution)/shard_map/all_to_all | solution.py:546
  19.7 99.0 %collective-permute-start = (bf16[384,512]{0,1:T(8,128)(2,1)S(1)}, bf16[384,512]{0,1:T(8,128)(2,1)}, u32[]{:S(2)}, u32[]{:S(2)}) collective-permute-start(bf16[384,512]{0,1:T(8,128)(2,1)S(1)} %pad_maximum_fusion.9), channel_id=1, source_target_pairs={{0,16},{16,0},{1,17},{17,1},{2,18},{18,2},{3,19},{19,3},{4,20},{20... | collective-permute-start | bytes 1179656 | tf_op jit(solution)/shard_map/ppermute | solution.py:443
  26.0 49.5 %collective-permute-start.1 = (bf16[4,128,2048]{2,1,0:T(8,128)(2,1)}, bf16[4,128,2048]{2,1,0:T(8,128)(2,1)}, u32[]{:S(2)}, u32[]{:S(2)}) collective-permute-start(bf16[4,128,2048]{2,1,0:T(8,128)(2,1)} %get-tuple-element.61), channel_id=1, source_target_pairs={{0,16},{16,0},{1,17},{17,1},{2,18},{18,2},{3,19},{19,3},{4,20},{20... | collective-permute-start | bytes 6291464 | tf_op jit(solution)/shard_map/ppermute | solution.py:443
  80.4 202.3 %all-to-all-start.1 = ((bf16[8,128,2048]{2,1,0:T(8,128)(2,1)}), bf16[8,128,2048]{2,1,0:T(8,128)(2,1)}, u32[]{:S(2)}, u32[]{:S(2)}) async-start(bf16[8,128,2048]{2,1,0:T(8,128)(2,1)} %pad_maximum_fusion), calls=%async_computation.1 | async-start | bytes 8388608 | tf_op jit(solution)/shard_map/all_to_all | solution.py:598
  85.4 542.0 %all-gather.9.cloned.1.call-start = ((), (), s32[]{:S(2)}) async-start(), calls=%async_computation.7 | async-start | bytes 4456448 | tf_op jit(solution)/shard_map/all_gather | solution.py:633
  185.6 97.1 %collective-permute-start.5 = (f32[1,2048]{1,0:T(1,128)}, f32[1,2048]{1,0:T(1,128)S(1)}, u32[]{:S(2)}, u32[]{:S(2)}) collective-permute-start(f32[1,2048]{1,0:T(1,128)} %bitcast.95), channel_id=1, source_target_pairs={{0,0},{1,1},{2,2},{3,3},{4,16},{5,17},{6,18},{7,19},{16,4},{17,5},... | collective-permute-start | bytes 24584 | tf_op jit(solution)/shard_map/ppermute | solution.py:457
  216.1 65.5 %collective-permute-start.3 = (bf16[384,512]{0,1:T(8,128)(2,1)}, bf16[384,512]{0,1:T(8,128)(2,1)}, u32[]{:S(2)}, u32[]{:S(2)}) collective-permute-start(bf16[384,512]{0,1:T(8,128)(2,1)} %slice_bitcast_fusion), channel_id=1, source_target_pairs={{0,0},{1,1},{2,2},{3,3},{4,16},{5,17},{6,18},{7,19},{16,4},{17,5},... | collective-permute-start | bytes 1179656 | tf_op jit(solution)/shard_map/ppermute | solution.py:457
  218.0 62.5 %collective-permute-start.4 = (bf16[384,512]{0,1:T(8,128)(2,1)}, bf16[384,512]{0,1:T(8,128)(2,1)}, u32[]{:S(2)}, u32[]{:S(2)}) collective-permute-start(bf16[384,512]{0,1:T(8,128)(2,1)} %collective-permute-done), channel_id=1, source_target_pairs={{0,4},{1,5},{2,6},{3,7},{20,16},{21,17},{22,18},{23,19},{8,12},{9,... | collective-permute-start | bytes 1179656 | tf_op jit(solution)/shard_map/ppermute | solution.py:590
  286.9 340.6 %all-gather.11.cloned.1.call-start = ((), (), s32[]{:S(2)}) async-start(), calls=%async_computation.8 | async-start | bytes 4456448 | tf_op jit(solution)/shard_map/all_gather | solution.py:633
  611.0 152.8 %collective-permute-start.9 = (bf16[128,2048]{1,0:T(8,128)(2,1)}, bf16[128,2048]{1,0:T(8,128)(2,1)}, u32[]{:S(2)}, u32[]{:S(2)}) collective-permute-start(bf16[128,2048]{1,0:T(8,128)(2,1)} %get-tuple-element.73), channel_id=1, source_target_pairs={{19,0},{0,1},{1,2},{2,3},{3,4},{16,5},{17,6},{18,7},{23,16},{4,17}... | collective-permute-start | bytes 1572872 | tf_op jit(solution)/shard_map/ppermute | solution.py:462
  625.2 148.8 %collective-permute-start.10 = (bf16[128,2048]{1,0:T(8,128)(2,1)}, bf16[128,2048]{1,0:T(8,128)(2,1)}, u32[]{:S(2)}, u32[]{:S(2)}) collective-permute-start(bf16[128,2048]{1,0:T(8,128)(2,1)} %get-tuple-element.74), channel_id=1, source_target_pairs={{18,0},{19,1},{0,2},{1,3},{2,4},{3,5},{16,6},{17,7},{22,16},{23,17... | collective-permute-start | bytes 1572872 | tf_op jit(solution)/shard_map/ppermute | solution.py:462
  625.3 148.8 %collective-permute-start.11 = (bf16[128,2048]{1,0:T(8,128)(2,1)}, bf16[128,2048]{1,0:T(8,128)(2,1)}, u32[]{:S(2)}, u32[]{:S(2)}) collective-permute-start(bf16[128,2048]{1,0:T(8,128)(2,1)} %get-tuple-element.75), channel_id=1, source_target_pairs={{17,0},{18,1},{19,2},{0,3},{1,4},{2,5},{3,6},{16,7},{21,16},{22,17... | collective-permute-start | bytes 1572872 | tf_op jit(solution)/shard_map/ppermute | solution.py:462
  627.4 146.7 %collective-permute-start.12 = (bf16[128,2048]{1,0:T(8,128)(2,1)}, bf16[128,2048]{1,0:T(8,128)(2,1)}, u32[]{:S(2)}, u32[]{:S(2)}) collective-permute-start(bf16[128,2048]{1,0:T(8,128)(2,1)} %get-tuple-element.76), channel_id=1, source_target_pairs={{16,0},{17,1},{18,2},{19,3},{0,4},{1,5},{2,6},{3,7},{20,16},{21,17... | collective-permute-start | bytes 1572872 | tf_op jit(solution)/shard_map/ppermute | solution.py:462
  629.6 85.7 %all-to-all-start.2 = ((bf16[4,128,512]{2,1,0:T(8,128)(2,1)}), bf16[4,128,512]{2,1,0:T(8,128)(2,1)S(1)}, u32[]{:S(2)}, u32[]{:S(2)}) async-start(bf16[4,128,512]{2,1,0:T(8,128)(2,1)} %bitcast.38), calls=%async_computation.2 | async-start | bytes 1048576 | tf_op jit(solution)/shard_map/all_to_all | solution.py:654
  706.4 131.8 %all-gather.13.cloned.1.call-start = ((), (), s32[]{:S(2)}) async-start(), calls=%async_computation.9 | async-start | bytes 1114112 | tf_op jit(solution)/shard_map/all_gather | solution.py:662
  763.8 157.3 %collective-permute-start.15 = (bf16[128,2048]{1,0:T(8,128)(2,1)}, bf16[128,2048]{1,0:T(8,128)(2,1)}, u32[]{:S(2)}, u32[]{:S(2)}) collective-permute-start(bf16[128,2048]{1,0:T(8,128)(2,1)} %get-tuple-element.83), channel_id=1, source_target_pairs={{0,0},{1,1},{2,2},{3,3},{16,4},{17,5},{18,6},{19,7},{4,16},{5,17},... | collective-permute-start | bytes 1572872 | tf_op jit(solution)/shard_map/ppermute | solution.py:462
  774.0 147.1 %collective-permute-start.16 = (bf16[128,2048]{1,0:T(8,128)(2,1)}, bf16[128,2048]{1,0:T(8,128)(2,1)}, u32[]{:S(2)}, u32[]{:S(2)}) collective-permute-start(bf16[128,2048]{1,0:T(8,128)(2,1)} %get-tuple-element.88), channel_id=1, source_target_pairs={{3,0},{16,1},{17,2},{18,3},{19,4},{0,5},{1,6},{2,7},{7,16},{20,17}... | collective-permute-start | bytes 1572872 | tf_op jit(solution)/shard_map/ppermute | solution.py:462
  781.3 53.7 %all-to-all-start.3 = ((bf16[16,64,640]{2,1,0:T(8,128)(2,1)}), bf16[16,64,640]{2,1,0:T(8,128)(2,1)}, u32[]{:S(2)}, u32[]{:S(2)}) async-start(bf16[16,64,640]{2,1,0:T(8,128)(2,1)} %pad_maximum_fusion.1), calls=%async_computation.3 | async-start | bytes 2621440 | tf_op jit(solution)/shard_map/all_to_all | solution.py:712
  844.1 69.5 %all-to-all-start.4 = ((bf16[32,2,4864]{2,1,0:T(2,128)(2,1)}), bf16[32,2,4864]{2,1,0:T(2,128)(2,1)}, u32[]{:S(2)}, u32[]{:S(2)}) async-start(bf16[32,2,4864]{2,1,0:T(2,128)(2,1)} %reshape.689), calls=%async_computation.4 | async-start | bytes 1245184 | tf_op jit(solution)/shard_map/all_to_all | solution.py:741
  856.5 57.0 %collective-permute-start.19 = (bf16[4352,128]{1,0:T(8,128)(2,1)S(1)}, bf16[4352,128]{1,0:T(8,128)(2,1)S(1)}, u32[]{:S(2)}, u32[]{:S(2)}) collective-permute-start(bf16[4352,128]{1,0:T(8,128)(2,1)S(1)} %pad_maximum_fusion.3), channel_id=1, source_target_pairs={{0,16},{16,0},{1,17},{17,1},{2,18},{18,2},{3,19},{19,3},{4,20},{20... | collective-permute-start | bytes 3342344 | tf_op jit(solution)/shard_map/ppermute | solution.py:774
  859.9 29.9 %collective-permute-start.14 = (bf16[16,16,512]{2,1,0:T(8,128)(2,1)S(1)}, bf16[16,16,512]{2,1,0:T(8,128)(2,1)S(1)}, u32[]{:S(2)}, u32[]{:S(2)}) collective-permute-start(bf16[16,16,512]{2,1,0:T(8,128)(2,1)S(1)} %copy-done.75), channel_id=1, source_target_pairs={{0,0},{1,1},{2,2},{3,3},{16,4},{17,5},{18,6},{19,7},{4,16},{5,17},... | collective-permute-start | bytes 786440 | tf_op jit(solution)/shard_map/ppermute | solution.py:462
  864.1 48.3 %collective-permute-start.20 = (bf16[512,512]{1,0:T(8,128)(2,1)S(1)}, bf16[512,512]{1,0:T(8,128)(2,1)S(1)}, u32[]{:S(2)}, u32[]{:S(2)}) collective-permute-start(bf16[512,512]{1,0:T(8,128)(2,1)S(1)} %convert_element_type.266), channel_id=1, source_target_pairs={{0,0},{1,1},{2,2},{3,3},{16,4},{17,5},{18,6},{19,7},{4,16},{5,17},... | collective-permute-start | bytes 1572872 | tf_op jit(solution)/shard_map/ppermute | solution.py:462
  889.9 31.3 %collective-permute-start.17 = (bf16[128,2048]{1,0:T(8,128)(2,1)}, bf16[128,2048]{1,0:T(8,128)(2,1)}, u32[]{:S(2)}, u32[]{:S(2)}) collective-permute-start(bf16[128,2048]{1,0:T(8,128)(2,1)} %get-tuple-element.89), channel_id=1, source_target_pairs={{2,0},{3,1},{16,2},{17,3},{18,4},{19,5},{0,6},{1,7},{6,16},{7,17},... | collective-permute-start | bytes 1572872 | tf_op jit(solution)/shard_map/ppermute | solution.py:462
  (87 other events, 2466.4 us)
Sparse Core Ops, SparseCore 0:
  11.4 174.1 all-gather.6
  287.0 68.2 all-gather.8
  357.5 62.6 all-gather.10
  729.4 50.4 all-gather.12

commit v15 on v12

--- a/solution.py
+++ b/solution.py
@@ -710,9 +710,7 @@
     last = jnp.transpose(own_last.reshape(tokens, 2, holders, cols), (2, 0, 1, 3))
     pair = jnp.concatenate([pair, last.reshape(holders, tokens, 2 * cols)], axis=2)
     pair = lax.all_to_all(pair, ("dir", "dp"), 0, 0).reshape(holders * tokens, -1)
-    grad_conv, pair, out_own, grad_cell, grad_gate[5:] = lax.optimization_barrier(
-        (grad_conv, pair, out_own, grad_cell, grad_gate[5:])
-    )
+    grad_conv, pair = lax.optimization_barrier((grad_conv, pair))
     small = (
         grad_table,
         spread(jnp.sum(grad_before, axis=0)),
@@ -739,12 +737,14 @@
         axis=1,
     ).astype(BF)
     summed = jnp.sum(lax.all_to_all(packed, ALL, 0, 0).astype(F32), axis=0)
+    summed, grad_gate, out_own, grad_cell = lax.optimization_barrier(
+        (summed, grad_gate, out_own, grad_cell)
+    )
     out_own = from_ranks(out_own, 0)
     grad_cell = from_ranks(grad_cell.astype(BF), 0)
-    summed, grad_gate = lax.optimization_barrier((summed, grad_gate))
-    grad_gate = join_cells(grad_gate)
     activations = jnp.einsum("rts,srd->rtd", own_order, out_own, preferred_element_type=BF)
     grad_cell = grad_cell.astype(F32)
+    grad_gate = join_cells(grad_gate)
     grad_conv = summed[: KMAX * CDIM * cols].reshape(KMAX * CDIM, cols)
     grad_bias = summed[KMAX * CDIM * cols + share :]
     last = pair[:, 4 * sub :].reshape(holders * tokens, 2, cols)

time: 947 us -> 962 us (1.016)
  waiting for transfers between devices: 136 us -> 185 us
  starting transfers between devices: 206 us -> 168 us
    ppermute x1, waiting for transfers between devices: 0.01 us -> 47.4 us  [local(): came = lax.ppermute(sent, 'pipe', [(0, 1), (1, 0)]).astype(F32)]
    all_to_all x1, starting transfers between devices: 47.5 us -> 19.4 us  [local(): lax.all_to_all(pair, ('dir', 'dp'), 0, 0).reshape(holders * tokens, -1)]
    ppermute x11, starting transfers between devices: 44.9 us -> 34.1 us  [from_ranks(): lax.ppermute(value, ('pipe', 'dp'), [(there, here) for here, there in pai...]
  transfers between devices with their start and end apart: 31 -> 31, of which waited for: 7 -> 11; matrix products, arithmetic and copies ran while one was open for 21% -> 21% of each run, Pallas kernels for 34% -> 33%
where the time goes in v15:
time: 962 us; the launch traced here: 951 us
  Pallas kernels  318 us (33%)
  waiting for transfers between devices  185 us (19%)
  starting transfers between devices  168 us (17%)
  local copies, waits for them, and re-layouts  87.6 us (9%)
  other arithmetic  69.4 us (7%)
  matrix products  66.3 us (7%)
  blocking collectives  40.4 us (4%)
  between operations  15.6 us (2%)
    pallas_call x1, Pallas kernels, lstm_call(): pl.pallas_call(functools.partial(lstm_kernel, n, chunk), out_shape=(sds((...  306 us
    all_to_all x1, starting transfers between devices, local(): lax.all_to_all(jnp.concatenate([grad_stored, grad_stored]).reshape(-1, gr...  77.4 us
    ppermute x1, waiting for transfers between devices, local(): lax.ppermute(swapped, ('pipe', 'dp'), [(k, wing + k) for k in range(wing)...  49.9 us
    ppermute x1, waiting for transfers between devices, local(): came = lax.ppermute(sent, 'pipe', [(0, 1), (1, 0)]).astype(F32)  47.4 us
    all_gather x1, waiting for transfers between devices, local(): lax.all_gather(jnp.concatenate([mine, proj_blocks], axis=1).astype(BF), (...  43.5 us
    ppermute x11, starting transfers between devices, from_ranks(): lax.ppermute(value, ('pipe', 'dp'), [(there, here) for here, there in pai...  34.1 us
    all_gather x3, blocking collectives, both_halves(): lax.all_gather(value, 'pipe').reshape(2, tokens, blocks, half // blocks)  27.1 us
    ppermute x11, waiting for transfers between devices, from_ranks(): lax.ppermute(value, ('pipe', 'dp'), [(there, here) for here, there in pai...  22.8 us
  transfers between devices with their start and end apart: 31, of which 11 were waited for; matrix products, arithmetic and copies ran while one was open for 21% of the time, Pallas kernels for 33%

profile of v15, /device:TPU:3, one launch (start us, length us, event | category | flops | bytes accessed | tf_op | source)
XLA Modules:
  0.0 950.6 jit_solution(16987357886934147314)
XLA Ops:
  12.1 6.5 all-to-all-start
  29.6 12.1 %gather_fusion = bf16[6400,16]{1,0:T(8,128)(2,1)S(1)} fusion(bf16[262,16]{1,0:T(8,128)(2,1)S(1)} %copy.242, s32[7168]{0:T(1024)S(1)} %pad_clamp_fusion), kind=kCustom, calls=%fused_computation.clone | custom fusion | bytes 435200 | tf_op jit(solution)/shard_map/jit(_take)/gather | solution.py:49
  45.8 10.8 %select_reduce_fusion = (f32[128,1024]{1,0:T(8,128)S(1)}, f32[128,50,1024]{2,0,1:T(8,128)}) fusion(pred[50,1024]{1,0:T(8,128)(4,1)S(1)} %iota_compare_fusion.6, bf16[128,50,112]{0,2,1:T(8,128)(2,1)S(1)} %slice_dynamic-update-slice_fusion, s32[1024]{0:T(1024)S(1)} %add_bitcast_fusion, s32[112]{0:T(128)S(1)} %and_select_fusion, ...), kind=kOutput, calls=%fused_computation.5 | convolution fusion | flops 1481785344 | bytes 28463620 | tf_op jit(solution)/shard_map/bpk,kf->bpf/dot_general | solution.py:51
  56.6 14.6 %fusion = (f32[128,1024]{1,0:T(8,128)}, f32[128,1024]{1,0:T(8,128)S(1)}) fusion(f32[128,50,1024]{2,0,1:T(8,128)} %get-tuple-element.206, f32[128,1024]{1,0:T(8,128)S(1)} %get-tuple-element.205, pred[50,1024]{1,0:T(8,128)(4,1)S(1)} %iota_compare_fusion.6, f32[128,1024]{1,0:T(8,128)S(1)} %is-finite_select_fusion.1), kind=kLoop, calls=%fused_computation.4 | loop fusion | flops 32505856 | bytes 28362752 | tf_op jit(solution)/shard_map/reduce_sum | solution.py:485
  71.5 10.4 %all_gather.32 = bf16[2,128,1024]{2,1,0:T(8,128)(2,1)S(1)} all-gather(bf16[1,128,1024]{2,1,0:T(8,128)(2,1)S(1)} %multiply_convert_fusion.5), channel_id=1, replica_groups=mesh['pipe'=2,'dir'=2,'dp'=8] {'pipe'}, dimensions={0}, use_global_device_ids=true | all-gather | bytes 786432 | tf_op jit(solution)/shard_map/all_gather | solution.py:478
  87.3 43.5 %all-gather.7.cloned.1.call-done = bf16[2,2304,2048]{2,1,0:T(8,128)(2,1)} async-done(((bf16[2,2304,128]{2,1,0:T(8,128)(2,1)}), bf16[2,2304,2048]{2,1,0:T(8,128)(2,1)}) %all-gather.7.cloned.1.call-update) | async-done | bytes 18874384 | tf_op jit(solution)/shard_map/all_gather | solution.py:543
  149.8 9.8 %all-gather = bf16[256,1024]{1,0:T(8,128)(2,1)S(1)} all-gather(bf16[128,1024]{1,0:T(8,128)(2,1)S(1)} %get-tuple-element.178), channel_id=2, replica_groups=mesh['pipe'=2,'dir'=2,'dp'=8] {'pipe'}, dimensions={0}, use_global_device_ids=true | all-gather | bytes 786432 | tf_op jit(solution)/shard_map/all_gather | solution.py:478
  166.3 6.8 all-gather.1
  181.1 13.3 %all_gather.37 = bf16[16,16,512]{2,1,0:T(8,128)(2,1)S(1)} all-gather(bf16[4,16,512]{2,1,0:T(8,128)(2,1)S(1)} %bitcast.305), channel_id=1, replica_groups=mesh['pipe'=2,'dir'=2,'dp'=8] {'dir','pipe'}, dimensions={0}, use_global_device_ids=true | all-gather | bytes 327680 | tf_op jit(solution)/shard_map/all_gather | solution.py:618
  195.5 49.9 %collective-permute-done.4 = bf16[384,512]{0,1:T(8,128)(2,1)} collective-permute-done((bf16[384,512]{0,1:T(8,128)(2,1)}, bf16[384,512]{0,1:T(8,128)(2,1)}, u32[]{:S(2)}, u32[]{:S(2)}) %collective-permute-start.4) | collective-permute-done | bytes 393248 | tf_op jit(solution)/shard_map/ppermute | solution.py:590
  261.8 305.6 %relay_lstm.1 = (bf16[16,16,512]{2,1,0:T(8,128)(2,1)}, f32[16,16,512]{2,1,0:T(8,128)}, f32[1,2048]{1,0:T(1,128)}, f32[512,512]{1,0:T(8,128)}, bf16[128,2048]{1,0...) custom-call(bf16[16,16,512]{2,1,0:T(8,128)(2,1)} %copy-done.73, ...), custom_call_target="tpu_custom_call" | custom-call | flops 299999985664 | bytes 67108864 | tf_op jit(solution)/shard_map/relay_lstm/pallas_call | solution.py:363
  574.3 14.5 %collective-permute-start.9 = (bf16[128,2048]{1,0:T(8,128)(2,1)}, bf16[128,2048]{1,0:T(8,128)(2,1)}, u32[]{:S(2)}, u32[]{:S(2)}) collective-permute-start(bf16[128,2048]{1,0:T(8,128)(2,1)} %get-tuple-element.75), channel_id=1, source_target_pairs={{19,0},{0,1},{1,2},{2,3},{3,4},{16,5},{17,6},{18,7},{23,16},{4,17}... | collective-permute-start | bytes 1572872 | tf_op jit(solution)/shard_map/ppermute | solution.py:462
  593.2 77.4 %all-to-all-start.2 = ((bf16[4,128,512]{2,1,0:T(8,128)(2,1)}), bf16[4,128,512]{2,1,0:T(8,128)(2,1)S(1)}, u32[]{:S(2)}, u32[]{:S(2)}) async-start(bf16[4,128,512]{2,1,0:T(8,128)(2,1)} %bitcast.38), calls=%async_computation.2 | async-start | bytes 1048576 | tf_op jit(solution)/shard_map/all_to_all | solution.py:654
  671.5 8.3 all-to-all-done.2
  683.6 6.3 fusion.1
  703.4 7.2 fusion.5
  728.3 8.9 collective-permute-done.13
  744.4 19.4 %all-to-all-start.3 = ((bf16[16,64,640]{2,1,0:T(8,128)(2,1)}), bf16[16,64,640]{2,1,0:T(8,128)(2,1)}, u32[]{:S(2)}, u32[]{:S(2)}) async-start(bf16[16,64,640]{2,1,0:T(8,128)(2,1)} %pad_maximum_fusion.1), calls=%async_computation.3 | async-start | bytes 2621440 | tf_op jit(solution)/shard_map/all_to_all | solution.py:712
  763.9 11.7 %multiply_convert_fusion = bf16[128,50,1024]{2,0,1:T(8,128)(2,1)S(1)} fusion(f32[128,50,1024]{2,0,1:T(8,128)} %get-tuple-element.206, f32[128,1024]{1,0:T(8,128)S(1)} %copy-done.20, f32[128,1024]{1,0:T(8,128)S(1)} %copy-done.4, f32[128,1024]{1,0:T(8,128)S(1)} %fusion.41, pred[50,1024]{1,0:T(8,128)(4,1)S(1)} %copy-done.39), kind=kLoop, calls=%fused_computation.1 | loop fusion | flops 32768000 | bytes 40945664 | tf_op jit(solution)/shard_map/convert_element_type | solution.py:486
  803.6 6.3 all-to-all-start.4
  829.6 47.4 %collective-permute-done.19 = bf16[4352,128]{1,0:T(8,128)(2,1)S(1)} collective-permute-done((bf16[4352,128]{1,0:T(8,128)(2,1)S(1)}, bf16[4352,128]{1,0:T(8,128)(2,1)S(1)}, u32[]{:S(2)}, u32[]{:S(2)}) %collective-permute-start.19) | collective-permute-done | bytes 1114144 | tf_op jit(solution)/shard_map/ppermute | solution.py:774
  884.6 9.9 %collective-permute-done.17.refs_7_ = bf16[128,2048]{1,0:T(8,128)(2,1)} collective-permute-done((bf16[128,2048]{1,0:T(8,128)(2,1)}, bf16[128,2048]{1,0:T(8,128)(2,1)}, u32[]{:S(2)}, u32[]{:S(2)}) %collective-permute-start.17) | collective-permute-done | bytes 524320 | tf_op jit(solution)/shard_map/ppermute | solution.py:462
  895.1 6.8 all-to-all-start.5
  932.4 9.3 collective-permute-done.20
  (397 shorter events, 218.0 us)
Async XLA Ops:
  7.2 123.6 %all-gather.7.cloned.1.call-start = ((), (), s32[]{:S(2)}) async-start(), calls=%async_computation.6 | async-start | bytes 20054016 | tf_op jit(solution)/shard_map/all_gather | solution.py:543
  12.1 33.7 %all-to-all-start = ((bf16[16,112,128]{2,1,0:T(8,128)(2,1)}), bf16[16,112,128]{2,1,0:T(8,128)(2,1)S(1)}, u32[]{:S(2)}, u32[]{:S(2)}) async-start(bf16[16,112,128]{2,1,0:T(8,128)(2,1)} %broadcast_in_dim.267), calls=%async_computation | async-start | bytes 917504 | tf_op jit(solution)/shard_map/all_to_all | solution.py:546
  20.4 67.0 %collective-permute-start.1 = (bf16[384,512]{0,1:T(8,128)(2,1)}, bf16[384,512]{0,1:T(8,128)(2,1)}, u32[]{:S(2)}, u32[]{:S(2)}) collective-permute-start(bf16[384,512]{0,1:T(8,128)(2,1)} %pad_maximum_fusion.9), channel_id=1, source_target_pairs={{0,16},{16,0},{1,17},{17,1},{2,18},{18,2},{3,19},{19,3},{4,20},{20... | collective-permute-start | bytes 1179656 | tf_op jit(solution)/shard_map/ppermute | solution.py:443
  26.6 55.7 %collective-permute-start = (bf16[4,128,2048]{2,1,0:T(8,128)(2,1)}, bf16[4,128,2048]{2,1,0:T(8,128)(2,1)}, u32[]{:S(2)}, u32[]{:S(2)}) collective-permute-start(bf16[4,128,2048]{2,1,0:T(8,128)(2,1)} %get-tuple-element.60), channel_id=1, source_target_pairs={{0,16},{16,0},{1,17},{17,1},{2,18},{18,2},{3,19},{19,3},{4,20},{20... | collective-permute-start | bytes 6291464 | tf_op jit(solution)/shard_map/ppermute | solution.py:443
  130.8 116.8 %all-to-all-start.1 = ((bf16[8,128,2048]{2,1,0:T(8,128)(2,1)}), bf16[8,128,2048]{2,1,0:T(8,128)(2,1)}, u32[]{:S(2)}, u32[]{:S(2)}) async-start(bf16[8,128,2048]{2,1,0:T(8,128)(2,1)} %pad_maximum_fusion), calls=%async_computation.1 | async-start | bytes 8388608 | tf_op jit(solution)/shard_map/all_to_all | solution.py:598
  135.5 455.6 %all-gather.9.cloned.1.call-start = ((), (), s32[]{:S(2)}) async-start(), calls=%async_computation.7 | async-start | bytes 4456448 | tf_op jit(solution)/shard_map/all_gather | solution.py:633
  135.7 111.9 %collective-permute-start.5 = (f32[1,2048]{1,0:T(1,128)S(1)}, f32[1,2048]{1,0:T(1,128)S(1)}, u32[]{:S(2)}, u32[]{:S(2)}) collective-permute-start(f32[1,2048]{1,0:T(1,128)S(1)} %bitcast.311), channel_id=1, source_target_pairs={{0,0},{1,1},{2,2},{3,3},{4,16},{5,17},{6,18},{7,19},{16,4},{17,5},... | collective-permute-start | bytes 24584 | tf_op jit(solution)/shard_map/ppermute | solution.py:457
  139.8 106.7 %collective-permute-start.3 = (bf16[384,512]{0,1:T(8,128)(2,1)}, bf16[384,512]{0,1:T(8,128)(2,1)}, u32[]{:S(2)}, u32[]{:S(2)}) collective-permute-start(bf16[384,512]{0,1:T(8,128)(2,1)} %slice_bitcast_fusion), channel_id=1, source_target_pairs={{0,0},{1,1},{2,2},{3,3},{4,16},{5,17},{6,18},{7,19},{16,4},{17,5},... | collective-permute-start | bytes 1179656 | tf_op jit(solution)/shard_map/ppermute | solution.py:457
  142.8 102.7 %collective-permute-start.4 = (bf16[384,512]{0,1:T(8,128)(2,1)}, bf16[384,512]{0,1:T(8,128)(2,1)}, u32[]{:S(2)}, u32[]{:S(2)}) collective-permute-start(bf16[384,512]{0,1:T(8,128)(2,1)} %collective-permute-done.1), channel_id=1, source_target_pairs={{0,4},{1,5},{2,6},{3,7},{20,16},{21,17},{22,18},{23,19},{8,12},{9,... | collective-permute-start | bytes 1179656 | tf_op jit(solution)/shard_map/ppermute | solution.py:590
  194.8 52.8 %collective-permute-start.2 = (bf16[16,16,512]{2,1,0:T(8,128)(2,1)S(1)}, bf16[16,16,512]{2,1,0:T(8,128)(2,1)S(1)}, u32[]{:S(2)}, u32[]{:S(2)}) collective-permute-start(bf16[16,16,512]{2,1,0:T(8,128)(2,1)S(1)} %bitcast.300), channel_id=1, source_target_pairs={{0,4},{1,5},{2,6},{3,7},{20,20},{21,21},{22,22},{23,23},{8,12},{9,... | collective-permute-start | bytes 786440 | tf_op jit(solution)/shard_map/ppermute | solution.py:622
  251.7 339.4 %all-gather.11.cloned.1.call-start = ((), (), s32[]{:S(2)}) async-start(), calls=%async_computation.8 | async-start | bytes 4456448 | tf_op jit(solution)/shard_map/all_gather | solution.py:633
  574.3 154.0 %collective-permute-start.9 = (bf16[128,2048]{1,0:T(8,128)(2,1)}, bf16[128,2048]{1,0:T(8,128)(2,1)}, u32[]{:S(2)}, u32[]{:S(2)}) collective-permute-start(bf16[128,2048]{1,0:T(8,128)(2,1)} %get-tuple-element.75), channel_id=1, source_target_pairs={{19,0},{0,1},{1,2},{2,3},{3,4},{16,5},{17,6},{18,7},{23,16},{4,17}... | collective-permute-start | bytes 1572872 | tf_op jit(solution)/shard_map/ppermute | solution.py:462
  588.8 139.5 %collective-permute-start.10 = (bf16[128,2048]{1,0:T(8,128)(2,1)}, bf16[128,2048]{1,0:T(8,128)(2,1)}, u32[]{:S(2)}, u32[]{:S(2)}) collective-permute-start(bf16[128,2048]{1,0:T(8,128)(2,1)} %get-tuple-element.76), channel_id=1, source_target_pairs={{18,0},{19,1},{0,2},{1,3},{2,4},{3,5},{16,6},{17,7},{22,16},{23,17... | collective-permute-start | bytes 1572872 | tf_op jit(solution)/shard_map/ppermute | solution.py:462
  588.9 139.5 %collective-permute-start.11 = (bf16[128,2048]{1,0:T(8,128)(2,1)}, bf16[128,2048]{1,0:T(8,128)(2,1)}, u32[]{:S(2)}, u32[]{:S(2)}) collective-permute-start(bf16[128,2048]{1,0:T(8,128)(2,1)} %get-tuple-element.77), channel_id=1, source_target_pairs={{17,0},{18,1},{19,2},{0,3},{1,4},{2,5},{3,6},{16,7},{21,16},{22,17... | collective-permute-start | bytes 1572872 | tf_op jit(solution)/shard_map/ppermute | solution.py:462
  591.1 137.3 %collective-permute-start.12 = (bf16[128,2048]{1,0:T(8,128)(2,1)}, bf16[128,2048]{1,0:T(8,128)(2,1)}, u32[]{:S(2)}, u32[]{:S(2)}) collective-permute-start(bf16[128,2048]{1,0:T(8,128)(2,1)} %get-tuple-element.78), channel_id=1, source_target_pairs={{16,0},{17,1},{18,2},{19,3},{0,4},{1,5},{2,6},{3,7},{20,16},{21,17... | collective-permute-start | bytes 1572872 | tf_op jit(solution)/shard_map/ppermute | solution.py:462
  593.2 86.6 %all-to-all-start.2 = ((bf16[4,128,512]{2,1,0:T(8,128)(2,1)}), bf16[4,128,512]{2,1,0:T(8,128)(2,1)S(1)}, u32[]{:S(2)}, u32[]{:S(2)}) async-start(bf16[4,128,512]{2,1,0:T(8,128)(2,1)} %bitcast.38), calls=%async_computation.2 | async-start | bytes 1048576 | tf_op jit(solution)/shard_map/all_to_all | solution.py:654
  670.7 127.1 %all-gather.13.cloned.1.call-start = ((), (), s32[]{:S(2)}) async-start(), calls=%async_computation.9 | async-start | bytes 1114112 | tf_op jit(solution)/shard_map/all_gather | solution.py:662
  744.4 50.1 %all-to-all-start.3 = ((bf16[16,64,640]{2,1,0:T(8,128)(2,1)}), bf16[16,64,640]{2,1,0:T(8,128)(2,1)}, u32[]{:S(2)}, u32[]{:S(2)}) async-start(bf16[16,64,640]{2,1,0:T(8,128)(2,1)} %pad_maximum_fusion.1), calls=%async_computation.3 | async-start | bytes 2621440 | tf_op jit(solution)/shard_map/all_to_all | solution.py:712
  803.6 73.5 %all-to-all-start.4 = ((bf16[32,2,4864]{2,1,0:T(2,128)(2,1)}), bf16[32,2,4864]{2,1,0:T(2,128)(2,1)}, u32[]{:S(2)}, u32[]{:S(2)}) async-start(bf16[32,2,4864]{2,1,0:T(2,128)(2,1)} %reshape.689), calls=%async_computation.4 | async-start | bytes 1245184 | tf_op jit(solution)/shard_map/all_to_all | solution.py:739
  815.1 61.9 %collective-permute-start.19 = (bf16[4352,128]{1,0:T(8,128)(2,1)S(1)}, bf16[4352,128]{1,0:T(8,128)(2,1)S(1)}, u32[]{:S(2)}, u32[]{:S(2)}) collective-permute-start(bf16[4352,128]{1,0:T(8,128)(2,1)S(1)} %pad_maximum_fusion.3), channel_id=1, source_target_pairs={{0,16},{16,0},{1,17},{17,1},{2,18},{18,2},{3,19},{19,3},{4,20},{20... | collective-permute-start | bytes 3342344 | tf_op jit(solution)/shard_map/ppermute | solution.py:774
  815.2 69.3 %collective-permute-start.14 = (bf16[128,2048]{1,0:T(8,128)(2,1)}, bf16[128,2048]{1,0:T(8,128)(2,1)}, u32[]{:S(2)}, u32[]{:S(2)}) collective-permute-start(bf16[128,2048]{1,0:T(8,128)(2,1)} %get-tuple-element.82), channel_id=1, source_target_pairs={{0,0},{1,1},{2,2},{3,3},{16,4},{17,5},{18,6},{19,7},{4,16},{5,17},... | collective-permute-start | bytes 1572872 | tf_op jit(solution)/shard_map/ppermute | solution.py:462
  820.3 64.2 %collective-permute-start.15 = (bf16[128,2048]{1,0:T(8,128)(2,1)}, bf16[128,2048]{1,0:T(8,128)(2,1)}, u32[]{:S(2)}, u32[]{:S(2)}) collective-permute-start(bf16[128,2048]{1,0:T(8,128)(2,1)} %get-tuple-element.87), channel_id=1, source_target_pairs={{3,0},{16,1},{17,2},{18,3},{19,4},{0,5},{1,6},{2,7},{7,16},{20,17}... | collective-permute-start | bytes 1572872 | tf_op jit(solution)/shard_map/ppermute | solution.py:462
  822.9 61.7 %collective-permute-start.16 = (bf16[128,2048]{1,0:T(8,128)(2,1)}, bf16[128,2048]{1,0:T(8,128)(2,1)}, u32[]{:S(2)}, u32[]{:S(2)}) collective-permute-start(bf16[128,2048]{1,0:T(8,128)(2,1)} %get-tuple-element.88), channel_id=1, source_target_pairs={{2,0},{3,1},{16,2},{17,3},{18,4},{19,5},{0,6},{1,7},{6,16},{7,17},... | collective-permute-start | bytes 1572872 | tf_op jit(solution)/shard_map/ppermute | solution.py:462
  822.9 71.6 %collective-permute-start.17 = (bf16[128,2048]{1,0:T(8,128)(2,1)}, bf16[128,2048]{1,0:T(8,128)(2,1)}, u32[]{:S(2)}, u32[]{:S(2)}) collective-permute-start(bf16[128,2048]{1,0:T(8,128)(2,1)} %get-tuple-element.89), channel_id=1, source_target_pairs={{1,0},{2,1},{3,2},{16,3},{17,4},{18,5},{19,6},{0,7},{5,16},{6,17},... | collective-permute-start | bytes 1572872 | tf_op jit(solution)/shard_map/ppermute | solution.py:462
  (84 other events, 2061.1 us)
Sparse Core Ops, SparseCore 0:
  11.3 119.4 all-gather.6
  251.8 66.1 all-gather.8
  320.3 62.5 all-gather.10
  693.8 50.2 all-gather.12
